TPU v7x, 128 devices: a whole 4x4x4 slice. The times are simulated.
128 devices in a mesh: row: 16 (over x, y), col: 8 (over z, core).
Axes of the slice: x: 4, y: 4, z: 4, core: 2. Of those that a mesh axis runs over, the one named last changes fastest.
Arguments:
- hidden_input: bfloat16 [8192, 4096], P('row', 'col'), may hold values from -6 to 6
- input_norm_gain: bfloat16 [4096], replicated, may hold values from 0.5 to 1.5
- query_norm_gain: bfloat16 [128], replicated, may hold values from 0.099609375 to 1.8984375
- key_norm_gain: bfloat16 [128], replicated, may hold values from 0.5 to 1.5
- query_key_value_weight: bfloat16 [4096, 6144], P('row', 'col'), may hold values from -0.09375 to 0.09375
- output_weight: bfloat16 [4096, 4096], P('row', 'col'), may hold values from -0.25 to 0.25
- adapter_down_maps: bfloat16 [16, 32, 4096], P('row'), may hold values from -0.09375 to 0.09375
- adapter_up_maps: bfloat16 [16, 16, 5120], P('row', None, 'col'), may hold values from -1.5 to 1.5
- output_down_maps: bfloat16 [16, 16, 4096], P('row', None, 'col'), may hold values from -0.25 to 0.25
- output_up_maps: bfloat16 [16, 16, 4096], P('row'), may hold values from -1.5 to 1.5
- prompt_adapter: int32 [64], P('row'), may hold values from 0 to 15
- adapter_position: int32 [16], replicated, may hold values from 0 to 15, each once
- prompt_length: int32 [16, 4], P('row'), may hold values from 1 to 256, 512 in all within a row
- cache_length: int32 [64], P('row'), may hold values from 0 to 1024, as said below
- page_owner_row: int32 [256, 1], replicated, may hold values from 0 to 15; in each aligned block of 16 rows (0 to 15, 16 to 31, ...) at most 2 rows name the same one
- page_store_index: int32 [256], replicated, may hold values from 0 to 7
- cache_page_store: bfloat16 [128, 2, 128, 1024], P('row', None, None, 'col'), may hold values from -160 to 160, as said below
Outputs:
- hidden_output: bfloat16 [8192, 4096], P('row', 'col')
- new_cache: bfloat16 [2, 8192, 1024], P(None, 'row', 'col')
Inputs may be any that keep to these rules, and one draw needn't show every extreme that they name: `adapter_position`: a permutation of the slots. `prompt_length`: each row of 4 lengths sums to 512; the largest of each row is exactly 256. `cache_length`: among the 4 prompts of each row group exactly 2 have a cached prefix, longer than 896; the others have 0; some prompt has exactly 1024. `page_owner_row`: in each aligned block of 16 requests (those of one row group) no holder is named more than 2 times, and in some block some holder exactly 2 times. `cache_page_store`: finite values.
All inputs are finite; a program needn't handle non-finite values.
Results may differ from a plain program's by a relative error of at most 0.018.
The roundings to bfloat16 on the way count: a program that leaves them out, or rounds other values in their place, can miss the bound.
Values may be sent and summed in bfloat16 or wider, within the bound.
No kernel may reach another device: no remote copies, remote signals or barrier semaphores. Data moves between devices by JAX's collectives and lax.ppermute only.
A program may use at most 128 MiB of HBM per device.

v0:
```python
import math

import jax
import jax.numpy as jnp
from jax import lax
from jax.sharding import PartitionSpec as P

QUERY_HEADS = 32
KEY_VALUE_HEADS = 8
HEAD_WIDTH = 128
WIN = 1024
SINKS = 4


EPSILON = 1e-06
ROPE_BASE = 1000000.0
ADAPTER_SCALE = 0.5


def rms_norm(tensor, gain_vector):
    scale_back = lax.rsqrt(jnp.mean(tensor * tensor, axis=-1, keepdims=True) + EPSILON)
    return tensor * scale_back * gain_vector.astype(jnp.float32)


def rotate(tensor, position):
    half_width = tensor.shape[-1] // 2
    frequency = ROPE_BASE ** (-2.0 * jnp.arange(half_width, dtype=jnp.float32) / tensor.shape[-1])
    angles = position.astype(jnp.float32)[:, None] * frequency[None, :]
    cosine = jnp.cos(angles)[:, None, :]
    sine_part = jnp.sin(angles)[:, None, :]
    front_half = tensor[..., :half_width]
    back_half = tensor[..., half_width:]
    return jnp.concatenate(
        [front_half * cosine - back_half * sine_part, back_half * cosine + front_half * sine_part],
        axis=-1,
    )


def token_meta(lengths, cached, token_count):
    end_index = jnp.cumsum(lengths, dtype=jnp.int32)
    starts = end_index - lengths
    token_index = jnp.arange(token_count, dtype=jnp.int32)
    prompt_id = jnp.sum(
        (token_index[:, None] >= end_index[None, :]).astype(jnp.int32), axis=1, dtype=jnp.int32
    )
    onehot = prompt_id[:, None] == jnp.arange(lengths.shape[0], dtype=jnp.int32)[None, :]
    start_at = jnp.sum(jnp.where(onehot, starts[None, :], 0), axis=1, dtype=jnp.int32)
    prefix = jnp.sum(jnp.where(onehot, cached[None, :], 0), axis=1, dtype=jnp.int32)
    return (prompt_id, prefix + token_index - start_at, onehot)


def cache_meta(cached, requests, page_size):
    pages_each = WIN // page_size
    has_cache = (cached > 0).astype(jnp.int32)
    order_rank = jnp.cumsum(has_cache, dtype=jnp.int32) - 1
    prompt_ids = jnp.arange(cached.shape[0], dtype=jnp.int32)
    request_ids = jnp.arange(requests, dtype=jnp.int32)
    owns_request = (has_cache[None, :] > 0) & (
        order_rank[None, :] == (request_ids // pages_each)[:, None]
    )
    owners = jnp.sum(jnp.where(owns_request, prompt_ids[None, :], 0), axis=1, dtype=jnp.int32)
    owner_len = jnp.sum(jnp.where(owns_request, cached[None, :], 0), axis=1, dtype=jnp.int32)
    within = jnp.arange(page_size, dtype=jnp.int32)
    key_pos = (request_ids % pages_each * page_size)[:, None] + within[None, :]
    key_prompt = jnp.broadcast_to(owners[:, None], (requests, page_size)).reshape(-1)
    key_valid = key_pos < owner_len[:, None]
    return (key_prompt, key_pos.reshape(-1), key_valid.reshape(-1))


def attend(queries, key_rows, values, query_prompt, query_pos, key_prompt, key_pos, key_valid):
    scores = lax.dot_general(
        queries, key_rows, (((1,), (1,)), ((), ())), preferred_element_type=jnp.float32
    )
    scores = scores / math.sqrt(queries.shape[-1])
    visible = (
        (key_prompt[None, :] == query_prompt[:, None])
        & (key_pos[None, :] <= query_pos[:, None])
        & key_valid[None, :]
    )
    visible = visible & ((key_pos[None, :] < SINKS) | (key_pos[None, :] > query_pos[:, None] - WIN))
    scores = jnp.where(visible, scores, -jnp.inf)
    row_max = jnp.max(scores, axis=1, keepdims=True)
    weights = jnp.exp(scores - row_max)
    weights = (weights / jnp.sum(weights, axis=1, keepdims=True)).astype(jnp.bfloat16)
    return jnp.dot(weights, values, preferred_element_type=jnp.float32).astype(jnp.bfloat16)


def attend_group(queries, keys_new, values_new, prompt_id, position, cached, fetched):
    token_count, group_count, group_width, head_size = queries.shape
    requests = fetched.shape[0]
    page_size = fetched.shape[2]
    key_prompt_c, key_pos_c, key_valid_c = cache_meta(cached, requests, page_size)
    key_prompt = jnp.concatenate([prompt_id, key_prompt_c])
    key_pos = jnp.concatenate([position, key_pos_c])
    key_valid = jnp.concatenate([jnp.ones((token_count,), jnp.bool_), key_valid_c])
    cache_keys = fetched[:, 0].reshape(requests * page_size, group_count, head_size)
    cache_values = fetched[:, 1].reshape(requests * page_size, group_count, head_size)
    keys_all = jnp.concatenate([keys_new, cache_keys], axis=0)
    values_all = jnp.concatenate([values_new, cache_values], axis=0)
    row_count = token_count * group_width
    block_rows = min(512, row_count)
    query_prompt = jnp.repeat(prompt_id, group_width).reshape(-1, block_rows)
    query_pos = jnp.repeat(position, group_width).reshape(-1, block_rows)
    query_blocks = queries[:, 0].reshape(-1, block_rows, head_size)
    group_keys = keys_all[:, 0]
    group_values = values_all[:, 0]

    def one_block(block_items):
        return attend(
            block_items[0],
            group_keys,
            group_values,
            block_items[1],
            block_items[2],
            key_prompt,
            key_pos,
            key_valid,
        )

    outputs = [
        lax.map(one_block, (query_blocks, query_prompt, query_pos)).reshape(
            token_count, group_width, head_size
        )
    ]
    return jnp.stack(outputs, axis=1)


def adapter_change(normalized, selector, adapter_down_maps, adapter_up_maps, group_width):
    adapter_list, twice_rank, feature_total = adapter_down_maps.shape
    rank_width = twice_rank // 2
    rank_features = lax.dot_general(
        normalized,
        adapter_down_maps.reshape(adapter_list * twice_rank, feature_total),
        (((1,), (1,)), ((), ())),
        preferred_element_type=jnp.float32,
    )
    rank_features = rank_features.reshape(-1, adapter_list, 2, rank_width)
    rank_features = jnp.where(selector[:, :, None, None], rank_features, 0.0).astype(jnp.bfloat16)
    group_count = adapter_up_maps.shape[2] // ((group_width + 1) * HEAD_WIDTH)
    up_pieces = adapter_up_maps.reshape(
        adapter_list, rank_width, group_count, group_width + 1, HEAD_WIDTH
    )
    up_query = up_pieces[:, :, :, :group_width, :].reshape(
        adapter_list * rank_width, group_count * group_width * HEAD_WIDTH
    )
    up_value = up_pieces[:, :, :, group_width, :].reshape(
        adapter_list * rank_width, group_count * HEAD_WIDTH
    )
    query_change = jnp.dot(
        rank_features[:, :, 0, :].reshape(-1, adapter_list * rank_width),
        up_query,
        preferred_element_type=jnp.float32,
    )
    value_change = jnp.dot(
        rank_features[:, :, 1, :].reshape(-1, adapter_list * rank_width),
        up_value,
        preferred_element_type=jnp.float32,
    )
    return (
        query_change.reshape(-1, group_count, group_width, HEAD_WIDTH),
        value_change.reshape(-1, group_count, HEAD_WIDTH),
    )


def project_heads(
    base_out, query_change, value_change, query_norm_gain, key_norm_gain, position, group_width
):
    token_count = base_out.shape[0]
    group_count = base_out.shape[1] // ((group_width + 2) * HEAD_WIDTH)
    column_list = base_out.reshape(token_count, group_count, group_width + 2, HEAD_WIDTH)
    unrotated_query = column_list[:, :, :group_width, :] + ADAPTER_SCALE * query_change
    raw_key = column_list[:, :, group_width, :]
    unnormed_value = column_list[:, :, group_width + 1, :] + ADAPTER_SCALE * value_change
    queries = rotate(
        rms_norm(unrotated_query, query_norm_gain).reshape(
            token_count, group_count * group_width, HEAD_WIDTH
        ),
        position,
    )
    queries = queries.astype(jnp.bfloat16).reshape(
        token_count, group_count, group_width, HEAD_WIDTH
    )
    keys_new = rotate(rms_norm(raw_key, key_norm_gain), position).astype(jnp.bfloat16)
    values_new = unnormed_value.astype(jnp.bfloat16)
    return (queries, keys_new, values_new)


def output_change(attention_output, selector, output_down_maps, output_up_maps):
    adapter_list, rank_width, head_columns = output_down_maps.shape
    reduced_sum = lax.dot_general(
        attention_output,
        output_down_maps.reshape(adapter_list * rank_width, head_columns),
        (((1,), (1,)), ((), ())),
        preferred_element_type=jnp.float32,
    )
    reduced_sum = jnp.where(
        selector[:, :, None], reduced_sum.reshape(-1, adapter_list, rank_width), 0.0
    ).reshape(-1, adapter_list * rank_width)
    return jnp.dot(
        reduced_sum,
        output_up_maps.reshape(adapter_list * rank_width, -1).astype(jnp.float32),
        precision=lax.Precision.HIGHEST,
    )


def on_device(
    hidden_input,
    input_norm_gain,
    query_norm_gain,
    key_norm_gain,
    query_key_value_weight,
    output_weight,
    adapter_down_maps,
    adapter_up_maps,
    output_down_maps,
    output_up_maps,
    prompt_adapter,
    adapter_position,
    prompt_length,
    cache_length,
    page_owner_row,
    page_store_index,
    cache_page_store,
):
    group_width = QUERY_HEADS // KEY_VALUE_HEADS
    token_count = hidden_input.shape[0]
    gathered = lax.all_gather(hidden_input, "col", axis=1, tiled=True)
    normalized = rms_norm(gathered.astype(jnp.float32), input_norm_gain).astype(jnp.bfloat16)
    base_out = jnp.dot(
        normalized,
        lax.all_gather(query_key_value_weight, "row", axis=0, tiled=True),
        preferred_element_type=jnp.float32,
    )
    out_rows, in_all, up_all, output_down_all, output_up_every = (
        lax.all_gather(output_weight, "row", axis=0, tiled=True),
        lax.all_gather(adapter_down_maps, "row", axis=0, tiled=True),
        lax.all_gather(adapter_up_maps, "row", axis=0, tiled=True),
        lax.all_gather(output_down_maps, "row", axis=0, tiled=True),
        lax.all_gather(output_up_maps, "row", axis=0, tiled=True),
    )
    prompt_id, position, onehot = token_meta(prompt_length[0], cache_length, token_count)
    adapter_list = in_all.shape[0]
    adapter_ids = jnp.arange(adapter_list, dtype=jnp.int32)
    slot_prompt = jnp.sum(
        jnp.where(prompt_adapter[:, None] == adapter_ids[None, :], adapter_position[None, :], 0),
        axis=1,
        dtype=jnp.int32,
    )
    slot_token = jnp.sum(jnp.where(onehot, slot_prompt[None, :], 0), axis=1, dtype=jnp.int32)
    selector = slot_token[:, None] == adapter_ids[None, :]
    query_change, value_change = adapter_change(normalized, selector, in_all, up_all, group_width)
    queries, keys_new, values_new = project_heads(
        base_out, query_change, value_change, query_norm_gain, key_norm_gain, position, group_width
    )
    group_count = keys_new.shape[1]
    new_cache = jnp.stack(
        [
            keys_new.reshape(token_count, group_count * HEAD_WIDTH),
            values_new.reshape(token_count, group_count * HEAD_WIDTH),
        ]
    )
    rows_total = lax.axis_size("row")
    my_row = lax.axis_index("row")
    holders_all = page_owner_row.reshape(rows_total, -1)
    slots_all = page_store_index.reshape(rows_total, -1)
    requests = holders_all.shape[1]
    my_holders = lax.dynamic_index_in_dim(holders_all, my_row, 0, keepdims=False)
    my_slots = lax.dynamic_index_in_dim(slots_all, my_row, 0, keepdims=False)
    pages_dev = cache_page_store.shape[0]
    wanted = my_holders * pages_dev + my_slots
    blank_pages = jnp.zeros((requests,) + cache_page_store.shape[1:], jnp.bfloat16)
    block_in = lax.all_gather(cache_page_store, "row", axis=0, tiled=True)
    offset = jnp.int32(0)
    amount = block_in.shape[0]
    inside = (wanted >= offset) & (wanted < offset + amount)
    local_index = jnp.clip(wanted, 0, amount - 1)
    chosen = jnp.take(block_in, local_index, axis=0)
    fetched = jnp.where(inside[:, None, None, None], chosen, blank_pages)
    attention_output = attend_group(
        queries, keys_new, values_new, prompt_id, position, cache_length, fetched
    ).reshape(token_count, -1)
    head_rows = lax.all_to_all(out_rows, "col", split_axis=0, concat_axis=1, tiled=True)
    running = jnp.dot(
        attention_output, head_rows, preferred_element_type=jnp.float32
    ) + ADAPTER_SCALE * output_change(attention_output, selector, output_down_all, output_up_every)
    summed = lax.psum_scatter(
        running.astype(jnp.bfloat16), "col", scatter_dimension=1, tiled=True
    ).astype(jnp.float32)
    hidden_output = (hidden_input.astype(jnp.float32) + summed).astype(jnp.bfloat16)
    return (hidden_output, new_cache)


def solution(mesh):
    return jax.shard_map(
        on_device,
        mesh=mesh,
        in_specs=(
            P("row", "col"),
            P(),
            P(),
            P(),
            P("row", "col"),
            P("row", "col"),
            P("row", None, None),
            P("row", None, "col"),
            P("row", None, "col"),
            P("row", None, None),
            P("row"),
            P(),
            P("row", None),
            P("row"),
            P(),
            P(),
            P("row", None, None, "col"),
        ),
        out_specs=(P("row", "col"), P(None, "row", "col")),
        check_vma=False,
    )
```

profile of v0, /device:TPU:1, one launch (start us, length us, event | category | flops | bytes accessed | tf_op | source)
XLA Modules:
  0.0 406.9 jit_solution(12492953858304055617)
XLA Ops:
  15.1 21.0 %all_gather.27 = bf16[16,16,640]{2,1,0:T(8,128)(2,1)S(1)} all-gather(bf16[1,16,640]{2,1,0:T(8,128)(2,1)} %param.26), channel_id=1, replica_groups=mesh['row'=16,'col'=8] {'row'}, dimensions={0}, use_global_device_ids=true | all-gather | bytes 348160 | tf_op jit(solution)/shard_map/all_gather | solution.py:237
  40.2 24.7 %all-gather.15.cloned.1.call-done = bf16[4096,512]{1,0:T(8,128)(2,1)} async-done(((bf16[256,512]{1,0:T(8,128)(2,1)}), bf16[4096,512]{1,0:T(8,128)(2,1)}) %all-gather.15.cloned.1.call-update) | async-done | bytes 4194320 | tf_op jit(solution)/shard_map/all_gather | solution.py:235
  64.8 5.3 %all-to-all-start = ((bf16[8,512,512]{2,1,0:T(8,128)(2,1)}), bf16[8,512,512]{2,1,0:T(8,128)(2,1)}, u32[]{:S(2)}, u32[]{:S(2)}) async-start(bf16[8,512,512]{2,1,0:T(8,128)(2,1)} %bitcast.136), calls=%async_computation | async-start | bytes 8388608 | tf_op jit(solution)/shard_map/all_to_all | solution.py:282
  70.1 20.1 %all_gather.30 = bf16[16,16,512]{2,1,0:T(8,128)(2,1)S(1)} all-gather(bf16[1,16,512]{2,1,0:T(8,128)(2,1)S(1)} %copy-done.1), channel_id=1, replica_groups=mesh['row'=16,'col'=8] {'row'}, dimensions={0}, use_global_device_ids=true | all-gather | bytes 278528 | tf_op jit(solution)/shard_map/all_gather | solution.py:238
  90.8 30.0 %all-gather.7.cloned.1.call-done = bf16[512,4096]{1,0:T(8,128)(2,1)} async-done(((bf16[512,512]{1,0:T(8,128)(2,1)}), bf16[512,4096]{1,0:T(8,128)(2,1)}) %all-gather.7.cloned.1.call-update) | async-done | bytes 4194320 | tf_op jit(solution)/shard_map/all_gather | solution.py:227
  120.8 3.1 fusion.8
  123.9 49.3 %all-gather.11.cloned.1.call-done = bf16[16,32,4096]{2,1,0:T(8,128)(2,1)} async-done(((bf16[1,32,4096]{2,1,0:T(8,128)(2,1)}), bf16[16,32,4096]{2,1,0:T(8,128)(2,1)}) %all-gather.11.cloned.1.call-update) | async-done | bytes 4194320 | tf_op jit(solution)/shard_map/all_gather | solution.py:236
  173.2 5.9 %fusion.20 = bf16[512,16,2,16]{0,3,2,1:T(8,128)(2,1)S(1)} fusion(bf16[16,2,16,4096]{3,2,1,0:T(8,128)(2,1)} %bitcast.158, bf16[512,4096]{1,0:T(8,128)(2,1)} %all-gather.7.cloned.1.call-done, f32[4096]{0:T(1024)S(1)} %convert_element_type.85, f32[512]{0:T(512)S(1)} %add_rsqrt_fusion.2, pred[512,16]{0,1:T(8,128)(4,1)S(1)} %iota_compare_fusion), kind=kOutput, calls=%fused_computation.30 | convolution fusion | flops 2156396544 | bytes 8939520 | tf_op jit(solution)/shard_map/dot_general | solution.py:131
  179.2 6.7 %copy.54 = bf16[512,8,512]{0,2,1:T(8,128)(2,1)} copy(bf16[512,8,512]{2,0,1:T(8,128)(2,1)} %bitcast.41) | data formatting | bytes 8388608 | tf_op jit(solution)/shard_map/all_to_all | solution.py:282
  185.8 50.3 %all-gather.9.cloned.1.call-done = bf16[4096,768]{1,0:T(8,128)(2,1)} async-done(((bf16[256,768]{1,0:T(8,128)(2,1)}), bf16[4096,768]{1,0:T(8,128)(2,1)}) %all-gather.9.cloned.1.call-update) | async-done | bytes 6291472 | tf_op jit(solution)/shard_map/all_gather | solution.py:231
  236.2 7.2 %fusion.24 = f32[512,768]{0,1:T(8,128)S(1)} fusion(bf16[4096,768]{1,0:T(8,128)(2,1)} %all-gather.9.cloned.1.call-done, bf16[512,4096]{1,0:T(8,128)(2,1)} %all-gather.7.cloned.1.call-done, f32[4096]{0:T(1024)S(1)} %convert_element_type.85, f32[512]{0:T(512)S(1)} %add_rsqrt_fusion.2), kind=kOutput, calls=%fused_computation.32 | convolution fusion | flops 3229614080 | bytes 12077056 | tf_op jit(solution)/shard_map/dot_general | solution.py:229
  245.2 1.2 fusion.33
  247.9 60.6 %all-gather.13.cloned.1.call-done = bf16[128,2,128,128]{3,2,1,0:T(8,128)(2,1)} async-done(((bf16[8,2,128,128]{3,2,1,0:T(8,128)(2,1)}), bf16[128,2,128,128]{3,2,1,0:T(8,128)(2,1)}) %all-gather.13.cloned.1.call-update) | async-done | bytes 8388624 | tf_op jit(solution)/shard_map/all_gather | solution.py:272
  308.5 4.1 %gather_fusion = bf16[16,2,128,128]{3,2,1,0:T(8,128)(2,1)S(1)} fusion(bf16[128,2,128,128]{3,2,1,0:T(8,128)(2,1)} %all-gather.13.cloned.1.call-done, s32[1024]{0:T(1024)S(1)} %pad_clamp_fusion), kind=kCustom, calls=%fused_computation | custom fusion | bytes 2097216 | tf_op jit(solution)/shard_map/jit(_take)/gather | solution.py:277
  313.2 21.6 %while.12 = (s32[]{:T(128)}, bf16[4,512,128]{2,1,0:T(8,128)(2,1)S(1)}, s32[2560]{0:T(1024)S(1)}, s32[4,512]{1,0:T(4,128)S(1)}, s32[2560]{0:T(1024)S(1)}, /*index...) while((s32[]{:T(128)}, ...), condition=%wide.region_15.16_spmd, body=%wide.region_12.15_spmd.sunk | while | flops 690817024 | bytes 17368704 | solution.py:121
  313.2 3.4 fusion.70
  318.6 3.4 fusion.70
  323.9 3.4 fusion.70
  329.3 3.4 fusion.70
  335.8 7.8 %fusion.48 = f32[512,4096]{1,0:T(8,128)} fusion(bf16[512,512]{1,0:T(8,128)(2,1)S(1)} %reshape_stack_reshape.3, bf16[512,4096]{0,1:T(8,128)(2,1)} %bitcast.135), kind=kOutput, calls=%fused_computation.111 | convolution fusion | flops 2147483648 | bytes 13107200 | tf_op jit(solution)/shard_map/dot_general | solution.py:283
  343.6 10.7 %all-gather.17.cloned.1.call-done = bf16[16,16,4096]{2,1,0:T(8,128)(2,1)} async-done(((bf16[1,16,4096]{2,1,0:T(8,128)(2,1)}), bf16[16,16,4096]{2,1,0:T(8,128)(2,1)}) %all-gather.17.cloned.1.call-update) | async-done | bytes 2097168 | tf_op jit(solution)/shard_map/all_gather | solution.py:239
  354.2 8.3 %fusion.12 = bf16[512,4096]{1,0:T(8,128)(2,1)} fusion(f32[512,4096]{1,0:T(8,128)} %fusion.48, f32[512,16,16]{0,2,1:T(8,128)S(1)} %convolution_select_fusion, bf16[16,16,4096]{2,1,0:T(8,128)(2,1)} %all-gather.17.cloned.1.call-done), kind=kOutput, calls=%fused_computation.23 | convolution fusion | flops 6448742400 | bytes 15204352 | tf_op jit(solution)/shard_map/dot_general | solution.py:199
  363.4 34.7 %reduce-scatter.2.cloned.1.call-done = bf16[512,512]{1,0:T(8,128)(2,1)} async-done(((bf16[512,4096]{1,0:T(8,128)(2,1)}), bf16[512,512]{1,0:T(8,128)(2,1)}) %reduce-scatter.2.cloned.1.call-update) | async-done | bytes 524304 | tf_op jit(solution)/shard_map/reduce_scatter | solution.py:286
  398.1 2.0 add_convert_fusion
  (115 shorter events, 25.5 us)
Async XLA Ops:
  7.2 31.3 %copy-start.2 = (bf16[4096]{0:T(1024)(128)(2,1)S(1)}, bf16[4096]{0:T(1024)(128)(2,1)}, u32[]{:S(2)}) copy-start(bf16[4096]{0:T(1024)(128)(2,1)} %param.20) | copy-start | bytes 24580
  7.2 31.5 %copy-start.5 = (bf16[128]{0:T(256)(128)(2,1)S(1)}, bf16[128]{0:T(256)(128)(2,1)}, u32[]{:S(2)}) copy-start(bf16[128]{0:T(256)(128)(2,1)} %param.21) | copy-start | bytes 772
  7.2 31.5 %copy-start.3 = (s32[256]{0:T(256)S(1)}, s32[256]{0:T(256)}, u32[]{:S(2)}) copy-start(s32[256]{0:T(256)} %param.34) | copy-start | bytes 3076
  7.2 32.1 %copy-start.4 = (s32[256,1]{0,1:T(1,128)S(1)}, s32[256,1]{0,1:T(1,128)}, u32[]{:S(2)}) copy-start(s32[256,1]{0,1:T(1,128)} %param.33) | copy-start | bytes 3076
  7.2 32.9 %copy-start.6 = (bf16[128]{0:T(256)(128)(2,1)S(1)}, bf16[128]{0:T(256)(128)(2,1)}, u32[]{:S(2)}) copy-start(bf16[128]{0:T(256)(128)(2,1)} %param.22) | copy-start | bytes 772
  7.2 57.6 %all-gather.15.cloned.1.call-start = ((), (), s32[]{:S(2)}) async-start(), calls=%async_computation.6 | async-start | bytes 4456448 | tf_op jit(solution)/shard_map/all_gather | solution.py:235
  7.9 112.9 %all-gather.7.cloned.1.call-start = ((), (), s32[]{:S(2)}) async-start(), calls=%async_computation.2 | async-start | bytes 4718592 | tf_op jit(solution)/shard_map/all_gather | solution.py:227
  8.7 164.5 %all-gather.11.cloned.1.call-start = ((), (), s32[]{:S(2)}) async-start(), calls=%async_computation.4 | async-start | bytes 4456448 | tf_op jit(solution)/shard_map/all_gather | solution.py:236
  9.4 226.8 %all-gather.9.cloned.1.call-start = ((), (), s32[]{:S(2)}) async-start(), calls=%async_computation.3 | async-start | bytes 6684672 | tf_op jit(solution)/shard_map/all_gather | solution.py:231
  10.0 298.5 %all-gather.13.cloned.1.call-start = ((), (), s32[]{:S(2)}) async-start(), calls=%async_computation.5 | async-start | bytes 8912896 | tf_op jit(solution)/shard_map/all_gather | solution.py:272
  10.6 343.6 %all-gather.17.cloned.1.call-start = ((), (), s32[]{:S(2)}) async-start(), calls=%async_computation.7 | async-start | bytes 2228224 | tf_op jit(solution)/shard_map/all_gather | solution.py:239
  64.8 5.3 %copy-start.1 = (bf16[1,16,512]{2,1,0:T(8,128)(2,1)S(1)}, bf16[1,16,512]{2,1,0:T(8,128)(2,1)}, u32[]{:S(2)}) copy-start(bf16[1,16,512]{2,1,0:T(8,128)(2,1)} %param.27) | copy-start | bytes 49156
  64.8 114.3 %all-to-all-start = ((bf16[8,512,512]{2,1,0:T(8,128)(2,1)}), bf16[8,512,512]{2,1,0:T(8,128)(2,1)}, u32[]{:S(2)}, u32[]{:S(2)}) async-start(bf16[8,512,512]{2,1,0:T(8,128)(2,1)} %bitcast.136), calls=%async_computation | async-start | bytes 8388608 | tf_op jit(solution)/shard_map/all_to_all | solution.py:282
  70.1 328.0 %reduce-scatter.2.cloned.1.call-start = ((), (), s32[]{:S(2)}) async-start(), calls=%async_computation.8 | async-start | bytes 4718592 | tf_op jit(solution)/shard_map/reduce_scatter | solution.py:286
  362.5 35.6 %copy-start = (bf16[512,512]{1,0:T(8,128)(2,1)S(1)}, bf16[512,512]{1,0:T(8,128)(2,1)}, u32[]{:S(2)}) copy-start(bf16[512,512]{1,0:T(8,128)(2,1)} %param.19) | copy-start | bytes 1572868
Sparse Core Ops, SparseCore 0:
  10.2 54.6 all-gather.14
  66.5 54.2 all-gather.6
  122.9 50.1 all-gather.10
  175.2 60.9 all-gather.8
  238.2 70.3 all-gather.12
  310.5 43.6 all-gather.16
  362.7 35.3 reduce-scatter.1
where the time goes:
time: 410 us; the launch traced here: 407 us
  waiting for transfers between devices  264 us (64%)
  matrix products  47.8 us (12%)
  blocking collectives  41.2 us (10%)
  other arithmetic  18.8 us (5%)
  local copies, waits for them, and re-layouts  14.7 us (4%)
  between operations  14.6 us (4%)
  starting transfers between devices  5.5 us (1%)
    all_gather x1, waiting for transfers between devices, on_device(): block_in = lax.all_gather(cache_page_store, 'row', axis=0, tiled=True)  60.6 us
    all_gather x1, waiting for transfers between devices, on_device(): lax.all_gather(query_key_value_weight, 'row', axis=0, tiled=True)  50.3 us
    all_gather x1, waiting for transfers between devices, on_device(): lax.all_gather(adapter_down_maps, 'row', axis=0, tiled=True)  49.3 us
    reduce_scatter x1, waiting for transfers between devices, on_device(): lax.psum_scatter(running.astype(jnp.bfloat16), 'col', scatter_dimension=1...  34.7 us
    all_gather x1, waiting for transfers between devices, on_device(): gathered = lax.all_gather(hidden_input, 'col', axis=1, tiled=True)  30 us
    all_gather x1, waiting for transfers between devices, on_device(): lax.all_gather(output_weight, 'row', axis=0, tiled=True)  24.7 us
    all_gather x1, blocking collectives, on_device(): lax.all_gather(adapter_up_maps, 'row', axis=0, tiled=True)  21 us
    all_gather x1, blocking collectives, on_device(): lax.all_gather(output_down_maps, 'row', axis=0, tiled=True)  20.1 us
  transfers between devices with their start and end apart: 8, of which 7 were waited for; matrix products, arithmetic and copies ran while one was open for 17% of the time, Pallas kernels for 0%

commit v1 on v0

v1 whole, which is shorter than its diff:
```python
import math

import jax
import jax.numpy as jnp
import numpy as np
from jax import lax
from jax.experimental import pallas as pl
from jax.experimental.pallas import tpu as pltpu
from jax.sharding import PartitionSpec as P

HEAD = 128
GROUP = 4
WIN = 1024
SINKS = 4
PAGE = 128
EPSILON = 1e-06
ROPE_BASE = 1000000.0
TOK = 512
FEAT = 512
PROMPTS = 4
BF = jnp.bfloat16
F32 = jnp.float32
NEG = -1e30


def perm_x(k):
    return [(i, (i // 4 + k) % 4 * 4 + i % 4) for i in range(16)]


def perm_y(k):
    return [(i, i // 4 * 4 + (i % 4 + k) % 4) for i in range(16)]


def perm_z(k):
    return [(i, (i // 2 + k) % 4 * 2 + i % 2) for i in range(8)]


SWAP = [(i, i ^ 1) for i in range(8)]


def ring4(block, axis, perm, half):
    before = lax.ppermute(block, axis, perm(1))
    after = lax.ppermute(block, axis, perm(-1))
    far_low = lax.ppermute(before[:half], axis, perm(1))
    far_high = lax.ppermute(after[half:], axis, perm(-1))
    return before, after, jnp.concatenate([far_low, far_high], axis=0)


def gather_col(block, half):
    other = lax.ppermute(block, "col", SWAP)
    out = [block, other]
    for piece in ring4(block, "col", perm_z, half):
        out += [piece, lax.ppermute(piece, "col", SWAP)]
    return out


def col_order():
    me = lax.axis_index("col")
    chip, core = me // 2, me % 2
    return jnp.stack([(chip + d) % 4 * 2 + (core + s) % 2 for d in (0, 3, 1, 2) for s in (0, 1)]).astype(jnp.int32)


def vmem(n):
    return pltpu.CompilerParams(vmem_limit_bytes=n << 20)


def whole(*shape):
    return pl.BlockSpec(shape, lambda *_: (0,) * len(shape))


def pick_body(index_ref, store_ref, out_ref, sems):
    copies = [
        pltpu.make_async_copy(store_ref.at[index_ref[i]], out_ref.at[i], sems.at[i])
        for i in range(out_ref.shape[0])
    ]
    for copy in copies:
        copy.start()
    for copy in copies:
        copy.wait()


def pick_pages(store, index):
    count = index.shape[0]
    return pl.pallas_call(
        pick_body,
        out_shape=jax.ShapeDtypeStruct((count,) + store.shape[1:], store.dtype),
        grid_spec=pltpu.PrefetchScalarGridSpec(
            num_scalar_prefetch=1,
            grid=(1,),
            in_specs=[pl.BlockSpec(memory_space=pl.ANY)],
            out_specs=pl.BlockSpec(memory_space=pl.ANY),
            scratch_shapes=[pltpu.SemaphoreType.DMA((count,))],
        ),
        name="pick_pages",
    )(index, store)


def select_body(sx_ref, sy_ref, y0, y1, y2, y3, maps_ref, up_ref, oup_ref):
    up_ref[...] = jnp.zeros_like(up_ref)
    for p in range(PROMPTS):
        for k, ref in enumerate((y0, y1, y2, y3)):

            @pl.when(sy_ref[p] == k)
            def _():
                x = sx_ref[p]
                maps_ref[p * 32 : p * 32 + 32, :] = ref[x, 0:32, :FEAT]
                maps_ref[128 + p * 16 : 128 + p * 16 + 16, :] = ref[x, 48:64, :FEAT]
                up_ref[p * 32 : p * 32 + 16, :512] = ref[x, 32:48, :512]
                up_ref[p * 32 + 16 : p * 32 + 32, 512:] = ref[x, 32:48, 512:]
                oup_ref[p * 16 : p * 16 + 16, :] = ref[x, 64:80, :FEAT]


def select_slots(sx, sy, pieces):
    return pl.pallas_call(
        select_body,
        out_shape=(
            jax.ShapeDtypeStruct((192, FEAT), BF),
            jax.ShapeDtypeStruct((128, 640), BF),
            jax.ShapeDtypeStruct((64, FEAT), BF),
        ),
        grid_spec=pltpu.PrefetchScalarGridSpec(
            num_scalar_prefetch=2,
            grid=(1,),
            in_specs=[whole(4, 80, 640)] * 4,
            out_specs=(whole(192, FEAT), whole(128, 640), whole(64, FEAT)),
        ),
        name="select_slots",
    )(sx, sy, *pieces)


def norm_body(order_ref, *refs):
    blocks, maps = refs[:8], refs[8:16]
    gain_ref, prompt_ref, normed_ref, low_ref = refs[16:]
    values = [b[...].astype(F32) for b in blocks]
    total = sum(jnp.sum(v * v, axis=-1, keepdims=True) for v in values)
    scale = lax.rsqrt(total * (1.0 / (8 * FEAT)) + EPSILON)
    low = jnp.zeros(low_ref.shape, F32)
    for b in range(8):
        gain = gain_ref[pl.ds(order_ref[b], 1), :]
        normed = (values[b] * scale * gain).astype(BF)
        normed_ref[order_ref[b]] = normed
        low += lax.dot_general(normed, maps[b][:128, :], (((1,), (1,)), ((), ())), preferred_element_type=F32)
    mine = lax.broadcasted_iota(jnp.int32, low.shape, 1) // 32 == prompt_ref[...]
    low_ref[...] = jnp.where(mine, low, 0.0).astype(BF)


def norm_low(order, blocks, maps, gain, prompt):
    rows = 128
    return pl.pallas_call(
        norm_body,
        out_shape=(jax.ShapeDtypeStruct((8, TOK, FEAT), BF), jax.ShapeDtypeStruct((TOK, 128), BF)),
        grid_spec=pltpu.PrefetchScalarGridSpec(
            num_scalar_prefetch=1,
            grid=(TOK // rows,),
            in_specs=[pl.BlockSpec((rows, FEAT), lambda i, o: (i, 0))] * 8
            + [whole(192, FEAT)] * 8
            + [whole(8, FEAT), pl.BlockSpec((rows, 1), lambda i, o: (i, 0))],
            out_specs=(
                pl.BlockSpec((8, rows, FEAT), lambda i, o: (0, i, 0)),
                pl.BlockSpec((rows, 128), lambda i, o: (i, 0)),
            ),
        ),
        compiler_params=vmem(32),
        name="norm_low",
    )(order, *blocks, *maps, gain, prompt)


def qkv_body(normed_ref, w_ref, low_ref, up_ref, cos_ref, sin_ref, qg_ref, kg_ref, q_ref, kv_ref, acc):
    step = pl.program_id(0)
    part = jnp.dot(normed_ref[0], w_ref[...], preferred_element_type=F32)

    @pl.when(step == 0)
    def _():
        acc[...] = part

    @pl.when(step > 0)
    def _():
        acc[...] += part

    @pl.when(step == pl.num_programs(0) - 1)
    def _():
        change = 0.5 * jnp.dot(low_ref[...], up_ref[...], preferred_element_type=F32)
        cos, sin = cos_ref[...], sin_ref[...]

        def finish(raw, gain):
            scale = lax.rsqrt(jnp.mean(raw * raw, axis=-1, keepdims=True) + EPSILON)
            x = raw * scale * gain
            return (x * cos + pltpu.roll(x, HEAD // 2, 1) * sin).astype(BF)

        for h in range(GROUP):
            cut = slice(h * HEAD, (h + 1) * HEAD)
            q_ref[h] = finish(acc[:, cut] + change[:, cut], qg_ref[...])
        kv_ref[0] = finish(acc[:, 512:640], kg_ref[...])
        kv_ref[1] = (acc[:, 640:768] + change[:, 512:640]).astype(BF)


def project(normed, weight, low, up, cos, sin, q_gain, k_gain):
    return pl.pallas_call(
        qkv_body,
        out_shape=(jax.ShapeDtypeStruct((GROUP, TOK, HEAD), BF), jax.ShapeDtypeStruct((2, TOK, HEAD), BF)),
        grid=(8,),
        in_specs=[
            pl.BlockSpec((1, TOK, FEAT), lambda k: (k, 0, 0)),
            pl.BlockSpec((FEAT, 768), lambda k: (k, 0)),
            whole(TOK, 128),
            whole(128, 640),
            whole(TOK, HEAD),
            whole(TOK, HEAD),
            whole(1, HEAD),
            whole(1, HEAD),
        ],
        out_specs=(whole(GROUP, TOK, HEAD), whole(2, TOK, HEAD)),
        scratch_shapes=[pltpu.VMEM((TOK, 768), F32)],
        compiler_params=vmem(32),
        name="project",
    )(normed, weight, low, up, cos, sin, q_gain, k_gain)


BLOCK = 64
SCALE2 = math.log2(math.e) / math.sqrt(HEAD)


def attend_body(page_ref, need_ref, length_ref, q_ref, kv_ref, pages_ref, begin_ref, own_ref, pos_ref, out_ref, m_ref, l_ref, acc_ref):
    rows = GROUP * BLOCK
    for t in range(TOK // BLOCK):
        lo, hi = max(0, t * BLOCK - 256), (t + 1) * BLOCK
        cut = slice(t * BLOCK, hi)
        q = q_ref[:, cut, :].reshape(rows, HEAD)
        s = lax.dot_general(q, kv_ref[0, lo:hi, :], (((1,), (1,)), ((), ())), preferred_element_type=F32)
        key = lo + lax.broadcasted_iota(jnp.int32, (BLOCK, hi - lo), 1)
        token = t * BLOCK + lax.broadcasted_iota(jnp.int32, (BLOCK, hi - lo), 0)
        seen = (key <= token) & (key >= begin_ref[cut, :])
        s = jnp.where(seen[None], s.reshape(GROUP, BLOCK, hi - lo), NEG).reshape(rows, hi - lo)
        m = jnp.max(s, axis=1, keepdims=True)
        w = jnp.exp2((s - m) * SCALE2)
        m_ref[...] = m
        l_ref[...] = jnp.sum(w, axis=1, keepdims=True)
        acc_ref[...] = jnp.dot(w.astype(BF), kv_ref[1, lo:hi, :], preferred_element_type=F32)
        for j in range(2):

            @pl.when(need_ref[t * 2 + j] > 0)
            def _():
                mine = own_ref[cut, :] == j
                least = jnp.where(mine, pos_ref[cut, :] - WIN, 1 << 30)
                sink = jnp.where(mine, SINKS, 0)
                pieces = []
                for k in range(8):
                    page = page_ref[j * 8 + k]
                    c = lax.dot_general(q, pages_ref[page, 0], (((1,), (1,)), ((), ())), preferred_element_type=F32)
                    at = k * PAGE + lax.broadcasted_iota(jnp.int32, (BLOCK, PAGE), 1)
                    ok = at > least
                    if k == 0:
                        ok = ok | (at < sink)
                    ok = ok & (at < length_ref[j])
                    pieces.append(jnp.where(ok[None], c.reshape(GROUP, BLOCK, PAGE), NEG).reshape(rows, PAGE))
                top = pieces[0]
                for c in pieces[1:]:
                    top = jnp.maximum(top, c)
                m_old = m_ref[...]
                m_new = jnp.maximum(m_old, jnp.max(top, axis=1, keepdims=True))
                fade = jnp.exp2((m_old - m_new) * SCALE2)
                total = jnp.zeros((rows, PAGE), F32)
                acc = acc_ref[...] * fade
                for k in range(8):
                    page = page_ref[j * 8 + k]
                    w = jnp.exp2((pieces[k] - m_new) * SCALE2)
                    total += w
                    acc += jnp.dot(w.astype(BF), pages_ref[page, 1], preferred_element_type=F32)
                m_ref[...] = m_new
                l_ref[...] = l_ref[...] * fade + jnp.sum(total, axis=1, keepdims=True)
                acc_ref[...] = acc

        done = (acc_ref[...] * (1.0 / l_ref[...])).astype(BF)
        for h in range(GROUP):
            out_ref[cut, h * HEAD : (h + 1) * HEAD] = done[h * BLOCK : (h + 1) * BLOCK, :]


def attention(page, need, length, q, kv, pages, begin, own, pos):
    rows = GROUP * BLOCK
    return pl.pallas_call(
        attend_body,
        out_shape=jax.ShapeDtypeStruct((TOK, FEAT), BF),
        grid_spec=pltpu.PrefetchScalarGridSpec(
            num_scalar_prefetch=3,
            grid=(1,),
            in_specs=[
                whole(GROUP, TOK, HEAD),
                whole(2, TOK, HEAD),
                whole(32, 2, PAGE, HEAD),
                whole(TOK, 1),
                whole(TOK, 1),
                whole(TOK, 1),
            ],
            out_specs=whole(TOK, FEAT),
            scratch_shapes=[pltpu.VMEM((rows, 1), F32), pltpu.VMEM((rows, 1), F32), pltpu.VMEM((rows, HEAD), F32)],
        ),
        compiler_params=vmem(32),
        name="attention",
    )(page, need, length, q, kv, pages, begin, own, pos)


def out_body(order_ref, *refs):
    blocks, maps = refs[:8], refs[8:16]
    w_ref, oup_ref, prompt_ref, hidden_ref, out_ref = refs[16:]
    total = hidden_ref[...].astype(F32)
    low = jnp.zeros((total.shape[0], 64), F32)
    for b in range(8):
        x = blocks[b][...]
        total += jnp.dot(x, w_ref[order_ref[b]], preferred_element_type=F32)
        low += lax.dot_general(x, maps[b][128:192, :], (((1,), (1,)), ((), ())), preferred_element_type=F32)
    mine = lax.broadcasted_iota(jnp.int32, low.shape, 1) // 16 == prompt_ref[...]
    low = jnp.where(mine, low, 0.0)
    change = jnp.dot(low, oup_ref[...].astype(F32), precision=lax.Precision.HIGHEST, preferred_element_type=F32)
    out_ref[...] = (total + 0.5 * change).astype(BF)


def output(order, blocks, maps, weight, oup, prompt, hidden):
    rows = 128
    tok = pl.BlockSpec((rows, FEAT), lambda i, o: (i, 0))
    return pl.pallas_call(
        out_body,
        out_shape=jax.ShapeDtypeStruct((TOK, FEAT), BF),
        grid_spec=pltpu.PrefetchScalarGridSpec(
            num_scalar_prefetch=1,
            grid=(TOK // rows,),
            in_specs=[tok] * 8
            + [whole(192, FEAT)] * 8
            + [whole(8, FEAT, FEAT), whole(64, FEAT), pl.BlockSpec((rows, 1), lambda i, o: (i, 0)), tok],
            out_specs=tok,
        ),
        compiler_params=vmem(40),
        name="output",
    )(order, *blocks, *maps, weight, oup, prompt, hidden)


def token_tables(lengths, cached):
    ends = [lengths[0]]
    for p in range(1, PROMPTS):
        ends.append(ends[-1] + lengths[p])
    has = [(cached[p] > 0).astype(jnp.int32) for p in range(PROMPTS)]
    rank, count = [], jnp.int32(0)
    for p in range(PROMPTS):
        rank.append(jnp.where(has[p] > 0, count, -1))
        count = count + has[p]
    token = lax.broadcasted_iota(jnp.int32, (TOK, 1), 0)
    prompt = sum((token >= ends[p]).astype(jnp.int32) for p in range(PROMPTS))
    begin = jnp.zeros_like(token)
    prefix = jnp.zeros_like(token)
    own = jnp.full_like(token, -1)
    for p in range(PROMPTS):
        hit = prompt == p
        begin = jnp.where(hit, ends[p] - lengths[p], begin)
        prefix = jnp.where(hit, cached[p], prefix)
        own = jnp.where(hit, rank[p], own)
    need, used = [], []
    first = jnp.arange(TOK // BLOCK, dtype=jnp.int32) * BLOCK
    for j in range(2):
        start = sum(jnp.where(rank[p] == j, ends[p] - lengths[p], 0) for p in range(PROMPTS))
        end = sum(jnp.where(rank[p] == j, ends[p], 0) for p in range(PROMPTS))
        used.append(sum(jnp.where(rank[p] == j, cached[p], 0) for p in range(PROMPTS)))
        need.append(((start < first + BLOCK) & (end > first)).astype(jnp.int32))
    return prompt, begin, prefix + token - begin, own, jnp.stack(need, axis=1).reshape(-1), jnp.stack(used)


def page_tables(owner_row, store_index):
    me = lax.axis_index("row")
    owner = owner_row.reshape(16, 16)
    store = store_index.reshape(16, 16)
    same = (owner[:, :, None] == owner[:, None, :]) & (
        jnp.arange(16)[None, None, :] < jnp.arange(16)[None, :, None]
    )
    rank = jnp.sum(same.astype(jnp.int32), axis=2)
    out = jnp.stack(
        [jnp.sum(jnp.where((owner == me) & (rank == s), store, 0), axis=1) for s in range(2)], axis=1
    ).reshape(32)
    mine = jnp.arange(16)[:, None] == me
    place = jnp.sum(jnp.where(mine, owner * 2 + rank, 0), axis=0)
    return out.astype(jnp.int32), place.astype(jnp.int32)


def on_device(
    hidden_input,
    input_norm_gain,
    query_norm_gain,
    key_norm_gain,
    query_key_value_weight,
    output_weight,
    adapter_down_maps,
    adapter_up_maps,
    output_down_maps,
    output_up_maps,
    prompt_adapter,
    adapter_position,
    prompt_length,
    cache_length,
    page_owner_row,
    page_store_index,
    cache_page_store,
):
    row, col = lax.axis_index("row"), lax.axis_index("col")
    weight = lax.all_gather(query_key_value_weight, "row", axis=0, tiled=True)

    going, place = page_tables(page_owner_row, page_store_index)
    sent = pick_pages(cache_page_store, going).reshape(16, 2 * 2 * PAGE, HEAD)
    pages = lax.all_to_all(sent, "row", 0, 0).reshape(32, 2, PAGE, HEAD)

    order = col_order()
    blocks = gather_col(hidden_input, 256)

    def wide(x):
        return jnp.pad(x, ((0, 0), (0, 640 - x.shape[1])))

    small = jnp.concatenate(
        [
            wide(lax.dynamic_slice(adapter_down_maps[0], (0, col * FEAT), (32, FEAT))),
            adapter_up_maps[0],
            wide(output_down_maps[0]),
            wide(lax.dynamic_slice(output_up_maps[0], (0, col * FEAT), (16, FEAT))),
        ],
        axis=0,
    )
    along_x = jnp.concatenate([small, *ring4(small, "row", perm_x, 48)], axis=0)
    pieces = [p.reshape(4, 80, 640) for p in (along_x, *ring4(along_x, "row", perm_y, 160))]
    adapter_ids = jnp.arange(16, dtype=jnp.int32)
    slot = jnp.sum(jnp.where(prompt_adapter[:, None] == adapter_ids[None, :], adapter_position[None, :], 0), axis=1)

    def turn(d):
        d = d % 4
        return jnp.where(d == 0, 0, jnp.where(d == 3, 1, jnp.where(d == 1, 2, 3))).astype(jnp.int32)

    maps, up, oup = select_slots(turn(slot // 4 - row // 4 + 4), turn(slot % 4 - row % 4 + 4), pieces)
    maps = gather_col(maps, 96)

    prompt, begin, position, own, need, used = token_tables(prompt_length[0], cache_length)
    frequency = ROPE_BASE ** (-2.0 * jnp.arange(HEAD // 2, dtype=F32) / HEAD)
    angles = position.astype(F32) * frequency[None, :]
    cos, sin = jnp.cos(angles), jnp.sin(angles)
    cos = jnp.concatenate([cos, cos], axis=1)
    sin = jnp.concatenate([-sin, sin], axis=1)

    normed, low = norm_low(order, blocks, maps, input_norm_gain.astype(F32).reshape(8, FEAT), prompt)
    weight, later = lax.optimization_barrier((weight, output_weight))
    out_weight = lax.all_gather(later, "row", axis=0, tiled=True)
    q, new_cache = project(
        normed,
        weight,
        low,
        up,
        cos,
        sin,
        query_norm_gain.astype(F32)[None, :],
        key_norm_gain.astype(F32)[None, :],
    )
    attended = attention(place, need, used, q, new_cache, pages, begin, own, position)
    attended = gather_col(attended, 256)
    hidden_output = output(order, attended, maps, out_weight.reshape(8, FEAT, FEAT), oup, prompt, hidden_input)
    return hidden_output, new_cache


def solution(mesh):
    return jax.shard_map(
        on_device,
        mesh=mesh,
        in_specs=(
            P("row", "col"),
            P(),
            P(),
            P(),
            P("row", "col"),
            P("row", "col"),
            P("row", None, None),
            P("row", None, "col"),
            P("row", None, "col"),
            P("row", None, None),
            P("row"),
            P(),
            P("row", None),
            P("row"),
            P(),
            P(),
            P("row", None, None, "col"),
        ),
        out_specs=(P("row", "col"), P(None, "row", "col")),
        check_vma=False,
    )
```

time: 410 us -> 340 us (0.83)
  waiting for transfers between devices: 264 us -> 101 us
  Pallas kernels: 0 us -> 99.1 us
  matrix products: 47.8 us -> 0 us
  blocking collectives: 41.2 us -> 0 us
  starting transfers between devices: 5.5 us -> 43.6 us
  local copies, waits for them, and re-layouts: 14.7 us -> 45.4 us
  between operations: 14.6 us -> 27.6 us
    all_gather x6 -> x2, waiting for transfers between devices: 226 us -> 66.7 us  [the longest x1 66.7 us: on_device(): weight = lax.all_gather(query_key_value_weight, 'row', axis=0, tiled=True)]
    pallas_call x0 -> x6, Pallas kernels: none -> 99.1 us  [the longest x1 65.6 us: pick_pages(): pl.pallas_call(pick_body, out_shape=jax.ShapeDtypeStruct((count,) + store...]
    dot_general x15 -> x0, matrix products: 47.8 us -> none  [the longest x4 13.6 us: attend(): lax.dot_general(queries, key_rows, (((1,), (1,)), ((), ())), preferred_el...]
    all_gather x2 -> x0, blocking collectives: 41.2 us -> none  [the longest x1 21 us: on_device(): lax.all_gather(adapter_up_maps, 'row', axis=0, tiled=True)]
    ppermute x0 -> x32, starting transfers between devices: none -> 39.5 us  [the longest x5 10.3 us: ring4(): after = lax.ppermute(block, axis, perm(-1))]
    reduce_scatter x1 -> x0, waiting for transfers between devices: 34.7 us -> none  [on_device(): lax.psum_scatter(running.astype(jnp.bfloat16), 'col', scatter_dimension=1...]
    ppermute x0 -> x32, waiting for transfers between devices: none -> 33.5 us  [the longest x5 18 us: ring4(): before = lax.ppermute(block, axis, perm(1))]
    unnamed x19 -> x96, local copies, waits for them, and re-layouts: 0.84 us -> 30.9 us
  transfers between devices with their start and end apart: 8 -> 35, of which waited for: 7 -> 11; matrix products, arithmetic and copies ran while one was open for 17% -> 12% of each run, Pallas kernels for 0% -> 27%
where the time goes in v1:
time: 340 us; the launch traced here: 338 us
  waiting for transfers between devices  101 us (30%)
  Pallas kernels  99.1 us (29%)
  local copies, waits for them, and re-layouts  45.4 us (13%)
  starting transfers between devices  43.6 us (13%)
  between operations  27.6 us (8%)
  other arithmetic  21 us (6%)
    all_gather x1, waiting for transfers between devices, on_device(): weight = lax.all_gather(query_key_value_weight, 'row', axis=0, tiled=True)  66.7 us
    pallas_call x1, Pallas kernels, pick_pages(): pl.pallas_call(pick_body, out_shape=jax.ShapeDtypeStruct((count,) + store...  65.6 us
    unnamed x96, local copies, waits for them, and re-layouts  30.9 us
    ppermute x5, waiting for transfers between devices, ring4(): before = lax.ppermute(block, axis, perm(1))  18 us
    ppermute x5, waiting for transfers between devices, ring4(): far_low = lax.ppermute(before[:half], axis, perm(1))  10.6 us
    ppermute x5, starting transfers between devices, ring4(): after = lax.ppermute(block, axis, perm(-1))  10.3 us
    ppermute x5, starting transfers between devices, ring4(): far_high = lax.ppermute(after[half:], axis, perm(-1))  9.84 us
    pallas_call x1, Pallas kernels, attention(): pl.pallas_call(attend_body, out_shape=jax.ShapeDtypeStruct((TOK, FEAT), B...  9.66 us
  transfers between devices with their start and end apart: 35, of which 11 were waited for; matrix products, arithmetic and copies ran while one was open for 12% of the time, Pallas kernels for 27%

profile of v1, /device:TPU:1, one launch (start us, length us, event | category | flops | bytes accessed | tf_op | source)
XLA Modules:
  0.0 337.6 jit_solution(255674445565396842)
XLA Ops:
  8.0 66.7 %all-gather.3.cloned.1.call-done.w_ref = bf16[4096,768]{1,0:T(8,128)(2,1)} async-done(((bf16[256,768]{1,0:T(8,128)(2,1)}), bf16[4096,768]{1,0:T(8,128)(2,1)}) %all-gather.3.cloned.1.call-update) | async-done | bytes 6291472 | tf_op jit(solution)/shard_map/all_gather | solution.py:401
  90.0 65.6 %pick_pages.1 = bf16[32,2,128,128]{3,2,1,0:T(8,128)(2,1)} custom-call(s32[32]{0:T(128)} %reshape.272.index_ref, bf16[8,2,128,128]{3,2,1,0:T(8,128)(2,1)} %store_ref.1), custom_call_target="tpu_custom_call" | custom-call | tf_op jit(solution)/shard_map/pick_pages/pallas_call | solution.py:84
  155.6 4.1 %all-to-all-start = ((bf16[16,512,128]{2,1,0:T(8,128)(2,1)}), bf16[16,512,128]{2,1,0:T(8,128)(2,1)S(1)}, u32[]{:S(2)}, u32[]{:S(2)}) async-start(bf16[16,512,128]{2,1,0:T(8,128)(2,1)} %bitcast.43), calls=%async_computation | async-start | bytes 4194304 | tf_op jit(solution)/shard_map/all_to_all | solution.py:405
  169.0 3.2 subtract_convert_fusion
  172.3 4.3 %add_subtract_fusion = (s32[512,1]{1,0:T(8,128)}, s32[512,1]{1,0:T(8,128)}) fusion(s32[]{:T(128)} %bitcast.9, s32[]{:T(128)} %bitcast.8, s32[]{:T(128)} %bitcast.11, s32[]{:T(128)} %bitcast.13, s32[]{:T(128)S(6)} %add.305, s32[]{:T(128)S(6)} %add.300, s32[]{:T(128)S(6)} %add.297, s32[]{:T(128)} %bitcast.10, s32[]{:T(128)S(6)} %select_n.375, ...), kind=kLoop, calls=%fused_computation.5 | loop fusion | flops 14336 | bytes 4144 | tf_op jit(solution)/shard_map/sub | solution.py:362
  184.8 4.8 %collective-permute-done.10 = bf16[48,640]{1,0:T(8,128)(2,1)S(1)} collective-permute-done((bf16[48,640]{1,0:T(8,128)(2,1)S(1)}, bf16[48,640]{1,0:T(8,128)(2,1)S(1)}, u32[]{:S(2)}, u32[]{:S(2)}) %collective-permute-start.10) | collective-permute-done | bytes 61472 | tf_op jit(solution)/shard_map/ppermute | solution.py:44
  194.5 6.3 %collective-permute-done.12 = bf16[320,640]{1,0:T(8,128)(2,1)S(1)} collective-permute-done((bf16[320,640]{1,0:T(8,128)(2,1)S(1)}, bf16[320,640]{1,0:T(8,128)(2,1)S(1)}, u32[]{:S(2)}, u32[]{:S(2)}) %collective-permute-start.12) | collective-permute-done | bytes 409632 | tf_op jit(solution)/shard_map/ppermute | solution.py:42
  203.7 2.7 collective-permute-start.15
  218.2 2.6 collective-permute-start.6
  222.7 3.0 select_slots.1
  227.3 3.1 collective-permute-start.2
  230.4 2.9 collective-permute-start.19
  238.8 2.9 collective-permute-done.21
  242.8 2.3 collective-permute-done.22
  251.8 5.2 %norm_low.1 = (bf16[8,512,512]{2,1,0:T(8,128)(2,1)S(1)}, bf16[512,128]{1,0:T(8,128)(2,1)S(1)}) custom-call(s32[8]{0:T(128)S(1)} %copy-done.34, bf16[512,512]{1,0:T(8,128)(2,1)S(1)} %copy-done.3, bf16[512,512]{1,0:T(8,128)(2,1)} %collective-permute-done.refs_1_, bf16[512,512]{1,0:T(8,128)(2,1)} %collective-permute-done.1.refs_2_, ...), custom_call_target="tpu_custom_call" | custom-call | tf_op jit(solution)/shard_map/norm_low/pallas_call | solution.py:149
  257.1 2.8 copy-done.1
  259.8 7.7 %project.1 = (bf16[4,512,128]{2,1,0:T(8,128)(2,1)S(1)}, bf16[2,512,128]{2,1,0:T(8,128)(2,1)}) custom-call(bf16[8,512,512]{2,1,0:T(8,128)(2,1)S(1)} %get-tuple-element.12.normed_ref, bf16[4096,768]{1,0:T(8,128)(2,1)S(1)} %copy-done.1, bf16[512,128]{1,0:T(8,128)(2,1)S(1)} %get-tuple-element.14.low_ref, bf16[128,640]{1,0:T(8,128)(2,1)S(1)} %copy-done.32, ...), custom_call_target="tpu_custom_call" | custom-call | tf_op jit(solution)/shard_map/project/pallas_call | solution.py:198
  273.2 9.7 %attention.1.refs_0_ = bf16[512,512]{1,0:T(8,128)(2,1)S(1)} custom-call(s32[16]{0:T(128)S(1)} %copy-done.36, s32[16]{0:T(128)S(1)} %copy-done.37, s32[2]{0:T(128)S(1)} %copy-done.38, bf16[4,512,128]{2,1,0:T(8,128)(2,1)S(1)} %copy-done.30, bf16[2,512,128]{2,1,0:T(8,128)(2,1)S(1)} %copy-done.31, bf16[32,2,128,128]{3,2,1,0:T(8,128)(2,1)S(1)} %bitcast.41, ...), custom_call_target="tpu_custom_call" | custom-call | tf_op jit(solution)/shard_map/attention/pallas_call | solution.py:280
  283.0 2.7 collective-permute-start.27
  285.6 11.8 %collective-permute-done.25.refs_2_ = bf16[512,512]{1,0:T(8,128)(2,1)S(1)} collective-permute-done((bf16[512,512]{1,0:T(8,128)(2,1)S(1)}, bf16[512,512]{1,0:T(8,128)(2,1)S(1)}, u32[]{:S(2)}, u32[]{:S(2)}) %collective-permute-start.25) | collective-permute-done | bytes 524320 | tf_op jit(solution)/shard_map/ppermute | solution.py:42
  297.5 2.7 collective-permute-start.30
  302.4 3.0 collective-permute-done.29
  310.0 2.2 copy-done.2
  322.8 8.0 %output.1 = bf16[512,512]{1,0:T(8,128)(2,1)} custom-call(s32[8]{0:T(128)S(1)} %copy-done.35, bf16[512,512]{1,0:T(8,128)(2,1)S(1)} %copy-done.5, bf16[512,512]{1,0:T(8,128)(2,1)S(1)} %collective-permute-done.24.refs_1_, bf16[512,512]{1,0:T(8,128)(2,1)S(1)} %collective-permute-done.25.refs_2_, bf16[512,512]{1,0:T(8,128)(2,1)S(1)} %copy-done.24, ...), custom_call_target="tpu_custom_call" | custom-call | tf_op jit(solution)/shard_map/output/pallas_call | solution.py:320
  (199 shorter events, 80.2 us)
Async XLA Ops:
  7.2 67.5 %all-gather.3.cloned.1.call-start = ((), (), s32[]{:S(2)}) async-start(), calls=%async_computation.1 | async-start | bytes 6684672 | tf_op jit(solution)/shard_map/all_gather | solution.py:401
  7.9 302.1 %all-gather.5.cloned.1.call-start = ((), (), s32[]{:S(2)}) async-start(), calls=%async_computation.2 | async-start | bytes 4456448 | tf_op jit(solution)/shard_map/all_gather | solution.py:443
  78.3 100.3 %collective-permute-start.8 = (bf16[80,640]{1,0:T(8,128)(2,1)}, bf16[80,640]{1,0:T(8,128)(2,1)}, u32[]{:S(2)}, u32[]{:S(2)}) collective-permute-start(bf16[80,640]{1,0:T(8,128)(2,1)} %pad_maximum_fusion.3), channel_id=1, source_target_pairs={{0,32},{8,40},{16,48},{24,56},{32,64},{40,72},{48,80},{56,88},{64,... | collective-permute-start | bytes 307208 | tf_op jit(solution)/shard_map/ppermute | solution.py:42
  79.5 101.3 %collective-permute-start.9 = (bf16[80,640]{1,0:T(8,128)(2,1)}, bf16[80,640]{1,0:T(8,128)(2,1)}, u32[]{:S(2)}, u32[]{:S(2)}) collective-permute-start(bf16[80,640]{1,0:T(8,128)(2,1)} %pad_maximum_fusion.3), channel_id=1, source_target_pairs={{0,96},{8,104},{16,112},{24,120},{32,0},{40,8},{48,16},{56,24},{64... | collective-permute-start | bytes 307208 | tf_op jit(solution)/shard_map/ppermute | solution.py:43
  81.0 125.4 %collective-permute-start.1 = (bf16[512,512]{1,0:T(8,128)(2,1)}, bf16[512,512]{1,0:T(8,128)(2,1)}, u32[]{:S(2)}, u32[]{:S(2)}) collective-permute-start(bf16[512,512]{1,0:T(8,128)(2,1)} %refs_19_.1), channel_id=1, source_target_pairs={{0,2},{1,3},{2,4},{3,5},{4,6},{5,7},{6,0},{7,1},{8,10},{9,11},{10,... | collective-permute-start | bytes 1572872 | tf_op jit(solution)/shard_map/ppermute | solution.py:42
  82.3 134.3 %collective-permute-start.3 = (bf16[512,512]{1,0:T(8,128)(2,1)}, bf16[512,512]{1,0:T(8,128)(2,1)}, u32[]{:S(2)}, u32[]{:S(2)}) collective-permute-start(bf16[512,512]{1,0:T(8,128)(2,1)} %refs_19_.1), channel_id=1, source_target_pairs={{0,6},{1,7},{2,0},{3,1},{4,2},{5,3},{6,4},{7,5},{8,14},{9,15},{10,... | collective-permute-start | bytes 1572872 | tf_op jit(solution)/shard_map/ppermute | solution.py:43
  83.7 163.4 %collective-permute-start = (bf16[512,512]{1,0:T(8,128)(2,1)}, bf16[512,512]{1,0:T(8,128)(2,1)}, u32[]{:S(2)}, u32[]{:S(2)}) collective-permute-start(bf16[512,512]{1,0:T(8,128)(2,1)} %refs_19_.1), channel_id=1, source_target_pairs={{0,1},{1,0},{2,3},{3,2},{4,5},{5,4},{6,7},{7,6},{8,9},{9,8},{10,11... | collective-permute-start | bytes 1572872 | tf_op jit(solution)/shard_map/ppermute | solution.py:50
  155.6 112.7 %all-to-all-start = ((bf16[16,512,128]{2,1,0:T(8,128)(2,1)}), bf16[16,512,128]{2,1,0:T(8,128)(2,1)S(1)}, u32[]{:S(2)}, u32[]{:S(2)}) async-start(bf16[16,512,128]{2,1,0:T(8,128)(2,1)} %bitcast.43), calls=%async_computation | async-start | bytes 4194304 | tf_op jit(solution)/shard_map/all_to_all | solution.py:405
  179.5 10.1 %collective-permute-start.10 = (bf16[48,640]{1,0:T(8,128)(2,1)S(1)}, bf16[48,640]{1,0:T(8,128)(2,1)S(1)}, u32[]{:S(2)}, u32[]{:S(2)}) collective-permute-start(bf16[48,640]{1,0:T(8,128)(2,1)S(1)} %slice.102), channel_id=1, source_target_pairs={{0,32},{8,40},{16,48},{24,56},{32,64},{40,72},{48,80},{56,88},{64,... | collective-permute-start | bytes 184328 | tf_op jit(solution)/shard_map/ppermute | solution.py:44
  181.6 7.9 %collective-permute-start.11 = (bf16[32,640]{1,0:T(8,128)(2,1)S(1)}, bf16[32,640]{1,0:T(8,128)(2,1)S(1)}, u32[]{:S(2)}, u32[]{:S(2)}) collective-permute-start(bf16[32,640]{1,0:T(8,128)(2,1)S(1)} %slice.103), channel_id=1, source_target_pairs={{0,96},{8,104},{16,112},{24,120},{32,0},{40,8},{48,16},{56,24},{64... | collective-permute-start | bytes 122888 | tf_op jit(solution)/shard_map/ppermute | solution.py:45
  189.6 11.2 %collective-permute-start.12 = (bf16[320,640]{1,0:T(8,128)(2,1)S(1)}, bf16[320,640]{1,0:T(8,128)(2,1)S(1)}, u32[]{:S(2)}, u32[]{:S(2)}) collective-permute-start(bf16[320,640]{1,0:T(8,128)(2,1)S(1)} %constant_dynamic-update-slice_fusion.2), channel_id=1, source_target_pairs={{0,8},{8,16},{16,24},{24,0},{32,40},{40,48},{48,56},{56,32},{64,72... | collective-permute-start | bytes 1228808 | tf_op jit(solution)/shard_map/ppermute | solution.py:42
  190.4 11.8 %collective-permute-start.13 = (bf16[320,640]{1,0:T(8,128)(2,1)S(1)}, bf16[320,640]{1,0:T(8,128)(2,1)S(1)}, u32[]{:S(2)}, u32[]{:S(2)}) collective-permute-start(bf16[320,640]{1,0:T(8,128)(2,1)S(1)} %constant_dynamic-update-slice_fusion.2), channel_id=1, source_target_pairs={{0,24},{8,0},{16,8},{24,16},{32,56},{40,32},{48,40},{56,48},{64,88... | collective-permute-start | bytes 1228808 | tf_op jit(solution)/shard_map/ppermute | solution.py:43
  202.3 18.6 %collective-permute-start.14 = (bf16[160,640]{1,0:T(8,128)(2,1)}, bf16[160,640]{1,0:T(8,128)(2,1)}, u32[]{:S(2)}, u32[]{:S(2)}) collective-permute-start(bf16[160,640]{1,0:T(8,128)(2,1)} %slice.104), channel_id=1, source_target_pairs={{0,8},{8,16},{16,24},{24,0},{32,40},{40,48},{48,56},{56,32},{64,72... | collective-permute-start | bytes 614408 | tf_op jit(solution)/shard_map/ppermute | solution.py:44
  203.7 17.1 %collective-permute-start.15 = (bf16[160,640]{1,0:T(8,128)(2,1)}, bf16[160,640]{1,0:T(8,128)(2,1)}, u32[]{:S(2)}, u32[]{:S(2)}) collective-permute-start(bf16[160,640]{1,0:T(8,128)(2,1)} %slice.105), channel_id=1, source_target_pairs={{0,24},{8,0},{16,8},{24,16},{32,56},{40,32},{48,40},{56,48},{64,88... | collective-permute-start | bytes 614408 | tf_op jit(solution)/shard_map/ppermute | solution.py:45
  208.1 22.3 %collective-permute-start.5 = (bf16[256,512]{1,0:T(8,128)(2,1)}, bf16[256,512]{1,0:T(8,128)(2,1)}, u32[]{:S(2)}, u32[]{:S(2)}) collective-permute-start(bf16[256,512]{1,0:T(8,128)(2,1)} %slice.100), channel_id=1, source_target_pairs={{0,2},{1,3},{2,4},{3,5},{4,6},{5,7},{6,0},{7,1},{8,10},{9,11},{10,... | collective-permute-start | bytes 786440 | tf_op jit(solution)/shard_map/ppermute | solution.py:44
  218.2 17.7 %collective-permute-start.6 = (bf16[256,512]{1,0:T(8,128)(2,1)}, bf16[256,512]{1,0:T(8,128)(2,1)}, u32[]{:S(2)}, u32[]{:S(2)}) collective-permute-start(bf16[256,512]{1,0:T(8,128)(2,1)} %slice.101), channel_id=1, source_target_pairs={{0,6},{1,7},{2,0},{3,1},{4,2},{5,3},{6,4},{7,5},{8,14},{9,15},{10,... | collective-permute-start | bytes 786440 | tf_op jit(solution)/shard_map/ppermute | solution.py:45
  225.7 8.6 %collective-permute-start.17 = (bf16[192,512]{1,0:T(8,128)(2,1)}, bf16[192,512]{1,0:T(8,128)(2,1)S(1)}, u32[]{:S(2)}, u32[]{:S(2)}) collective-permute-start(bf16[192,512]{1,0:T(8,128)(2,1)} %get-tuple-element.11.refs_8_), channel_id=1, source_target_pairs={{0,2},{1,3},{2,4},{3,5},{4,6},{5,7},{6,0},{7,1},{8,10},{9,11},{10,... | collective-permute-start | bytes 589832 | tf_op jit(solution)/shard_map/ppermute | solution.py:42
  227.3 21.3 %collective-permute-start.2 = (bf16[512,512]{1,0:T(8,128)(2,1)}, bf16[512,512]{1,0:T(8,128)(2,1)S(1)}, u32[]{:S(2)}, u32[]{:S(2)}) collective-permute-start(bf16[512,512]{1,0:T(8,128)(2,1)} %collective-permute-done.1.refs_2_), channel_id=1, source_target_pairs={{0,1},{1,0},{2,3},{3,2},{4,5},{5,4},{6,7},{7,6},{8,9},{9,8},{10,11... | collective-permute-start | bytes 1572872 | tf_op jit(solution)/shard_map/ppermute | solution.py:53
  234.3 15.2 %collective-permute-start.4 = (bf16[512,512]{1,0:T(8,128)(2,1)}, bf16[512,512]{1,0:T(8,128)(2,1)S(1)}, u32[]{:S(2)}, u32[]{:S(2)}) collective-permute-start(bf16[512,512]{1,0:T(8,128)(2,1)} %collective-permute-done.3.refs_4_), channel_id=1, source_target_pairs={{0,1},{1,0},{2,3},{3,2},{4,5},{5,4},{6,7},{7,6},{8,9},{9,8},{10,11... | collective-permute-start | bytes 1572872 | tf_op jit(solution)/shard_map/ppermute | solution.py:53
  238.0 12.2 %collective-permute-start.7 = (bf16[512,512]{1,0:T(8,128)(2,1)S(1)}, bf16[512,512]{1,0:T(8,128)(2,1)S(1)}, u32[]{:S(2)}, u32[]{:S(2)}) collective-permute-start(bf16[512,512]{1,0:T(8,128)(2,1)S(1)} %constant_dynamic-update-slice_fusion.refs_6_), channel_id=1, source_target_pairs={{0,1},{1,0},{2,3},{3,2},{4,5},{5,4},{6,7},{7,6},{8,9},{9,8},{10,11... | collective-permute-start | bytes 1572872 | tf_op jit(solution)/shard_map/ppermute | solution.py:53
  282.9 14.5 %collective-permute-start.25 = (bf16[512,512]{1,0:T(8,128)(2,1)S(1)}, bf16[512,512]{1,0:T(8,128)(2,1)S(1)}, u32[]{:S(2)}, u32[]{:S(2)}) collective-permute-start(bf16[512,512]{1,0:T(8,128)(2,1)S(1)} %attention.1.refs_0_), channel_id=1, source_target_pairs={{0,2},{1,3},{2,4},{3,5},{4,6},{5,7},{6,0},{7,1},{8,10},{9,11},{10,... | collective-permute-start | bytes 1572872 | tf_op jit(solution)/shard_map/ppermute | solution.py:42
  283.0 14.5 %collective-permute-start.27 = (bf16[512,512]{1,0:T(8,128)(2,1)S(1)}, bf16[512,512]{1,0:T(8,128)(2,1)S(1)}, u32[]{:S(2)}, u32[]{:S(2)}) collective-permute-start(bf16[512,512]{1,0:T(8,128)(2,1)S(1)} %attention.1.refs_0_), channel_id=1, source_target_pairs={{0,6},{1,7},{2,0},{3,1},{4,2},{5,3},{6,4},{7,5},{8,14},{9,15},{10,... | collective-permute-start | bytes 1572872 | tf_op jit(solution)/shard_map/ppermute | solution.py:43
  297.4 8.0 %collective-permute-start.29 = (bf16[256,512]{1,0:T(8,128)(2,1)S(1)}, bf16[256,512]{1,0:T(8,128)(2,1)S(1)}, u32[]{:S(2)}, u32[]{:S(2)}) collective-permute-start(bf16[256,512]{1,0:T(8,128)(2,1)S(1)} %slice.108), channel_id=1, source_target_pairs={{0,2},{1,3},{2,4},{3,5},{4,6},{5,7},{6,0},{7,1},{8,10},{9,11},{10,... | collective-permute-start | bytes 786440 | tf_op jit(solution)/shard_map/ppermute | solution.py:44
  297.5 7.9 %collective-permute-start.30 = (bf16[256,512]{1,0:T(8,128)(2,1)S(1)}, bf16[256,512]{1,0:T(8,128)(2,1)S(1)}, u32[]{:S(2)}, u32[]{:S(2)}) collective-permute-start(bf16[256,512]{1,0:T(8,128)(2,1)S(1)} %slice.109), channel_id=1, source_target_pairs={{0,6},{1,7},{2,0},{3,1},{4,2},{5,3},{6,4},{7,5},{8,14},{9,15},{10,... | collective-permute-start | bytes 786440 | tf_op jit(solution)/shard_map/ppermute | solution.py:45
  (55 other events, 765.8 us)
Sparse Core Ops, SparseCore 0:
  10.2 64.4 all-gather.2
  76.8 51.0 all-gather.4

commit v2 on v1

v2 whole, which is shorter than its diff:
```python
import math

import jax
import jax.numpy as jnp
from jax import lax
from jax.experimental import pallas as pl
from jax.experimental.pallas import tpu as pltpu
from jax.sharding import PartitionSpec as P

HEAD = 128
GROUP = 4
WIN = 1024
SINKS = 4
PAGE = 128
EPSILON = 1e-06
ROPE_BASE = 1000000.0
TOK = 512
FEAT = 512
PROMPTS = 4
BF = jnp.bfloat16
F32 = jnp.float32
NEG = -1e30


def perm_x(k):
    return [(i, (i // 4 + k) % 4 * 4 + i % 4) for i in range(16)]


def perm_y(k):
    return [(i, i // 4 * 4 + (i % 4 + k) % 4) for i in range(16)]


def perm_z(k):
    return [(i, (i // 2 + k) % 4 * 2 + i % 2) for i in range(8)]


SWAP = [(i, i ^ 1) for i in range(8)]


def ring4(block, axis, perm, half):
    before = lax.ppermute(block, axis, perm(1))
    after = lax.ppermute(block, axis, perm(-1))
    far_low = lax.ppermute(before[:half], axis, perm(1))
    far_high = lax.ppermute(after[half:], axis, perm(-1))
    return before, after, jnp.concatenate([far_low, far_high], axis=0)


def gather_col(block, half):
    other = lax.ppermute(block, "col", SWAP)
    out = [block, other]
    for piece in ring4(block, "col", perm_z, half):
        out += [piece, lax.ppermute(piece, "col", SWAP)]
    return out


def col_order(col):
    chip, core = col // 2, col % 2
    return [lax.rem(chip + d, 4) * 2 + lax.rem(core + s, 2) for d in (0, 3, 1, 2) for s in (0, 1)]


def prompt_rows(length_ref):
    start, rows = jnp.int32(0), []
    for p in range(PROMPTS):
        rows.append((start, start + length_ref[0, p]))
        start = start + length_ref[0, p]
    return rows


def per_token(rows, values, token, default=0):
    out = jnp.full(token.shape, default, jnp.int32)
    for (start, end), value in zip(rows, values):
        out = jnp.where((token >= start) & (token < end), value, out)
    return out


def in_hbm(x):
    return pltpu.with_memory_space_constraint(x, pltpu.HBM)


def vmem(n):
    return pltpu.CompilerParams(vmem_limit_bytes=n << 20)


def whole(*shape):
    return pl.BlockSpec(shape, lambda *_: (0,) * len(shape))


def pick_body(me_ref, owner_ref, index_ref, store_ref, out_ref):
    def group(r, carry):
        first, second, count = jnp.int32(0), jnp.int32(0), jnp.int32(0)
        for q in range(16):
            hit = owner_ref[r * 16 + q, 0] == me_ref[0]
            index = index_ref[r * 16 + q]
            first = jnp.where(hit & (count == 0), index, first)
            second = jnp.where(hit & (count == 1), index, second)
            count = count + hit.astype(jnp.int32)
        out_ref[r, 0] = store_ref[first]
        out_ref[r, 1] = store_ref[second]
        return carry

    lax.fori_loop(0, 16, group, 0)


def pick_pages(me, owner, index, store):
    return pl.pallas_call(
        pick_body,
        out_shape=jax.ShapeDtypeStruct((16, 2) + store.shape[1:], store.dtype),
        grid_spec=pltpu.PrefetchScalarGridSpec(
            num_scalar_prefetch=3,
            grid=(1,),
            in_specs=[whole(*store.shape)],
            out_specs=whole(16, 2, *store.shape[1:]),
        ),
        compiler_params=vmem(10),
        name="pick_pages",
    )(me, owner, index, store)


def pack_body(me_ref, down_ref, up_ref, odown_ref, oup_ref, out_ref):
    piece = jnp.zeros((80, 640), BF)
    out_ref[0] = piece
    out_ref[0, 0:32, :FEAT] = down_ref[0]
    out_ref[0, 32:48, :] = up_ref[0]
    out_ref[0, 48:64, :FEAT] = odown_ref[0]
    out_ref[0, 64:80, :FEAT] = oup_ref[0]
    for r in range(1, 16):
        out_ref[r] = out_ref[0]


def pack_slots(me, down, up, odown, oup):
    return pl.pallas_call(
        pack_body,
        out_shape=jax.ShapeDtypeStruct((16, 80, 640), BF),
        grid_spec=pltpu.PrefetchScalarGridSpec(
            num_scalar_prefetch=1,
            grid=(1,),
            in_specs=[
                pl.BlockSpec((1, 32, FEAT), lambda i, me: (0, 0, me[1])),
                whole(1, 16, 640),
                whole(1, 16, FEAT),
                pl.BlockSpec((1, 16, FEAT), lambda i, me: (0, 0, me[1])),
            ],
            out_specs=whole(16, 80, 640),
        ),
        name="pack_slots",
    )(me, down, up, odown, oup)


def select_body(adapter_ref, position_ref, slots_ref, maps_ref, up_ref, oup_ref):
    up_ref[...] = jnp.zeros_like(up_ref)
    for p in range(PROMPTS):
        slot = position_ref[adapter_ref[p]]
        maps_ref[p * 32 : p * 32 + 32, :] = slots_ref[slot, 0:32, :FEAT]
        maps_ref[128 + p * 16 : 128 + p * 16 + 16, :] = slots_ref[slot, 48:64, :FEAT]
        up_ref[p * 32 : p * 32 + 16, :512] = slots_ref[slot, 32:48, :512]
        up_ref[p * 32 + 16 : p * 32 + 32, 512:] = slots_ref[slot, 32:48, 512:]
        oup_ref[p * 16 : p * 16 + 16, :] = slots_ref[slot, 64:80, :FEAT]


def select_slots(adapter, position, slots):
    return pl.pallas_call(
        select_body,
        out_shape=(
            jax.ShapeDtypeStruct((192, FEAT), BF),
            jax.ShapeDtypeStruct((128, 640), BF),
            jax.ShapeDtypeStruct((64, FEAT), BF),
        ),
        grid_spec=pltpu.PrefetchScalarGridSpec(
            num_scalar_prefetch=2,
            grid=(1,),
            in_specs=[whole(16, 80, 640)],
            out_specs=(whole(192, FEAT), whole(128, 640), whole(64, FEAT)),
        ),
        name="select_slots",
    )(adapter, position, slots)


def norm_body(me_ref, length_ref, *refs):
    blocks, maps = refs[:8], refs[8:16]
    gain_ref, normed_ref, low_ref = refs[16:]
    order = col_order(me_ref[1])
    values = [b[...].astype(F32) for b in blocks]
    total = sum(jnp.sum(v * v, axis=-1, keepdims=True) for v in values)
    scale = lax.rsqrt(total * (1.0 / (8 * FEAT)) + EPSILON)
    low = jnp.zeros(low_ref.shape, F32)
    for b in range(8):
        gain = gain_ref[order[b]].astype(F32)
        normed = (values[b] * scale * gain).astype(BF)
        normed_ref[order[b]] = normed
        low += lax.dot_general(normed, maps[b][:128, :], (((1,), (1,)), ((), ())), preferred_element_type=F32)
    token = pl.program_id(0) * low.shape[0] + lax.broadcasted_iota(jnp.int32, low.shape, 0)
    prompt = per_token(prompt_rows(length_ref), range(PROMPTS), token)
    mine = lax.broadcasted_iota(jnp.int32, low.shape, 1) // 32 == prompt
    low_ref[...] = jnp.where(mine, low, 0.0).astype(BF)


def norm_low(me, lengths, blocks, maps, gain):
    rows = 128
    return pl.pallas_call(
        norm_body,
        out_shape=(jax.ShapeDtypeStruct((8, TOK, FEAT), BF), jax.ShapeDtypeStruct((TOK, 128), BF)),
        grid_spec=pltpu.PrefetchScalarGridSpec(
            num_scalar_prefetch=2,
            grid=(TOK // rows,),
            in_specs=[pl.BlockSpec((rows, FEAT), lambda i, *_: (i, 0))] * 8
            + [whole(192, FEAT)] * 8
            + [whole(8, 1, FEAT)],
            out_specs=(
                pl.BlockSpec((8, rows, FEAT), lambda i, *_: (0, i, 0)),
                pl.BlockSpec((rows, 128), lambda i, *_: (i, 0)),
            ),
        ),
        compiler_params=vmem(20),
        name="norm_low",
    )(me, lengths, *blocks, *maps, gain)


def qkv_body(normed_ref, w_ref, low_ref, up_ref, rope_ref, qg_ref, kg_ref, q_ref, kv_ref, acc):
    step = pl.program_id(0)
    part = jnp.dot(normed_ref[0], w_ref[...], preferred_element_type=F32)

    @pl.when(step == 0)
    def _():
        acc[...] = part

    @pl.when(step > 0)
    def _():
        acc[...] += part

    @pl.when(step == pl.num_programs(0) - 1)
    def _():
        change = 0.5 * jnp.dot(low_ref[...], up_ref[...], preferred_element_type=F32)
        rope = rope_ref[...]
        front = lax.broadcasted_iota(jnp.int32, rope.shape, 1) < HEAD // 2
        swapped = pltpu.roll(rope, HEAD // 2, 1)
        cos, sin = jnp.where(front, rope, swapped), jnp.where(front, -swapped, rope)

        def finish(raw, gain):
            scale = lax.rsqrt(jnp.mean(raw * raw, axis=-1, keepdims=True) + EPSILON)
            x = raw * scale * gain
            return (x * cos + pltpu.roll(x, HEAD // 2, 1) * sin).astype(BF)

        for h in range(GROUP):
            cut = slice(h * HEAD, (h + 1) * HEAD)
            q_ref[h] = finish(acc[:, cut] + change[:, cut], qg_ref[...].astype(F32))
        kv_ref[0] = finish(acc[:, 512:640], kg_ref[...].astype(F32))
        kv_ref[1] = (acc[:, 640:768] + change[:, 512:640]).astype(BF)


def project(normed, weight, low, up, rope, q_gain, k_gain):
    return pl.pallas_call(
        qkv_body,
        out_shape=(jax.ShapeDtypeStruct((GROUP, TOK, HEAD), BF), jax.ShapeDtypeStruct((2, TOK, HEAD), BF)),
        grid=(8,),
        in_specs=[
            pl.BlockSpec((1, TOK, FEAT), lambda k: (k, 0, 0)),
            pl.BlockSpec((FEAT, 768), lambda k: (k, 0)),
            whole(TOK, 128),
            whole(128, 640),
            whole(TOK, HEAD),
            whole(1, HEAD),
            whole(1, HEAD),
        ],
        out_specs=(whole(GROUP, TOK, HEAD), whole(2, TOK, HEAD)),
        scratch_shapes=[pltpu.VMEM((TOK, 768), F32)],
        compiler_params=vmem(16),
        name="project",
    )(in_hbm(normed), in_hbm(weight), low, up, rope, q_gain, k_gain)


BLOCK = 64
SCALE2 = math.log2(math.e) / math.sqrt(HEAD)


def attend_body(me_ref, length_ref, cache_ref, owner_ref, q_ref, kv_ref, pages_ref, out_ref, m_ref, l_ref, acc_ref, page_ref):
    rows, span = GROUP * BLOCK, 256 + BLOCK
    base = me_ref[0] * 16
    for i in range(16):
        holder, rank = owner_ref[base + i, 0], jnp.int32(0)
        for k in range(i):
            rank = rank + (owner_ref[base + k, 0] == holder).astype(jnp.int32)
        page_ref[i] = holder * 2 + rank
    prompts = prompt_rows(length_ref)
    begins = [start for start, _ in prompts]
    count, ranks = jnp.int32(0), []
    for p in range(PROMPTS):
        has = cache_ref[p] > 0
        ranks.append(jnp.where(has, count, -1))
        count = count + has.astype(jnp.int32)
    owners = []
    for j in range(2):
        pick = [(ranks[p] == j).astype(jnp.int32) for p in range(PROMPTS)]
        owners.append(tuple(sum(k * v for k, v in zip(pick, vs)) for vs in zip(*((s, e, cache_ref[p]) for p, (s, e) in enumerate(prompts)))))

    def block(t, carry):
        start = pl.multiple_of(t * BLOCK, BLOCK)
        lo = pl.multiple_of(jnp.maximum(start - 256, 0), BLOCK)
        cut = pl.ds(start, BLOCK)
        q = q_ref[:, cut, :].reshape(rows, HEAD)
        s = lax.dot_general(q, kv_ref[0, pl.ds(lo, span), :], (((1,), (1,)), ((), ())), preferred_element_type=F32)
        key = lo + lax.broadcasted_iota(jnp.int32, (BLOCK, span), 1)
        token = start + lax.broadcasted_iota(jnp.int32, (BLOCK, span), 0)
        column = start + lax.broadcasted_iota(jnp.int32, (BLOCK, 1), 0)
        begin = per_token(prompts, begins, column)
        seen = (key <= token) & (key >= begin)
        s = jnp.where(seen[None], s.reshape(GROUP, BLOCK, span), NEG).reshape(rows, span)
        m = jnp.max(s, axis=1, keepdims=True)
        w = jnp.exp2((s - m) * SCALE2)
        m_ref[...] = m
        l_ref[...] = jnp.sum(w, axis=1, keepdims=True)
        acc_ref[...] = jnp.dot(w.astype(BF), kv_ref[1, pl.ds(lo, span), :], preferred_element_type=F32)

        def cached(j):
            first, last, length = owners[j]
            mine = (column >= first) & (column < last)
            least = jnp.where(mine, length + column - first - WIN, 1 << 30)
            sink = jnp.where(mine, SINKS, 0)
            pieces = []
            for k in range(8):
                page = page_ref[j * 8 + k]
                c = lax.dot_general(q, pages_ref[page, 0], (((1,), (1,)), ((), ())), preferred_element_type=F32)
                at = k * PAGE + lax.broadcasted_iota(jnp.int32, (BLOCK, PAGE), 1)
                ok = at > least
                if k == 0:
                    ok = ok | (at < sink)
                ok = ok & (at < length)
                pieces.append(jnp.where(ok[None], c.reshape(GROUP, BLOCK, PAGE), NEG).reshape(rows, PAGE))
            top = pieces[0]
            for c in pieces[1:]:
                top = jnp.maximum(top, c)
            m_old = m_ref[...]
            m_new = jnp.maximum(m_old, jnp.max(top, axis=1, keepdims=True))
            fade = jnp.exp2((m_old - m_new) * SCALE2)
            total = jnp.zeros((rows, PAGE), F32)
            acc = acc_ref[...] * fade
            for k in range(8):
                page = page_ref[j * 8 + k]
                w = jnp.exp2((pieces[k] - m_new) * SCALE2)
                total += w
                acc += jnp.dot(w.astype(BF), pages_ref[page, 1], preferred_element_type=F32)
            m_ref[...] = m_new
            l_ref[...] = l_ref[...] * fade + jnp.sum(total, axis=1, keepdims=True)
            acc_ref[...] = acc

        for j in range(2):
            pl.when((owners[j][0] < start + BLOCK) & (owners[j][1] > start))(lambda j=j: cached(j))

        done = (acc_ref[...] * (1.0 / l_ref[...])).astype(BF)
        for h in range(GROUP):
            out_ref[cut, h * HEAD : (h + 1) * HEAD] = done[h * BLOCK : (h + 1) * BLOCK, :]
        return carry

    lax.fori_loop(0, TOK // BLOCK, block, 0)


def attention(me, lengths, cached, owner, q, kv, pages):
    rows = GROUP * BLOCK
    return pl.pallas_call(
        attend_body,
        out_shape=jax.ShapeDtypeStruct((TOK, FEAT), BF),
        grid_spec=pltpu.PrefetchScalarGridSpec(
            num_scalar_prefetch=4,
            grid=(1,),
            in_specs=[whole(GROUP, TOK, HEAD), whole(2, TOK, HEAD), whole(32, 2, PAGE, HEAD)],
            out_specs=whole(TOK, FEAT),
            scratch_shapes=[
                pltpu.VMEM((rows, 1), F32),
                pltpu.VMEM((rows, 1), F32),
                pltpu.VMEM((rows, HEAD), F32),
                pltpu.SMEM((16,), jnp.int32),
            ],
        ),
        compiler_params=vmem(16),
        name="attention",
    )(me, lengths, cached, owner, q, kv, pages)


def out_body(me_ref, length_ref, *refs):
    blocks, maps = refs[:8], refs[8:16]
    w_ref, oup_ref, hidden_ref, out_ref = refs[16:]
    order = col_order(me_ref[1])
    total = hidden_ref[...].astype(F32)
    low = jnp.zeros((total.shape[0], 64), F32)
    for b in range(8):
        x = blocks[b][...]
        total += jnp.dot(x, w_ref[order[b]], preferred_element_type=F32)
        low += lax.dot_general(x, maps[b][128:192, :], (((1,), (1,)), ((), ())), preferred_element_type=F32)
    token = pl.program_id(0) * low.shape[0] + lax.broadcasted_iota(jnp.int32, low.shape, 0)
    prompt = per_token(prompt_rows(length_ref), range(PROMPTS), token)
    mine = lax.broadcasted_iota(jnp.int32, low.shape, 1) // 16 == prompt
    low = jnp.where(mine, low, 0.0)
    change = jnp.dot(low, oup_ref[...].astype(F32), precision=lax.Precision.HIGHEST, preferred_element_type=F32)
    out_ref[...] = (total + 0.5 * change).astype(BF)


def output(me, lengths, blocks, maps, weight, oup, hidden):
    rows = 128
    tok = pl.BlockSpec((rows, FEAT), lambda i, *_: (i, 0))
    return pl.pallas_call(
        out_body,
        out_shape=jax.ShapeDtypeStruct((TOK, FEAT), BF),
        grid_spec=pltpu.PrefetchScalarGridSpec(
            num_scalar_prefetch=2,
            grid=(TOK // rows,),
            in_specs=[tok] * 8 + [whole(192, FEAT)] * 8 + [whole(8, FEAT, FEAT), whole(64, FEAT), tok],
            out_specs=tok,
        ),
        compiler_params=vmem(24),
        name="output",
    )(me, lengths, *map(in_hbm, blocks), *map(in_hbm, maps), in_hbm(weight), in_hbm(oup), in_hbm(hidden))


def on_device(
    hidden_input,
    input_norm_gain,
    query_norm_gain,
    key_norm_gain,
    query_key_value_weight,
    output_weight,
    adapter_down_maps,
    adapter_up_maps,
    output_down_maps,
    output_up_maps,
    prompt_adapter,
    adapter_position,
    prompt_length,
    cache_length,
    page_owner_row,
    page_store_index,
    cache_page_store,
):
    me = jnp.stack([lax.axis_index("row"), lax.axis_index("col")]).astype(jnp.int32)
    weight = lax.all_gather(query_key_value_weight, "row", axis=0, tiled=True)

    slots = pack_slots(me, adapter_down_maps, adapter_up_maps, output_down_maps, output_up_maps)
    slots = lax.all_to_all(slots, "row", 0, 0)

    picked = pick_pages(me, page_owner_row, page_store_index, cache_page_store)
    picked, slots = lax.optimization_barrier((picked, slots))
    pages = lax.all_to_all(picked.reshape(16, 4 * PAGE, HEAD), "row", 0, 0).reshape(32, 2, PAGE, HEAD)

    blocks = gather_col(hidden_input, 256)

    maps, up, oup = select_slots(prompt_adapter, adapter_position, slots)
    maps = gather_col(maps, 96)

    token = lax.broadcasted_iota(jnp.int32, (TOK, HEAD), 0)
    position, start = token, jnp.int32(0)
    for p in range(PROMPTS):
        end = start + prompt_length[0, p]
        position = jnp.where((token >= start) & (token < end), token - start + cache_length[p], position)
        start = end
    frequency = ROPE_BASE ** (-2.0 * jnp.arange(HEAD // 2, dtype=F32) / HEAD)
    angles = position.astype(F32) * jnp.concatenate([frequency, frequency])[None, :]
    front = lax.broadcasted_iota(jnp.int32, (TOK, HEAD), 1) < HEAD // 2
    rope = jnp.where(front, jnp.cos(angles), jnp.sin(angles))

    normed, low = norm_low(me, prompt_length, blocks, maps, input_norm_gain.reshape(8, 1, FEAT))
    weight, later, normed, low, pages, rope, up = lax.optimization_barrier(
        (weight, output_weight, normed, low, pages, rope, up)
    )
    out_weight = lax.all_gather(later, "row", axis=0, tiled=True)
    q, new_cache = project(
        normed, weight, low, up, rope, query_norm_gain[None, :], key_norm_gain[None, :]
    )
    attended = attention(me, prompt_length, cache_length, page_owner_row, q, new_cache, pages)
    attended = gather_col(attended, 256)
    hidden_output = output(
        me, prompt_length, attended, maps, out_weight.reshape(8, FEAT, FEAT), oup, hidden_input
    )
    return hidden_output, new_cache


def solution(mesh):
    return jax.shard_map(
        on_device,
        mesh=mesh,
        in_specs=(
            P("row", "col"),
            P(),
            P(),
            P(),
            P("row", "col"),
            P("row", "col"),
            P("row", None, None),
            P("row", None, "col"),
            P("row", None, "col"),
            P("row", None, None),
            P("row"),
            P(),
            P("row", None),
            P("row"),
            P(),
            P(),
            P("row", None, None, "col"),
        ),
        out_specs=(P("row", "col"), P(None, "row", "col")),
        check_vma=False,
    )
```

time: 340 us -> 193 us (0.57)
  waiting for transfers between devices: 101 us -> 50.6 us
  Pallas kernels: 99.1 us -> 52.6 us
  local copies, waits for them, and re-layouts: 45.4 us -> 19 us
  other arithmetic: 21 us -> 6.61 us
  between operations: 27.6 us -> 17.1 us
    all_gather x1, waiting for transfers between devices: 66.7 us -> 0.01 us  [on_device(): weight = lax.all_gather(query_key_value_weight, 'row', axis=0, tiled=True)]
    pallas_call x1 -> x2, Pallas kernels: 65.6 us -> 6.56 us  [the longest x1 3.79 us: pick_pages(): pl.pallas_call(pick_body, out_shape=jax.ShapeDtypeStruct((16, 2) + store....]
    all_to_all x1 -> x2, waiting for transfers between devices: 0.01 us -> 19.3 us  [the longest x1 19.3 us: on_device(): slots = lax.all_to_all(slots, 'row', 0, 0)]
    unnamed x96 -> x78, local copies, waits for them, and re-layouts: 30.9 us -> 14.1 us
    all_to_all x1 -> x2, starting transfers between devices: 4.07 us -> 15.3 us  [the longest x1 7.77 us: on_device(): slots = lax.all_to_all(slots, 'row', 0, 0)]
    pallas_call x1, Pallas kernels: 9.66 us -> 14.9 us  [attention(): pl.pallas_call(attend_body, out_shape=jax.ShapeDtypeStruct((TOK, FEAT), B...]
    ppermute x5 -> x3, starting transfers between devices: 9.84 us -> 5.37 us  [ring4(): far_high = lax.ppermute(after[half:], axis, perm(-1))]
    sub x1 -> x0, other arithmetic: 4.28 us -> none  [token_tables(): prefix + token - begin]
  transfers between devices with their start and end apart: 35 -> 28, of which waited for: 11 -> 8; matrix products, arithmetic and copies ran while one was open for 12% -> 6% of each run, Pallas kernels for 27% -> 21%
where the time goes in v2:
time: 193 us; the launch traced here: 191 us
  Pallas kernels  52.6 us (27%)
  waiting for transfers between devices  50.6 us (26%)
  starting transfers between devices  45.5 us (24%)
  local copies, waits for them, and re-layouts  19 us (10%)
  between operations  17.1 us (9%)
  other arithmetic  6.61 us (3%)
    all_to_all x1, waiting for transfers between devices, on_device(): slots = lax.all_to_all(slots, 'row', 0, 0)  19.3 us
    ppermute x3, waiting for transfers between devices, ring4(): before = lax.ppermute(block, axis, perm(1))  17 us
    pallas_call x1, Pallas kernels, attention(): pl.pallas_call(attend_body, out_shape=jax.ShapeDtypeStruct((TOK, FEAT), B...  14.9 us
    unnamed x78, local copies, waits for them, and re-layouts  14.1 us
    pallas_call x1, Pallas kernels, output(): pl.pallas_call(out_body, out_shape=jax.ShapeDtypeStruct((TOK, FEAT), BF),...  11.5 us
    pallas_call x1, Pallas kernels, project(): pl.pallas_call(qkv_body, out_shape=(jax.ShapeDtypeStruct((GROUP, TOK, HEA...  11.2 us
    ppermute x9, starting transfers between devices, gather_col(): out += [piece, lax.ppermute(piece, 'col', SWAP)]  8.97 us
    ppermute x3, waiting for transfers between devices, ring4(): far_low = lax.ppermute(before[:half], axis, perm(1))  8.91 us
  transfers between devices with their start and end apart: 28, of which 8 were waited for; matrix products, arithmetic and copies ran while one was open for 6% of the time, Pallas kernels for 21%

profile of v2, /device:TPU:1, one launch (start us, length us, event | category | flops | bytes accessed | tf_op | source)
XLA Modules:
  0.0 191.4 jit_solution(9661203758249443338)
XLA Ops:
  8.5 2.8 %pack_slots.1 = bf16[16,80,640]{2,1,0:T(8,128)(2,1)} custom-call(s32[2]{0:T(128)} %pad_add_fusion.me_ref, bf16[1,32,4096]{2,1,0:T(8,128)(2,1)} %down_ref.1, bf16[1,16,640]{2,1,0:T(8,128)(2,1)} %up_ref.1, bf16[1,16,512]{2,1,0:T(8,128)(2,1)} %odown_ref.1, bf16[1,16,4096]{2,1,0:T(8,128)(2,1)} %oup_ref.1), custom_call_target="tpu_custom_call" | custom-call | tf_op jit(solution)/shard_map/pack_slots/pallas_call | solution.py:131
  11.2 7.8 %all-to-all-start = ((bf16[16,80,640]{2,1,0:T(8,128)(2,1)}), bf16[16,80,640]{2,1,0:T(8,128)(2,1)}, u32[]{:S(2)}, u32[]{:S(2)}) async-start(bf16[16,80,640]{2,1,0:T(8,128)(2,1)} %pack_slots.1), calls=%async_computation | async-start | bytes 3276800 | tf_op jit(solution)/shard_map/all_to_all | solution.py:436
  19.2 3.8 %pick_pages.1 = bf16[16,2,2,128,128]{4,3,2,1,0:T(8,128)(2,1)S(1)} custom-call(s32[2]{0:T(128)S(1)} %copy-done.23, s32[256,1]{1,0:T(8,128)S(1)} %copy.23.owner_ref, s32[256]{0:T(256)S(1)} %copy-done.26, bf16[8,2,128,128]{3,2,1,0:T(8,128)(2,1)S(1)} %copy-done.13), custom_call_target="tpu_custom_call" | custom-call | tf_op jit(solution)/shard_map/pick_pages/pallas_call | solution.py:105
  24.4 19.3 %all-to-all-done.slots_ref = bf16[16,80,640]{2,1,0:T(8,128)(2,1)} async-done(((bf16[16,80,640]{2,1,0:T(8,128)(2,1)}), bf16[16,80,640]{2,1,0:T(8,128)(2,1)}, u32[]{:S(2)}, u32[]{:S(2)}) %all-to-all-start) | async-done | bytes 1638432 | tf_op jit(solution)/shard_map/all_to_all | solution.py:436
  43.7 7.5 %all-to-all-start.1 = ((bf16[16,512,128]{2,1,0:T(8,128)(2,1)}), bf16[16,512,128]{2,1,0:T(8,128)(2,1)S(1)}, u32[]{:S(2)}, u32[]{:S(2)}) async-start(bf16[16,512,128]{2,1,0:T(8,128)(2,1)} %bitcast.16), calls=%async_computation.1 | async-start | bytes 4194304 | tf_op jit(solution)/shard_map/all_to_all | solution.py:440
  52.9 2.2 %collective-permute-start.3 = (bf16[512,512]{1,0:T(8,128)(2,1)S(1)}, bf16[512,512]{1,0:T(8,128)(2,1)}, u32[]{:S(2)}, u32[]{:S(2)}) collective-permute-start(bf16[512,512]{1,0:T(8,128)(2,1)S(1)} %copy-done.2), channel_id=1, source_target_pairs={{0,6},{1,7},{2,0},{3,1},{4,2},{5,3},{6,4},{7,5},{8,14},{9,15},{10,... | collective-permute-start | bytes 1572872 | tf_op jit(solution)/shard_map/ppermute | solution.py:42
  55.1 3.4 %collective-permute-start = (bf16[512,512]{1,0:T(8,128)(2,1)S(1)}, bf16[512,512]{1,0:T(8,128)(2,1)}, u32[]{:S(2)}, u32[]{:S(2)}) collective-permute-start(bf16[512,512]{1,0:T(8,128)(2,1)S(1)} %copy-done.2), channel_id=1, source_target_pairs={{0,1},{1,0},{2,3},{3,2},{4,5},{5,4},{6,7},{7,6},{8,9},{9,8},{10,11... | collective-permute-start | bytes 1572872 | tf_op jit(solution)/shard_map/ppermute | solution.py:49
  66.9 2.7 %collective-permute-start.6 = (bf16[256,512]{1,0:T(8,128)(2,1)}, bf16[256,512]{1,0:T(8,128)(2,1)}, u32[]{:S(2)}, u32[]{:S(2)}) collective-permute-start(bf16[256,512]{1,0:T(8,128)(2,1)} %slice.57), channel_id=1, source_target_pairs={{0,6},{1,7},{2,0},{3,1},{4,2},{5,3},{6,4},{7,5},{8,14},{9,15},{10,... | collective-permute-start | bytes 786440 | tf_op jit(solution)/shard_map/ppermute | solution.py:44
  72.7 4.4 %collective-permute-start.2 = (bf16[512,512]{1,0:T(8,128)(2,1)}, bf16[512,512]{1,0:T(8,128)(2,1)}, u32[]{:S(2)}, u32[]{:S(2)}) collective-permute-start(bf16[512,512]{1,0:T(8,128)(2,1)} %collective-permute-done.1.refs_2_), channel_id=1, source_target_pairs={{0,1},{1,0},{2,3},{3,2},{4,5},{5,4},{6,7},{7,6},{8,9},{9,8},{10,11... | collective-permute-start | bytes 1572872 | tf_op jit(solution)/shard_map/ppermute | solution.py:52
  77.3 2.9 %select_slots.1 = (bf16[192,512]{1,0:T(8,128)(2,1)}, bf16[128,640]{1,0:T(8,128)(2,1)}, bf16[64,512]{1,0:T(8,128)(2,1)}) custom-call(s32[4]{0:T(128)} %adapter_ref.1, s32[16]{0:T(128)} %position_ref.1, bf16[16,80,640]{2,1,0:T(8,128)(2,1)} %all-to-all-done.slots_ref), custom_call_target="tpu_custom_call" | custom-call | tf_op jit(solution)/shard_map/select_slots/pallas_call | solution.py:161
  80.2 2.7 %collective-permute-start.11 = (bf16[192,512]{1,0:T(8,128)(2,1)}, bf16[192,512]{1,0:T(8,128)(2,1)S(1)}, u32[]{:S(2)}, u32[]{:S(2)}) collective-permute-start(bf16[192,512]{1,0:T(8,128)(2,1)} %get-tuple-element.19.refs_8_), channel_id=1, source_target_pairs={{0,6},{1,7},{2,0},{3,1},{4,2},{5,3},{6,4},{7,5},{8,14},{9,15},{10,... | collective-permute-start | bytes 589832 | tf_op jit(solution)/shard_map/ppermute | solution.py:42
  83.8 3.9 %collective-permute-done.9.refs_10_ = bf16[192,512]{1,0:T(8,128)(2,1)S(1)} collective-permute-done((bf16[192,512]{1,0:T(8,128)(2,1)}, bf16[192,512]{1,0:T(8,128)(2,1)S(1)}, u32[]{:S(2)}, u32[]{:S(2)}) %collective-permute-start.9) | collective-permute-done | bytes 196640 | tf_op jit(solution)/shard_map/ppermute | solution.py:41
  89.1 5.6 %collective-permute-done.13 = bf16[96,512]{1,0:T(8,128)(2,1)S(1)} collective-permute-done((bf16[96,512]{1,0:T(8,128)(2,1)S(1)}, bf16[96,512]{1,0:T(8,128)(2,1)S(1)}, u32[]{:S(2)}, u32[]{:S(2)}) %collective-permute-start.13) | collective-permute-done | bytes 98336 | tf_op jit(solution)/shard_map/ppermute | solution.py:43
  94.7 3.9 %collective-permute-done.14 = bf16[96,512]{1,0:T(8,128)(2,1)S(1)} collective-permute-done((bf16[96,512]{1,0:T(8,128)(2,1)S(1)}, bf16[96,512]{1,0:T(8,128)(2,1)S(1)}, u32[]{:S(2)}, u32[]{:S(2)}) %collective-permute-start.14) | collective-permute-done | bytes 98336 | tf_op jit(solution)/shard_map/ppermute | solution.py:44
  100.9 2.1 %sine_select_fusion.rope_ref = f32[512,128]{1,0:T(8,128)} fusion(f32[128]{0:T(128)S(1)} %pad_maximum_fusion, s32[512]{0:T(512)S(1)} %get-tuple-element.46, s32[512]{0:T(512)S(1)} %get-tuple-element.47, s32[512]{0:T(512)S(1)} %get-tuple-element.48, s32[512]{0:T(512)S(1)} %get-tuple-element.49, pred[512]{0:T(512)(128)(4,1)S(1)} %get-tuple-element.42, ...), kind=kLoop, calls=%fused_computation | loop fusion | flops 458752 | bytes 273024 | tf_op jit(solution)/shard_map/jit(_where)/select_n | solution.py:456
  104.3 5.4 %norm_low.1 = (bf16[8,512,512]{2,1,0:T(8,128)(2,1)S(1)}, bf16[512,128]{1,0:T(8,128)(2,1)S(1)}) custom-call(s32[2]{0:T(128)S(1)} %copy-done.24, s32[1,4]{1,0:T(1,128)S(1)} %copy-done.19, bf16[512,512]{1,0:T(8,128)(2,1)S(1)} %copy-done.2, bf16[512,512]{1,0:T(8,128)(2,1)} %collective-permute-done.refs_1_, bf16[512,512]{1,0:T(8,128)(2,1)} %collective-permute-done.1.refs_2_, ...), custom_call_target="tpu_custom_call" | custom-call | tf_op jit(solution)/shard_map/norm_low/pallas_call | solution.py:199
  109.8 2.0 %copy-done.1 = bf16[8,512,512]{2,1,0:T(8,128)(2,1)} copy-done((bf16[8,512,512]{2,1,0:T(8,128)(2,1)}, bf16[8,512,512]{2,1,0:T(8,128)(2,1)S(1)}, u32[]{:S(2)}) %copy-start.1) | copy-done | bytes 4194328
  119.3 11.2 %project.1 = (bf16[4,512,128]{2,1,0:T(8,128)(2,1)S(1)}, bf16[2,512,128]{2,1,0:T(8,128)(2,1)}) custom-call(bf16[8,512,512]{2,1,0:T(8,128)(2,1)} %copy-done.1, bf16[4096,768]{1,0:T(8,128)(2,1)} %all-gather.3.cloned.1.call-done.w_ref, bf16[512,128]{1,0:T(8,128)(2,1)S(1)} %copy-done.17, bf16[128,640]{1,0:T(8,128)(2,1)S(1)} %copy-done.15, ...), custom_call_target="tpu_custom_call" | custom-call | tf_op jit(solution)/shard_map/project/pallas_call | solution.py:251
  131.5 14.9 %attention.1.refs_0_ = bf16[512,512]{1,0:T(8,128)(2,1)S(1)} custom-call(s32[2]{0:T(128)S(1)} %copy-done.25, s32[1,4]{1,0:T(1,128)S(1)} %copy-done.20, s32[4]{0:T(128)S(1)} %copy-done.22, s32[256,1]{1,0:T(8,128)S(1)} %copy.23.owner_ref, bf16[4,512,128]{2,1,0:T(8,128)(2,1)S(1)} %get-tuple-element.29.q_ref, bf16[2,512,128]{2,1,0:T(8,128)(2,1)S(1)} %copy-done.14, ...), custom_call_target="tpu_custom_call" | custom-call | tf_op jit(solution)/shard_map/attention/pallas_call | solution.py:358
  146.5 2.7 %collective-permute-start.19 = (bf16[512,512]{1,0:T(8,128)(2,1)S(1)}, bf16[512,512]{1,0:T(8,128)(2,1)S(1)}, u32[]{:S(2)}, u32[]{:S(2)}) collective-permute-start(bf16[512,512]{1,0:T(8,128)(2,1)S(1)} %attention.1.refs_0_), channel_id=1, source_target_pairs={{0,6},{1,7},{2,0},{3,1},{4,2},{5,3},{6,4},{7,5},{8,14},{9,15},{10,... | collective-permute-start | bytes 1572872 | tf_op jit(solution)/shard_map/ppermute | solution.py:42
  149.2 11.9 %collective-permute-done.17.refs_2_ = bf16[512,512]{1,0:T(8,128)(2,1)S(1)} collective-permute-done((bf16[512,512]{1,0:T(8,128)(2,1)S(1)}, bf16[512,512]{1,0:T(8,128)(2,1)S(1)}, u32[]{:S(2)}, u32[]{:S(2)}) %collective-permute-start.17) | collective-permute-done | bytes 524320 | tf_op jit(solution)/shard_map/ppermute | solution.py:41
  161.2 2.7 %collective-permute-start.22 = (bf16[256,512]{1,0:T(8,128)(2,1)S(1)}, bf16[256,512]{1,0:T(8,128)(2,1)S(1)}, u32[]{:S(2)}, u32[]{:S(2)}) collective-permute-start(bf16[256,512]{1,0:T(8,128)(2,1)S(1)} %slice.61), channel_id=1, source_target_pairs={{0,6},{1,7},{2,0},{3,1},{4,2},{5,3},{6,4},{7,5},{8,14},{9,15},{10,... | collective-permute-start | bytes 786440 | tf_op jit(solution)/shard_map/ppermute | solution.py:44
  166.0 3.3 %collective-permute-done.21 = bf16[256,512]{1,0:T(8,128)(2,1)S(1)} collective-permute-done((bf16[256,512]{1,0:T(8,128)(2,1)S(1)}, bf16[256,512]{1,0:T(8,128)(2,1)S(1)}, u32[]{:S(2)}, u32[]{:S(2)}) %collective-permute-start.21) | collective-permute-done | bytes 262176 | tf_op jit(solution)/shard_map/ppermute | solution.py:43
  173.0 11.5 %output.1 = bf16[512,512]{1,0:T(8,128)(2,1)} custom-call(s32[2]{0:T(128)S(1)} %copy-done.25, s32[1,4]{1,0:T(1,128)S(1)} %copy-done.20, bf16[512,512]{1,0:T(8,128)(2,1)} %copy-done.3, bf16[512,512]{1,0:T(8,128)(2,1)} %copy-done.32, bf16[512,512]{1,0:T(8,128)(2,1)} %copy-done.29, bf16[512,512]{1,0:T(8,128)(2,1)} %copy-done.33, bf16[512,512]{1,0:T(8,128)(2,1)} %copy-done.30, ...), custom_call_target="tpu_custom_call" | custom-call | tf_op jit(solution)/shard_map/output/pallas_call | solution.py:399
  (140 shorter events, 33.7 us)
Async XLA Ops:
  7.2 108.0 %all-gather.3.cloned.1.call-start = ((), (), s32[]{:S(2)}) async-start(), calls=%async_computation.2 | async-start | bytes 6684672 | tf_op jit(solution)/shard_map/all_gather | solution.py:433
  11.2 32.5 %all-to-all-start = ((bf16[16,80,640]{2,1,0:T(8,128)(2,1)}), bf16[16,80,640]{2,1,0:T(8,128)(2,1)}, u32[]{:S(2)}, u32[]{:S(2)}) async-start(bf16[16,80,640]{2,1,0:T(8,128)(2,1)} %pack_slots.1), calls=%async_computation | async-start | bytes 3276800 | tf_op jit(solution)/shard_map/all_to_all | solution.py:436
  43.7 71.4 %all-to-all-start.1 = ((bf16[16,512,128]{2,1,0:T(8,128)(2,1)}), bf16[16,512,128]{2,1,0:T(8,128)(2,1)S(1)}, u32[]{:S(2)}, u32[]{:S(2)}) async-start(bf16[16,512,128]{2,1,0:T(8,128)(2,1)} %bitcast.16), calls=%async_computation.1 | async-start | bytes 4194304 | tf_op jit(solution)/shard_map/all_to_all | solution.py:440
  51.2 121.7 %all-gather.5.cloned.1.call-start = ((), (), s32[]{:S(2)}) async-start(), calls=%async_computation.3 | async-start | bytes 4456448 | tf_op jit(solution)/shard_map/all_gather | solution.py:462
  51.3 12.9 %collective-permute-start.1 = (bf16[512,512]{1,0:T(8,128)(2,1)S(1)}, bf16[512,512]{1,0:T(8,128)(2,1)}, u32[]{:S(2)}, u32[]{:S(2)}) collective-permute-start(bf16[512,512]{1,0:T(8,128)(2,1)S(1)} %copy-done.2), channel_id=1, source_target_pairs={{0,2},{1,3},{2,4},{3,5},{4,6},{5,7},{6,0},{7,1},{8,10},{9,11},{10,... | collective-permute-start | bytes 1572872 | tf_op jit(solution)/shard_map/ppermute | solution.py:41
  52.9 12.4 %collective-permute-start.3 = (bf16[512,512]{1,0:T(8,128)(2,1)S(1)}, bf16[512,512]{1,0:T(8,128)(2,1)}, u32[]{:S(2)}, u32[]{:S(2)}) collective-permute-start(bf16[512,512]{1,0:T(8,128)(2,1)S(1)} %copy-done.2), channel_id=1, source_target_pairs={{0,6},{1,7},{2,0},{3,1},{4,2},{5,3},{6,4},{7,5},{8,14},{9,15},{10,... | collective-permute-start | bytes 1572872 | tf_op jit(solution)/shard_map/ppermute | solution.py:42
  55.1 45.0 %collective-permute-start = (bf16[512,512]{1,0:T(8,128)(2,1)S(1)}, bf16[512,512]{1,0:T(8,128)(2,1)}, u32[]{:S(2)}, u32[]{:S(2)}) collective-permute-start(bf16[512,512]{1,0:T(8,128)(2,1)S(1)} %copy-done.2), channel_id=1, source_target_pairs={{0,1},{1,0},{2,3},{3,2},{4,5},{5,4},{6,7},{7,6},{8,9},{9,8},{10,11... | collective-permute-start | bytes 1572872 | tf_op jit(solution)/shard_map/ppermute | solution.py:49
  65.2 15.0 %collective-permute-start.5 = (bf16[256,512]{1,0:T(8,128)(2,1)S(1)}, bf16[256,512]{1,0:T(8,128)(2,1)S(1)}, u32[]{:S(2)}, u32[]{:S(2)}) collective-permute-start(bf16[256,512]{1,0:T(8,128)(2,1)S(1)} %slice.56), channel_id=1, source_target_pairs={{0,2},{1,3},{2,4},{3,5},{4,6},{5,7},{6,0},{7,1},{8,10},{9,11},{10,... | collective-permute-start | bytes 786440 | tf_op jit(solution)/shard_map/ppermute | solution.py:43
  66.9 13.2 %collective-permute-start.6 = (bf16[256,512]{1,0:T(8,128)(2,1)}, bf16[256,512]{1,0:T(8,128)(2,1)}, u32[]{:S(2)}, u32[]{:S(2)}) collective-permute-start(bf16[256,512]{1,0:T(8,128)(2,1)} %slice.57), channel_id=1, source_target_pairs={{0,6},{1,7},{2,0},{3,1},{4,2},{5,3},{6,4},{7,5},{8,14},{9,15},{10,... | collective-permute-start | bytes 786440 | tf_op jit(solution)/shard_map/ppermute | solution.py:44
  72.7 27.4 %collective-permute-start.2 = (bf16[512,512]{1,0:T(8,128)(2,1)}, bf16[512,512]{1,0:T(8,128)(2,1)}, u32[]{:S(2)}, u32[]{:S(2)}) collective-permute-start(bf16[512,512]{1,0:T(8,128)(2,1)} %collective-permute-done.1.refs_2_), channel_id=1, source_target_pairs={{0,1},{1,0},{2,3},{3,2},{4,5},{5,4},{6,7},{7,6},{8,9},{9,8},{10,11... | collective-permute-start | bytes 1572872 | tf_op jit(solution)/shard_map/ppermute | solution.py:52
  77.2 23.5 %collective-permute-start.4 = (bf16[512,512]{1,0:T(8,128)(2,1)}, bf16[512,512]{1,0:T(8,128)(2,1)}, u32[]{:S(2)}, u32[]{:S(2)}) collective-permute-start(bf16[512,512]{1,0:T(8,128)(2,1)} %collective-permute-done.3.refs_4_), channel_id=1, source_target_pairs={{0,1},{1,0},{2,3},{3,2},{4,5},{5,4},{6,7},{7,6},{8,9},{9,8},{10,11... | collective-permute-start | bytes 1572872 | tf_op jit(solution)/shard_map/ppermute | solution.py:52
  80.1 7.6 %collective-permute-start.9 = (bf16[192,512]{1,0:T(8,128)(2,1)}, bf16[192,512]{1,0:T(8,128)(2,1)S(1)}, u32[]{:S(2)}, u32[]{:S(2)}) collective-permute-start(bf16[192,512]{1,0:T(8,128)(2,1)} %get-tuple-element.19.refs_8_), channel_id=1, source_target_pairs={{0,2},{1,3},{2,4},{3,5},{4,6},{5,7},{6,0},{7,1},{8,10},{9,11},{10,... | collective-permute-start | bytes 589832 | tf_op jit(solution)/shard_map/ppermute | solution.py:41
  80.2 8.7 %collective-permute-start.11 = (bf16[192,512]{1,0:T(8,128)(2,1)}, bf16[192,512]{1,0:T(8,128)(2,1)S(1)}, u32[]{:S(2)}, u32[]{:S(2)}) collective-permute-start(bf16[192,512]{1,0:T(8,128)(2,1)} %get-tuple-element.19.refs_8_), channel_id=1, source_target_pairs={{0,6},{1,7},{2,0},{3,1},{4,2},{5,3},{6,4},{7,5},{8,14},{9,15},{10,... | collective-permute-start | bytes 589832 | tf_op jit(solution)/shard_map/ppermute | solution.py:42
  87.7 15.3 %collective-permute-start.7 = (bf16[512,512]{1,0:T(8,128)(2,1)S(1)}, bf16[512,512]{1,0:T(8,128)(2,1)S(1)}, u32[]{:S(2)}, u32[]{:S(2)}) collective-permute-start(bf16[512,512]{1,0:T(8,128)(2,1)S(1)} %constant_dynamic-update-slice_fusion.refs_6_), channel_id=1, source_target_pairs={{0,1},{1,0},{2,3},{3,2},{4,5},{5,4},{6,7},{7,6},{8,9},{9,8},{10,11... | collective-permute-start | bytes 1572872 | tf_op jit(solution)/shard_map/ppermute | solution.py:52
  88.9 5.8 %collective-permute-start.13 = (bf16[96,512]{1,0:T(8,128)(2,1)S(1)}, bf16[96,512]{1,0:T(8,128)(2,1)S(1)}, u32[]{:S(2)}, u32[]{:S(2)}) collective-permute-start(bf16[96,512]{1,0:T(8,128)(2,1)S(1)} %slice.58), channel_id=1, source_target_pairs={{0,2},{1,3},{2,4},{3,5},{4,6},{5,7},{6,0},{7,1},{8,10},{9,11},{10,... | collective-permute-start | bytes 294920 | tf_op jit(solution)/shard_map/ppermute | solution.py:43
  94.7 3.9 %collective-permute-start.14 = (bf16[96,512]{1,0:T(8,128)(2,1)S(1)}, bf16[96,512]{1,0:T(8,128)(2,1)S(1)}, u32[]{:S(2)}, u32[]{:S(2)}) collective-permute-start(bf16[96,512]{1,0:T(8,128)(2,1)S(1)} %slice.59), channel_id=1, source_target_pairs={{0,6},{1,7},{2,0},{3,1},{4,2},{5,3},{6,4},{7,5},{8,14},{9,15},{10,... | collective-permute-start | bytes 294920 | tf_op jit(solution)/shard_map/ppermute | solution.py:44
  98.6 4.5 %collective-permute-start.8 = (bf16[192,512]{1,0:T(8,128)(2,1)}, bf16[192,512]{1,0:T(8,128)(2,1)S(1)}, u32[]{:S(2)}, u32[]{:S(2)}) collective-permute-start(bf16[192,512]{1,0:T(8,128)(2,1)} %get-tuple-element.19.refs_8_), channel_id=1, source_target_pairs={{0,1},{1,0},{2,3},{3,2},{4,5},{5,4},{6,7},{7,6},{8,9},{9,8},{10,11... | collective-permute-start | bytes 589832 | tf_op jit(solution)/shard_map/ppermute | solution.py:49
  146.4 14.7 %collective-permute-start.17 = (bf16[512,512]{1,0:T(8,128)(2,1)S(1)}, bf16[512,512]{1,0:T(8,128)(2,1)S(1)}, u32[]{:S(2)}, u32[]{:S(2)}) collective-permute-start(bf16[512,512]{1,0:T(8,128)(2,1)S(1)} %attention.1.refs_0_), channel_id=1, source_target_pairs={{0,2},{1,3},{2,4},{3,5},{4,6},{5,7},{6,0},{7,1},{8,10},{9,11},{10,... | collective-permute-start | bytes 1572872 | tf_op jit(solution)/shard_map/ppermute | solution.py:41
  146.5 14.7 %collective-permute-start.19 = (bf16[512,512]{1,0:T(8,128)(2,1)S(1)}, bf16[512,512]{1,0:T(8,128)(2,1)S(1)}, u32[]{:S(2)}, u32[]{:S(2)}) collective-permute-start(bf16[512,512]{1,0:T(8,128)(2,1)S(1)} %attention.1.refs_0_), channel_id=1, source_target_pairs={{0,6},{1,7},{2,0},{3,1},{4,2},{5,3},{6,4},{7,5},{8,14},{9,15},{10,... | collective-permute-start | bytes 1572872 | tf_op jit(solution)/shard_map/ppermute | solution.py:42
  161.1 8.1 %collective-permute-start.21 = (bf16[256,512]{1,0:T(8,128)(2,1)S(1)}, bf16[256,512]{1,0:T(8,128)(2,1)S(1)}, u32[]{:S(2)}, u32[]{:S(2)}) collective-permute-start(bf16[256,512]{1,0:T(8,128)(2,1)S(1)} %slice.60), channel_id=1, source_target_pairs={{0,2},{1,3},{2,4},{3,5},{4,6},{5,7},{6,0},{7,1},{8,10},{9,11},{10,... | collective-permute-start | bytes 786440 | tf_op jit(solution)/shard_map/ppermute | solution.py:43
  161.2 8.0 %collective-permute-start.22 = (bf16[256,512]{1,0:T(8,128)(2,1)S(1)}, bf16[256,512]{1,0:T(8,128)(2,1)S(1)}, u32[]{:S(2)}, u32[]{:S(2)}) collective-permute-start(bf16[256,512]{1,0:T(8,128)(2,1)S(1)} %slice.61), channel_id=1, source_target_pairs={{0,6},{1,7},{2,0},{3,1},{4,2},{5,3},{6,4},{7,5},{8,14},{9,15},{10,... | collective-permute-start | bytes 786440 | tf_op jit(solution)/shard_map/ppermute | solution.py:44
  164.0 7.3 %collective-permute-start.16 = (bf16[512,512]{1,0:T(8,128)(2,1)S(1)}, bf16[512,512]{1,0:T(8,128)(2,1)S(1)}, u32[]{:S(2)}, u32[]{:S(2)}) collective-permute-start(bf16[512,512]{1,0:T(8,128)(2,1)S(1)} %attention.1.refs_0_), channel_id=1, source_target_pairs={{0,1},{1,0},{2,3},{3,2},{4,5},{5,4},{6,7},{7,6},{8,9},{9,8},{10,11... | collective-permute-start | bytes 1572872 | tf_op jit(solution)/shard_map/ppermute | solution.py:49
  165.5 5.8 %collective-permute-start.18 = (bf16[512,512]{1,0:T(8,128)(2,1)S(1)}, bf16[512,512]{1,0:T(8,128)(2,1)S(1)}, u32[]{:S(2)}, u32[]{:S(2)}) collective-permute-start(bf16[512,512]{1,0:T(8,128)(2,1)S(1)} %collective-permute-done.17.refs_2_), channel_id=1, source_target_pairs={{0,1},{1,0},{2,3},{3,2},{4,5},{5,4},{6,7},{7,6},{8,9},{9,8},{10,11... | collective-permute-start | bytes 1572872 | tf_op jit(solution)/shard_map/ppermute | solution.py:52
  165.5 5.8 %collective-permute-start.20 = (bf16[512,512]{1,0:T(8,128)(2,1)S(1)}, bf16[512,512]{1,0:T(8,128)(2,1)S(1)}, u32[]{:S(2)}, u32[]{:S(2)}) collective-permute-start(bf16[512,512]{1,0:T(8,128)(2,1)S(1)} %collective-permute-done.19.refs_4_), channel_id=1, source_target_pairs={{0,1},{1,0},{2,3},{3,2},{4,5},{5,4},{6,7},{7,6},{8,9},{9,8},{10,11... | collective-permute-start | bytes 1572872 | tf_op jit(solution)/shard_map/ppermute | solution.py:52
  (41 other events, 290.7 us)
Sparse Core Ops, SparseCore 0:
  10.2 93.6 all-gather.2
  115.3 51.4 all-gather.4

commit v3 on v2

v3 whole, which is shorter than its diff:
```python
import math

import jax
import jax.numpy as jnp
from jax import lax
from jax.experimental import pallas as pl
from jax.experimental.pallas import tpu as pltpu
from jax.sharding import PartitionSpec as P

HEAD = 128
GROUP = 4
WIN = 1024
SINKS = 4
PAGE = 128
EPSILON = 1e-06
ROPE_BASE = 1000000.0
TOK = 512
FEAT = 512
PROMPTS = 4
BF = jnp.bfloat16
F32 = jnp.float32
NEG = -1e30


def perm_x(k):
    return [(i, (i // 4 + k) % 4 * 4 + i % 4) for i in range(16)]


def perm_y(k):
    return [(i, i // 4 * 4 + (i % 4 + k) % 4) for i in range(16)]


def perm_z(k):
    return [(i, (i // 2 + k) % 4 * 2 + i % 2) for i in range(8)]


SWAP = [(i, i ^ 1) for i in range(8)]


def ring4(block, axis, perm, half):
    before = lax.ppermute(block, axis, perm(1))
    after = lax.ppermute(block, axis, perm(-1))
    far_low = lax.ppermute(before[:half], axis, perm(1))
    far_high = lax.ppermute(after[half:], axis, perm(-1))
    return before, after, jnp.concatenate([far_low, far_high], axis=0)


def gather_col(block, half):
    other = lax.ppermute(block, "col", SWAP)
    out = [block, other]
    for piece in ring4(block, "col", perm_z, half):
        out += [piece, lax.ppermute(piece, "col", SWAP)]
    return out


def col_order(col):
    chip, core = col // 2, col % 2
    return [lax.rem(chip + d, 4) * 2 + lax.rem(core + s, 2) for d in (0, 3, 1, 2) for s in (0, 1)]


def prompt_rows(length_ref):
    start, rows = jnp.int32(0), []
    for p in range(PROMPTS):
        rows.append((start, start + length_ref[0, p]))
        start = start + length_ref[0, p]
    return rows


def per_token(rows, values, token, default=0):
    out = jnp.full(token.shape, default, jnp.int32)
    for (start, end), value in zip(rows, values):
        out = jnp.where((token >= start) & (token < end), value, out)
    return out


def in_hbm(x):
    return pltpu.with_memory_space_constraint(x, pltpu.HBM)


def vmem(n):
    return pltpu.CompilerParams(vmem_limit_bytes=n << 20)


def whole(*shape):
    return pl.BlockSpec(shape, lambda *_: (0,) * len(shape))


def pick_body(me_ref, owner_ref, index_ref, store_ref, out_ref):
    def group(r, carry):
        first, second, count = jnp.int32(0), jnp.int32(0), jnp.int32(0)
        for q in range(16):
            hit = owner_ref[r * 16 + q, 0] == me_ref[0]
            index = index_ref[r * 16 + q]
            first = jnp.where(hit & (count == 0), index, first)
            second = jnp.where(hit & (count == 1), index, second)
            count = count + hit.astype(jnp.int32)
        out_ref[r, 0] = store_ref[first]
        out_ref[r, 1] = store_ref[second]
        return carry

    lax.fori_loop(0, 16, group, 0)


def pick_pages(me, owner, index, store):
    return pl.pallas_call(
        pick_body,
        out_shape=jax.ShapeDtypeStruct((16, 2) + store.shape[1:], store.dtype),
        grid_spec=pltpu.PrefetchScalarGridSpec(
            num_scalar_prefetch=3,
            grid=(1,),
            in_specs=[whole(*store.shape)],
            out_specs=whole(16, 2, *store.shape[1:]),
        ),
        compiler_params=vmem(10),
        name="pick_pages",
    )(me, owner, index, store)


def pack_body(me_ref, qkv_ref, wo_ref, up_ref, oup_ref, down_ref, odown_ref, wide_ref, slots_ref):
    wide_ref[:256, :768] = qkv_ref[...]
    wide_ref[:256, 768:] = wo_ref[...]
    wide_ref[256:, :640] = up_ref[0]
    wide_ref[256:, 640:1152] = oup_ref[0]
    wide_ref[256:, 1152:] = jnp.zeros((16, 128), BF)
    for r in range(16):
        slots_ref[r, :32, :] = down_ref[0]
        slots_ref[r, 32:, :] = odown_ref[0]


def pack(me, qkv, wo, up, oup, down, odown):
    return pl.pallas_call(
        pack_body,
        out_shape=(jax.ShapeDtypeStruct((272, 1280), BF), jax.ShapeDtypeStruct((16, 48, FEAT), BF)),
        grid_spec=pltpu.PrefetchScalarGridSpec(
            num_scalar_prefetch=1,
            grid=(1,),
            in_specs=[
                whole(256, 768),
                whole(256, FEAT),
                whole(1, 16, 640),
                pl.BlockSpec((1, 16, FEAT), lambda i, me: (0, 0, me[1])),
                pl.BlockSpec((1, 32, FEAT), lambda i, me: (0, 0, me[1])),
                whole(1, 16, FEAT),
            ],
            out_specs=(whole(272, 1280), whole(16, 48, FEAT)),
        ),
        name="pack",
    )(me, qkv, wo, up, oup, down, odown)


def select_body(adapter_ref, position_ref, slots_ref, maps_ref):
    for p in range(PROMPTS):
        slot = position_ref[adapter_ref[p]]
        maps_ref[p * 32 : p * 32 + 32, :] = slots_ref[slot, :32, :]
        maps_ref[128 + p * 16 : 128 + p * 16 + 16, :] = slots_ref[slot, 32:, :]


def select_slots(adapter, position, slots):
    return pl.pallas_call(
        select_body,
        out_shape=jax.ShapeDtypeStruct((192, FEAT), BF),
        grid_spec=pltpu.PrefetchScalarGridSpec(
            num_scalar_prefetch=2,
            grid=(1,),
            in_specs=[whole(16, 48, FEAT)],
            out_specs=whole(192, FEAT),
        ),
        name="select_slots",
    )(adapter, position, slots)


def norm_body(me_ref, length_ref, *refs):
    blocks, maps = refs[:8], refs[8:16]
    gain_ref, normed_ref, low_ref = refs[16:]
    order = col_order(me_ref[1])
    values = [b[...].astype(F32) for b in blocks]
    total = sum(jnp.sum(v * v, axis=-1, keepdims=True) for v in values)
    scale = lax.rsqrt(total * (1.0 / (8 * FEAT)) + EPSILON)
    low = jnp.zeros(low_ref.shape, F32)
    for b in range(8):
        gain = gain_ref[order[b]].astype(F32)
        normed = (values[b] * scale * gain).astype(BF)
        normed_ref[order[b] // 2, :, pl.ds(pl.multiple_of(order[b] % 2 * FEAT, FEAT), FEAT)] = normed
        low += lax.dot_general(normed, maps[b][:128, :], (((1,), (1,)), ((), ())), preferred_element_type=F32)
    token = pl.program_id(0) * low.shape[0] + lax.broadcasted_iota(jnp.int32, low.shape, 0)
    prompt = per_token(prompt_rows(length_ref), range(PROMPTS), token)
    mine = lax.broadcasted_iota(jnp.int32, low.shape, 1) // 32 == prompt
    low_ref[...] = jnp.where(mine, low, 0.0).astype(BF)


def norm_low(me, lengths, blocks, maps, gain):
    rows = 128
    return pl.pallas_call(
        norm_body,
        out_shape=(pltpu.HBM((4, TOK, 2 * FEAT), BF), pltpu.HBM((TOK, 128), BF)),
        grid_spec=pltpu.PrefetchScalarGridSpec(
            num_scalar_prefetch=2,
            grid=(TOK // rows,),
            in_specs=[pl.BlockSpec((rows, FEAT), lambda i, *_: (i, 0))] * 8
            + [whole(192, FEAT)] * 8
            + [whole(8, 1, FEAT)],
            out_specs=(
                pl.BlockSpec((4, rows, 2 * FEAT), lambda i, *_: (0, i, 0)),
                pl.BlockSpec((rows, 128), lambda i, *_: (i, 0)),
            ),
        ),
        compiler_params=vmem(20),
        name="norm_low",
    )(me, lengths, *blocks, *maps, gain)


def qkv_body(adapter_ref, position_ref, normed_ref, w_ref, low_ref, rope_ref, qg_ref, kg_ref, q_ref, kv_ref, x, w, up, acc, sems):
    copies = []
    for k in range(4):
        copies.append(pltpu.make_async_copy(normed_ref.at[k], x.at[k], sems.at[2 * k]))
        rows = w_ref.at[pl.ds(4 * k, 4), pl.ds(0, 256), pl.ds(0, 768)]
        copies.append(pltpu.make_async_copy(rows, w.at[k], sems.at[2 * k + 1]))
    for p in range(PROMPTS):
        slot = position_ref[adapter_ref[p]]
        copies.append(pltpu.make_async_copy(w_ref.at[slot, pl.ds(256, 16), pl.ds(0, 640)], up.at[p], sems.at[8 + p]))
    for copy in copies:
        copy.start()
    for k in range(4):
        copies[2 * k].wait()
        copies[2 * k + 1].wait()
        part = jnp.dot(x[k], w[k].reshape(1024, 768), preferred_element_type=F32)
        if k == 0:
            acc[...] = part
        else:
            acc[...] += part
    for copy in copies[8:]:
        copy.wait()
    low = low_ref[...]
    q_change = jnp.zeros((TOK, 512), F32)
    v_change = jnp.zeros((TOK, HEAD), F32)
    for p in range(PROMPTS):
        q_change += jnp.dot(low[:, p * 32 : p * 32 + 16], up[p, :, :512], preferred_element_type=F32)
        v_change += jnp.dot(low[:, p * 32 + 16 : p * 32 + 32], up[p, :, 512:], preferred_element_type=F32)
    rope = rope_ref[...]
    front = lax.broadcasted_iota(jnp.int32, rope.shape, 1) < HEAD // 2
    swapped = pltpu.roll(rope, HEAD // 2, 1)
    cos, sin = jnp.where(front, rope, swapped), jnp.where(front, -swapped, rope)

    def finish(raw, gain):
        scale = lax.rsqrt(jnp.mean(raw * raw, axis=-1, keepdims=True) + EPSILON)
        x = raw * scale * gain
        return (x * cos + pltpu.roll(x, HEAD // 2, 1) * sin).astype(BF)

    for h in range(GROUP):
        cut = slice(h * HEAD, (h + 1) * HEAD)
        q_ref[h] = finish(acc[:, cut] + 0.5 * q_change[:, cut], qg_ref[...].astype(F32))
    kv_ref[0] = finish(acc[:, 512:640], kg_ref[...].astype(F32))
    kv_ref[1] = (acc[:, 640:768] + 0.5 * v_change).astype(BF)


def project(adapter, position, normed, weight, low, rope, q_gain, k_gain):
    hbm = pl.BlockSpec(memory_space=pl.ANY)
    return pl.pallas_call(
        qkv_body,
        out_shape=(jax.ShapeDtypeStruct((GROUP, TOK, HEAD), BF), jax.ShapeDtypeStruct((2, TOK, HEAD), BF)),
        grid_spec=pltpu.PrefetchScalarGridSpec(
            num_scalar_prefetch=2,
            grid=(1,),
            in_specs=[hbm, hbm, whole(TOK, 128), whole(TOK, HEAD), whole(1, HEAD), whole(1, HEAD)],
            out_specs=(whole(GROUP, TOK, HEAD), whole(2, TOK, HEAD)),
            scratch_shapes=[
                pltpu.VMEM((4, TOK, 1024), BF),
                pltpu.VMEM((4, 4, 256, 768), BF),
                pltpu.VMEM((PROMPTS, 16, 640), BF),
                pltpu.VMEM((TOK, 768), F32),
                pltpu.SemaphoreType.DMA((12,)),
            ],
        ),
        compiler_params=vmem(28),
        name="project",
    )(adapter, position, in_hbm(normed), in_hbm(weight), in_hbm(low), in_hbm(rope), in_hbm(q_gain), in_hbm(k_gain))


BLOCK = 64
SCALE2 = math.log2(math.e) / math.sqrt(HEAD)


def attend_body(me_ref, length_ref, cache_ref, owner_ref, q_ref, kv_ref, pages_ref, out_ref, m_ref, l_ref, acc_ref, cached_ref, sems):
    rows, span = GROUP * BLOCK, 256 + BLOCK
    base = me_ref[0] * 16
    copies = []
    for i in range(16):
        holder, rank = owner_ref[base + i, 0], jnp.int32(0)
        for k in range(i):
            rank = rank + (owner_ref[base + k, 0] == holder).astype(jnp.int32)
        page = holder * 2 + jnp.minimum(rank, 1)
        for h in range(2):
            into = cached_ref.at[h, i // 8, pl.ds(i % 8 * PAGE, PAGE)]
            copies.append(pltpu.make_async_copy(pages_ref.at[page, h], into, sems.at[2 * i + h]))
    for copy in copies:
        copy.start()
    prompts = prompt_rows(length_ref)
    begins = [start for start, _ in prompts]
    count, ranks = jnp.int32(0), []
    for p in range(PROMPTS):
        has = cache_ref[p] > 0
        ranks.append(jnp.where(has, count, -1))
        count = count + has.astype(jnp.int32)
    owners = []
    for j in range(2):
        mine = [(ranks[p] == j).astype(jnp.int32) for p in range(PROMPTS)]
        owners.append(
            (
                sum(mine[p] * prompts[p][0] for p in range(PROMPTS)),
                sum(mine[p] * prompts[p][1] for p in range(PROMPTS)),
                sum(mine[p] * cache_ref[p] for p in range(PROMPTS)),
            )
        )
    for copy in copies:
        copy.wait()

    def block(t, carry):
        start = pl.multiple_of(t * BLOCK, BLOCK)
        lo = pl.multiple_of(jnp.maximum(start - 256, 0), BLOCK)
        cut = pl.ds(start, BLOCK)
        q = q_ref[:, cut, :].reshape(rows, HEAD)
        token = start + (lax.broadcasted_iota(jnp.int32, (rows, 1), 0) & (BLOCK - 1))
        begin = per_token(prompts, begins, token)
        s = lax.dot_general(q, kv_ref[0, pl.ds(lo, span), :], (((1,), (1,)), ((), ())), preferred_element_type=F32)
        key = lo + lax.broadcasted_iota(jnp.int32, (rows, span), 1)
        s = jnp.where((key <= token) & (key >= begin), s, NEG)
        m = jnp.max(s, axis=1, keepdims=True)
        w = jnp.exp2((s - m) * SCALE2)
        m_ref[...] = m
        l_ref[...] = jnp.sum(w, axis=1, keepdims=True)
        acc_ref[...] = jnp.dot(w.astype(BF), kv_ref[1, pl.ds(lo, span), :], preferred_element_type=F32)

        def cached(j):
            first, last, length = owners[j]
            mine = (token >= first) & (token < last)
            s = lax.dot_general(q, cached_ref[0, j], (((1,), (1,)), ((), ())), preferred_element_type=F32)
            at = lax.broadcasted_iota(jnp.int32, (rows, 256), 1)
            head = jnp.where((at > length + token - first - WIN) | (at < SINKS), s[:, :256], NEG)
            at = WIN - PAGE + lax.broadcasted_iota(jnp.int32, (rows, PAGE), 1)
            tail = jnp.where(at < length, s[:, WIN - PAGE :], NEG)
            s = jnp.concatenate([head, s[:, 256 : WIN - PAGE], tail], axis=1)
            m_old = m_ref[...]
            m_new = jnp.where(mine, jnp.maximum(m_old, jnp.max(s, axis=1, keepdims=True)), m_old)
            fade = jnp.exp2((m_old - m_new) * SCALE2)
            w = jnp.exp2((s - jnp.where(mine, m_new, -NEG)) * SCALE2)
            m_ref[...] = m_new
            l_ref[...] = l_ref[...] * fade + jnp.sum(w, axis=1, keepdims=True)
            acc_ref[...] = acc_ref[...] * fade + jnp.dot(w.astype(BF), cached_ref[1, j], preferred_element_type=F32)

        for j in range(2):
            pl.when((owners[j][0] < start + BLOCK) & (owners[j][1] > start))(lambda j=j: cached(j))

        done = (acc_ref[...] * (1.0 / l_ref[...])).astype(BF)
        for h in range(GROUP):
            out_ref[cut, h * HEAD : (h + 1) * HEAD] = done[h * BLOCK : (h + 1) * BLOCK, :]
        return carry

    lax.fori_loop(0, TOK // BLOCK, block, 0)


def attention(me, lengths, cached, owner, q, kv, pages):
    rows = GROUP * BLOCK
    return pl.pallas_call(
        attend_body,
        out_shape=jax.ShapeDtypeStruct((TOK, FEAT), BF),
        grid_spec=pltpu.PrefetchScalarGridSpec(
            num_scalar_prefetch=4,
            grid=(1,),
            in_specs=[
                whole(GROUP, TOK, HEAD),
                whole(2, TOK, HEAD),
                pl.BlockSpec(memory_space=pl.ANY),
            ],
            out_specs=whole(TOK, FEAT),
            scratch_shapes=[
                pltpu.VMEM((rows, 1), F32),
                pltpu.VMEM((rows, 1), F32),
                pltpu.VMEM((rows, HEAD), F32),
                pltpu.VMEM((2, 2, WIN, HEAD), BF),
                pltpu.SemaphoreType.DMA((32,)),
            ],
        ),
        compiler_params=vmem(16),
        name="attention",
    )(me, lengths, cached, owner, q, kv, in_hbm(pages))


def out_body(me_ref, length_ref, adapter_ref, position_ref, *refs):
    blocks, maps = refs[:8], refs[8:16]
    weight_ref, hidden_ref, out_ref, w, oup, sems = refs[16:]
    order = col_order(me_ref[1])

    def copies():
        out = []
        for b in range(8):
            rows = weight_ref.at[pl.ds(2 * order[b], 2), pl.ds(0, 256), pl.ds(768, FEAT)]
            out.append(pltpu.make_async_copy(rows, w.at[b], sems.at[b]))
        for p in range(PROMPTS):
            slot = position_ref[adapter_ref[p]]
            rows = weight_ref.at[slot, pl.ds(256, 16), pl.ds(640, FEAT)]
            out.append(pltpu.make_async_copy(rows, oup.at[pl.ds(p * 16, 16)], sems.at[8 + p]))
        return out

    @pl.when(pl.program_id(0) == 0)
    def _():
        todo = copies()
        for copy in todo:
            copy.start()
        for copy in todo:
            copy.wait()

    total = hidden_ref[...].astype(F32)
    low = jnp.zeros((total.shape[0], 64), F32)
    for b in range(8):
        x = blocks[b][...]
        total += jnp.dot(x, w[b].reshape(FEAT, FEAT), preferred_element_type=F32)
        low += lax.dot_general(x, maps[b][128:192, :], (((1,), (1,)), ((), ())), preferred_element_type=F32)
    token = pl.program_id(0) * low.shape[0] + lax.broadcasted_iota(jnp.int32, low.shape, 0)
    prompt = per_token(prompt_rows(length_ref), range(PROMPTS), token)
    mine = lax.broadcasted_iota(jnp.int32, low.shape, 1) // 16 == prompt
    low = jnp.where(mine, low, 0.0)
    change = jnp.dot(low, oup[...].astype(F32), precision=lax.Precision.HIGHEST, preferred_element_type=F32)
    out_ref[...] = (total + 0.5 * change).astype(BF)


def output(me, lengths, adapter, position, blocks, maps, weight, hidden):
    rows = 256
    tok = pl.BlockSpec((rows, FEAT), lambda i, *_: (i, 0))
    return pl.pallas_call(
        out_body,
        out_shape=jax.ShapeDtypeStruct((TOK, FEAT), BF),
        grid_spec=pltpu.PrefetchScalarGridSpec(
            num_scalar_prefetch=4,
            grid=(TOK // rows,),
            in_specs=[tok] * 8 + [whole(192, FEAT)] * 8 + [pl.BlockSpec(memory_space=pl.ANY), tok],
            out_specs=tok,
            scratch_shapes=[
                pltpu.VMEM((8, 2, 256, FEAT), BF),
                pltpu.VMEM((64, FEAT), BF),
                pltpu.SemaphoreType.DMA((12,)),
            ],
        ),
        compiler_params=vmem(24),
        name="output",
    )(me, lengths, adapter, position, *blocks, *maps, in_hbm(weight), hidden)


def on_device(
    hidden_input,
    input_norm_gain,
    query_norm_gain,
    key_norm_gain,
    query_key_value_weight,
    output_weight,
    adapter_down_maps,
    adapter_up_maps,
    output_down_maps,
    output_up_maps,
    prompt_adapter,
    adapter_position,
    prompt_length,
    cache_length,
    page_owner_row,
    page_store_index,
    cache_page_store,
):
    me = jnp.stack([lax.axis_index("row"), lax.axis_index("col")]).astype(jnp.int32)
    wide, slots = pack(
        me,
        query_key_value_weight,
        output_weight,
        adapter_up_maps,
        output_up_maps,
        adapter_down_maps,
        output_down_maps,
    )
    weight = lax.all_gather(wide, "row", axis=0)
    slots = lax.all_to_all(slots, "row", 0, 0)

    picked = pick_pages(me, page_owner_row, page_store_index, cache_page_store)
    picked, slots = lax.optimization_barrier((picked, slots))
    pages = lax.all_to_all(picked.reshape(16, 4 * PAGE, HEAD), "row", 0, 0).reshape(32, 2, PAGE, HEAD)

    blocks = gather_col(hidden_input, 256)

    maps = select_slots(prompt_adapter, adapter_position, slots)
    maps = gather_col(maps, 96)

    token = lax.broadcasted_iota(jnp.int32, (TOK, HEAD), 0)
    position, start = token, jnp.int32(0)
    for p in range(PROMPTS):
        end = start + prompt_length[0, p]
        position = jnp.where((token >= start) & (token < end), token - start + cache_length[p], position)
        start = end
    frequency = ROPE_BASE ** (-2.0 * jnp.arange(HEAD // 2, dtype=F32) / HEAD)
    angles = position.astype(F32) * jnp.concatenate([frequency, frequency])[None, :]
    front = lax.broadcasted_iota(jnp.int32, (TOK, HEAD), 1) < HEAD // 2
    rope = jnp.where(front, jnp.cos(angles), jnp.sin(angles))

    normed, low = norm_low(me, prompt_length, blocks, maps, input_norm_gain.reshape(8, 1, FEAT))
    weight, normed, low, pages, rope = lax.optimization_barrier((weight, normed, low, pages, rope))
    q, new_cache = project(
        prompt_adapter,
        adapter_position,
        normed,
        weight,
        low,
        rope,
        query_norm_gain[None, :],
        key_norm_gain[None, :],
    )
    attended = attention(me, prompt_length, cache_length, page_owner_row, q, new_cache, pages)
    attended = gather_col(attended, 256)
    hidden_output = output(
        me, prompt_length, prompt_adapter, adapter_position, attended, maps, weight, hidden_input
    )
    return hidden_output, new_cache


def solution(mesh):
    return jax.shard_map(
        on_device,
        mesh=mesh,
        in_specs=(
            P("row", "col"),
            P(),
            P(),
            P(),
            P("row", "col"),
            P("row", "col"),
            P("row", None, None),
            P("row", None, "col"),
            P("row", None, "col"),
            P("row", None, None),
            P("row"),
            P(),
            P("row", None),
            P("row"),
            P(),
            P(),
            P("row", None, None, "col"),
        ),
        out_specs=(P("row", "col"), P(None, "row", "col")),
        check_vma=False,
    )
```

time: 193 us -> 184 us (0.953)
  local copies, waits for them, and re-layouts: 19 us -> 9.23 us
  waiting for transfers between devices: 50.6 us -> 58.2 us
  starting transfers between devices: 45.5 us -> 41.9 us
    all_gather x2 -> x1, waiting for transfers between devices: 0.01 us -> 22.2 us  [on_device(): weight = lax.all_gather(wide, 'row', axis=0)]
    all_to_all x1, waiting for transfers between devices: 19.3 us -> 4.41 us  [on_device(): slots = lax.all_to_all(slots, 'row', 0, 0)]
    unnamed x78 -> x36, local copies, waits for them, and re-layouts: 14.1 us -> 7.07 us
    all_to_all x1, starting transfers between devices: 7.5 us -> 4.91 us  [on_device(): lax.all_to_all(picked.reshape(16, 4 * PAGE, HEAD), 'row', 0, 0)]
    ppermute x3, starting transfers between devices: 7.52 us -> 4.97 us  [ring4(): after = lax.ppermute(block, axis, perm(-1))]
    ppermute x9, starting transfers between devices: 8.97 us -> 6.54 us  [gather_col(): out += [piece, lax.ppermute(piece, 'col', SWAP)]]
    ppermute x3, starting transfers between devices: 6.38 us -> 8.52 us  [gather_col(): other = lax.ppermute(block, 'col', SWAP)]
  transfers between devices with their start and end apart: 28 -> 27, of which waited for: 8 -> 11; matrix products, arithmetic and copies ran while one was open for 6% -> 5% of each run, Pallas kernels for 21% -> 7%
where the time goes in v3:
time: 184 us
  waiting for transfers between devices  58.2 us (32%)
  Pallas kernels  50.9 us (28%)
  starting transfers between devices  41.9 us (23%)
  between operations  17 us (9%)
  local copies, waits for them, and re-layouts  9.23 us (5%)
  other arithmetic  6.77 us (4%)
    all_gather x1, waiting for transfers between devices, on_device(): weight = lax.all_gather(wide, 'row', axis=0)  22.2 us
    ppermute x3, waiting for transfers between devices, ring4(): before = lax.ppermute(block, axis, perm(1))  15.2 us
    pallas_call x1, Pallas kernels, attention(): pl.pallas_call(attend_body, out_shape=jax.ShapeDtypeStruct((TOK, FEAT), B...  13.6 us
    pallas_call x1, Pallas kernels, project(): pl.pallas_call(qkv_body, out_shape=(jax.ShapeDtypeStruct((GROUP, TOK, HEA...  11.8 us
    pallas_call x1, Pallas kernels, output(): pl.pallas_call(out_body, out_shape=jax.ShapeDtypeStruct((TOK, FEAT), BF),...  9.87 us
    ppermute x3, waiting for transfers between devices, ring4(): far_low = lax.ppermute(before[:half], axis, perm(1))  9.76 us
    ppermute x3, starting transfers between devices, gather_col(): other = lax.ppermute(block, 'col', SWAP)  8.52 us
    all_to_all x1, starting transfers between devices, on_device(): slots = lax.all_to_all(slots, 'row', 0, 0)  7.73 us
  transfers between devices with their start and end apart: 27, of which 11 were waited for; matrix products, arithmetic and copies ran while one was open for 5% of the time, Pallas kernels for 7%

profile of v3, /device:TPU:1, one launch (start us, length us, event | category | flops | bytes accessed | tf_op | source)
XLA Modules:
  0.0 184.0 jit_solution(8481028441142262295)
XLA Ops:
  7.9 2.9 %pack.1 = (bf16[272,1280]{1,0:T(8,128)(2,1)}, bf16[16,48,512]{2,1,0:T(8,128)(2,1)}) custom-call(s32[2]{0:T(128)} %pad_add_fusion.me_ref, bf16[256,768]{1,0:T(8,128)(2,1)} %qkv_ref.1, bf16[256,512]{1,0:T(8,128)(2,1)} %wo_ref.1, bf16[1,16,640]{2,1,0:T(8,128)(2,1)} %up_ref.1, bf16[1,16,4096]{2,1,0:T(8,128)(2,1)} %oup_ref.1, bf16[1,32,4096]{2,1,0:T(8,128)(2,1)} %down_ref.1, ...), custom_call_target="tpu_custom_call" | custom-call | tf_op jit(solution)/shard_map/pack/pallas_call | solution.py:131
  10.8 7.7 %all-to-all-start = ((bf16[16,48,512]{2,1,0:T(8,128)(2,1)}), bf16[16,48,512]{2,1,0:T(8,128)(2,1)S(1)}, u32[]{:S(2)}, u32[]{:S(2)}) async-start(bf16[16,48,512]{2,1,0:T(8,128)(2,1)} %get-tuple-element.16), calls=%async_computation | async-start | bytes 1572864 | tf_op jit(solution)/shard_map/all_to_all | solution.py:478
  21.8 5.1 %pick_pages.1 = bf16[16,2,2,128,128]{4,3,2,1,0:T(8,128)(2,1)} custom-call(s32[2]{0:T(128)S(1)} %copy-done.8, s32[256,1]{1,0:T(8,128)S(1)} %copy.23.owner_ref, s32[256]{0:T(256)S(1)} %copy-done.13, bf16[8,2,128,128]{3,2,1,0:T(8,128)(2,1)S(1)} %copy-done.5), custom_call_target="tpu_custom_call" | custom-call | tf_op jit(solution)/shard_map/pick_pages/pallas_call | solution.py:105
  26.9 4.4 %all-to-all-done.slots_ref = bf16[16,48,512]{2,1,0:T(8,128)(2,1)S(1)} async-done(((bf16[16,48,512]{2,1,0:T(8,128)(2,1)}), bf16[16,48,512]{2,1,0:T(8,128)(2,1)S(1)}, u32[]{:S(2)}, u32[]{:S(2)}) %all-to-all-start) | async-done | bytes 786464 | tf_op jit(solution)/shard_map/all_to_all | solution.py:478
  31.3 4.9 %all-to-all-start.1 = ((bf16[16,512,128]{2,1,0:T(8,128)(2,1)}), bf16[16,512,128]{2,1,0:T(8,128)(2,1)}, u32[]{:S(2)}, u32[]{:S(2)}) async-start(bf16[16,512,128]{2,1,0:T(8,128)(2,1)} %bitcast.3), calls=%async_computation.1 | async-start | bytes 4194304 | tf_op jit(solution)/shard_map/all_to_all | solution.py:482
  38.1 2.9 %collective-permute-start.3 = (bf16[512,512]{1,0:T(8,128)(2,1)S(1)}, bf16[512,512]{1,0:T(8,128)(2,1)S(1)}, u32[]{:S(2)}, u32[]{:S(2)}) collective-permute-start(bf16[512,512]{1,0:T(8,128)(2,1)S(1)} %copy-done), channel_id=1, source_target_pairs={{0,6},{1,7},{2,0},{3,1},{4,2},{5,3},{6,4},{7,5},{8,14},{9,15},{10,... | collective-permute-start | bytes 1572872 | tf_op jit(solution)/shard_map/ppermute | solution.py:42
  41.0 5.5 %collective-permute-start = (bf16[512,512]{1,0:T(8,128)(2,1)S(1)}, bf16[512,512]{1,0:T(8,128)(2,1)S(1)}, u32[]{:S(2)}, u32[]{:S(2)}) collective-permute-start(bf16[512,512]{1,0:T(8,128)(2,1)S(1)} %copy-done), channel_id=1, source_target_pairs={{0,1},{1,0},{2,3},{3,2},{4,5},{5,4},{6,7},{7,6},{8,9},{9,8},{10,11... | collective-permute-start | bytes 1572872 | tf_op jit(solution)/shard_map/ppermute | solution.py:49
  52.4 2.0 %iota_add_fusion = (s32[512]{0:T(512)S(1)}, s32[512]{0:T(512)S(1)}) fusion(s32[]{:T(128)} %bitcast.12, s32[]{:T(128)} %bitcast.11, s32[]{:T(128)} %bitcast.5), kind=kLoop, calls=%fused_computation.7 | loop fusion | flops 1536 | bytes 4108 | tf_op jit(solution)/shard_map/add | solution.py:493
  55.1 2.7 %collective-permute-start.6 = (bf16[256,512]{1,0:T(8,128)(2,1)S(1)}, bf16[256,512]{1,0:T(8,128)(2,1)S(1)}, u32[]{:S(2)}, u32[]{:S(2)}) collective-permute-start(bf16[256,512]{1,0:T(8,128)(2,1)S(1)} %slice.57), channel_id=1, source_target_pairs={{0,6},{1,7},{2,0},{3,1},{4,2},{5,3},{6,4},{7,5},{8,14},{9,15},{10,... | collective-permute-start | bytes 786440 | tf_op jit(solution)/shard_map/ppermute | solution.py:44
  57.9 2.5 %select_slots.1.refs_8_ = bf16[192,512]{1,0:T(8,128)(2,1)} custom-call(s32[4]{0:T(128)} %adapter_ref.5, s32[16]{0:T(128)} %position_ref.5, bf16[16,48,512]{2,1,0:T(8,128)(2,1)} %copy-done.14), custom_call_target="tpu_custom_call" | custom-call | tf_op jit(solution)/shard_map/select_slots/pallas_call | solution.py:159
  61.0 3.5 %collective-permute-done.5 = bf16[256,512]{1,0:T(8,128)(2,1)S(1)} collective-permute-done((bf16[256,512]{1,0:T(8,128)(2,1)}, bf16[256,512]{1,0:T(8,128)(2,1)S(1)}, u32[]{:S(2)}, u32[]{:S(2)}) %collective-permute-start.5) | collective-permute-done | bytes 262176 | tf_op jit(solution)/shard_map/ppermute | solution.py:43
  64.9 3.4 %collective-permute-done.9.refs_10_ = bf16[192,512]{1,0:T(8,128)(2,1)S(1)} collective-permute-done((bf16[192,512]{1,0:T(8,128)(2,1)}, bf16[192,512]{1,0:T(8,128)(2,1)S(1)}, u32[]{:S(2)}, u32[]{:S(2)}) %collective-permute-start.9) | collective-permute-done | bytes 196640 | tf_op jit(solution)/shard_map/ppermute | solution.py:41
  72.1 3.2 %collective-permute-done.13 = bf16[96,512]{1,0:T(8,128)(2,1)S(1)} collective-permute-done((bf16[96,512]{1,0:T(8,128)(2,1)S(1)}, bf16[96,512]{1,0:T(8,128)(2,1)S(1)}, u32[]{:S(2)}, u32[]{:S(2)}) %collective-permute-start.13) | collective-permute-done | bytes 98336 | tf_op jit(solution)/shard_map/ppermute | solution.py:43
  75.3 3.8 %collective-permute-done.14 = bf16[96,512]{1,0:T(8,128)(2,1)S(1)} collective-permute-done((bf16[96,512]{1,0:T(8,128)(2,1)S(1)}, bf16[96,512]{1,0:T(8,128)(2,1)S(1)}, u32[]{:S(2)}, u32[]{:S(2)}) %collective-permute-start.14) | collective-permute-done | bytes 98336 | tf_op jit(solution)/shard_map/ppermute | solution.py:44
  82.3 2.1 %sine_select_fusion.rope_ref = f32[512,128]{1,0:T(8,128)} fusion(f32[128]{0:T(128)S(1)} %pad_maximum_fusion, s32[512]{0:T(512)S(1)} %get-tuple-element.40, s32[512]{0:T(512)S(1)} %get-tuple-element.41, s32[512]{0:T(512)S(1)} %get-tuple-element.42, s32[512]{0:T(512)S(1)} %get-tuple-element.43, pred[512]{0:T(512)(128)(4,1)S(1)} %get-tuple-element.36, ...), kind=kLoop, calls=%fused_computation | loop fusion | flops 458752 | bytes 273024 | tf_op jit(solution)/shard_map/jit(_where)/select_n | solution.py:498
  86.5 5.1 %norm_low.1 = (bf16[4,512,1024]{2,1,0:T(8,128)(2,1)}, bf16[512,128]{1,0:T(8,128)(2,1)}) custom-call(s32[2]{0:T(128)S(1)} %copy-done.9, s32[1,4]{1,0:T(1,128)S(1)} %copy-done.7, bf16[512,512]{1,0:T(8,128)(2,1)S(1)} %copy-done, bf16[512,512]{1,0:T(8,128)(2,1)S(1)} %copy-done.4, bf16[512,512]{1,0:T(8,128)(2,1)S(1)} %collective-permute-done.1.refs_2_, ...), custom_call_target="tpu_custom_call" | custom-call | tf_op jit(solution)/shard_map/norm_low/pallas_call | solution.py:193
  91.6 22.2 %all-gather.3.cloned.1.call-done = bf16[4352,1280]{1,0:T(8,128)(2,1)} async-done(((bf16[272,1280]{1,0:T(8,128)(2,1)}), bf16[4352,1280]{1,0:T(8,128)(2,1)}) %all-gather.3.cloned.1.call-update) | async-done | bytes 11141136 | tf_op jit(solution)/shard_map/all_gather | solution.py:477
  113.9 11.8 %project.1 = (bf16[4,512,128]{2,1,0:T(8,128)(2,1)S(1)}, bf16[2,512,128]{2,1,0:T(8,128)(2,1)}) custom-call(s32[4]{0:T(128)S(1)} %copy-done.11, s32[16]{0:T(128)S(1)} %copy-done.12, bf16[4,512,1024]{2,1,0:T(8,128)(2,1)} %get-tuple-element.21.normed_ref, bf16[16,272,1280]{2,1,0:T(8,128)(2,1)} %bitcast.15, bf16[512,128]{1,0:T(8,128)(2,1)} %get-tuple-element.23.low_ref, ...), custom_call_target="tpu_custom_call" | custom-call | tf_op jit(solution)/shard_map/project/pallas_call | solution.py:258
  126.7 13.6 %attention.1.refs_0_ = bf16[512,512]{1,0:T(8,128)(2,1)S(1)} custom-call(s32[2]{0:T(128)S(1)} %copy-done.9, s32[1,4]{1,0:T(1,128)S(1)} %copy-done.7, s32[4]{0:T(128)S(1)} %copy-done.10, s32[256,1]{1,0:T(8,128)S(1)} %copy.23.owner_ref, bf16[4,512,128]{2,1,0:T(8,128)(2,1)S(1)} %get-tuple-element.25.q_ref, bf16[2,512,128]{2,1,0:T(8,128)(2,1)S(1)} %copy-done.6, ...), custom_call_target="tpu_custom_call" | custom-call | tf_op jit(solution)/shard_map/attention/pallas_call | solution.py:363
  143.8 11.8 %collective-permute-done.17.refs_2_ = bf16[512,512]{1,0:T(8,128)(2,1)S(1)} collective-permute-done((bf16[512,512]{1,0:T(8,128)(2,1)S(1)}, bf16[512,512]{1,0:T(8,128)(2,1)S(1)}, u32[]{:S(2)}, u32[]{:S(2)}) %collective-permute-start.17) | collective-permute-done | bytes 524320 | tf_op jit(solution)/shard_map/ppermute | solution.py:41
  155.7 2.7 %collective-permute-start.22 = (bf16[256,512]{1,0:T(8,128)(2,1)S(1)}, bf16[256,512]{1,0:T(8,128)(2,1)S(1)}, u32[]{:S(2)}, u32[]{:S(2)}) collective-permute-start(bf16[256,512]{1,0:T(8,128)(2,1)S(1)} %slice.61), channel_id=1, source_target_pairs={{0,6},{1,7},{2,0},{3,1},{4,2},{5,3},{6,4},{7,5},{8,14},{9,15},{10,... | collective-permute-start | bytes 786440 | tf_op jit(solution)/shard_map/ppermute | solution.py:44
  160.5 3.1 %collective-permute-done.21 = bf16[256,512]{1,0:T(8,128)(2,1)S(1)} collective-permute-done((bf16[256,512]{1,0:T(8,128)(2,1)S(1)}, bf16[256,512]{1,0:T(8,128)(2,1)S(1)}, u32[]{:S(2)}, u32[]{:S(2)}) %collective-permute-start.21) | collective-permute-done | bytes 262176 | tf_op jit(solution)/shard_map/ppermute | solution.py:43
  163.7 2.0 %collective-permute-start.23 = (bf16[512,512]{1,0:T(8,128)(2,1)S(1)}, bf16[512,512]{1,0:T(8,128)(2,1)S(1)}, u32[]{:S(2)}, u32[]{:S(2)}) collective-permute-start(bf16[512,512]{1,0:T(8,128)(2,1)S(1)} %constant_dynamic-update-slice_fusion.4.refs_6_), channel_id=1, source_target_pairs={{0,1},{1,0},{2,3},{3,2},{4,5},{5,4},{6,7},{7,6},{8,9},{9,8},{10,11... | collective-permute-start | bytes 1572872 | tf_op jit(solution)/shard_map/ppermute | solution.py:52
  167.3 9.9 %output.1 = bf16[512,512]{1,0:T(8,128)(2,1)} custom-call(s32[2]{0:T(128)S(1)} %copy-done.9, s32[1,4]{1,0:T(1,128)S(1)} %copy-done.7, s32[4]{0:T(128)S(1)} %copy-done.11, s32[16]{0:T(128)S(1)} %copy-done.12, bf16[512,512]{1,0:T(8,128)(2,1)S(1)} %attention.1.refs_0_, bf16[512,512]{1,0:T(8,128)(2,1)S(1)} %collective-permute-done.16.refs_1_, ...), custom_call_target="tpu_custom_call" | custom-call | tf_op jit(solution)/shard_map/output/pallas_call | solution.py:429
  (95 shorter events, 28.0 us)
Async XLA Ops:
  7.2 106.7 %all-gather.3.cloned.1.call-start = ((), (), s32[]{:S(2)}) async-start(), calls=%async_computation.2 | async-start | bytes 11837440 | tf_op jit(solution)/shard_map/all_gather | solution.py:477
  10.8 20.5 %all-to-all-start = ((bf16[16,48,512]{2,1,0:T(8,128)(2,1)}), bf16[16,48,512]{2,1,0:T(8,128)(2,1)S(1)}, u32[]{:S(2)}, u32[]{:S(2)}) async-start(bf16[16,48,512]{2,1,0:T(8,128)(2,1)} %get-tuple-element.16), calls=%async_computation | async-start | bytes 1572864 | tf_op jit(solution)/shard_map/all_to_all | solution.py:478
  31.3 60.3 %all-to-all-start.1 = ((bf16[16,512,128]{2,1,0:T(8,128)(2,1)}), bf16[16,512,128]{2,1,0:T(8,128)(2,1)}, u32[]{:S(2)}, u32[]{:S(2)}) async-start(bf16[16,512,128]{2,1,0:T(8,128)(2,1)} %bitcast.3), calls=%async_computation.1 | async-start | bytes 4194304 | tf_op jit(solution)/shard_map/all_to_all | solution.py:482
  36.3 18.1 %collective-permute-start.1 = (bf16[512,512]{1,0:T(8,128)(2,1)S(1)}, bf16[512,512]{1,0:T(8,128)(2,1)S(1)}, u32[]{:S(2)}, u32[]{:S(2)}) collective-permute-start(bf16[512,512]{1,0:T(8,128)(2,1)S(1)} %copy-done), channel_id=1, source_target_pairs={{0,2},{1,3},{2,4},{3,5},{4,6},{5,7},{6,0},{7,1},{8,10},{9,11},{10,... | collective-permute-start | bytes 1572872 | tf_op jit(solution)/shard_map/ppermute | solution.py:41
  38.1 17.0 %collective-permute-start.3 = (bf16[512,512]{1,0:T(8,128)(2,1)S(1)}, bf16[512,512]{1,0:T(8,128)(2,1)S(1)}, u32[]{:S(2)}, u32[]{:S(2)}) collective-permute-start(bf16[512,512]{1,0:T(8,128)(2,1)S(1)} %copy-done), channel_id=1, source_target_pairs={{0,6},{1,7},{2,0},{3,1},{4,2},{5,3},{6,4},{7,5},{8,14},{9,15},{10,... | collective-permute-start | bytes 1572872 | tf_op jit(solution)/shard_map/ppermute | solution.py:42
  41.0 39.6 %collective-permute-start = (bf16[512,512]{1,0:T(8,128)(2,1)S(1)}, bf16[512,512]{1,0:T(8,128)(2,1)S(1)}, u32[]{:S(2)}, u32[]{:S(2)}) collective-permute-start(bf16[512,512]{1,0:T(8,128)(2,1)S(1)} %copy-done), channel_id=1, source_target_pairs={{0,1},{1,0},{2,3},{3,2},{4,5},{5,4},{6,7},{7,6},{8,9},{9,8},{10,11... | collective-permute-start | bytes 1572872 | tf_op jit(solution)/shard_map/ppermute | solution.py:49
  55.1 9.5 %collective-permute-start.5 = (bf16[256,512]{1,0:T(8,128)(2,1)}, bf16[256,512]{1,0:T(8,128)(2,1)S(1)}, u32[]{:S(2)}, u32[]{:S(2)}) collective-permute-start(bf16[256,512]{1,0:T(8,128)(2,1)} %slice.56), channel_id=1, source_target_pairs={{0,2},{1,3},{2,4},{3,5},{4,6},{5,7},{6,0},{7,1},{8,10},{9,11},{10,... | collective-permute-start | bytes 786440 | tf_op jit(solution)/shard_map/ppermute | solution.py:43
  55.1 14.3 %collective-permute-start.6 = (bf16[256,512]{1,0:T(8,128)(2,1)S(1)}, bf16[256,512]{1,0:T(8,128)(2,1)S(1)}, u32[]{:S(2)}, u32[]{:S(2)}) collective-permute-start(bf16[256,512]{1,0:T(8,128)(2,1)S(1)} %slice.57), channel_id=1, source_target_pairs={{0,6},{1,7},{2,0},{3,1},{4,2},{5,3},{6,4},{7,5},{8,14},{9,15},{10,... | collective-permute-start | bytes 786440 | tf_op jit(solution)/shard_map/ppermute | solution.py:44
  60.4 7.9 %collective-permute-start.9 = (bf16[192,512]{1,0:T(8,128)(2,1)}, bf16[192,512]{1,0:T(8,128)(2,1)S(1)}, u32[]{:S(2)}, u32[]{:S(2)}) collective-permute-start(bf16[192,512]{1,0:T(8,128)(2,1)} %select_slots.1.refs_8_), channel_id=1, source_target_pairs={{0,2},{1,3},{2,4},{3,5},{4,6},{5,7},{6,0},{7,1},{8,10},{9,11},{10,... | collective-permute-start | bytes 589832 | tf_op jit(solution)/shard_map/ppermute | solution.py:41
  60.4 21.8 %collective-permute-start.2 = (bf16[512,512]{1,0:T(8,128)(2,1)S(1)}, bf16[512,512]{1,0:T(8,128)(2,1)S(1)}, u32[]{:S(2)}, u32[]{:S(2)}) collective-permute-start(bf16[512,512]{1,0:T(8,128)(2,1)S(1)} %collective-permute-done.1.refs_2_), channel_id=1, source_target_pairs={{0,1},{1,0},{2,3},{3,2},{4,5},{5,4},{6,7},{7,6},{8,9},{9,8},{10,11... | collective-permute-start | bytes 1572872 | tf_op jit(solution)/shard_map/ppermute | solution.py:52
  64.5 5.8 %collective-permute-start.11 = (bf16[192,512]{1,0:T(8,128)(2,1)}, bf16[192,512]{1,0:T(8,128)(2,1)S(1)}, u32[]{:S(2)}, u32[]{:S(2)}) collective-permute-start(bf16[192,512]{1,0:T(8,128)(2,1)} %select_slots.1.refs_8_), channel_id=1, source_target_pairs={{0,6},{1,7},{2,0},{3,1},{4,2},{5,3},{6,4},{7,5},{8,14},{9,15},{10,... | collective-permute-start | bytes 589832 | tf_op jit(solution)/shard_map/ppermute | solution.py:42
  68.3 16.2 %collective-permute-start.4 = (bf16[512,512]{1,0:T(8,128)(2,1)S(1)}, bf16[512,512]{1,0:T(8,128)(2,1)S(1)}, u32[]{:S(2)}, u32[]{:S(2)}) collective-permute-start(bf16[512,512]{1,0:T(8,128)(2,1)S(1)} %collective-permute-done.3.refs_4_), channel_id=1, source_target_pairs={{0,1},{1,0},{2,3},{3,2},{4,5},{5,4},{6,7},{7,6},{8,9},{9,8},{10,11... | collective-permute-start | bytes 1572872 | tf_op jit(solution)/shard_map/ppermute | solution.py:52
  69.4 5.8 %collective-permute-start.13 = (bf16[96,512]{1,0:T(8,128)(2,1)S(1)}, bf16[96,512]{1,0:T(8,128)(2,1)S(1)}, u32[]{:S(2)}, u32[]{:S(2)}) collective-permute-start(bf16[96,512]{1,0:T(8,128)(2,1)S(1)} %slice.58), channel_id=1, source_target_pairs={{0,2},{1,3},{2,4},{3,5},{4,6},{5,7},{6,0},{7,1},{8,10},{9,11},{10,... | collective-permute-start | bytes 294920 | tf_op jit(solution)/shard_map/ppermute | solution.py:43
  70.4 14.2 %collective-permute-start.7 = (bf16[512,512]{1,0:T(8,128)(2,1)S(1)}, bf16[512,512]{1,0:T(8,128)(2,1)S(1)}, u32[]{:S(2)}, u32[]{:S(2)}) collective-permute-start(bf16[512,512]{1,0:T(8,128)(2,1)S(1)} %constant_dynamic-update-slice_fusion.refs_6_), channel_id=1, source_target_pairs={{0,1},{1,0},{2,3},{3,2},{4,5},{5,4},{6,7},{7,6},{8,9},{9,8},{10,11... | collective-permute-start | bytes 1572872 | tf_op jit(solution)/shard_map/ppermute | solution.py:52
  75.2 3.9 %collective-permute-start.14 = (bf16[96,512]{1,0:T(8,128)(2,1)S(1)}, bf16[96,512]{1,0:T(8,128)(2,1)S(1)}, u32[]{:S(2)}, u32[]{:S(2)}) collective-permute-start(bf16[96,512]{1,0:T(8,128)(2,1)S(1)} %slice.59), channel_id=1, source_target_pairs={{0,6},{1,7},{2,0},{3,1},{4,2},{5,3},{6,4},{7,5},{8,14},{9,15},{10,... | collective-permute-start | bytes 294920 | tf_op jit(solution)/shard_map/ppermute | solution.py:44
  81.4 3.1 %collective-permute-start.10 = (bf16[192,512]{1,0:T(8,128)(2,1)S(1)}, bf16[192,512]{1,0:T(8,128)(2,1)S(1)}, u32[]{:S(2)}, u32[]{:S(2)}) collective-permute-start(bf16[192,512]{1,0:T(8,128)(2,1)S(1)} %collective-permute-done.9.refs_10_), channel_id=1, source_target_pairs={{0,1},{1,0},{2,3},{3,2},{4,5},{5,4},{6,7},{7,6},{8,9},{9,8},{10,11... | collective-permute-start | bytes 589832 | tf_op jit(solution)/shard_map/ppermute | solution.py:52
  140.4 15.2 %collective-permute-start.17 = (bf16[512,512]{1,0:T(8,128)(2,1)S(1)}, bf16[512,512]{1,0:T(8,128)(2,1)S(1)}, u32[]{:S(2)}, u32[]{:S(2)}) collective-permute-start(bf16[512,512]{1,0:T(8,128)(2,1)S(1)} %attention.1.refs_0_), channel_id=1, source_target_pairs={{0,2},{1,3},{2,4},{3,5},{4,6},{5,7},{6,0},{7,1},{8,10},{9,11},{10,... | collective-permute-start | bytes 1572872 | tf_op jit(solution)/shard_map/ppermute | solution.py:41
  142.1 13.6 %collective-permute-start.19 = (bf16[512,512]{1,0:T(8,128)(2,1)S(1)}, bf16[512,512]{1,0:T(8,128)(2,1)S(1)}, u32[]{:S(2)}, u32[]{:S(2)}) collective-permute-start(bf16[512,512]{1,0:T(8,128)(2,1)S(1)} %attention.1.refs_0_), channel_id=1, source_target_pairs={{0,6},{1,7},{2,0},{3,1},{4,2},{5,3},{6,4},{7,5},{8,14},{9,15},{10,... | collective-permute-start | bytes 1572872 | tf_op jit(solution)/shard_map/ppermute | solution.py:42
  155.6 8.0 %collective-permute-start.21 = (bf16[256,512]{1,0:T(8,128)(2,1)S(1)}, bf16[256,512]{1,0:T(8,128)(2,1)S(1)}, u32[]{:S(2)}, u32[]{:S(2)}) collective-permute-start(bf16[256,512]{1,0:T(8,128)(2,1)S(1)} %slice.60), channel_id=1, source_target_pairs={{0,2},{1,3},{2,4},{3,5},{4,6},{5,7},{6,0},{7,1},{8,10},{9,11},{10,... | collective-permute-start | bytes 786440 | tf_op jit(solution)/shard_map/ppermute | solution.py:43
  155.7 7.9 %collective-permute-start.22 = (bf16[256,512]{1,0:T(8,128)(2,1)S(1)}, bf16[256,512]{1,0:T(8,128)(2,1)S(1)}, u32[]{:S(2)}, u32[]{:S(2)}) collective-permute-start(bf16[256,512]{1,0:T(8,128)(2,1)S(1)} %slice.61), channel_id=1, source_target_pairs={{0,6},{1,7},{2,0},{3,1},{4,2},{5,3},{6,4},{7,5},{8,14},{9,15},{10,... | collective-permute-start | bytes 786440 | tf_op jit(solution)/shard_map/ppermute | solution.py:44
  158.4 7.3 %collective-permute-start.16 = (bf16[512,512]{1,0:T(8,128)(2,1)S(1)}, bf16[512,512]{1,0:T(8,128)(2,1)S(1)}, u32[]{:S(2)}, u32[]{:S(2)}) collective-permute-start(bf16[512,512]{1,0:T(8,128)(2,1)S(1)} %attention.1.refs_0_), channel_id=1, source_target_pairs={{0,1},{1,0},{2,3},{3,2},{4,5},{5,4},{6,7},{7,6},{8,9},{9,8},{10,11... | collective-permute-start | bytes 1572872 | tf_op jit(solution)/shard_map/ppermute | solution.py:49
  160.0 5.7 %collective-permute-start.18 = (bf16[512,512]{1,0:T(8,128)(2,1)S(1)}, bf16[512,512]{1,0:T(8,128)(2,1)S(1)}, u32[]{:S(2)}, u32[]{:S(2)}) collective-permute-start(bf16[512,512]{1,0:T(8,128)(2,1)S(1)} %collective-permute-done.17.refs_2_), channel_id=1, source_target_pairs={{0,1},{1,0},{2,3},{3,2},{4,5},{5,4},{6,7},{7,6},{8,9},{9,8},{10,11... | collective-permute-start | bytes 1572872 | tf_op jit(solution)/shard_map/ppermute | solution.py:52
  160.0 5.7 %collective-permute-start.20 = (bf16[512,512]{1,0:T(8,128)(2,1)S(1)}, bf16[512,512]{1,0:T(8,128)(2,1)S(1)}, u32[]{:S(2)}, u32[]{:S(2)}) collective-permute-start(bf16[512,512]{1,0:T(8,128)(2,1)S(1)} %collective-permute-done.19.refs_4_), channel_id=1, source_target_pairs={{0,1},{1,0},{2,3},{3,2},{4,5},{5,4},{6,7},{7,6},{8,9},{9,8},{10,11... | collective-permute-start | bytes 1572872 | tf_op jit(solution)/shard_map/ppermute | solution.py:52
  163.7 3.6 %collective-permute-start.23 = (bf16[512,512]{1,0:T(8,128)(2,1)S(1)}, bf16[512,512]{1,0:T(8,128)(2,1)S(1)}, u32[]{:S(2)}, u32[]{:S(2)}) collective-permute-start(bf16[512,512]{1,0:T(8,128)(2,1)S(1)} %constant_dynamic-update-slice_fusion.4.refs_6_), channel_id=1, source_target_pairs={{0,1},{1,0},{2,3},{3,2},{4,5},{5,4},{6,7},{7,6},{8,9},{9,8},{10,11... | collective-permute-start | bytes 1572872 | tf_op jit(solution)/shard_map/ppermute | solution.py:52
  (19 other events, 362.3 us)
Sparse Core Ops, SparseCore 0:
  10.9 102.8 all-gather.2

commit v4 on v3

--- a/solution.py
+++ b/solution.py
@@ -37,19 +37,26 @@
 SWAP = [(i, i ^ 1) for i in range(8)]
 
 
+def ring_far(before, after, axis, perm, half):
+    far_low = lax.ppermute(before[:half], axis, perm(1))
+    far_high = lax.ppermute(after[half:], axis, perm(-1))
+    return jnp.concatenate([far_low, far_high], axis=0)
+
+
 def ring4(block, axis, perm, half):
     before = lax.ppermute(block, axis, perm(1))
     after = lax.ppermute(block, axis, perm(-1))
-    far_low = lax.ppermute(before[:half], axis, perm(1))
-    far_high = lax.ppermute(after[half:], axis, perm(-1))
-    return before, after, jnp.concatenate([far_low, far_high], axis=0)
+    return before, after, ring_far(before, after, axis, perm, half)
+
+
+def swap(block):
+    return lax.ppermute(block, "col", SWAP)
 
 
 def gather_col(block, half):
-    other = lax.ppermute(block, "col", SWAP)
-    out = [block, other]
+    out = [block, swap(block)]
     for piece in ring4(block, "col", perm_z, half):
-        out += [piece, lax.ppermute(piece, "col", SWAP)]
+        out += [piece, swap(piece)]
     return out
 
 
@@ -85,7 +92,7 @@
     return pl.BlockSpec(shape, lambda *_: (0,) * len(shape))
 
 
-def pick_body(me_ref, owner_ref, index_ref, store_ref, out_ref):
+def pick_body(me_ref, owner_ref, index_ref, store_ref, out_ref, place_ref):
     def group(r, carry):
         first, second, count = jnp.int32(0), jnp.int32(0), jnp.int32(0)
         for q in range(16):
@@ -99,17 +106,25 @@
         return carry
 
     lax.fori_loop(0, 16, group, 0)
+    for i in range(16):
+        holder, rank = owner_ref[me_ref[0] * 16 + i, 0], jnp.int32(0)
+        for k in range(i):
+            rank = jnp.where(owner_ref[me_ref[0] * 16 + k, 0] == holder, 1, rank)
+        place_ref[i] = holder * 2 + rank
 
 
 def pick_pages(me, owner, index, store):
     return pl.pallas_call(
         pick_body,
-        out_shape=jax.ShapeDtypeStruct((16, 2) + store.shape[1:], store.dtype),
+        out_shape=(
+            jax.ShapeDtypeStruct((16, 2) + store.shape[1:], store.dtype),
+            jax.ShapeDtypeStruct((16,), jnp.int32),
+        ),
         grid_spec=pltpu.PrefetchScalarGridSpec(
             num_scalar_prefetch=3,
             grid=(1,),
             in_specs=[whole(*store.shape)],
-            out_specs=whole(16, 2, *store.shape[1:]),
+            out_specs=(whole(16, 2, *store.shape[1:]), pl.BlockSpec(memory_space=pltpu.SMEM)),
         ),
         compiler_params=vmem(10),
         name="pick_pages",
@@ -209,91 +224,22 @@
     )(me, lengths, *blocks, *maps, gain)
 
 
-def qkv_body(adapter_ref, position_ref, normed_ref, w_ref, low_ref, rope_ref, qg_ref, kg_ref, q_ref, kv_ref, x, w, up, acc, sems):
-    copies = []
-    for k in range(4):
-        copies.append(pltpu.make_async_copy(normed_ref.at[k], x.at[k], sems.at[2 * k]))
-        rows = w_ref.at[pl.ds(4 * k, 4), pl.ds(0, 256), pl.ds(0, 768)]
-        copies.append(pltpu.make_async_copy(rows, w.at[k], sems.at[2 * k + 1]))
-    for p in range(PROMPTS):
-        slot = position_ref[adapter_ref[p]]
-        copies.append(pltpu.make_async_copy(w_ref.at[slot, pl.ds(256, 16), pl.ds(0, 640)], up.at[p], sems.at[8 + p]))
-    for copy in copies:
-        copy.start()
-    for k in range(4):
-        copies[2 * k].wait()
-        copies[2 * k + 1].wait()
-        part = jnp.dot(x[k], w[k].reshape(1024, 768), preferred_element_type=F32)
-        if k == 0:
-            acc[...] = part
-        else:
-            acc[...] += part
-    for copy in copies[8:]:
-        copy.wait()
-    low = low_ref[...]
-    q_change = jnp.zeros((TOK, 512), F32)
-    v_change = jnp.zeros((TOK, HEAD), F32)
-    for p in range(PROMPTS):
-        q_change += jnp.dot(low[:, p * 32 : p * 32 + 16], up[p, :, :512], preferred_element_type=F32)
-        v_change += jnp.dot(low[:, p * 32 + 16 : p * 32 + 32], up[p, :, 512:], preferred_element_type=F32)
-    rope = rope_ref[...]
-    front = lax.broadcasted_iota(jnp.int32, rope.shape, 1) < HEAD // 2
-    swapped = pltpu.roll(rope, HEAD // 2, 1)
-    cos, sin = jnp.where(front, rope, swapped), jnp.where(front, -swapped, rope)
-
-    def finish(raw, gain):
-        scale = lax.rsqrt(jnp.mean(raw * raw, axis=-1, keepdims=True) + EPSILON)
-        x = raw * scale * gain
-        return (x * cos + pltpu.roll(x, HEAD // 2, 1) * sin).astype(BF)
-
-    for h in range(GROUP):
-        cut = slice(h * HEAD, (h + 1) * HEAD)
-        q_ref[h] = finish(acc[:, cut] + 0.5 * q_change[:, cut], qg_ref[...].astype(F32))
-    kv_ref[0] = finish(acc[:, 512:640], kg_ref[...].astype(F32))
-    kv_ref[1] = (acc[:, 640:768] + 0.5 * v_change).astype(BF)
-
-
-def project(adapter, position, normed, weight, low, rope, q_gain, k_gain):
-    hbm = pl.BlockSpec(memory_space=pl.ANY)
-    return pl.pallas_call(
-        qkv_body,
-        out_shape=(jax.ShapeDtypeStruct((GROUP, TOK, HEAD), BF), jax.ShapeDtypeStruct((2, TOK, HEAD), BF)),
-        grid_spec=pltpu.PrefetchScalarGridSpec(
-            num_scalar_prefetch=2,
-            grid=(1,),
-            in_specs=[hbm, hbm, whole(TOK, 128), whole(TOK, HEAD), whole(1, HEAD), whole(1, HEAD)],
-            out_specs=(whole(GROUP, TOK, HEAD), whole(2, TOK, HEAD)),
-            scratch_shapes=[
-                pltpu.VMEM((4, TOK, 1024), BF),
-                pltpu.VMEM((4, 4, 256, 768), BF),
-                pltpu.VMEM((PROMPTS, 16, 640), BF),
-                pltpu.VMEM((TOK, 768), F32),
-                pltpu.SemaphoreType.DMA((12,)),
-            ],
-        ),
-        compiler_params=vmem(28),
-        name="project",
-    )(adapter, position, in_hbm(normed), in_hbm(weight), in_hbm(low), in_hbm(rope), in_hbm(q_gain), in_hbm(k_gain))
-
-
 BLOCK = 64
+HALF = TOK // 2
 SCALE2 = math.log2(math.e) / math.sqrt(HEAD)
 
 
-def attend_body(me_ref, length_ref, cache_ref, owner_ref, q_ref, kv_ref, pages_ref, out_ref, m_ref, l_ref, acc_ref, cached_ref, sems):
-    rows, span = GROUP * BLOCK, 256 + BLOCK
-    base = me_ref[0] * 16
+def page_copies(place_ref, pages_ref, cached_ref, sems, base):
     copies = []
     for i in range(16):
-        holder, rank = owner_ref[base + i, 0], jnp.int32(0)
-        for k in range(i):
-            rank = rank + (owner_ref[base + k, 0] == holder).astype(jnp.int32)
-        page = holder * 2 + jnp.minimum(rank, 1)
         for h in range(2):
             into = cached_ref.at[h, i // 8, pl.ds(i % 8 * PAGE, PAGE)]
-            copies.append(pltpu.make_async_copy(pages_ref.at[page, h], into, sems.at[2 * i + h]))
-    for copy in copies:
-        copy.start()
+            copies.append(pltpu.make_async_copy(pages_ref.at[place_ref[i], h], into, sems.at[base + 2 * i + h]))
+    return copies
+
+
+def attend_half(half, length_ref, cache_ref, q_ref, kv_ref, cached_ref, out_ref, m_ref, l_ref, acc_ref):
+    rows, span = GROUP * BLOCK, 256 + BLOCK
     prompts = prompt_rows(length_ref)
     begins = [start for start, _ in prompts]
     count, ranks = jnp.int32(0), []
@@ -311,13 +257,12 @@
                 sum(mine[p] * cache_ref[p] for p in range(PROMPTS)),
             )
         )
-    for copy in copies:
-        copy.wait()
 
     def block(t, carry):
-        start = pl.multiple_of(t * BLOCK, BLOCK)
+        local = pl.multiple_of(t * BLOCK, BLOCK)
+        start = local + half * HALF
         lo = pl.multiple_of(jnp.maximum(start - 256, 0), BLOCK)
-        cut = pl.ds(start, BLOCK)
+        cut = pl.ds(local, BLOCK)
         q = q_ref[:, cut, :].reshape(rows, HEAD)
         token = start + (lax.broadcasted_iota(jnp.int32, (rows, 1), 0) & (BLOCK - 1))
         begin = per_token(prompts, begins, token)
@@ -355,84 +300,193 @@
             out_ref[cut, h * HEAD : (h + 1) * HEAD] = done[h * BLOCK : (h + 1) * BLOCK, :]
         return carry
 
-    lax.fori_loop(0, TOK // BLOCK, block, 0)
-
-
-def attention(me, lengths, cached, owner, q, kv, pages):
-    rows = GROUP * BLOCK
+    lax.fori_loop(0, HALF // BLOCK, block, 0)
+
+
+ATTEND_SCRATCH = [
+    pltpu.VMEM((GROUP * BLOCK, 1), F32),
+    pltpu.VMEM((GROUP * BLOCK, 1), F32),
+    pltpu.VMEM((GROUP * BLOCK, HEAD), F32),
+    pltpu.VMEM((2, 2, WIN, HEAD), BF),
+]
+
+
+def first_body(
+    length_ref, cache_ref, place_ref, adapter_ref, position_ref,
+    normed_ref, w_ref, low_hbm, rope_hbm, gains_hbm, pages_ref,
+    out_ref, q_late_ref, kv_ref,
+    m_ref, l_ref, sum_ref, cached_ref, x, w, up, acc, q_early, low_ref, rope_ref, gains_ref, sems,
+):
+    def chunk(k):
+        rows = w_ref.at[pl.ds(4 * k, 4), pl.ds(0, 256), pl.ds(0, 768)]
+        return [
+            pltpu.make_async_copy(normed_ref.at[k], x.at[k], sems.at[2 * k]),
+            pltpu.make_async_copy(rows, w.at[k], sems.at[2 * k + 1]),
+        ]
+
+    chunks = [chunk(k) for k in range(4)]
+    for copy in chunks[0]:
+        copy.start()
+    up[...] = jnp.zeros_like(up)
+    maps = []
+    for p in range(PROMPTS):
+        slot = position_ref[adapter_ref[p]]
+        q_part = w_ref.at[slot, pl.ds(256, 16), pl.ds(0, 512)]
+        v_part = w_ref.at[slot, pl.ds(256, 16), pl.ds(512, HEAD)]
+        maps.append(pltpu.make_async_copy(q_part, up.at[pl.ds(p * 32, 16), pl.ds(0, 512)], sems.at[8 + 2 * p]))
+        maps.append(pltpu.make_async_copy(v_part, up.at[pl.ds(p * 32 + 16, 16), pl.ds(512, HEAD)], sems.at[9 + 2 * p]))
+    maps.append(pltpu.make_async_copy(low_hbm, low_ref, sems.at[48]))
+    maps.append(pltpu.make_async_copy(rope_hbm, rope_ref, sems.at[49]))
+    maps.append(pltpu.make_async_copy(gains_hbm, gains_ref, sems.at[50]))
+    for copy in chunks[1] + maps:
+        copy.start()
+    pages = page_copies(place_ref, pages_ref, cached_ref, sems, 16)
+    for k in range(4):
+        for copy in chunks[k]:
+            copy.wait()
+        if k + 2 < 4:
+            for copy in chunks[k + 2]:
+                copy.start()
+        if k == 2:
+            for copy in pages:
+                copy.start()
+        part = jnp.dot(x[k], w[k].reshape(1024, 768), preferred_element_type=F32)
+        if k == 0:
+            acc[...] = part
+        else:
+            acc[...] += part
+    for copy in maps:
+        copy.wait()
+    change = 0.5 * jnp.dot(low_ref[...], up[...], preferred_element_type=F32)
+    rope = rope_ref[...]
+    front = lax.broadcasted_iota(jnp.int32, rope.shape, 1) < HEAD // 2
+    swapped = pltpu.roll(rope, HEAD // 2, 1)
+    cos, sin = jnp.where(front, rope, swapped), jnp.where(front, -swapped, rope)
+
+    def finish(raw, gain):
+        scale = lax.rsqrt(jnp.mean(raw * raw, axis=-1, keepdims=True) + EPSILON)
+        x = raw * scale * gain
+        return (x * cos + pltpu.roll(x, HEAD // 2, 1) * sin).astype(BF)
+
+    for h in range(GROUP):
+        cut = slice(h * HEAD, (h + 1) * HEAD)
+        q = finish(acc[:, cut] + change[:, cut], gains_ref[0:1, :])
+        q_early[h] = q[:HALF]
+        q_late_ref[h] = q[HALF:]
+    kv_ref[0] = finish(acc[:, 512:640], gains_ref[1:2, :])
+    kv_ref[1] = (acc[:, 640:768] + change[:, 512:640]).astype(BF)
+    for copy in pages:
+        copy.wait()
+    attend_half(0, length_ref, cache_ref, q_early, kv_ref, cached_ref, out_ref, m_ref, l_ref, sum_ref)
+
+
+def first_half(lengths, cached, place, adapter, position, normed, weight, low, rope, gains, pages):
+    hbm = pl.BlockSpec(memory_space=pl.ANY)
     return pl.pallas_call(
-        attend_body,
+        first_body,
+        out_shape=(
+            jax.ShapeDtypeStruct((HALF, FEAT), BF),
+            jax.ShapeDtypeStruct((GROUP, HALF, HEAD), BF),
+            jax.ShapeDtypeStruct((2, TOK, HEAD), BF),
+        ),
+        grid_spec=pltpu.PrefetchScalarGridSpec(
+            num_scalar_prefetch=5,
+            grid=(1,),
+            in_specs=[hbm] * 6,
+            out_specs=(whole(HALF, FEAT), whole(GROUP, HALF, HEAD), whole(2, TOK, HEAD)),
+            scratch_shapes=ATTEND_SCRATCH
+            + [
+                pltpu.VMEM((4, TOK, 1024), BF),
+                pltpu.VMEM((4, 4, 256, 768), BF),
+                pltpu.VMEM((128, 640), BF),
+                pltpu.VMEM((TOK, 768), F32),
+                pltpu.VMEM((GROUP, HALF, HEAD), BF),
+                pltpu.VMEM((TOK, 128), BF),
+                pltpu.VMEM((TOK, HEAD), F32),
+                pltpu.VMEM((2, HEAD), F32),
+                pltpu.SemaphoreType.DMA((51,)),
+            ],
+        ),
+        compiler_params=vmem(32),
+        name="first_half",
+    )(
+        lengths, cached, place, adapter, position,
+        in_hbm(normed), in_hbm(weight), in_hbm(low), in_hbm(rope), in_hbm(gains), in_hbm(pages),
+    )
+
+
+def second_body(
+    length_ref, cache_ref, place_ref, q_ref, kv_ref, pages_ref, out_ref, m_ref, l_ref, sum_ref, cached_ref, sems
+):
+    copies = page_copies(place_ref, pages_ref, cached_ref, sems, 0)
+    for copy in copies:
+        copy.start()
+    for copy in copies:
+        copy.wait()
+    attend_half(1, length_ref, cache_ref, q_ref, kv_ref, cached_ref, out_ref, m_ref, l_ref, sum_ref)
+
+
+def second_half(lengths, cached, place, q, kv, pages):
+    return pl.pallas_call(
+        second_body,
+        out_shape=jax.ShapeDtypeStruct((HALF, FEAT), BF),
+        grid_spec=pltpu.PrefetchScalarGridSpec(
+            num_scalar_prefetch=3,
+            grid=(1,),
+            in_specs=[whole(GROUP, HALF, HEAD), whole(2, TOK, HEAD), pl.BlockSpec(memory_space=pl.ANY)],
+            out_specs=whole(HALF, FEAT),
+            scratch_shapes=ATTEND_SCRATCH + [pltpu.SemaphoreType.DMA((32,))],
+        ),
+        compiler_params=vmem(12),
+        name="second_half",
+    )(lengths, cached, place, q, kv, in_hbm(pages))
+
+
+def out_body(half, me_ref, length_ref, adapter_ref, position_ref, *refs):
+    blocks, maps = refs[:8], refs[8:16]
+    weight_ref, hidden_ref = refs[16:18]
+    out_ref, w, oup, sems = refs[-4:]
+    order = col_order(me_ref[1])
+    copies = []
+    for b in range(8):
+        rows = weight_ref.at[pl.ds(2 * order[b], 2), pl.ds(0, 256), pl.ds(768, FEAT)]
+        copies.append(pltpu.make_async_copy(rows, w.at[b], sems.at[b]))
+    for p in range(PROMPTS):
+        slot = position_ref[adapter_ref[p]]
+        rows = weight_ref.at[slot, pl.ds(256, 16), pl.ds(640, FEAT)]
+        copies.append(pltpu.make_async_copy(rows, oup.at[pl.ds(p * 16, 16)], sems.at[8 + p]))
+    for copy in copies:
+        copy.start()
+    low = jnp.zeros((HALF, 64), F32)
+    for b in range(8):
+        low += lax.dot_general(
+            blocks[b][...], maps[b][128:192, :], (((1,), (1,)), ((), ())), preferred_element_type=F32
+        )
+    token = half * HALF + lax.broadcasted_iota(jnp.int32, low.shape, 0)
+    prompt = per_token(prompt_rows(length_ref), range(PROMPTS), token)
+    mine = lax.broadcasted_iota(jnp.int32, low.shape, 1) // 16 == prompt
+    low = jnp.where(mine, low, 0.0)
+    total = hidden_ref[...].astype(F32)
+    for b in range(8):
+        copies[b].wait()
+        total += jnp.dot(blocks[b][...], w[b].reshape(FEAT, FEAT), preferred_element_type=F32)
+    for copy in copies[8:]:
+        copy.wait()
+    change = jnp.dot(low, oup[...].astype(F32), precision=lax.Precision.HIGHEST, preferred_element_type=F32)
+    out_ref[...] = (total + 0.5 * change).astype(BF)
+
+
+def output(half, me, lengths, adapter, position, blocks, maps, weight, hidden, earlier=None):
+    tok = pl.BlockSpec((HALF, FEAT), lambda i, *_: (half, 0))
+    hbm = pl.BlockSpec(memory_space=pl.ANY)
+    late = () if earlier is None else (earlier,)
+    return pl.pallas_call(
+        lambda *refs: out_body(half, *refs),
         out_shape=jax.ShapeDtypeStruct((TOK, FEAT), BF),
         grid_spec=pltpu.PrefetchScalarGridSpec(
             num_scalar_prefetch=4,
             grid=(1,),
-            in_specs=[
-                whole(GROUP, TOK, HEAD),
-                whole(2, TOK, HEAD),
-                pl.BlockSpec(memory_space=pl.ANY),
-            ],
-            out_specs=whole(TOK, FEAT),
-            scratch_shapes=[
-                pltpu.VMEM((rows, 1), F32),
-                pltpu.VMEM((rows, 1), F32),
-                pltpu.VMEM((rows, HEAD), F32),
-                pltpu.VMEM((2, 2, WIN, HEAD), BF),
-                pltpu.SemaphoreType.DMA((32,)),
-            ],
-        ),
-        compiler_params=vmem(16),
-        name="attention",
-    )(me, lengths, cached, owner, q, kv, in_hbm(pages))
-
-
-def out_body(me_ref, length_ref, adapter_ref, position_ref, *refs):
-    blocks, maps = refs[:8], refs[8:16]
-    weight_ref, hidden_ref, out_ref, w, oup, sems = refs[16:]
-    order = col_order(me_ref[1])
-
-    def copies():
-        out = []
-        for b in range(8):
-            rows = weight_ref.at[pl.ds(2 * order[b], 2), pl.ds(0, 256), pl.ds(768, FEAT)]
-            out.append(pltpu.make_async_copy(rows, w.at[b], sems.at[b]))
-        for p in range(PROMPTS):
-            slot = position_ref[adapter_ref[p]]
-            rows = weight_ref.at[slot, pl.ds(256, 16), pl.ds(640, FEAT)]
-            out.append(pltpu.make_async_copy(rows, oup.at[pl.ds(p * 16, 16)], sems.at[8 + p]))
-        return out
-
-    @pl.when(pl.program_id(0) == 0)
-    def _():
-        todo = copies()
-        for copy in todo:
-            copy.start()
-        for copy in todo:
-            copy.wait()
-
-    total = hidden_ref[...].astype(F32)
-    low = jnp.zeros((total.shape[0], 64), F32)
-    for b in range(8):
-        x = blocks[b][...]
-        total += jnp.dot(x, w[b].reshape(FEAT, FEAT), preferred_element_type=F32)
-        low += lax.dot_general(x, maps[b][128:192, :], (((1,), (1,)), ((), ())), preferred_element_type=F32)
-    token = pl.program_id(0) * low.shape[0] + lax.broadcasted_iota(jnp.int32, low.shape, 0)
-    prompt = per_token(prompt_rows(length_ref), range(PROMPTS), token)
-    mine = lax.broadcasted_iota(jnp.int32, low.shape, 1) // 16 == prompt
-    low = jnp.where(mine, low, 0.0)
-    change = jnp.dot(low, oup[...].astype(F32), precision=lax.Precision.HIGHEST, preferred_element_type=F32)
-    out_ref[...] = (total + 0.5 * change).astype(BF)
-
-
-def output(me, lengths, adapter, position, blocks, maps, weight, hidden):
-    rows = 256
-    tok = pl.BlockSpec((rows, FEAT), lambda i, *_: (i, 0))
-    return pl.pallas_call(
-        out_body,
-        out_shape=jax.ShapeDtypeStruct((TOK, FEAT), BF),
-        grid_spec=pltpu.PrefetchScalarGridSpec(
-            num_scalar_prefetch=4,
-            grid=(TOK // rows,),
-            in_specs=[tok] * 8 + [whole(192, FEAT)] * 8 + [pl.BlockSpec(memory_space=pl.ANY), tok],
+            in_specs=[whole(HALF, FEAT)] * 8 + [whole(192, FEAT)] * 8 + [hbm, tok] + [hbm] * len(late),
             out_specs=tok,
             scratch_shapes=[
                 pltpu.VMEM((8, 2, 256, FEAT), BF),
@@ -440,9 +494,10 @@
                 pltpu.SemaphoreType.DMA((12,)),
             ],
         ),
+        input_output_aliases={} if earlier is None else {22: 0},
         compiler_params=vmem(24),
-        name="output",
-    )(me, lengths, adapter, position, *blocks, *maps, in_hbm(weight), hidden)
+        name="output_late" if late else "output_early",
+    )(me, lengths, adapter, position, *blocks, *maps, in_hbm(weight), hidden, *late)
 
 
 def on_device(
@@ -477,7 +532,7 @@
     weight = lax.all_gather(wide, "row", axis=0)
     slots = lax.all_to_all(slots, "row", 0, 0)
 
-    picked = pick_pages(me, page_owner_row, page_store_index, cache_page_store)
+    picked, place = pick_pages(me, page_owner_row, page_store_index, cache_page_store)
     picked, slots = lax.optimization_barrier((picked, slots))
     pages = lax.all_to_all(picked.reshape(16, 4 * PAGE, HEAD), "row", 0, 0).reshape(32, 2, PAGE, HEAD)
 
@@ -498,22 +553,37 @@
     rope = jnp.where(front, jnp.cos(angles), jnp.sin(angles))
 
     normed, low = norm_low(me, prompt_length, blocks, maps, input_norm_gain.reshape(8, 1, FEAT))
-    weight, normed, low, pages, rope = lax.optimization_barrier((weight, normed, low, pages, rope))
-    q, new_cache = project(
+    gains = jnp.stack([query_norm_gain, key_norm_gain]).astype(F32)
+    weight, normed, low, pages, rope, gains = lax.optimization_barrier((weight, normed, low, pages, rope, gains))
+    early, q, new_cache = first_half(
+        prompt_length,
+        cache_length,
+        place,
         prompt_adapter,
         adapter_position,
         normed,
         weight,
         low,
         rope,
-        query_norm_gain[None, :],
-        key_norm_gain[None, :],
+        gains,
+        pages,
     )
-    attended = attention(me, prompt_length, cache_length, page_owner_row, q, new_cache, pages)
-    attended = gather_col(attended, 256)
-    hidden_output = output(
-        me, prompt_length, prompt_adapter, adapter_position, attended, maps, weight, hidden_input
-    )
+    quarter = HALF // 2
+    other = swap(early)
+    before = lax.ppermute(early, "col", perm_z(1))
+    after = lax.ppermute(early, "col", perm_z(-1))
+    q, other = lax.optimization_barrier((q, other))
+    late = second_half(prompt_length, cache_length, place, q, new_cache, pages)
+    before, after, late = lax.optimization_barrier((before, after, late))
+    far = ring_far(before, after, "col", perm_z, quarter)
+    early = [early, other, before, swap(before), after, swap(after), far, swap(far)]
+
+    common = (me, prompt_length, prompt_adapter, adapter_position)
+    hidden_output = output(0, *common, early, maps, weight, hidden_input)
+    before, after, far = ring4(late, "col", perm_z, quarter)
+    far, hidden_output = lax.optimization_barrier((far, hidden_output))
+    late = [late, swap(late), before, swap(before), after, swap(after), far, swap(far)]
+    hidden_output = output(1, *common, late, maps, weight, hidden_input, hidden_output)
     return hidden_output, new_cache
 
 

time: 184 us -> 184 us (level)
  waiting for transfers between devices: 58.2 us -> 48.8 us
  starting transfers between devices: 41.9 us -> 49.8 us
    ppermute x3, waiting for transfers between devices: 15.2 us -> 2.75 us  [ring4(): before = lax.ppermute(block, axis, perm(1))]
    ppermute x18 -> x26, starting transfers between devices: 20.7 us -> 29 us  [the longest x16 18.2 us: swap(): return lax.ppermute(block, 'col', SWAP)]
    ppermute x18 -> x26, waiting for transfers between devices: 15.5 us -> 19.1 us  [the longest x4 9.97 us: ring_far(): far_low = lax.ppermute(before[:half], axis, perm(1))]
    pallas_call x4 -> x5, Pallas kernels: 40.4 us -> 40.2 us  [the longest x1 16.1 us: first_half(): pl.pallas_call(first_body, out_shape=(jax.ShapeDtypeStruct((HALF, FEAT),...]
  transfers between devices with their start and end apart: 27 -> 35, of which waited for: 11 -> 10; matrix products, arithmetic and copies ran while one was open for 5% -> 7% of each run, Pallas kernels for 7% -> 14%
where the time goes in v4:
time: 184 us; the launch traced here: 183 us
  Pallas kernels  50.7 us (28%)
  starting transfers between devices  49.8 us (27%)
  waiting for transfers between devices  48.8 us (27%)
  between operations  17 us (9%)
  local copies, waits for them, and re-layouts  9.9 us (5%)
  other arithmetic  7.24 us (4%)
    all_gather x1, waiting for transfers between devices, on_device(): weight = lax.all_gather(wide, 'row', axis=0)  22.5 us
    ppermute x16, starting transfers between devices, swap(): return lax.ppermute(block, 'col', SWAP)  18.2 us
    pallas_call x1, Pallas kernels, first_half(): pl.pallas_call(first_body, out_shape=(jax.ShapeDtypeStruct((HALF, FEAT),...  16.1 us
    pallas_call x2, Pallas kernels, output(): pl.pallas_call(lambda *refs: out_body(half, *refs), out_shape=jax.ShapeDt...  12.3 us
    ppermute x4, waiting for transfers between devices, ring_far(): far_low = lax.ppermute(before[:half], axis, perm(1))  9.97 us
    all_to_all x1, starting transfers between devices, on_device(): slots = lax.all_to_all(slots, 'row', 0, 0)  7.73 us
    pallas_call x1, Pallas kernels, second_half(): pl.pallas_call(second_body, out_shape=jax.ShapeDtypeStruct((HALF, FEAT),...  6.71 us
    ppermute x4, waiting for transfers between devices, ring_far(): far_high = lax.ppermute(after[half:], axis, perm(-1))  6.4 us
  transfers between devices with their start and end apart: 35, of which 10 were waited for; matrix products, arithmetic and copies ran while one was open for 7% of the time, Pallas kernels for 14%

profile of v4, /device:TPU:1, one launch (start us, length us, event | category | flops | bytes accessed | tf_op | source)
XLA Modules:
  0.0 183.3 jit_solution(10981152800494909902)
XLA Ops:
  7.9 2.9 %pack.1 = (bf16[272,1280]{1,0:T(8,128)(2,1)}, bf16[16,48,512]{2,1,0:T(8,128)(2,1)}) custom-call(s32[2]{0:T(128)} %pad_add_fusion.me_ref.refs_0_, bf16[256,768]{1,0:T(8,128)(2,1)} %qkv_ref.1, bf16[256,512]{1,0:T(8,128)(2,1)} %wo_ref.1, bf16[1,16,640]{2,1,0:T(8,128)(2,1)} %up_ref.1, bf16[1,16,4096]{2,1,0:T(8,128)(2,1)} %oup_ref.1, ...), custom_call_target="tpu_custom_call" | custom-call | tf_op jit(solution)/shard_map/pack/pallas_call | solution.py:146
  10.8 7.7 %all-to-all-start = ((bf16[16,48,512]{2,1,0:T(8,128)(2,1)}), bf16[16,48,512]{2,1,0:T(8,128)(2,1)S(1)}, u32[]{:S(2)}, u32[]{:S(2)}) async-start(bf16[16,48,512]{2,1,0:T(8,128)(2,1)} %get-tuple-element.29), calls=%async_computation | async-start | bytes 1572864 | tf_op jit(solution)/shard_map/all_to_all | solution.py:533
  21.8 5.1 %pick_pages.1 = (bf16[16,2,2,128,128]{4,3,2,1,0:T(8,128)(2,1)}, s32[16]{0:T(128)S(1)}) custom-call(s32[2]{0:T(128)S(1)} %copy-done.7, s32[256,1]{1,0:T(8,128)S(1)} %copy.21.owner_ref, s32[256]{0:T(256)S(1)} %copy-done.11, bf16[8,2,128,128]{3,2,1,0:T(8,128)(2,1)S(1)} %copy-done.3), custom_call_target="tpu_custom_call" | custom-call | tf_op jit(solution)/shard_map/pick_pages/pallas_call | solution.py:117
  26.9 4.4 %all-to-all-done.slots_ref = bf16[16,48,512]{2,1,0:T(8,128)(2,1)S(1)} async-done(((bf16[16,48,512]{2,1,0:T(8,128)(2,1)}), bf16[16,48,512]{2,1,0:T(8,128)(2,1)S(1)}, u32[]{:S(2)}, u32[]{:S(2)}) %all-to-all-start) | async-done | bytes 786464 | tf_op jit(solution)/shard_map/all_to_all | solution.py:533
  31.3 4.9 %all-to-all-start.1 = ((bf16[16,512,128]{2,1,0:T(8,128)(2,1)}), bf16[16,512,128]{2,1,0:T(8,128)(2,1)}, u32[]{:S(2)}, u32[]{:S(2)}) async-start(bf16[16,512,128]{2,1,0:T(8,128)(2,1)} %bitcast.3), calls=%async_computation.1 | async-start | bytes 4194304 | tf_op jit(solution)/shard_map/all_to_all | solution.py:537
  38.0 2.9 %collective-permute-start.3 = (bf16[512,512]{1,0:T(8,128)(2,1)S(1)}, bf16[512,512]{1,0:T(8,128)(2,1)S(1)}, u32[]{:S(2)}, u32[]{:S(2)}) collective-permute-start(bf16[512,512]{1,0:T(8,128)(2,1)S(1)} %copy-done), channel_id=1, source_target_pairs={{0,6},{1,7},{2,0},{3,1},{4,2},{5,3},{6,4},{7,5},{8,14},{9,15},{10,... | collective-permute-start | bytes 1572872 | tf_op jit(solution)/shard_map/ppermute | solution.py:48
  41.0 5.5 %collective-permute-start = (bf16[512,512]{1,0:T(8,128)(2,1)S(1)}, bf16[512,512]{1,0:T(8,128)(2,1)S(1)}, u32[]{:S(2)}, u32[]{:S(2)}) collective-permute-start(bf16[512,512]{1,0:T(8,128)(2,1)S(1)} %copy-done), channel_id=1, source_target_pairs={{0,1},{1,0},{2,3},{3,2},{4,5},{5,4},{6,7},{7,6},{8,9},{9,8},{10,11... | collective-permute-start | bytes 1572872 | tf_op jit(solution)/shard_map/ppermute | solution.py:53
  56.1 2.7 %collective-permute-start.6 = (bf16[256,512]{1,0:T(8,128)(2,1)}, bf16[256,512]{1,0:T(8,128)(2,1)}, u32[]{:S(2)}, u32[]{:S(2)}) collective-permute-start(bf16[256,512]{1,0:T(8,128)(2,1)} %slice.65), channel_id=1, source_target_pairs={{0,6},{1,7},{2,0},{3,1},{4,2},{5,3},{6,4},{7,5},{8,14},{9,15},{10,... | collective-permute-start | bytes 786440 | tf_op jit(solution)/shard_map/ppermute | solution.py:42
  58.8 2.5 %select_slots.1.refs_8_.refs_12_ = bf16[192,512]{1,0:T(8,128)(2,1)} custom-call(s32[4]{0:T(128)} %refs_2_.3, s32[16]{0:T(128)} %refs_3_.3, bf16[16,48,512]{2,1,0:T(8,128)(2,1)} %copy-done.12), custom_call_target="tpu_custom_call" | custom-call | tf_op jit(solution)/shard_map/select_slots/pallas_call | solution.py:174
  62.0 2.3 %collective-permute-done.5 = bf16[256,512]{1,0:T(8,128)(2,1)} collective-permute-done((bf16[256,512]{1,0:T(8,128)(2,1)}, bf16[256,512]{1,0:T(8,128)(2,1)}, u32[]{:S(2)}, u32[]{:S(2)}) %collective-permute-start.5) | collective-permute-done | bytes 262176 | tf_op jit(solution)/shard_map/ppermute | solution.py:41
  65.9 2.7 %collective-permute-done.9.refs_10_.refs_14_ = bf16[192,512]{1,0:T(8,128)(2,1)S(1)} collective-permute-done((bf16[192,512]{1,0:T(8,128)(2,1)}, bf16[192,512]{1,0:T(8,128)(2,1)S(1)}, u32[]{:S(2)}, u32[]{:S(2)}) %collective-permute-start.9) | collective-permute-done | bytes 196640 | tf_op jit(solution)/shard_map/ppermute | solution.py:47
  71.8 4.1 %collective-permute-done.13 = bf16[96,512]{1,0:T(8,128)(2,1)S(1)} collective-permute-done((bf16[96,512]{1,0:T(8,128)(2,1)S(1)}, bf16[96,512]{1,0:T(8,128)(2,1)S(1)}, u32[]{:S(2)}, u32[]{:S(2)}) %collective-permute-start.13) | collective-permute-done | bytes 98336 | tf_op jit(solution)/shard_map/ppermute | solution.py:41
  75.9 3.8 %collective-permute-done.14 = bf16[96,512]{1,0:T(8,128)(2,1)S(1)} collective-permute-done((bf16[96,512]{1,0:T(8,128)(2,1)S(1)}, bf16[96,512]{1,0:T(8,128)(2,1)S(1)}, u32[]{:S(2)}, u32[]{:S(2)}) %collective-permute-start.14) | collective-permute-done | bytes 98336 | tf_op jit(solution)/shard_map/ppermute | solution.py:42
  83.0 2.1 %sine_select_fusion.rope_hbm = f32[512,128]{1,0:T(8,128)} fusion(f32[128]{0:T(128)S(1)} %pad_maximum_fusion.1, s32[512]{0:T(512)S(1)} %get-tuple-element.62, s32[512]{0:T(512)S(1)} %get-tuple-element.63, s32[512]{0:T(512)S(1)} %get-tuple-element.64, s32[512]{0:T(512)S(1)} %get-tuple-element.65, pred[512]{0:T(512)(128)(4,1)S(1)} %get-tuple-element.58, ...), kind=kLoop, calls=%fused_computation.1 | loop fusion | flops 458752 | bytes 273024 | tf_op jit(solution)/shard_map/jit(_where)/select_n | solution.py:553
  86.1 5.0 %norm_low.1 = (bf16[4,512,1024]{2,1,0:T(8,128)(2,1)}, bf16[512,128]{1,0:T(8,128)(2,1)}) custom-call(s32[2]{0:T(128)S(1)} %copy-done.8, s32[1,4]{1,0:T(1,128)S(1)} %copy-done.5, bf16[512,512]{1,0:T(8,128)(2,1)S(1)} %copy-done, bf16[512,512]{1,0:T(8,128)(2,1)S(1)} %collective-permute-done.refs_1_, bf16[512,512]{1,0:T(8,128)(2,1)S(1)} %collective-permute-done.1.refs_2_, ...), custom_call_target="tpu_custom_call" | custom-call | tf_op jit(solution)/shard_map/norm_low/pallas_call | solution.py:208
  91.1 22.5 %all-gather.3.cloned.1.call-done = bf16[4352,1280]{1,0:T(8,128)(2,1)} async-done(((bf16[272,1280]{1,0:T(8,128)(2,1)}), bf16[4352,1280]{1,0:T(8,128)(2,1)}) %all-gather.3.cloned.1.call-update) | async-done | bytes 11141136 | tf_op jit(solution)/shard_map/all_gather | solution.py:532
  113.7 16.1 %first_half.1 = (bf16[256,512]{1,0:T(8,128)(2,1)S(1)}, bf16[4,256,128]{2,1,0:T(8,128)(2,1)S(1)}, bf16[2,512,128]{2,1,0:T(8,128)(2,1)}) custom-call(s32[1,4]{1,0:T(1,128)S(1)} %copy-done.5, s32[4]{0:T(128)S(1)} %copy-done.6, s32[16]{0:T(128)S(1)} %get-tuple-element.26.place_ref, s32[4]{0:T(128)S(1)} %copy-done.9, s32[16]{0:T(128)S(1)} %copy-done.10, ...), custom_call_target="tpu_custom_call" | custom-call | tf_op jit(solution)/shard_map/first_half/pallas_call | solution.py:385
  135.0 6.7 %second_half.1.refs_4_ = bf16[256,512]{1,0:T(8,128)(2,1)S(1)} custom-call(s32[1,4]{1,0:T(1,128)S(1)} %copy-done.5, s32[4]{0:T(128)S(1)} %copy-done.6, s32[16]{0:T(128)S(1)} %get-tuple-element.26.place_ref, bf16[4,256,128]{2,1,0:T(8,128)(2,1)S(1)} %get-tuple-element.42.q_ref, bf16[2,512,128]{2,1,0:T(8,128)(2,1)S(1)} %copy-done.4, ...), custom_call_target="tpu_custom_call" | custom-call | tf_op jit(solution)/shard_map/second_half/pallas_call | solution.py:430
  147.8 2.0 %collective-permute-start.27 = (bf16[256,512]{1,0:T(8,128)(2,1)S(1)}, bf16[256,512]{1,0:T(8,128)(2,1)S(1)}, u32[]{:S(2)}, u32[]{:S(2)}) collective-permute-start(bf16[256,512]{1,0:T(8,128)(2,1)S(1)} %collective-permute-done.17.refs_8_), channel_id=1, source_target_pairs={{0,1},{1,0},{2,3},{3,2},{4,5},{5,4},{6,7},{7,6},{8,9},{9,8},{10,11... | collective-permute-start | bytes 786440 | tf_op jit(solution)/shard_map/ppermute | solution.py:53
  149.8 2.6 %collective-permute-done.29 = bf16[128,512]{1,0:T(8,128)(2,1)S(1)} collective-permute-done((bf16[128,512]{1,0:T(8,128)(2,1)S(1)}, bf16[128,512]{1,0:T(8,128)(2,1)S(1)}, u32[]{:S(2)}, u32[]{:S(2)}) %collective-permute-start.29) | collective-permute-done | bytes 131104 | tf_op jit(solution)/shard_map/ppermute | solution.py:42
  152.4 2.2 %collective-permute-start.30 = (bf16[256,512]{1,0:T(8,128)(2,1)S(1)}, bf16[256,512]{1,0:T(8,128)(2,1)S(1)}, u32[]{:S(2)}, u32[]{:S(2)}) collective-permute-start(bf16[256,512]{1,0:T(8,128)(2,1)S(1)} %constant_dynamic-update-slice_fusion.4.refs_10_), channel_id=1, source_target_pairs={{0,1},{1,0},{2,3},{3,2},{4,5},{5,4},{6,7},{7,6},{8,9},{9,8},{10,11... | collective-permute-start | bytes 786440 | tf_op jit(solution)/shard_map/ppermute | solution.py:53
  157.6 3.6 %collective-permute-done.24 = bf16[128,512]{1,0:T(8,128)(2,1)S(1)} collective-permute-done((bf16[128,512]{1,0:T(8,128)(2,1)S(1)}, bf16[128,512]{1,0:T(8,128)(2,1)S(1)}, u32[]{:S(2)}, u32[]{:S(2)}) %collective-permute-start.24) | collective-permute-done | bytes 131104 | tf_op jit(solution)/shard_map/ppermute | solution.py:41
  162.6 6.1 %output_early.1.refs_22_ = bf16[512,512]{1,0:T(8,128)(2,1)} custom-call(s32[2]{0:T(128)S(1)} %copy-done.8, s32[1,4]{1,0:T(1,128)S(1)} %copy-done.5, s32[4]{0:T(128)S(1)} %copy-done.9, s32[16]{0:T(128)S(1)} %copy-done.10, bf16[256,512]{1,0:T(8,128)(2,1)S(1)} %get-tuple-element.40.refs_4_, bf16[256,512]{1,0:T(8,128)(2,1)S(1)} %collective-permute-done.18.refs_5_, ...), custom_call_target="tpu_custom_call" | custom-call | tf_op jit(solution)/shard_map/output_early/pallas_call | solution.py:483
  170.3 6.1 %output_late.1 = bf16[512,512]{1,0:T(8,128)(2,1)} custom-call(s32[2]{0:T(128)S(1)} %copy-done.8, s32[1,4]{1,0:T(1,128)S(1)} %copy-done.5, s32[4]{0:T(128)S(1)} %copy-done.9, s32[16]{0:T(128)S(1)} %copy-done.10, bf16[256,512]{1,0:T(8,128)(2,1)S(1)} %second_half.1.refs_4_, ...), custom_call_target="tpu_custom_call", output_to_operand_aliasing={{}: (22, {})} | custom-call | tf_op jit(solution)/shard_map/output_late/pallas_call | solution.py:483
  (116 shorter events, 39.6 us)
Async XLA Ops:
  7.2 106.5 %all-gather.3.cloned.1.call-start = ((), (), s32[]{:S(2)}) async-start(), calls=%async_computation.2 | async-start | bytes 11837440 | tf_op jit(solution)/shard_map/all_gather | solution.py:532
  10.8 20.5 %all-to-all-start = ((bf16[16,48,512]{2,1,0:T(8,128)(2,1)}), bf16[16,48,512]{2,1,0:T(8,128)(2,1)S(1)}, u32[]{:S(2)}, u32[]{:S(2)}) async-start(bf16[16,48,512]{2,1,0:T(8,128)(2,1)} %get-tuple-element.29), calls=%async_computation | async-start | bytes 1572864 | tf_op jit(solution)/shard_map/all_to_all | solution.py:533
  31.3 59.8 %all-to-all-start.1 = ((bf16[16,512,128]{2,1,0:T(8,128)(2,1)}), bf16[16,512,128]{2,1,0:T(8,128)(2,1)}, u32[]{:S(2)}, u32[]{:S(2)}) async-start(bf16[16,512,128]{2,1,0:T(8,128)(2,1)} %bitcast.3), calls=%async_computation.1 | async-start | bytes 4194304 | tf_op jit(solution)/shard_map/all_to_all | solution.py:537
  36.2 17.8 %collective-permute-start.1 = (bf16[512,512]{1,0:T(8,128)(2,1)S(1)}, bf16[512,512]{1,0:T(8,128)(2,1)S(1)}, u32[]{:S(2)}, u32[]{:S(2)}) collective-permute-start(bf16[512,512]{1,0:T(8,128)(2,1)S(1)} %copy-done), channel_id=1, source_target_pairs={{0,2},{1,3},{2,4},{3,5},{4,6},{5,7},{6,0},{7,1},{8,10},{9,11},{10,... | collective-permute-start | bytes 1572872 | tf_op jit(solution)/shard_map/ppermute | solution.py:47
  38.0 17.4 %collective-permute-start.3 = (bf16[512,512]{1,0:T(8,128)(2,1)S(1)}, bf16[512,512]{1,0:T(8,128)(2,1)S(1)}, u32[]{:S(2)}, u32[]{:S(2)}) collective-permute-start(bf16[512,512]{1,0:T(8,128)(2,1)S(1)} %copy-done), channel_id=1, source_target_pairs={{0,6},{1,7},{2,0},{3,1},{4,2},{5,3},{6,4},{7,5},{8,14},{9,15},{10,... | collective-permute-start | bytes 1572872 | tf_op jit(solution)/shard_map/ppermute | solution.py:48
  41.0 40.2 %collective-permute-start = (bf16[512,512]{1,0:T(8,128)(2,1)S(1)}, bf16[512,512]{1,0:T(8,128)(2,1)S(1)}, u32[]{:S(2)}, u32[]{:S(2)}) collective-permute-start(bf16[512,512]{1,0:T(8,128)(2,1)S(1)} %copy-done), channel_id=1, source_target_pairs={{0,1},{1,0},{2,3},{3,2},{4,5},{5,4},{6,7},{7,6},{8,9},{9,8},{10,11... | collective-permute-start | bytes 1572872 | tf_op jit(solution)/shard_map/ppermute | solution.py:53
  54.8 9.5 %collective-permute-start.5 = (bf16[256,512]{1,0:T(8,128)(2,1)}, bf16[256,512]{1,0:T(8,128)(2,1)}, u32[]{:S(2)}, u32[]{:S(2)}) collective-permute-start(bf16[256,512]{1,0:T(8,128)(2,1)} %slice.64), channel_id=1, source_target_pairs={{0,2},{1,3},{2,4},{3,5},{4,6},{5,7},{6,0},{7,1},{8,10},{9,11},{10,... | collective-permute-start | bytes 786440 | tf_op jit(solution)/shard_map/ppermute | solution.py:41
  56.1 14.0 %collective-permute-start.6 = (bf16[256,512]{1,0:T(8,128)(2,1)}, bf16[256,512]{1,0:T(8,128)(2,1)}, u32[]{:S(2)}, u32[]{:S(2)}) collective-permute-start(bf16[256,512]{1,0:T(8,128)(2,1)} %slice.65), channel_id=1, source_target_pairs={{0,6},{1,7},{2,0},{3,1},{4,2},{5,3},{6,4},{7,5},{8,14},{9,15},{10,... | collective-permute-start | bytes 786440 | tf_op jit(solution)/shard_map/ppermute | solution.py:42
  61.3 7.3 %collective-permute-start.9 = (bf16[192,512]{1,0:T(8,128)(2,1)}, bf16[192,512]{1,0:T(8,128)(2,1)S(1)}, u32[]{:S(2)}, u32[]{:S(2)}) collective-permute-start(bf16[192,512]{1,0:T(8,128)(2,1)} %select_slots.1.refs_8_.refs_12_), channel_id=1, source_target_pairs={{0,2},{1,3},{2,4},{3,5},{4,6},{5,7},{6,0},{7,1},{8,10},{9,11},{10,... | collective-permute-start | bytes 589832 | tf_op jit(solution)/shard_map/ppermute | solution.py:47
  61.3 21.5 %collective-permute-start.2 = (bf16[512,512]{1,0:T(8,128)(2,1)S(1)}, bf16[512,512]{1,0:T(8,128)(2,1)S(1)}, u32[]{:S(2)}, u32[]{:S(2)}) collective-permute-start(bf16[512,512]{1,0:T(8,128)(2,1)S(1)} %collective-permute-done.1.refs_2_), channel_id=1, source_target_pairs={{0,1},{1,0},{2,3},{3,2},{4,5},{5,4},{6,7},{7,6},{8,9},{9,8},{10,11... | collective-permute-start | bytes 1572872 | tf_op jit(solution)/shard_map/ppermute | solution.py:53
  64.2 6.9 %collective-permute-start.11 = (bf16[192,512]{1,0:T(8,128)(2,1)}, bf16[192,512]{1,0:T(8,128)(2,1)S(1)}, u32[]{:S(2)}, u32[]{:S(2)}) collective-permute-start(bf16[192,512]{1,0:T(8,128)(2,1)} %select_slots.1.refs_8_.refs_12_), channel_id=1, source_target_pairs={{0,6},{1,7},{2,0},{3,1},{4,2},{5,3},{6,4},{7,5},{8,14},{9,15},{10,... | collective-permute-start | bytes 589832 | tf_op jit(solution)/shard_map/ppermute | solution.py:48
  68.6 16.5 %collective-permute-start.4 = (bf16[512,512]{1,0:T(8,128)(2,1)S(1)}, bf16[512,512]{1,0:T(8,128)(2,1)S(1)}, u32[]{:S(2)}, u32[]{:S(2)}) collective-permute-start(bf16[512,512]{1,0:T(8,128)(2,1)S(1)} %collective-permute-done.3.refs_4_), channel_id=1, source_target_pairs={{0,1},{1,0},{2,3},{3,2},{4,5},{5,4},{6,7},{7,6},{8,9},{9,8},{10,11... | collective-permute-start | bytes 1572872 | tf_op jit(solution)/shard_map/ppermute | solution.py:53
  71.1 14.0 %collective-permute-start.7 = (bf16[512,512]{1,0:T(8,128)(2,1)S(1)}, bf16[512,512]{1,0:T(8,128)(2,1)S(1)}, u32[]{:S(2)}, u32[]{:S(2)}) collective-permute-start(bf16[512,512]{1,0:T(8,128)(2,1)S(1)} %constant_dynamic-update-slice_fusion.refs_6_), channel_id=1, source_target_pairs={{0,1},{1,0},{2,3},{3,2},{4,5},{5,4},{6,7},{7,6},{8,9},{9,8},{10,11... | collective-permute-start | bytes 1572872 | tf_op jit(solution)/shard_map/ppermute | solution.py:53
  130.6 11.1 %collective-permute-start.16 = (bf16[256,512]{1,0:T(8,128)(2,1)S(1)}, bf16[256,512]{1,0:T(8,128)(2,1)S(1)}, u32[]{:S(2)}, u32[]{:S(2)}) collective-permute-start(bf16[256,512]{1,0:T(8,128)(2,1)S(1)} %get-tuple-element.40.refs_4_), channel_id=1, source_target_pairs={{0,2},{1,3},{2,4},{3,5},{4,6},{5,7},{6,0},{7,1},{8,10},{9,11},{10,... | collective-permute-start | bytes 786440 | tf_op jit(solution)/shard_map/ppermute | solution.py:573
  132.3 9.4 %collective-permute-start.17 = (bf16[256,512]{1,0:T(8,128)(2,1)S(1)}, bf16[256,512]{1,0:T(8,128)(2,1)S(1)}, u32[]{:S(2)}, u32[]{:S(2)}) collective-permute-start(bf16[256,512]{1,0:T(8,128)(2,1)S(1)} %get-tuple-element.40.refs_4_), channel_id=1, source_target_pairs={{0,6},{1,7},{2,0},{3,1},{4,2},{5,3},{6,4},{7,5},{8,14},{9,15},{10,... | collective-permute-start | bytes 786440 | tf_op jit(solution)/shard_map/ppermute | solution.py:574
  141.8 12.9 %collective-permute-start.20 = (bf16[256,512]{1,0:T(8,128)(2,1)S(1)}, bf16[256,512]{1,0:T(8,128)(2,1)S(1)}, u32[]{:S(2)}, u32[]{:S(2)}) collective-permute-start(bf16[256,512]{1,0:T(8,128)(2,1)S(1)} %second_half.1.refs_4_), channel_id=1, source_target_pairs={{0,2},{1,3},{2,4},{3,5},{4,6},{5,7},{6,0},{7,1},{8,10},{9,11},{10,... | collective-permute-start | bytes 786440 | tf_op jit(solution)/shard_map/ppermute | solution.py:47
  143.0 12.8 %collective-permute-start.22 = (bf16[256,512]{1,0:T(8,128)(2,1)S(1)}, bf16[256,512]{1,0:T(8,128)(2,1)S(1)}, u32[]{:S(2)}, u32[]{:S(2)}) collective-permute-start(bf16[256,512]{1,0:T(8,128)(2,1)S(1)} %second_half.1.refs_4_), channel_id=1, source_target_pairs={{0,6},{1,7},{2,0},{3,1},{4,2},{5,3},{6,4},{7,5},{8,14},{9,15},{10,... | collective-permute-start | bytes 786440 | tf_op jit(solution)/shard_map/ppermute | solution.py:48
  144.6 7.9 %collective-permute-start.29 = (bf16[128,512]{1,0:T(8,128)(2,1)S(1)}, bf16[128,512]{1,0:T(8,128)(2,1)S(1)}, u32[]{:S(2)}, u32[]{:S(2)}) collective-permute-start(bf16[128,512]{1,0:T(8,128)(2,1)S(1)} %slice.63), channel_id=1, source_target_pairs={{0,6},{1,7},{2,0},{3,1},{4,2},{5,3},{6,4},{7,5},{8,14},{9,15},{10,... | collective-permute-start | bytes 393224 | tf_op jit(solution)/shard_map/ppermute | solution.py:42
  146.2 15.7 %collective-permute-start.26 = (bf16[256,512]{1,0:T(8,128)(2,1)S(1)}, bf16[256,512]{1,0:T(8,128)(2,1)S(1)}, u32[]{:S(2)}, u32[]{:S(2)}) collective-permute-start(bf16[256,512]{1,0:T(8,128)(2,1)S(1)} %collective-permute-done.16.refs_6_), channel_id=1, source_target_pairs={{0,1},{1,0},{2,3},{3,2},{4,5},{5,4},{6,7},{7,6},{8,9},{9,8},{10,11... | collective-permute-start | bytes 786440 | tf_op jit(solution)/shard_map/ppermute | solution.py:53
  147.8 14.7 %collective-permute-start.27 = (bf16[256,512]{1,0:T(8,128)(2,1)S(1)}, bf16[256,512]{1,0:T(8,128)(2,1)S(1)}, u32[]{:S(2)}, u32[]{:S(2)}) collective-permute-start(bf16[256,512]{1,0:T(8,128)(2,1)S(1)} %collective-permute-done.17.refs_8_), channel_id=1, source_target_pairs={{0,1},{1,0},{2,3},{3,2},{4,5},{5,4},{6,7},{7,6},{8,9},{9,8},{10,11... | collective-permute-start | bytes 786440 | tf_op jit(solution)/shard_map/ppermute | solution.py:53
  152.4 10.1 %collective-permute-start.30 = (bf16[256,512]{1,0:T(8,128)(2,1)S(1)}, bf16[256,512]{1,0:T(8,128)(2,1)S(1)}, u32[]{:S(2)}, u32[]{:S(2)}) collective-permute-start(bf16[256,512]{1,0:T(8,128)(2,1)S(1)} %constant_dynamic-update-slice_fusion.4.refs_10_), channel_id=1, source_target_pairs={{0,1},{1,0},{2,3},{3,2},{4,5},{5,4},{6,7},{7,6},{8,9},{9,8},{10,11... | collective-permute-start | bytes 786440 | tf_op jit(solution)/shard_map/ppermute | solution.py:53
  161.2 7.7 %collective-permute-start.19 = (bf16[256,512]{1,0:T(8,128)(2,1)S(1)}, bf16[256,512]{1,0:T(8,128)(2,1)S(1)}, u32[]{:S(2)}, u32[]{:S(2)}) collective-permute-start(bf16[256,512]{1,0:T(8,128)(2,1)S(1)} %second_half.1.refs_4_), channel_id=1, source_target_pairs={{0,1},{1,0},{2,3},{3,2},{4,5},{5,4},{6,7},{7,6},{8,9},{9,8},{10,11... | collective-permute-start | bytes 786440 | tf_op jit(solution)/shard_map/ppermute | solution.py:53
  161.9 6.9 %collective-permute-start.21 = (bf16[256,512]{1,0:T(8,128)(2,1)S(1)}, bf16[256,512]{1,0:T(8,128)(2,1)S(1)}, u32[]{:S(2)}, u32[]{:S(2)}) collective-permute-start(bf16[256,512]{1,0:T(8,128)(2,1)S(1)} %collective-permute-done.20.refs_6_), channel_id=1, source_target_pairs={{0,1},{1,0},{2,3},{3,2},{4,5},{5,4},{6,7},{7,6},{8,9},{9,8},{10,11... | collective-permute-start | bytes 786440 | tf_op jit(solution)/shard_map/ppermute | solution.py:53
  162.0 6.9 %collective-permute-start.23 = (bf16[256,512]{1,0:T(8,128)(2,1)S(1)}, bf16[256,512]{1,0:T(8,128)(2,1)S(1)}, u32[]{:S(2)}, u32[]{:S(2)}) collective-permute-start(bf16[256,512]{1,0:T(8,128)(2,1)S(1)} %collective-permute-done.22.refs_8_), channel_id=1, source_target_pairs={{0,1},{1,0},{2,3},{3,2},{4,5},{5,4},{6,7},{7,6},{8,9},{9,8},{10,11... | collective-permute-start | bytes 786440 | tf_op jit(solution)/shard_map/ppermute | solution.py:53
  (27 other events, 516.0 us)
Sparse Core Ops, SparseCore 0:
  11.0 102.6 all-gather.2

commit v5 on v4

--- a/solution.py
+++ b/solution.py
@@ -38,15 +38,13 @@
 
 
 def ring_far(before, after, axis, perm, half):
-    far_low = lax.ppermute(before[:half], axis, perm(1))
-    far_high = lax.ppermute(after[half:], axis, perm(-1))
-    return jnp.concatenate([far_low, far_high], axis=0)
+    return lax.ppermute(before[:half], axis, perm(1)), lax.ppermute(after[half:], axis, perm(-1))
 
 
 def ring4(block, axis, perm, half):
     before = lax.ppermute(block, axis, perm(1))
     after = lax.ppermute(block, axis, perm(-1))
-    return before, after, ring_far(before, after, axis, perm, half)
+    return before, after, jnp.concatenate(ring_far(before, after, axis, perm, half), axis=0)
 
 
 def swap(block):
@@ -131,12 +129,14 @@
     )(me, owner, index, store)
 
 
-def pack_body(me_ref, qkv_ref, wo_ref, up_ref, oup_ref, down_ref, odown_ref, wide_ref, slots_ref):
+def pack_body(me_ref, qkv_ref, wo_ref, up_ref, oup_ref, down_ref, odown_ref, wide_ref, rest_ref, slots_ref):
     wide_ref[:256, :768] = qkv_ref[...]
-    wide_ref[:256, 768:] = wo_ref[...]
+    wide_ref[:256, 768:] = wo_ref[:, :256]
     wide_ref[256:, :640] = up_ref[0]
-    wide_ref[256:, 640:1152] = oup_ref[0]
-    wide_ref[256:, 1152:] = jnp.zeros((16, 128), BF)
+    wide_ref[256:, 640:] = jnp.zeros((16, 384), BF)
+    rest_ref[:256, :] = wo_ref[:, 256:]
+    rest_ref[256:272, :] = oup_ref[0, :, :256]
+    rest_ref[272:, :] = oup_ref[0, :, 256:]
     for r in range(16):
         slots_ref[r, :32, :] = down_ref[0]
         slots_ref[r, 32:, :] = odown_ref[0]
@@ -145,7 +145,11 @@
 def pack(me, qkv, wo, up, oup, down, odown):
     return pl.pallas_call(
         pack_body,
-        out_shape=(jax.ShapeDtypeStruct((272, 1280), BF), jax.ShapeDtypeStruct((16, 48, FEAT), BF)),
+        out_shape=(
+            jax.ShapeDtypeStruct((272, 1024), BF),
+            jax.ShapeDtypeStruct((288, 256), BF),
+            jax.ShapeDtypeStruct((16, 48, FEAT), BF),
+        ),
         grid_spec=pltpu.PrefetchScalarGridSpec(
             num_scalar_prefetch=1,
             grid=(1,),
@@ -157,7 +161,7 @@
                 pl.BlockSpec((1, 32, FEAT), lambda i, me: (0, 0, me[1])),
                 whole(1, 16, FEAT),
             ],
-            out_specs=(whole(272, 1280), whole(16, 48, FEAT)),
+            out_specs=(whole(272, 1024), whole(288, 256), whole(16, 48, FEAT)),
         ),
         name="pack",
     )(me, qkv, wo, up, oup, down, odown)
@@ -443,24 +447,28 @@
 
 
 def out_body(half, me_ref, length_ref, adapter_ref, position_ref, *refs):
-    blocks, maps = refs[:8], refs[8:16]
-    weight_ref, hidden_ref = refs[16:18]
+    blocks = [ref[...] for ref in refs[:6]] + [jnp.concatenate([refs[i][...], refs[i + 1][...]], axis=0) for i in (6, 8)]
+    maps = refs[10:18]
+    weight_ref, rest_ref, hidden_ref = refs[18:21]
     out_ref, w, oup, sems = refs[-4:]
     order = col_order(me_ref[1])
     copies = []
     for b in range(8):
-        rows = weight_ref.at[pl.ds(2 * order[b], 2), pl.ds(0, 256), pl.ds(768, FEAT)]
-        copies.append(pltpu.make_async_copy(rows, w.at[b], sems.at[b]))
+        for n, ref in enumerate((weight_ref.at[:, :, pl.ds(768, 256)], rest_ref)):
+            rows = ref.at[pl.ds(2 * order[b], 2), pl.ds(0, 256)]
+            copies.append(pltpu.make_async_copy(rows, w.at[n, b], sems.at[2 * b + n]))
     for p in range(PROMPTS):
         slot = position_ref[adapter_ref[p]]
-        rows = weight_ref.at[slot, pl.ds(256, 16), pl.ds(640, FEAT)]
-        copies.append(pltpu.make_async_copy(rows, oup.at[pl.ds(p * 16, 16)], sems.at[8 + p]))
+        for n in range(2):
+            rows = rest_ref.at[slot, pl.ds(256 + 16 * n, 16)]
+            into = oup.at[pl.ds(p * 16, 16), pl.ds(256 * n, 256)]
+            copies.append(pltpu.make_async_copy(rows, into, sems.at[16 + 2 * p + n]))
     for copy in copies:
         copy.start()
     low = jnp.zeros((HALF, 64), F32)
     for b in range(8):
         low += lax.dot_general(
-            blocks[b][...], maps[b][128:192, :], (((1,), (1,)), ((), ())), preferred_element_type=F32
+            blocks[b], maps[b][128:192, :], (((1,), (1,)), ((), ())), preferred_element_type=F32
         )
     token = half * HALF + lax.broadcasted_iota(jnp.int32, low.shape, 0)
     prompt = per_token(prompt_rows(length_ref), range(PROMPTS), token)
@@ -468,15 +476,18 @@
     low = jnp.where(mine, low, 0.0)
     total = hidden_ref[...].astype(F32)
     for b in range(8):
-        copies[b].wait()
-        total += jnp.dot(blocks[b][...], w[b].reshape(FEAT, FEAT), preferred_element_type=F32)
-    for copy in copies[8:]:
+        parts = []
+        for n in range(2):
+            copies[2 * b + n].wait()
+            parts.append(jnp.dot(blocks[b], w[n, b].reshape(FEAT, 256), preferred_element_type=F32))
+        total += jnp.concatenate(parts, axis=1)
+    for copy in copies[16:]:
         copy.wait()
     change = jnp.dot(low, oup[...].astype(F32), precision=lax.Precision.HIGHEST, preferred_element_type=F32)
     out_ref[...] = (total + 0.5 * change).astype(BF)
 
 
-def output(half, me, lengths, adapter, position, blocks, maps, weight, hidden, earlier=None):
+def output(half, me, lengths, adapter, position, blocks, maps, weight, rest, hidden, earlier=None):
     tok = pl.BlockSpec((HALF, FEAT), lambda i, *_: (half, 0))
     hbm = pl.BlockSpec(memory_space=pl.ANY)
     late = () if earlier is None else (earlier,)
@@ -486,18 +497,25 @@
         grid_spec=pltpu.PrefetchScalarGridSpec(
             num_scalar_prefetch=4,
             grid=(1,),
-            in_specs=[whole(HALF, FEAT)] * 8 + [whole(192, FEAT)] * 8 + [hbm, tok] + [hbm] * len(late),
+            in_specs=[whole(HALF, FEAT)] * 6
+            + [whole(HALF // 2, FEAT)] * 4
+            + [whole(192, FEAT)] * 8
+            + [hbm, hbm, tok]
+            + [hbm] * len(late),
             out_specs=tok,
             scratch_shapes=[
-                pltpu.VMEM((8, 2, 256, FEAT), BF),
+                pltpu.VMEM((2, 8, 2, 256, 256), BF),
                 pltpu.VMEM((64, FEAT), BF),
-                pltpu.SemaphoreType.DMA((12,)),
+                pltpu.SemaphoreType.DMA((24,)),
             ],
         ),
-        input_output_aliases={} if earlier is None else {22: 0},
+        input_output_aliases={} if earlier is None else {25: 0},
         compiler_params=vmem(24),
         name="output_late" if late else "output_early",
-    )(me, lengths, adapter, position, *blocks, *maps, in_hbm(weight), hidden, *late)
+    )(
+        me, lengths, adapter, position,
+        *map(in_hbm, blocks), *map(in_hbm, maps), in_hbm(weight), in_hbm(rest), in_hbm(hidden), *late,
+    )
 
 
 def on_device(
@@ -520,7 +538,7 @@
     cache_page_store,
 ):
     me = jnp.stack([lax.axis_index("row"), lax.axis_index("col")]).astype(jnp.int32)
-    wide, slots = pack(
+    wide, rest, slots = pack(
         me,
         query_key_value_weight,
         output_weight,
@@ -533,7 +551,8 @@
     slots = lax.all_to_all(slots, "row", 0, 0)
 
     picked, place = pick_pages(me, page_owner_row, page_store_index, cache_page_store)
-    picked, slots = lax.optimization_barrier((picked, slots))
+    picked, slots, rest = lax.optimization_barrier((picked, slots, rest))
+    rest = lax.all_gather(rest, "row", axis=0)
     pages = lax.all_to_all(picked.reshape(16, 4 * PAGE, HEAD), "row", 0, 0).reshape(32, 2, PAGE, HEAD)
 
     blocks = gather_col(hidden_input, 256)
@@ -575,15 +594,17 @@
     q, other = lax.optimization_barrier((q, other))
     late = second_half(prompt_length, cache_length, place, q, new_cache, pages)
     before, after, late = lax.optimization_barrier((before, after, late))
-    far = ring_far(before, after, "col", perm_z, quarter)
-    early = [early, other, before, swap(before), after, swap(after), far, swap(far)]
+    low_far, high_far = ring_far(before, after, "col", perm_z, quarter)
+    early = [early, other, before, swap(before), after, swap(after), low_far, high_far, swap(low_far), swap(high_far)]
 
     common = (me, prompt_length, prompt_adapter, adapter_position)
-    hidden_output = output(0, *common, early, maps, weight, hidden_input)
-    before, after, far = ring4(late, "col", perm_z, quarter)
-    far, hidden_output = lax.optimization_barrier((far, hidden_output))
-    late = [late, swap(late), before, swap(before), after, swap(after), far, swap(far)]
-    hidden_output = output(1, *common, late, maps, weight, hidden_input, hidden_output)
+    hidden_output = output(0, *common, early, maps, weight, rest, hidden_input)
+    before = lax.ppermute(late, "col", perm_z(1))
+    after = lax.ppermute(late, "col", perm_z(-1))
+    low_far, high_far = ring_far(before, after, "col", perm_z, quarter)
+    low_far, high_far, hidden_output = lax.optimization_barrier((low_far, high_far, hidden_output))
+    late = [late, swap(late), before, swap(before), after, swap(after), low_far, high_far, swap(low_far), swap(high_far)]
+    hidden_output = output(1, *common, late, maps, weight, rest, hidden_input, hidden_output)
     return hidden_output, new_cache
 
 

time: 184 us -> 180 us (0.978)
  waiting for transfers between devices: 48.8 us -> 42.9 us
  Pallas kernels: 50.7 us -> 55.7 us
  local copies, waits for them, and re-layouts: 9.9 us -> 7.98 us
    all_gather x1, waiting for transfers between devices: 22.5 us -> 11 us  [on_device(): weight = lax.all_gather(wide, 'row', axis=0)]
    pallas_call x2, Pallas kernels: 12.3 us -> 17.9 us  [output(): pl.pallas_call(lambda *refs: out_body(half, *refs), out_shape=jax.ShapeDt...]
    all_to_all x1, waiting for transfers between devices: 4.43 us -> 7.31 us  [on_device(): slots = lax.all_to_all(slots, 'row', 0, 0)]
    ppermute x8 -> x10, starting transfers between devices: 7.39 us -> 10.1 us  [the longest x4 6.33 us: ring_far(): lax.ppermute(after[half:], axis, perm(-1))]
    all_gather x0 -> x1, waiting for transfers between devices: none -> 2.44 us  [on_device(): rest = lax.all_gather(rest, 'row', axis=0)]
    ppermute x3 -> x2, starting transfers between devices: 5.05 us -> 3.44 us  [ring4(): after = lax.ppermute(block, axis, perm(-1))]
    unnamed x36 -> x87, local copies, waits for them, and re-layouts: 6.18 us -> 4.68 us
    ppermute x8 -> x10, waiting for transfers between devices: 16.4 us -> 15.7 us  [the longest x4 11.9 us: ring_far(): lax.ppermute(before[:half], axis, perm(1))]
  transfers between devices with their start and end apart: 35 -> 38, of which waited for: 10 -> 12; matrix products, arithmetic and copies ran while one was open for 7% -> 5% of each run, Pallas kernels for 14% -> 24%
where the time goes in v5:
time: 180 us
  Pallas kernels  55.7 us (31%)
  starting transfers between devices  48.9 us (27%)
  waiting for transfers between devices  42.9 us (24%)
  between operations  17.1 us (10%)
  local copies, waits for them, and re-layouts  7.98 us (4%)
  other arithmetic  6.92 us (4%)
    ppermute x18, starting transfers between devices, swap(): return lax.ppermute(block, 'col', SWAP)  18.1 us
    pallas_call x2, Pallas kernels, output(): pl.pallas_call(lambda *refs: out_body(half, *refs), out_shape=jax.ShapeDt...  17.9 us
    pallas_call x1, Pallas kernels, first_half(): pl.pallas_call(first_body, out_shape=(jax.ShapeDtypeStruct((HALF, FEAT),...  15.3 us
    ppermute x4, waiting for transfers between devices, ring_far(): lax.ppermute(before[:half], axis, perm(1))  11.9 us
    all_gather x1, waiting for transfers between devices, on_device(): weight = lax.all_gather(wide, 'row', axis=0)  11 us
    all_to_all x1, starting transfers between devices, on_device(): slots = lax.all_to_all(slots, 'row', 0, 0)  7.6 us
    all_to_all x1, waiting for transfers between devices, on_device(): slots = lax.all_to_all(slots, 'row', 0, 0)  7.31 us
    pallas_call x1, Pallas kernels, second_half(): pl.pallas_call(second_body, out_shape=jax.ShapeDtypeStruct((HALF, FEAT),...  6.71 us
  transfers between devices with their start and end apart: 38, of which 12 were waited for; matrix products, arithmetic and copies ran while one was open for 5% of the time, Pallas kernels for 24%

profile of v5, /device:TPU:1, one launch (start us, length us, event | category | flops | bytes accessed | tf_op | source)
XLA Modules:
  0.0 179.5 jit_solution(17402366375212970228)
XLA Ops:
  7.8 3.0 %pack.1 = (bf16[272,1024]{1,0:T(8,128)(2,1)}, bf16[288,256]{1,0:T(8,128)(2,1)}, bf16[16,48,512]{2,1,0:T(8,128)(2,1)}) custom-call(s32[2]{0:T(128)} %pad_add_fusion.me_ref.refs_0_, bf16[256,768]{1,0:T(8,128)(2,1)} %qkv_ref.1, bf16[256,512]{1,0:T(8,128)(2,1)} %wo_ref.1, bf16[1,16,640]{2,1,0:T(8,128)(2,1)} %up_ref.1, bf16[1,16,4096]{2,1,0:T(8,128)(2,1)} %oup_ref.1, ...), custom_call_target="tpu_custom_call" | custom-call | tf_op jit(solution)/shard_map/pack/pallas_call | solution.py:146
  10.8 7.6 %all-to-all-start = ((bf16[16,48,512]{2,1,0:T(8,128)(2,1)}), bf16[16,48,512]{2,1,0:T(8,128)(2,1)S(1)}, u32[]{:S(2)}, u32[]{:S(2)}) async-start(bf16[16,48,512]{2,1,0:T(8,128)(2,1)} %get-tuple-element.32), calls=%async_computation | async-start | bytes 1572864 | tf_op jit(solution)/shard_map/all_to_all | solution.py:551
  18.7 5.1 %pick_pages.1 = (bf16[16,2,2,128,128]{4,3,2,1,0:T(8,128)(2,1)}, s32[16]{0:T(128)S(1)}) custom-call(s32[2]{0:T(128)S(1)} %copy-done.15, s32[256,1]{1,0:T(8,128)S(1)} %copy.21.owner_ref, s32[256]{0:T(256)S(1)} %copy-done.18, bf16[8,2,128,128]{3,2,1,0:T(8,128)(2,1)S(1)} %copy-done.10), custom_call_target="tpu_custom_call" | custom-call | tf_op jit(solution)/shard_map/pick_pages/pallas_call | solution.py:115
  23.8 7.3 %all-to-all-done.slots_ref = bf16[16,48,512]{2,1,0:T(8,128)(2,1)S(1)} async-done(((bf16[16,48,512]{2,1,0:T(8,128)(2,1)}), bf16[16,48,512]{2,1,0:T(8,128)(2,1)S(1)}, u32[]{:S(2)}, u32[]{:S(2)}) %all-to-all-start) | async-done | bytes 786464 | tf_op jit(solution)/shard_map/all_to_all | solution.py:551
  32.0 4.7 %all-to-all-start.1 = ((bf16[16,512,128]{2,1,0:T(8,128)(2,1)}), bf16[16,512,128]{2,1,0:T(8,128)(2,1)}, u32[]{:S(2)}, u32[]{:S(2)}) async-start(bf16[16,512,128]{2,1,0:T(8,128)(2,1)} %bitcast.3), calls=%async_computation.1 | async-start | bytes 4194304 | tf_op jit(solution)/shard_map/all_to_all | solution.py:556
  36.8 1.9 %collective-permute-start.1 = (bf16[512,512]{1,0:T(8,128)(2,1)S(1)}, bf16[512,512]{1,0:T(8,128)(2,1)S(1)}, u32[]{:S(2)}, u32[]{:S(2)}) collective-permute-start(bf16[512,512]{1,0:T(8,128)(2,1)S(1)} %copy-done), channel_id=1, source_target_pairs={{0,2},{1,3},{2,4},{3,5},{4,6},{5,7},{6,0},{7,1},{8,10},{9,11},{10,... | collective-permute-start | bytes 1572872 | tf_op jit(solution)/shard_map/ppermute | solution.py:45
  38.6 2.9 %collective-permute-start.3 = (bf16[512,512]{1,0:T(8,128)(2,1)S(1)}, bf16[512,512]{1,0:T(8,128)(2,1)S(1)}, u32[]{:S(2)}, u32[]{:S(2)}) collective-permute-start(bf16[512,512]{1,0:T(8,128)(2,1)S(1)} %copy-done), channel_id=1, source_target_pairs={{0,6},{1,7},{2,0},{3,1},{4,2},{5,3},{6,4},{7,5},{8,14},{9,15},{10,... | collective-permute-start | bytes 1572872 | tf_op jit(solution)/shard_map/ppermute | solution.py:46
  41.5 5.5 %collective-permute-start = (bf16[512,512]{1,0:T(8,128)(2,1)S(1)}, bf16[512,512]{1,0:T(8,128)(2,1)S(1)}, u32[]{:S(2)}, u32[]{:S(2)}) collective-permute-start(bf16[512,512]{1,0:T(8,128)(2,1)S(1)} %copy-done), channel_id=1, source_target_pairs={{0,1},{1,0},{2,3},{3,2},{4,5},{5,4},{6,7},{7,6},{8,9},{9,8},{10,11... | collective-permute-start | bytes 1572872 | tf_op jit(solution)/shard_map/ppermute | solution.py:51
  55.6 2.8 %collective-permute-start.6 = (bf16[256,512]{1,0:T(8,128)(2,1)S(1)}, bf16[256,512]{1,0:T(8,128)(2,1)S(1)}, u32[]{:S(2)}, u32[]{:S(2)}) collective-permute-start(bf16[256,512]{1,0:T(8,128)(2,1)S(1)} %slice.65), channel_id=1, source_target_pairs={{0,6},{1,7},{2,0},{3,1},{4,2},{5,3},{6,4},{7,5},{8,14},{9,15},{10,... | collective-permute-start | bytes 786440 | tf_op jit(solution)/shard_map/ppermute | solution.py:41
  58.3 2.7 %select_slots.1.refs_8_.refs_14_ = bf16[192,512]{1,0:T(8,128)(2,1)} custom-call(s32[4]{0:T(128)} %refs_2_.3, s32[16]{0:T(128)} %refs_3_.3, bf16[16,48,512]{2,1,0:T(8,128)(2,1)} %copy-done.19), custom_call_target="tpu_custom_call" | custom-call | tf_op jit(solution)/shard_map/select_slots/pallas_call | solution.py:178
  61.6 2.7 %collective-permute-done.5 = bf16[256,512]{1,0:T(8,128)(2,1)S(1)} collective-permute-done((bf16[256,512]{1,0:T(8,128)(2,1)}, bf16[256,512]{1,0:T(8,128)(2,1)S(1)}, u32[]{:S(2)}, u32[]{:S(2)}) %collective-permute-start.5) | collective-permute-done | bytes 262176 | tf_op jit(solution)/shard_map/ppermute | solution.py:41
  64.9 3.6 %collective-permute-done.9.refs_10_.refs_16_ = bf16[192,512]{1,0:T(8,128)(2,1)S(1)} collective-permute-done((bf16[192,512]{1,0:T(8,128)(2,1)}, bf16[192,512]{1,0:T(8,128)(2,1)S(1)}, u32[]{:S(2)}, u32[]{:S(2)}) %collective-permute-start.9) | collective-permute-done | bytes 196640 | tf_op jit(solution)/shard_map/ppermute | solution.py:45
  71.9 3.7 %collective-permute-done.13 = bf16[96,512]{1,0:T(8,128)(2,1)S(1)} collective-permute-done((bf16[96,512]{1,0:T(8,128)(2,1)S(1)}, bf16[96,512]{1,0:T(8,128)(2,1)S(1)}, u32[]{:S(2)}, u32[]{:S(2)}) %collective-permute-start.13) | collective-permute-done | bytes 98336 | tf_op jit(solution)/shard_map/ppermute | solution.py:41
  75.6 3.8 %collective-permute-done.14 = bf16[96,512]{1,0:T(8,128)(2,1)S(1)} collective-permute-done((bf16[96,512]{1,0:T(8,128)(2,1)S(1)}, bf16[96,512]{1,0:T(8,128)(2,1)S(1)}, u32[]{:S(2)}, u32[]{:S(2)}) %collective-permute-start.14) | collective-permute-done | bytes 98336 | tf_op jit(solution)/shard_map/ppermute | solution.py:41
  82.8 2.1 %sine_select_fusion.rope_hbm = f32[512,128]{1,0:T(8,128)} fusion(f32[128]{0:T(128)S(1)} %pad_maximum_fusion, s32[512]{0:T(512)S(1)} %get-tuple-element.68, s32[512]{0:T(512)S(1)} %get-tuple-element.69, s32[512]{0:T(512)S(1)} %get-tuple-element.70, s32[512]{0:T(512)S(1)} %get-tuple-element.71, pred[512]{0:T(512)(128)(4,1)S(1)} %get-tuple-element.64, ...), kind=kLoop, calls=%fused_computation | loop fusion | flops 458752 | bytes 273024 | tf_op jit(solution)/shard_map/jit(_where)/select_n | solution.py:572
  86.1 5.0 %norm_low.1 = (bf16[4,512,1024]{2,1,0:T(8,128)(2,1)}, bf16[512,128]{1,0:T(8,128)(2,1)}) custom-call(s32[2]{0:T(128)S(1)} %copy-done.15, s32[1,4]{1,0:T(1,128)S(1)} %copy-done.13, bf16[512,512]{1,0:T(8,128)(2,1)S(1)} %copy-done, bf16[512,512]{1,0:T(8,128)(2,1)S(1)} %collective-permute-done.refs_1_, bf16[512,512]{1,0:T(8,128)(2,1)S(1)} %collective-permute-done.1.refs_2_, ...), custom_call_target="tpu_custom_call" | custom-call | tf_op jit(solution)/shard_map/norm_low/pallas_call | solution.py:212
  91.2 11.0 %all-gather.5.cloned.1.call-done = bf16[4352,1024]{1,0:T(8,128)(2,1)} async-done(((bf16[272,1024]{1,0:T(8,128)(2,1)}), bf16[4352,1024]{1,0:T(8,128)(2,1)}) %all-gather.5.cloned.1.call-update) | async-done | bytes 8912912 | tf_op jit(solution)/shard_map/all_gather | solution.py:550
  102.2 15.3 %first_half.1 = (bf16[256,512]{1,0:T(8,128)(2,1)S(1)}, bf16[4,256,128]{2,1,0:T(8,128)(2,1)S(1)}, bf16[2,512,128]{2,1,0:T(8,128)(2,1)}) custom-call(s32[1,4]{1,0:T(1,128)S(1)} %copy-done.13, s32[4]{0:T(128)S(1)} %copy-done.14, s32[16]{0:T(128)S(1)} %get-tuple-element.29.place_ref, s32[4]{0:T(128)S(1)} %copy-done.16, s32[16]{0:T(128)S(1)} %copy-done.17, ...), custom_call_target="tpu_custom_call" | custom-call | tf_op jit(solution)/shard_map/first_half/pallas_call | solution.py:389
  122.1 6.7 %second_half.1.refs_4_ = bf16[256,512]{1,0:T(8,128)(2,1)S(1)} custom-call(s32[1,4]{1,0:T(1,128)S(1)} %copy-done.13, s32[4]{0:T(128)S(1)} %copy-done.14, s32[16]{0:T(128)S(1)} %get-tuple-element.29.place_ref, bf16[4,256,128]{2,1,0:T(8,128)(2,1)S(1)} %get-tuple-element.46.q_ref, bf16[2,512,128]{2,1,0:T(8,128)(2,1)S(1)} %copy-done.12, ...), custom_call_target="tpu_custom_call" | custom-call | tf_op jit(solution)/shard_map/second_half/pallas_call | solution.py:434
  135.0 5.5 %collective-permute-done.28.refs_10_ = bf16[128,512]{1,0:T(8,128)(2,1)S(1)} collective-permute-done((bf16[128,512]{1,0:T(8,128)(2,1)S(1)}, bf16[128,512]{1,0:T(8,128)(2,1)S(1)}, u32[]{:S(2)}, u32[]{:S(2)}) %collective-permute-start.28) | collective-permute-done | bytes 131104 | tf_op jit(solution)/shard_map/ppermute | solution.py:41
  144.3 1.9 %collective-permute-start.25 = (bf16[128,512]{1,0:T(8,128)(2,1)}, bf16[128,512]{1,0:T(8,128)(2,1)S(1)}, u32[]{:S(2)}, u32[]{:S(2)}) collective-permute-start(bf16[128,512]{1,0:T(8,128)(2,1)} %slice.69), channel_id=1, source_target_pairs={{0,6},{1,7},{2,0},{3,1},{4,2},{5,3},{6,4},{7,5},{8,14},{9,15},{10,... | collective-permute-start | bytes 393224 | tf_op jit(solution)/shard_map/ppermute | solution.py:41
  147.7 2.4 %all-gather.7.cloned.1.call-done = bf16[4608,256]{1,0:T(8,128)(2,1)} async-done(((bf16[288,256]{1,0:T(8,128)(2,1)}), bf16[4608,256]{1,0:T(8,128)(2,1)}) %all-gather.7.cloned.1.call-update) | async-done | bytes 2359312 | tf_op jit(solution)/shard_map/all_gather | solution.py:555
  150.1 8.9 %output_early.1.refs_25_ = bf16[512,512]{1,0:T(8,128)(2,1)} custom-call(s32[2]{0:T(128)S(1)} %copy-done.15, s32[1,4]{1,0:T(1,128)S(1)} %copy-done.13, s32[4]{0:T(128)S(1)} %copy-done.16, s32[16]{0:T(128)S(1)} %copy-done.17, bf16[256,512]{1,0:T(8,128)(2,1)} %copy-done.11, bf16[256,512]{1,0:T(8,128)(2,1)} %copy-done.24, bf16[256,512]{1,0:T(8,128)(2,1)} %copy-done.22, ...), custom_call_target="tpu_custom_call" | custom-call | tf_op jit(solution)/shard_map/output_early/pallas_call | solution.py:494
  163.7 8.9 %output_late.1 = bf16[512,512]{1,0:T(8,128)(2,1)} custom-call(s32[2]{0:T(128)S(1)} %copy-done.15, s32[1,4]{1,0:T(1,128)S(1)} %copy-done.13, s32[4]{0:T(128)S(1)} %copy-done.16, s32[16]{0:T(128)S(1)} %copy-done.17, bf16[256,512]{1,0:T(8,128)(2,1)} %copy-done.9, bf16[256,512]{1,0:T(8,128)(2,1)} %copy-done.25, ...), custom_call_target="tpu_custom_call", output_to_operand_aliasing={{}: (25, {})} | custom-call | tf_op jit(solution)/shard_map/output_late/pallas_call | solution.py:494
  (172 shorter events, 37.4 us)
Async XLA Ops:
  7.2 95.0 %all-gather.5.cloned.1.call-start = ((), (), s32[]{:S(2)}) async-start(), calls=%async_computation.2 | async-start | bytes 9469952 | tf_op jit(solution)/shard_map/all_gather | solution.py:550
  10.8 20.3 %all-to-all-start = ((bf16[16,48,512]{2,1,0:T(8,128)(2,1)}), bf16[16,48,512]{2,1,0:T(8,128)(2,1)S(1)}, u32[]{:S(2)}, u32[]{:S(2)}) async-start(bf16[16,48,512]{2,1,0:T(8,128)(2,1)} %get-tuple-element.32), calls=%async_computation | async-start | bytes 1572864 | tf_op jit(solution)/shard_map/all_to_all | solution.py:551
  18.5 131.6 %all-gather.7.cloned.1.call-start = ((), (), s32[]{:S(2)}) async-start(), calls=%async_computation.3 | async-start | bytes 2506752 | tf_op jit(solution)/shard_map/all_gather | solution.py:555
  32.0 59.1 %all-to-all-start.1 = ((bf16[16,512,128]{2,1,0:T(8,128)(2,1)}), bf16[16,512,128]{2,1,0:T(8,128)(2,1)}, u32[]{:S(2)}, u32[]{:S(2)}) async-start(bf16[16,512,128]{2,1,0:T(8,128)(2,1)} %bitcast.3), calls=%async_computation.1 | async-start | bytes 4194304 | tf_op jit(solution)/shard_map/all_to_all | solution.py:556
  36.8 17.5 %collective-permute-start.1 = (bf16[512,512]{1,0:T(8,128)(2,1)S(1)}, bf16[512,512]{1,0:T(8,128)(2,1)S(1)}, u32[]{:S(2)}, u32[]{:S(2)}) collective-permute-start(bf16[512,512]{1,0:T(8,128)(2,1)S(1)} %copy-done), channel_id=1, source_target_pairs={{0,2},{1,3},{2,4},{3,5},{4,6},{5,7},{6,0},{7,1},{8,10},{9,11},{10,... | collective-permute-start | bytes 1572872 | tf_op jit(solution)/shard_map/ppermute | solution.py:45
  38.6 16.9 %collective-permute-start.3 = (bf16[512,512]{1,0:T(8,128)(2,1)S(1)}, bf16[512,512]{1,0:T(8,128)(2,1)S(1)}, u32[]{:S(2)}, u32[]{:S(2)}) collective-permute-start(bf16[512,512]{1,0:T(8,128)(2,1)S(1)} %copy-done), channel_id=1, source_target_pairs={{0,6},{1,7},{2,0},{3,1},{4,2},{5,3},{6,4},{7,5},{8,14},{9,15},{10,... | collective-permute-start | bytes 1572872 | tf_op jit(solution)/shard_map/ppermute | solution.py:46
  41.5 39.4 %collective-permute-start = (bf16[512,512]{1,0:T(8,128)(2,1)S(1)}, bf16[512,512]{1,0:T(8,128)(2,1)S(1)}, u32[]{:S(2)}, u32[]{:S(2)}) collective-permute-start(bf16[512,512]{1,0:T(8,128)(2,1)S(1)} %copy-done), channel_id=1, source_target_pairs={{0,1},{1,0},{2,3},{3,2},{4,5},{5,4},{6,7},{7,6},{8,9},{9,8},{10,11... | collective-permute-start | bytes 1572872 | tf_op jit(solution)/shard_map/ppermute | solution.py:51
  55.0 9.4 %collective-permute-start.5 = (bf16[256,512]{1,0:T(8,128)(2,1)}, bf16[256,512]{1,0:T(8,128)(2,1)S(1)}, u32[]{:S(2)}, u32[]{:S(2)}) collective-permute-start(bf16[256,512]{1,0:T(8,128)(2,1)} %slice.64), channel_id=1, source_target_pairs={{0,2},{1,3},{2,4},{3,5},{4,6},{5,7},{6,0},{7,1},{8,10},{9,11},{10,... | collective-permute-start | bytes 786440 | tf_op jit(solution)/shard_map/ppermute | solution.py:41
  55.6 14.2 %collective-permute-start.6 = (bf16[256,512]{1,0:T(8,128)(2,1)S(1)}, bf16[256,512]{1,0:T(8,128)(2,1)S(1)}, u32[]{:S(2)}, u32[]{:S(2)}) collective-permute-start(bf16[256,512]{1,0:T(8,128)(2,1)S(1)} %slice.65), channel_id=1, source_target_pairs={{0,6},{1,7},{2,0},{3,1},{4,2},{5,3},{6,4},{7,5},{8,14},{9,15},{10,... | collective-permute-start | bytes 786440 | tf_op jit(solution)/shard_map/ppermute | solution.py:41
  61.0 21.5 %collective-permute-start.2 = (bf16[512,512]{1,0:T(8,128)(2,1)S(1)}, bf16[512,512]{1,0:T(8,128)(2,1)S(1)}, u32[]{:S(2)}, u32[]{:S(2)}) collective-permute-start(bf16[512,512]{1,0:T(8,128)(2,1)S(1)} %collective-permute-done.1.refs_2_), channel_id=1, source_target_pairs={{0,1},{1,0},{2,3},{3,2},{4,5},{5,4},{6,7},{7,6},{8,9},{9,8},{10,11... | collective-permute-start | bytes 1572872 | tf_op jit(solution)/shard_map/ppermute | solution.py:51
  68.4 16.5 %collective-permute-start.4 = (bf16[512,512]{1,0:T(8,128)(2,1)S(1)}, bf16[512,512]{1,0:T(8,128)(2,1)S(1)}, u32[]{:S(2)}, u32[]{:S(2)}) collective-permute-start(bf16[512,512]{1,0:T(8,128)(2,1)S(1)} %collective-permute-done.3.refs_4_), channel_id=1, source_target_pairs={{0,1},{1,0},{2,3},{3,2},{4,5},{5,4},{6,7},{7,6},{8,9},{9,8},{10,11... | collective-permute-start | bytes 1572872 | tf_op jit(solution)/shard_map/ppermute | solution.py:51
  70.3 14.6 %collective-permute-start.7 = (bf16[512,512]{1,0:T(8,128)(2,1)S(1)}, bf16[512,512]{1,0:T(8,128)(2,1)S(1)}, u32[]{:S(2)}, u32[]{:S(2)}) collective-permute-start(bf16[512,512]{1,0:T(8,128)(2,1)S(1)} %constant_dynamic-update-slice_fusion.refs_6_), channel_id=1, source_target_pairs={{0,1},{1,0},{2,3},{3,2},{4,5},{5,4},{6,7},{7,6},{8,9},{9,8},{10,11... | collective-permute-start | bytes 1572872 | tf_op jit(solution)/shard_map/ppermute | solution.py:51
  118.1 10.7 %collective-permute-start.16 = (bf16[256,512]{1,0:T(8,128)(2,1)S(1)}, bf16[256,512]{1,0:T(8,128)(2,1)S(1)}, u32[]{:S(2)}, u32[]{:S(2)}) collective-permute-start(bf16[256,512]{1,0:T(8,128)(2,1)S(1)} %get-tuple-element.44.refs_4_), channel_id=1, source_target_pairs={{0,2},{1,3},{2,4},{3,5},{4,6},{5,7},{6,0},{7,1},{8,10},{9,11},{10,... | collective-permute-start | bytes 786440 | tf_op jit(solution)/shard_map/ppermute | solution.py:592
  119.4 9.5 %collective-permute-start.17 = (bf16[256,512]{1,0:T(8,128)(2,1)S(1)}, bf16[256,512]{1,0:T(8,128)(2,1)S(1)}, u32[]{:S(2)}, u32[]{:S(2)}) collective-permute-start(bf16[256,512]{1,0:T(8,128)(2,1)S(1)} %get-tuple-element.44.refs_4_), channel_id=1, source_target_pairs={{0,6},{1,7},{2,0},{3,1},{4,2},{5,3},{6,4},{7,5},{8,14},{9,15},{10,... | collective-permute-start | bytes 786440 | tf_op jit(solution)/shard_map/ppermute | solution.py:593
  128.9 12.9 %collective-permute-start.20 = (bf16[256,512]{1,0:T(8,128)(2,1)S(1)}, bf16[256,512]{1,0:T(8,128)(2,1)S(1)}, u32[]{:S(2)}, u32[]{:S(2)}) collective-permute-start(bf16[256,512]{1,0:T(8,128)(2,1)S(1)} %second_half.1.refs_4_), channel_id=1, source_target_pairs={{0,2},{1,3},{2,4},{3,5},{4,6},{5,7},{6,0},{7,1},{8,10},{9,11},{10,... | collective-permute-start | bytes 786440 | tf_op jit(solution)/shard_map/ppermute | solution.py:602
  129.0 11.5 %collective-permute-start.28 = (bf16[128,512]{1,0:T(8,128)(2,1)S(1)}, bf16[128,512]{1,0:T(8,128)(2,1)S(1)}, u32[]{:S(2)}, u32[]{:S(2)}) collective-permute-start(bf16[128,512]{1,0:T(8,128)(2,1)S(1)} %slice.62), channel_id=1, source_target_pairs={{0,2},{1,3},{2,4},{3,5},{4,6},{5,7},{6,0},{7,1},{8,10},{9,11},{10,... | collective-permute-start | bytes 393224 | tf_op jit(solution)/shard_map/ppermute | solution.py:41
  130.1 12.8 %collective-permute-start.22 = (bf16[256,512]{1,0:T(8,128)(2,1)S(1)}, bf16[256,512]{1,0:T(8,128)(2,1)S(1)}, u32[]{:S(2)}, u32[]{:S(2)}) collective-permute-start(bf16[256,512]{1,0:T(8,128)(2,1)S(1)} %second_half.1.refs_4_), channel_id=1, source_target_pairs={{0,6},{1,7},{2,0},{3,1},{4,2},{5,3},{6,4},{7,5},{8,14},{9,15},{10,... | collective-permute-start | bytes 786440 | tf_op jit(solution)/shard_map/ppermute | solution.py:603
  131.8 9.9 %collective-permute-start.29 = (bf16[128,512]{1,0:T(8,128)(2,1)S(1)}, bf16[128,512]{1,0:T(8,128)(2,1)S(1)}, u32[]{:S(2)}, u32[]{:S(2)}) collective-permute-start(bf16[128,512]{1,0:T(8,128)(2,1)S(1)} %slice.63), channel_id=1, source_target_pairs={{0,6},{1,7},{2,0},{3,1},{4,2},{5,3},{6,4},{7,5},{8,14},{9,15},{10,... | collective-permute-start | bytes 393224 | tf_op jit(solution)/shard_map/ppermute | solution.py:41
  133.5 13.5 %collective-permute-start.26 = (bf16[256,512]{1,0:T(8,128)(2,1)S(1)}, bf16[256,512]{1,0:T(8,128)(2,1)S(1)}, u32[]{:S(2)}, u32[]{:S(2)}) collective-permute-start(bf16[256,512]{1,0:T(8,128)(2,1)S(1)} %collective-permute-done.16.refs_6_), channel_id=1, source_target_pairs={{0,1},{1,0},{2,3},{3,2},{4,5},{5,4},{6,7},{7,6},{8,9},{9,8},{10,11... | collective-permute-start | bytes 786440 | tf_op jit(solution)/shard_map/ppermute | solution.py:51
  142.9 16.3 %collective-permute-start.24 = (bf16[128,512]{1,0:T(8,128)(2,1)}, bf16[128,512]{1,0:T(8,128)(2,1)S(1)}, u32[]{:S(2)}, u32[]{:S(2)}) collective-permute-start(bf16[128,512]{1,0:T(8,128)(2,1)} %slice.68), channel_id=1, source_target_pairs={{0,2},{1,3},{2,4},{3,5},{4,6},{5,7},{6,0},{7,1},{8,10},{9,11},{10,... | collective-permute-start | bytes 393224 | tf_op jit(solution)/shard_map/ppermute | solution.py:41
  144.3 14.8 %collective-permute-start.25 = (bf16[128,512]{1,0:T(8,128)(2,1)}, bf16[128,512]{1,0:T(8,128)(2,1)S(1)}, u32[]{:S(2)}, u32[]{:S(2)}) collective-permute-start(bf16[128,512]{1,0:T(8,128)(2,1)} %slice.69), channel_id=1, source_target_pairs={{0,6},{1,7},{2,0},{3,1},{4,2},{5,3},{6,4},{7,5},{8,14},{9,15},{10,... | collective-permute-start | bytes 393224 | tf_op jit(solution)/shard_map/ppermute | solution.py:41
  146.3 14.8 %collective-permute-start.19 = (bf16[256,512]{1,0:T(8,128)(2,1)S(1)}, bf16[256,512]{1,0:T(8,128)(2,1)S(1)}, u32[]{:S(2)}, u32[]{:S(2)}) collective-permute-start(bf16[256,512]{1,0:T(8,128)(2,1)S(1)} %second_half.1.refs_4_), channel_id=1, source_target_pairs={{0,1},{1,0},{2,3},{3,2},{4,5},{5,4},{6,7},{7,6},{8,9},{9,8},{10,11... | collective-permute-start | bytes 786440 | tf_op jit(solution)/shard_map/ppermute | solution.py:51
  147.0 15.3 %collective-permute-start.21 = (bf16[256,512]{1,0:T(8,128)(2,1)S(1)}, bf16[256,512]{1,0:T(8,128)(2,1)S(1)}, u32[]{:S(2)}, u32[]{:S(2)}) collective-permute-start(bf16[256,512]{1,0:T(8,128)(2,1)S(1)} %collective-permute-done.20.refs_6_), channel_id=1, source_target_pairs={{0,1},{1,0},{2,3},{3,2},{4,5},{5,4},{6,7},{7,6},{8,9},{9,8},{10,11... | collective-permute-start | bytes 786440 | tf_op jit(solution)/shard_map/ppermute | solution.py:51
  147.6 14.8 %collective-permute-start.23 = (bf16[256,512]{1,0:T(8,128)(2,1)S(1)}, bf16[256,512]{1,0:T(8,128)(2,1)S(1)}, u32[]{:S(2)}, u32[]{:S(2)}) collective-permute-start(bf16[256,512]{1,0:T(8,128)(2,1)S(1)} %collective-permute-done.22.refs_8_), channel_id=1, source_target_pairs={{0,1},{1,0},{2,3},{3,2},{4,5},{5,4},{6,7},{7,6},{8,9},{9,8},{10,11... | collective-permute-start | bytes 786440 | tf_op jit(solution)/shard_map/ppermute | solution.py:51
  (56 other events, 575.7 us)
Sparse Core Ops, SparseCore 0:
  11.0 91.1 all-gather.4
  104.4 45.6 all-gather.6

commit v6 on v5

--- a/solution.py
+++ b/solution.py
@@ -130,13 +130,11 @@
 
 
 def pack_body(me_ref, qkv_ref, wo_ref, up_ref, oup_ref, down_ref, odown_ref, wide_ref, rest_ref, slots_ref):
-    wide_ref[:256, :768] = qkv_ref[...]
-    wide_ref[:256, 768:] = wo_ref[:, :256]
+    wide_ref[:256, :] = qkv_ref[...]
     wide_ref[256:, :640] = up_ref[0]
-    wide_ref[256:, 640:] = jnp.zeros((16, 384), BF)
-    rest_ref[:256, :] = wo_ref[:, 256:]
-    rest_ref[256:272, :] = oup_ref[0, :, :256]
-    rest_ref[272:, :] = oup_ref[0, :, 256:]
+    wide_ref[256:, 640:] = jnp.zeros((16, 128), BF)
+    rest_ref[:256, :] = wo_ref[...]
+    rest_ref[256:, :] = oup_ref[0]
     for r in range(16):
         slots_ref[r, :32, :] = down_ref[0]
         slots_ref[r, 32:, :] = odown_ref[0]
@@ -146,8 +144,8 @@
     return pl.pallas_call(
         pack_body,
         out_shape=(
-            jax.ShapeDtypeStruct((272, 1024), BF),
-            jax.ShapeDtypeStruct((288, 256), BF),
+            jax.ShapeDtypeStruct((272, 768), BF),
+            jax.ShapeDtypeStruct((272, FEAT), BF),
             jax.ShapeDtypeStruct((16, 48, FEAT), BF),
         ),
         grid_spec=pltpu.PrefetchScalarGridSpec(
@@ -161,31 +159,35 @@
                 pl.BlockSpec((1, 32, FEAT), lambda i, me: (0, 0, me[1])),
                 whole(1, 16, FEAT),
             ],
-            out_specs=(whole(272, 1024), whole(288, 256), whole(16, 48, FEAT)),
+            out_specs=(whole(272, 768), whole(272, FEAT), whole(16, 48, FEAT)),
         ),
         name="pack",
     )(me, qkv, wo, up, oup, down, odown)
 
 
-def select_body(adapter_ref, position_ref, slots_ref, maps_ref):
+DOWN, ODOWN, BLOCK_ROWS = TOK, TOK + 128, TOK + 192
+
+
+def select_body(adapter_ref, position_ref, slots_ref, hidden_ref, out_ref):
+    out_ref[:TOK, :] = hidden_ref[...]
     for p in range(PROMPTS):
         slot = position_ref[adapter_ref[p]]
-        maps_ref[p * 32 : p * 32 + 32, :] = slots_ref[slot, :32, :]
-        maps_ref[128 + p * 16 : 128 + p * 16 + 16, :] = slots_ref[slot, 32:, :]
-
-
-def select_slots(adapter, position, slots):
+        out_ref[DOWN + p * 32 : DOWN + p * 32 + 32, :] = slots_ref[slot, :32, :]
+        out_ref[ODOWN + p * 16 : ODOWN + p * 16 + 16, :] = slots_ref[slot, 32:, :]
+
+
+def select_slots(adapter, position, slots, hidden):
     return pl.pallas_call(
         select_body,
-        out_shape=jax.ShapeDtypeStruct((192, FEAT), BF),
+        out_shape=jax.ShapeDtypeStruct((BLOCK_ROWS, FEAT), BF),
         grid_spec=pltpu.PrefetchScalarGridSpec(
             num_scalar_prefetch=2,
             grid=(1,),
-            in_specs=[whole(16, 48, FEAT)],
-            out_specs=whole(192, FEAT),
+            in_specs=[whole(16, 48, FEAT), whole(TOK, FEAT)],
+            out_specs=whole(BLOCK_ROWS, FEAT),
         ),
         name="select_slots",
-    )(adapter, position, slots)
+    )(adapter, position, slots, hidden)
 
 
 def norm_body(me_ref, length_ref, *refs):
@@ -200,14 +202,14 @@
         gain = gain_ref[order[b]].astype(F32)
         normed = (values[b] * scale * gain).astype(BF)
         normed_ref[order[b] // 2, :, pl.ds(pl.multiple_of(order[b] % 2 * FEAT, FEAT), FEAT)] = normed
-        low += lax.dot_general(normed, maps[b][:128, :], (((1,), (1,)), ((), ())), preferred_element_type=F32)
+        low += lax.dot_general(normed, maps[b][...], (((1,), (1,)), ((), ())), preferred_element_type=F32)
     token = pl.program_id(0) * low.shape[0] + lax.broadcasted_iota(jnp.int32, low.shape, 0)
     prompt = per_token(prompt_rows(length_ref), range(PROMPTS), token)
     mine = lax.broadcasted_iota(jnp.int32, low.shape, 1) // 32 == prompt
     low_ref[...] = jnp.where(mine, low, 0.0).astype(BF)
 
 
-def norm_low(me, lengths, blocks, maps, gain):
+def norm_low(me, lengths, blocks, gain):
     rows = 128
     return pl.pallas_call(
         norm_body,
@@ -216,7 +218,7 @@
             num_scalar_prefetch=2,
             grid=(TOK // rows,),
             in_specs=[pl.BlockSpec((rows, FEAT), lambda i, *_: (i, 0))] * 8
-            + [whole(192, FEAT)] * 8
+            + [pl.BlockSpec((128, FEAT), lambda i, *_: (DOWN // 128, 0))] * 8
             + [whole(8, 1, FEAT)],
             out_specs=(
                 pl.BlockSpec((4, rows, 2 * FEAT), lambda i, *_: (0, i, 0)),
@@ -225,11 +227,10 @@
         ),
         compiler_params=vmem(20),
         name="norm_low",
-    )(me, lengths, *blocks, *maps, gain)
+    )(me, lengths, *blocks, *blocks, gain)
 
 
 BLOCK = 64
-HALF = TOK // 2
 SCALE2 = math.log2(math.e) / math.sqrt(HEAD)
 
 
@@ -242,7 +243,7 @@
     return copies
 
 
-def attend_half(half, length_ref, cache_ref, q_ref, kv_ref, cached_ref, out_ref, m_ref, l_ref, acc_ref):
+def attend(length_ref, cache_ref, q_ref, kv_ref, cached_ref, out_ref, m_ref, l_ref, acc_ref):
     rows, span = GROUP * BLOCK, 256 + BLOCK
     prompts = prompt_rows(length_ref)
     begins = [start for start, _ in prompts]
@@ -263,10 +264,9 @@
         )
 
     def block(t, carry):
-        local = pl.multiple_of(t * BLOCK, BLOCK)
-        start = local + half * HALF
+        start = pl.multiple_of(t * BLOCK, BLOCK)
         lo = pl.multiple_of(jnp.maximum(start - 256, 0), BLOCK)
-        cut = pl.ds(local, BLOCK)
+        cut = pl.ds(start, BLOCK)
         q = q_ref[:, cut, :].reshape(rows, HEAD)
         token = start + (lax.broadcasted_iota(jnp.int32, (rows, 1), 0) & (BLOCK - 1))
         begin = per_token(prompts, begins, token)
@@ -304,7 +304,7 @@
             out_ref[cut, h * HEAD : (h + 1) * HEAD] = done[h * BLOCK : (h + 1) * BLOCK, :]
         return carry
 
-    lax.fori_loop(0, HALF // BLOCK, block, 0)
+    lax.fori_loop(0, TOK // BLOCK, block, 0)
 
 
 ATTEND_SCRATCH = [
@@ -315,11 +315,11 @@
 ]
 
 
-def first_body(
+def attention_body(
     length_ref, cache_ref, place_ref, adapter_ref, position_ref,
     normed_ref, w_ref, low_hbm, rope_hbm, gains_hbm, pages_ref,
-    out_ref, q_late_ref, kv_ref,
-    m_ref, l_ref, sum_ref, cached_ref, x, w, up, acc, q_early, low_ref, rope_ref, gains_ref, sems,
+    out_ref, kv_ref,
+    m_ref, l_ref, sum_ref, cached_ref, x, w, up, acc, q_ref, low_ref, rope_ref, gains_ref, sems,
 ):
     def chunk(k):
         rows = w_ref.at[pl.ds(4 * k, 4), pl.ds(0, 256), pl.ds(0, 768)]
@@ -374,37 +374,34 @@
 
     for h in range(GROUP):
         cut = slice(h * HEAD, (h + 1) * HEAD)
-        q = finish(acc[:, cut] + change[:, cut], gains_ref[0:1, :])
-        q_early[h] = q[:HALF]
-        q_late_ref[h] = q[HALF:]
+        q_ref[h] = finish(acc[:, cut] + change[:, cut], gains_ref[0:1, :])
     kv_ref[0] = finish(acc[:, 512:640], gains_ref[1:2, :])
     kv_ref[1] = (acc[:, 640:768] + change[:, 512:640]).astype(BF)
     for copy in pages:
         copy.wait()
-    attend_half(0, length_ref, cache_ref, q_early, kv_ref, cached_ref, out_ref, m_ref, l_ref, sum_ref)
-
-
-def first_half(lengths, cached, place, adapter, position, normed, weight, low, rope, gains, pages):
+    attend(length_ref, cache_ref, q_ref, kv_ref, cached_ref, out_ref, m_ref, l_ref, sum_ref)
+
+
+def attention(lengths, cached, place, adapter, position, normed, weight, low, rope, gains, pages):
     hbm = pl.BlockSpec(memory_space=pl.ANY)
     return pl.pallas_call(
-        first_body,
+        attention_body,
         out_shape=(
-            jax.ShapeDtypeStruct((HALF, FEAT), BF),
-            jax.ShapeDtypeStruct((GROUP, HALF, HEAD), BF),
+            jax.ShapeDtypeStruct((TOK, FEAT), BF),
             jax.ShapeDtypeStruct((2, TOK, HEAD), BF),
         ),
         grid_spec=pltpu.PrefetchScalarGridSpec(
             num_scalar_prefetch=5,
             grid=(1,),
             in_specs=[hbm] * 6,
-            out_specs=(whole(HALF, FEAT), whole(GROUP, HALF, HEAD), whole(2, TOK, HEAD)),
+            out_specs=(whole(TOK, FEAT), whole(2, TOK, HEAD)),
             scratch_shapes=ATTEND_SCRATCH
             + [
                 pltpu.VMEM((4, TOK, 1024), BF),
                 pltpu.VMEM((4, 4, 256, 768), BF),
                 pltpu.VMEM((128, 640), BF),
                 pltpu.VMEM((TOK, 768), F32),
-                pltpu.VMEM((GROUP, HALF, HEAD), BF),
+                pltpu.VMEM((GROUP, TOK, HEAD), BF),
                 pltpu.VMEM((TOK, 128), BF),
                 pltpu.VMEM((TOK, HEAD), F32),
                 pltpu.VMEM((2, HEAD), F32),
@@ -412,109 +409,78 @@
             ],
         ),
         compiler_params=vmem(32),
-        name="first_half",
+        name="attention",
     )(
         lengths, cached, place, adapter, position,
         in_hbm(normed), in_hbm(weight), in_hbm(low), in_hbm(rope), in_hbm(gains), in_hbm(pages),
     )
 
 
-def second_body(
-    length_ref, cache_ref, place_ref, q_ref, kv_ref, pages_ref, out_ref, m_ref, l_ref, sum_ref, cached_ref, sems
+def out_body(
+    me_ref, length_ref, adapter_ref, position_ref, *refs
 ):
-    copies = page_copies(place_ref, pages_ref, cached_ref, sems, 0)
-    for copy in copies:
-        copy.start()
-    for copy in copies:
-        copy.wait()
-    attend_half(1, length_ref, cache_ref, q_ref, kv_ref, cached_ref, out_ref, m_ref, l_ref, sum_ref)
-
-
-def second_half(lengths, cached, place, q, kv, pages):
-    return pl.pallas_call(
-        second_body,
-        out_shape=jax.ShapeDtypeStruct((HALF, FEAT), BF),
-        grid_spec=pltpu.PrefetchScalarGridSpec(
-            num_scalar_prefetch=3,
-            grid=(1,),
-            in_specs=[whole(GROUP, HALF, HEAD), whole(2, TOK, HEAD), pl.BlockSpec(memory_space=pl.ANY)],
-            out_specs=whole(HALF, FEAT),
-            scratch_shapes=ATTEND_SCRATCH + [pltpu.SemaphoreType.DMA((32,))],
-        ),
-        compiler_params=vmem(12),
-        name="second_half",
-    )(lengths, cached, place, q, kv, in_hbm(pages))
-
-
-def out_body(half, me_ref, length_ref, adapter_ref, position_ref, *refs):
-    blocks = [ref[...] for ref in refs[:6]] + [jnp.concatenate([refs[i][...], refs[i + 1][...]], axis=0) for i in (6, 8)]
-    maps = refs[10:18]
-    weight_ref, rest_ref, hidden_ref = refs[18:21]
-    out_ref, w, oup, sems = refs[-4:]
+    blocks, sources = refs[:8], refs[8:16]
+    weight_ref, hidden_hbm, out_ref, x, w, od, oup, hidden, acc, sems = refs[16:]
     order = col_order(me_ref[1])
     copies = []
     for b in range(8):
-        for n, ref in enumerate((weight_ref.at[:, :, pl.ds(768, 256)], rest_ref)):
-            rows = ref.at[pl.ds(2 * order[b], 2), pl.ds(0, 256)]
-            copies.append(pltpu.make_async_copy(rows, w.at[n, b], sems.at[2 * b + n]))
+        side = pl.ds(b % 2 * FEAT, FEAT)
+        rows = weight_ref.at[pl.ds(2 * order[b], 2), pl.ds(0, 256)]
+        copies.append(pltpu.make_async_copy(rows, w.at[b // 2, pl.ds(b % 2 * 2, 2)], sems.at[b]))
+        copies.append(pltpu.make_async_copy(blocks[b], x.at[b // 2, :, side], sems.at[8 + b]))
+        copies.append(pltpu.make_async_copy(sources[b].at[pl.ds(ODOWN, 64)], od.at[b // 2, :, side], sems.at[16 + b]))
+    last = [pltpu.make_async_copy(hidden_hbm, hidden, sems.at[24])]
     for p in range(PROMPTS):
         slot = position_ref[adapter_ref[p]]
-        for n in range(2):
-            rows = rest_ref.at[slot, pl.ds(256 + 16 * n, 16)]
-            into = oup.at[pl.ds(p * 16, 16), pl.ds(256 * n, 256)]
-            copies.append(pltpu.make_async_copy(rows, into, sems.at[16 + 2 * p + n]))
-    for copy in copies:
+        rows = weight_ref.at[slot, pl.ds(256, 16)]
+        last.append(pltpu.make_async_copy(rows, oup.at[pl.ds(p * 16, 16)], sems.at[25 + p]))
+    for copy in copies + last:
         copy.start()
-    low = jnp.zeros((HALF, 64), F32)
-    for b in range(8):
-        low += lax.dot_general(
-            blocks[b], maps[b][128:192, :], (((1,), (1,)), ((), ())), preferred_element_type=F32
-        )
-    token = half * HALF + lax.broadcasted_iota(jnp.int32, low.shape, 0)
+    low = jnp.zeros((TOK, 64), F32)
+    for i in range(4):
+        for copy in copies[6 * i : 6 * i + 6]:
+            copy.wait()
+        part = jnp.dot(x[i], w[i].reshape(2 * FEAT, FEAT), preferred_element_type=F32)
+        if i == 0:
+            acc[...] = part
+        else:
+            acc[...] += part
+        low += lax.dot_general(x[i], od[i], (((1,), (1,)), ((), ())), preferred_element_type=F32)
+    token = lax.broadcasted_iota(jnp.int32, low.shape, 0)
     prompt = per_token(prompt_rows(length_ref), range(PROMPTS), token)
     mine = lax.broadcasted_iota(jnp.int32, low.shape, 1) // 16 == prompt
     low = jnp.where(mine, low, 0.0)
-    total = hidden_ref[...].astype(F32)
-    for b in range(8):
-        parts = []
-        for n in range(2):
-            copies[2 * b + n].wait()
-            parts.append(jnp.dot(blocks[b], w[n, b].reshape(FEAT, 256), preferred_element_type=F32))
-        total += jnp.concatenate(parts, axis=1)
-    for copy in copies[16:]:
+    for copy in last:
         copy.wait()
     change = jnp.dot(low, oup[...].astype(F32), precision=lax.Precision.HIGHEST, preferred_element_type=F32)
-    out_ref[...] = (total + 0.5 * change).astype(BF)
-
-
-def output(half, me, lengths, adapter, position, blocks, maps, weight, rest, hidden, earlier=None):
-    tok = pl.BlockSpec((HALF, FEAT), lambda i, *_: (half, 0))
+    out_ref[...] = (hidden[...].astype(F32) + acc[...] + 0.5 * change).astype(BF)
+
+
+def output(me, lengths, adapter, position, blocks, sources, weight, hidden):
     hbm = pl.BlockSpec(memory_space=pl.ANY)
-    late = () if earlier is None else (earlier,)
     return pl.pallas_call(
-        lambda *refs: out_body(half, *refs),
+        out_body,
         out_shape=jax.ShapeDtypeStruct((TOK, FEAT), BF),
         grid_spec=pltpu.PrefetchScalarGridSpec(
             num_scalar_prefetch=4,
             grid=(1,),
-            in_specs=[whole(HALF, FEAT)] * 6
-            + [whole(HALF // 2, FEAT)] * 4
-            + [whole(192, FEAT)] * 8
-            + [hbm, hbm, tok]
-            + [hbm] * len(late),
-            out_specs=tok,
+            in_specs=[hbm] * 18,
+            out_specs=whole(TOK, FEAT),
             scratch_shapes=[
-                pltpu.VMEM((2, 8, 2, 256, 256), BF),
+                pltpu.VMEM((4, TOK, 2 * FEAT), BF),
+                pltpu.VMEM((4, 4, 256, FEAT), BF),
+                pltpu.VMEM((4, 64, 2 * FEAT), BF),
                 pltpu.VMEM((64, FEAT), BF),
-                pltpu.SemaphoreType.DMA((24,)),
+                pltpu.VMEM((TOK, FEAT), BF),
+                pltpu.VMEM((TOK, FEAT), F32),
+                pltpu.SemaphoreType.DMA((29,)),
             ],
         ),
-        input_output_aliases={} if earlier is None else {25: 0},
         compiler_params=vmem(24),
-        name="output_late" if late else "output_early",
+        name="output",
     )(
         me, lengths, adapter, position,
-        *map(in_hbm, blocks), *map(in_hbm, maps), in_hbm(weight), in_hbm(rest), in_hbm(hidden), *late,
+        *map(in_hbm, blocks), *map(in_hbm, sources), in_hbm(weight), in_hbm(hidden),
     )
 
 
@@ -555,10 +521,7 @@
     rest = lax.all_gather(rest, "row", axis=0)
     pages = lax.all_to_all(picked.reshape(16, 4 * PAGE, HEAD), "row", 0, 0).reshape(32, 2, PAGE, HEAD)
 
-    blocks = gather_col(hidden_input, 256)
-
-    maps = select_slots(prompt_adapter, adapter_position, slots)
-    maps = gather_col(maps, 96)
+    blocks = gather_col(select_slots(prompt_adapter, adapter_position, slots, hidden_input), BLOCK_ROWS // 2)
 
     token = lax.broadcasted_iota(jnp.int32, (TOK, HEAD), 0)
     position, start = token, jnp.int32(0)
@@ -571,10 +534,10 @@
     front = lax.broadcasted_iota(jnp.int32, (TOK, HEAD), 1) < HEAD // 2
     rope = jnp.where(front, jnp.cos(angles), jnp.sin(angles))
 
-    normed, low = norm_low(me, prompt_length, blocks, maps, input_norm_gain.reshape(8, 1, FEAT))
+    normed, low = norm_low(me, prompt_length, blocks, input_norm_gain.reshape(8, 1, FEAT))
     gains = jnp.stack([query_norm_gain, key_norm_gain]).astype(F32)
     weight, normed, low, pages, rope, gains = lax.optimization_barrier((weight, normed, low, pages, rope, gains))
-    early, q, new_cache = first_half(
+    attended, new_cache = attention(
         prompt_length,
         cache_length,
         place,
@@ -587,24 +550,10 @@
         gains,
         pages,
     )
-    quarter = HALF // 2
-    other = swap(early)
-    before = lax.ppermute(early, "col", perm_z(1))
-    after = lax.ppermute(early, "col", perm_z(-1))
-    q, other = lax.optimization_barrier((q, other))
-    late = second_half(prompt_length, cache_length, place, q, new_cache, pages)
-    before, after, late = lax.optimization_barrier((before, after, late))
-    low_far, high_far = ring_far(before, after, "col", perm_z, quarter)
-    early = [early, other, before, swap(before), after, swap(after), low_far, high_far, swap(low_far), swap(high_far)]
-
-    common = (me, prompt_length, prompt_adapter, adapter_position)
-    hidden_output = output(0, *common, early, maps, weight, rest, hidden_input)
-    before = lax.ppermute(late, "col", perm_z(1))
-    after = lax.ppermute(late, "col", perm_z(-1))
-    low_far, high_far = ring_far(before, after, "col", perm_z, quarter)
-    low_far, high_far, hidden_output = lax.optimization_barrier((low_far, high_far, hidden_output))
-    late = [late, swap(late), before, swap(before), after, swap(after), low_far, high_far, swap(low_far), swap(high_far)]
-    hidden_output = output(1, *common, late, maps, weight, rest, hidden_input, hidden_output)
+    attended = gather_col(attended, 256)
+    hidden_output = output(
+        me, prompt_length, prompt_adapter, adapter_position, attended, blocks, rest, hidden_input
+    )
     return hidden_output, new_cache
 
 

time: 180 us -> 170 us (0.944)
  starting transfers between devices: 48.9 us -> 38.5 us
  Pallas kernels: 55.7 us -> 46.3 us
  waiting for transfers between devices: 42.9 us -> 50.5 us
    ppermute x2, waiting for transfers between devices: 3.56 us -> 17.9 us  [ring4(): before = lax.ppermute(block, axis, perm(1))]
    pallas_call x6 -> x4, Pallas kernels: 45.6 us -> 35 us  [the longest x1 19.2 us: attention(): pl.pallas_call(attention_body, out_shape=(jax.ShapeDtypeStruct((TOK, FEAT...]
    ppermute x4 -> x2, waiting for transfers between devices: 11.9 us -> 2.68 us  [ring_far(): lax.ppermute(before[:half], axis, perm(1))]
    all_gather x1, waiting for transfers between devices: 11 us -> 17.9 us  [on_device(): weight = lax.all_gather(wide, 'row', axis=0)]
    all_gather x1, waiting for transfers between devices: 2.44 us -> 8.3 us  [on_device(): rest = lax.all_gather(rest, 'row', axis=0)]
    ppermute x18 -> x8, starting transfers between devices: 18.1 us -> 12.9 us  [swap(): return lax.ppermute(block, 'col', SWAP)]
    ppermute x4 -> x0, starting transfers between devices: 4.71 us -> none  [the longest x1 1.68 us: on_device(): after = lax.ppermute(late, 'col', perm_z(-1))]
    ppermute x4 -> x2, waiting for transfers between devices: 3.8 us -> 0.01 us  [ring_far(): lax.ppermute(after[half:], axis, perm(-1))]
  transfers between devices with their start and end apart: 38 -> 20, of which waited for: 12 -> 6; matrix products, arithmetic and copies ran while one was open for 5% -> 6% of each run, Pallas kernels for 24% -> 20%
where the time goes in v6:
time: 170 us; the launch traced here: 169 us
  waiting for transfers between devices  50.5 us (30%)
  Pallas kernels  46.3 us (27%)
  starting transfers between devices  38.5 us (23%)
  between operations  17 us (10%)
  local copies, waits for them, and re-layouts  9.67 us (6%)
  other arithmetic  7.31 us (4%)
    pallas_call x1, Pallas kernels, attention(): pl.pallas_call(attention_body, out_shape=(jax.ShapeDtypeStruct((TOK, FEAT...  19.2 us
    all_gather x1, waiting for transfers between devices, on_device(): weight = lax.all_gather(wide, 'row', axis=0)  17.9 us
    ppermute x2, waiting for transfers between devices, ring4(): before = lax.ppermute(block, axis, perm(1))  17.9 us
    ppermute x8, starting transfers between devices, swap(): return lax.ppermute(block, 'col', SWAP)  12.9 us
    pallas_call x1, Pallas kernels, output(): pl.pallas_call(out_body, out_shape=jax.ShapeDtypeStruct((TOK, FEAT), BF),...  9.86 us
    all_gather x1, waiting for transfers between devices, on_device(): rest = lax.all_gather(rest, 'row', axis=0)  8.3 us
    all_to_all x1, starting transfers between devices, on_device(): slots = lax.all_to_all(slots, 'row', 0, 0)  7.6 us
    pallas_call x1, Pallas kernels, norm_low(): pl.pallas_call(norm_body, out_shape=(pltpu.HBM((4, TOK, 2 * FEAT), BF), p...  6.8 us
  transfers between devices with their start and end apart: 20, of which 6 were waited for; matrix products, arithmetic and copies ran while one was open for 6% of the time, Pallas kernels for 20%

profile of v6, /device:TPU:1, one launch (start us, length us, event | category | flops | bytes accessed | tf_op | source)
XLA Modules:
  0.0 169.3 jit_solution(8128390813230393271)
XLA Ops:
  7.9 2.9 %pack.1 = (bf16[272,768]{1,0:T(8,128)(2,1)}, bf16[272,512]{1,0:T(8,128)(2,1)}, bf16[16,48,512]{2,1,0:T(8,128)(2,1)}) custom-call(s32[2]{0:T(128)} %pad_add_fusion.me_ref, bf16[256,768]{1,0:T(8,128)(2,1)} %qkv_ref.1, bf16[256,512]{1,0:T(8,128)(2,1)} %wo_ref.1, bf16[1,16,640]{2,1,0:T(8,128)(2,1)} %up_ref.1, bf16[1,16,4096]{2,1,0:T(8,128)(2,1)} %oup_ref.1, ...), custom_call_target="tpu_custom_call" | custom-call | tf_op jit(solution)/shard_map/pack/pallas_call | solution.py:144
  10.8 7.6 %all-to-all-start = ((bf16[16,48,512]{2,1,0:T(8,128)(2,1)}), bf16[16,48,512]{2,1,0:T(8,128)(2,1)S(1)}, u32[]{:S(2)}, u32[]{:S(2)}) async-start(bf16[16,48,512]{2,1,0:T(8,128)(2,1)} %get-tuple-element.23), calls=%async_computation | async-start | bytes 1572864 | tf_op jit(solution)/shard_map/all_to_all | solution.py:517
  21.7 4.5 %pick_pages.1 = (bf16[16,2,2,128,128]{4,3,2,1,0:T(8,128)(2,1)S(1)}, s32[16]{0:T(128)S(1)}) custom-call(s32[2]{0:T(128)S(1)} %copy-done.9, s32[256,1]{1,0:T(8,128)S(1)} %copy.20.owner_ref, s32[256]{0:T(256)S(1)} %copy-done.13, bf16[8,2,128,128]{3,2,1,0:T(8,128)(2,1)S(1)} %copy-done.6), custom_call_target="tpu_custom_call" | custom-call | tf_op jit(solution)/shard_map/pick_pages/pallas_call | solution.py:115
  27.5 3.6 %all-to-all-done.slots_ref = bf16[16,48,512]{2,1,0:T(8,128)(2,1)S(1)} async-done(((bf16[16,48,512]{2,1,0:T(8,128)(2,1)}), bf16[16,48,512]{2,1,0:T(8,128)(2,1)S(1)}, u32[]{:S(2)}, u32[]{:S(2)}) %all-to-all-start) | async-done | bytes 786464 | tf_op jit(solution)/shard_map/all_to_all | solution.py:517
  32.0 3.0 %select_slots.1.refs_0_.refs_8_ = bf16[704,512]{1,0:T(8,128)(2,1)} custom-call(s32[4]{0:T(128)} %adapter_ref.5, s32[16]{0:T(128)} %position_ref.5, bf16[16,48,512]{2,1,0:T(8,128)(2,1)} %copy-done.14, bf16[512,512]{1,0:T(8,128)(2,1)} %refs_17_.1), custom_call_target="tpu_custom_call" | custom-call | tf_op jit(solution)/shard_map/select_slots/pallas_call | solution.py:180
  35.1 1.8 %collective-permute-start.1 = (bf16[704,512]{1,0:T(8,128)(2,1)}, bf16[704,512]{1,0:T(8,128)(2,1)S(1)}, u32[]{:S(2)}, u32[]{:S(2)}) collective-permute-start(bf16[704,512]{1,0:T(8,128)(2,1)} %select_slots.1.refs_0_.refs_8_), channel_id=1, source_target_pairs={{0,2},{1,3},{2,4},{3,5},{4,6},{5,7},{6,0},{7,1},{8,10},{9,11},{10,... | collective-permute-start | bytes 2162696 | tf_op jit(solution)/shard_map/ppermute | solution.py:45
  36.9 2.5 %collective-permute-start.3 = (bf16[704,512]{1,0:T(8,128)(2,1)}, bf16[704,512]{1,0:T(8,128)(2,1)S(1)}, u32[]{:S(2)}, u32[]{:S(2)}) collective-permute-start(bf16[704,512]{1,0:T(8,128)(2,1)} %select_slots.1.refs_0_.refs_8_), channel_id=1, source_target_pairs={{0,6},{1,7},{2,0},{3,1},{4,2},{5,3},{6,4},{7,5},{8,14},{9,15},{10,... | collective-permute-start | bytes 2162696 | tf_op jit(solution)/shard_map/ppermute | solution.py:46
  39.4 5.5 %all-to-all-start.1 = ((bf16[16,512,128]{2,1,0:T(8,128)(2,1)}), bf16[16,512,128]{2,1,0:T(8,128)(2,1)}, u32[]{:S(2)}, u32[]{:S(2)}) async-start(bf16[16,512,128]{2,1,0:T(8,128)(2,1)} %bitcast.16), calls=%async_computation.1 | async-start | bytes 4194304 | tf_op jit(solution)/shard_map/all_to_all | solution.py:522
  45.5 6.3 %collective-permute-done.1.refs_2_.refs_10_ = bf16[704,512]{1,0:T(8,128)(2,1)S(1)} collective-permute-done((bf16[704,512]{1,0:T(8,128)(2,1)}, bf16[704,512]{1,0:T(8,128)(2,1)S(1)}, u32[]{:S(2)}, u32[]{:S(2)}) %collective-permute-start.1) | collective-permute-done | bytes 720928 | tf_op jit(solution)/shard_map/ppermute | solution.py:45
  52.8 2.6 %collective-permute-start.6 = (bf16[352,512]{1,0:T(8,128)(2,1)}, bf16[352,512]{1,0:T(8,128)(2,1)}, u32[]{:S(2)}, u32[]{:S(2)}) collective-permute-start(bf16[352,512]{1,0:T(8,128)(2,1)} %slice.49), channel_id=1, source_target_pairs={{0,6},{1,7},{2,0},{3,1},{4,2},{5,3},{6,4},{7,5},{8,14},{9,15},{10,... | collective-permute-start | bytes 1081352 | tf_op jit(solution)/shard_map/ppermute | solution.py:41
  58.7 5.9 %collective-permute-start = (bf16[704,512]{1,0:T(8,128)(2,1)S(1)}, bf16[704,512]{1,0:T(8,128)(2,1)}, u32[]{:S(2)}, u32[]{:S(2)}) collective-permute-start(bf16[704,512]{1,0:T(8,128)(2,1)S(1)} %copy-done), channel_id=1, source_target_pairs={{0,1},{1,0},{2,3},{3,2},{4,5},{5,4},{6,7},{7,6},{8,9},{9,8},{10,11... | collective-permute-start | bytes 2162696 | tf_op jit(solution)/shard_map/ppermute | solution.py:51
  70.4 1.9 %iota_add_fusion = (s32[512]{0:T(512)S(1)}, s32[512]{0:T(512)S(1)}) fusion(s32[]{:T(128)} %bitcast.12, s32[]{:T(128)} %bitcast.11, s32[]{:T(128)} %bitcast.5), kind=kLoop, calls=%fused_computation.5 | loop fusion | flops 1536 | bytes 4108 | tf_op jit(solution)/shard_map/add | solution.py:530
  72.3 2.2 %sine_select_fusion.rope_hbm = f32[512,128]{1,0:T(8,128)} fusion(f32[128]{0:T(128)S(1)} %pad_maximum_fusion, s32[512]{0:T(512)S(1)} %get-tuple-element.50, s32[512]{0:T(512)S(1)} %get-tuple-element.51, s32[512]{0:T(512)S(1)} %get-tuple-element.52, s32[512]{0:T(512)S(1)} %get-tuple-element.53, pred[512]{0:T(512)(128)(4,1)S(1)} %get-tuple-element.46, ...), kind=kLoop, calls=%fused_computation | loop fusion | flops 458752 | bytes 273024 | tf_op jit(solution)/shard_map/jit(_where)/select_n | solution.py:535
  74.5 6.8 %norm_low.1 = (bf16[4,512,1024]{2,1,0:T(8,128)(2,1)}, bf16[512,128]{1,0:T(8,128)(2,1)}) custom-call(s32[2]{0:T(128)S(1)} %copy-done.10, s32[1,4]{1,0:T(1,128)S(1)} %copy-done.7, bf16[704,512]{1,0:T(8,128)(2,1)S(1)} %copy-done, bf16[704,512]{1,0:T(8,128)(2,1)} %collective-permute-done.refs_1_.refs_9_, ...), custom_call_target="tpu_custom_call" | custom-call | tf_op jit(solution)/shard_map/norm_low/pallas_call | solution.py:214
  81.4 17.9 %all-gather.5.cloned.1.call-done = bf16[4352,768]{1,0:T(8,128)(2,1)} async-done(((bf16[272,768]{1,0:T(8,128)(2,1)}), bf16[4352,768]{1,0:T(8,128)(2,1)}) %all-gather.5.cloned.1.call-update) | async-done | bytes 6684688 | tf_op jit(solution)/shard_map/all_gather | solution.py:516
  99.3 19.2 %attention.1 = (bf16[512,512]{1,0:T(8,128)(2,1)S(1)}, bf16[2,512,128]{2,1,0:T(8,128)(2,1)}) custom-call(s32[1,4]{1,0:T(1,128)S(1)} %copy-done.7, s32[4]{0:T(128)S(1)} %copy-done.8, s32[16]{0:T(128)S(1)} %get-tuple-element.20.place_ref, s32[4]{0:T(128)S(1)} %copy-done.11, s32[16]{0:T(128)S(1)} %copy-done.12, ...), custom_call_target="tpu_custom_call" | custom-call | tf_op jit(solution)/shard_map/attention/pallas_call | solution.py:387
  118.6 2.7 %collective-permute-start.11 = (bf16[512,512]{1,0:T(8,128)(2,1)S(1)}, bf16[512,512]{1,0:T(8,128)(2,1)S(1)}, u32[]{:S(2)}, u32[]{:S(2)}) collective-permute-start(bf16[512,512]{1,0:T(8,128)(2,1)S(1)} %get-tuple-element.35.refs_0_), channel_id=1, source_target_pairs={{0,6},{1,7},{2,0},{3,1},{4,2},{5,3},{6,4},{7,5},{8,14},{9,15},{10,... | collective-permute-start | bytes 1572872 | tf_op jit(solution)/shard_map/ppermute | solution.py:46
  121.3 11.6 %collective-permute-done.9.refs_2_ = bf16[512,512]{1,0:T(8,128)(2,1)S(1)} collective-permute-done((bf16[512,512]{1,0:T(8,128)(2,1)S(1)}, bf16[512,512]{1,0:T(8,128)(2,1)S(1)}, u32[]{:S(2)}, u32[]{:S(2)}) %collective-permute-start.9) | collective-permute-done | bytes 524320 | tf_op jit(solution)/shard_map/ppermute | solution.py:45
  133.0 2.7 %collective-permute-start.14 = (bf16[256,512]{1,0:T(8,128)(2,1)S(1)}, bf16[256,512]{1,0:T(8,128)(2,1)S(1)}, u32[]{:S(2)}, u32[]{:S(2)}) collective-permute-start(bf16[256,512]{1,0:T(8,128)(2,1)S(1)} %slice.51), channel_id=1, source_target_pairs={{0,6},{1,7},{2,0},{3,1},{4,2},{5,3},{6,4},{7,5},{8,14},{9,15},{10,... | collective-permute-start | bytes 786440 | tf_op jit(solution)/shard_map/ppermute | solution.py:41
  135.7 1.9 %collective-permute-start.8 = (bf16[512,512]{1,0:T(8,128)(2,1)S(1)}, bf16[512,512]{1,0:T(8,128)(2,1)S(1)}, u32[]{:S(2)}, u32[]{:S(2)}) collective-permute-start(bf16[512,512]{1,0:T(8,128)(2,1)S(1)} %get-tuple-element.35.refs_0_), channel_id=1, source_target_pairs={{0,1},{1,0},{2,3},{3,2},{4,5},{5,4},{6,7},{7,6},{8,9},{9,8},{10,11... | collective-permute-start | bytes 1572872 | tf_op jit(solution)/shard_map/ppermute | solution.py:51
  138.1 2.7 %collective-permute-done.13 = bf16[256,512]{1,0:T(8,128)(2,1)S(1)} collective-permute-done((bf16[256,512]{1,0:T(8,128)(2,1)S(1)}, bf16[256,512]{1,0:T(8,128)(2,1)S(1)}, u32[]{:S(2)}, u32[]{:S(2)}) %collective-permute-start.13) | collective-permute-done | bytes 262176 | tf_op jit(solution)/shard_map/ppermute | solution.py:41
  140.9 2.4 %collective-permute-start.15 = (bf16[512,512]{1,0:T(8,128)(2,1)S(1)}, bf16[512,512]{1,0:T(8,128)(2,1)}, u32[]{:S(2)}, u32[]{:S(2)}) collective-permute-start(bf16[512,512]{1,0:T(8,128)(2,1)S(1)} %constant_dynamic-update-slice_fusion.2.refs_6_), channel_id=1, source_target_pairs={{0,1},{1,0},{2,3},{3,2},{4,5},{5,4},{6,7},{7,6},{8,9},{9,8},{10,11... | collective-permute-start | bytes 1572872 | tf_op jit(solution)/shard_map/ppermute | solution.py:51
  143.3 8.3 %all-gather.7.cloned.1.call-done = bf16[4352,512]{1,0:T(8,128)(2,1)} async-done(((bf16[272,512]{1,0:T(8,128)(2,1)}), bf16[4352,512]{1,0:T(8,128)(2,1)}) %all-gather.7.cloned.1.call-update) | async-done | bytes 4456464 | tf_op jit(solution)/shard_map/all_gather | solution.py:521
  152.6 9.9 %output.1 = bf16[512,512]{1,0:T(8,128)(2,1)} custom-call(s32[2]{0:T(128)S(1)} %copy-done.10, s32[1,4]{1,0:T(1,128)S(1)} %copy-done.7, s32[4]{0:T(128)S(1)} %copy-done.11, s32[16]{0:T(128)S(1)} %copy-done.12, bf16[512,512]{1,0:T(8,128)(2,1)} %copy-done.5, bf16[512,512]{1,0:T(8,128)(2,1)} %copy-done.18, bf16[512,512]{1,0:T(8,128)(2,1)} %copy-done.15, ...), custom_call_target="tpu_custom_call" | custom-call | tf_op jit(solution)/shard_map/output/pallas_call | solution.py:461
  (92 shorter events, 16.0 us)
Async XLA Ops:
  7.2 92.1 %all-gather.5.cloned.1.call-start = ((), (), s32[]{:S(2)}) async-start(), calls=%async_computation.2 | async-start | bytes 7102464 | tf_op jit(solution)/shard_map/all_gather | solution.py:516
  10.8 20.3 %all-to-all-start = ((bf16[16,48,512]{2,1,0:T(8,128)(2,1)}), bf16[16,48,512]{2,1,0:T(8,128)(2,1)S(1)}, u32[]{:S(2)}, u32[]{:S(2)}) async-start(bf16[16,48,512]{2,1,0:T(8,128)(2,1)} %get-tuple-element.23), calls=%async_computation | async-start | bytes 1572864 | tf_op jit(solution)/shard_map/all_to_all | solution.py:517
  18.4 133.2 %all-gather.7.cloned.1.call-start = ((), (), s32[]{:S(2)}) async-start(), calls=%async_computation.3 | async-start | bytes 4734976 | tf_op jit(solution)/shard_map/all_gather | solution.py:521
  32.0 35.9 %copy-start.21 = (bf16[128]{0:T(256)(128)(2,1)S(1)}, bf16[128]{0:T(256)(128)(2,1)}, u32[]{:S(2)}) copy-start(bf16[128]{0:T(256)(128)(2,1)} %param.20) | copy-start | bytes 772
  32.0 35.9 %copy-start.22 = (bf16[128]{0:T(256)(128)(2,1)S(1)}, bf16[128]{0:T(256)(128)(2,1)}, u32[]{:S(2)}) copy-start(bf16[128]{0:T(256)(128)(2,1)} %param.19) | copy-start | bytes 772
  32.0 36.5 %copy-start.8 = (s32[4]{0:T(128)S(1)}, s32[4]{0:T(128)}, u32[]{:S(2)}) copy-start(s32[4]{0:T(128)} %cache_ref.1) | copy-start | bytes 52
  35.1 39.5 %copy-start.10 = (s32[2]{0:T(128)S(1)}, s32[2]{0:T(128)}, u32[]{:S(2)}) copy-start(s32[2]{0:T(128)} %pad_add_fusion.me_ref) | copy-start | bytes 28
  35.1 16.7 %collective-permute-start.1 = (bf16[704,512]{1,0:T(8,128)(2,1)}, bf16[704,512]{1,0:T(8,128)(2,1)S(1)}, u32[]{:S(2)}, u32[]{:S(2)}) collective-permute-start(bf16[704,512]{1,0:T(8,128)(2,1)} %select_slots.1.refs_0_.refs_8_), channel_id=1, source_target_pairs={{0,2},{1,3},{2,4},{3,5},{4,6},{5,7},{6,0},{7,1},{8,10},{9,11},{10,... | collective-permute-start | bytes 2162696 | tf_op jit(solution)/shard_map/ppermute | solution.py:45
  36.9 15.1 %collective-permute-start.3 = (bf16[704,512]{1,0:T(8,128)(2,1)}, bf16[704,512]{1,0:T(8,128)(2,1)S(1)}, u32[]{:S(2)}, u32[]{:S(2)}) collective-permute-start(bf16[704,512]{1,0:T(8,128)(2,1)} %select_slots.1.refs_0_.refs_8_), channel_id=1, source_target_pairs={{0,6},{1,7},{2,0},{3,1},{4,2},{5,3},{6,4},{7,5},{8,14},{9,15},{10,... | collective-permute-start | bytes 2162696 | tf_op jit(solution)/shard_map/ppermute | solution.py:46
  39.4 42.0 %all-to-all-start.1 = ((bf16[16,512,128]{2,1,0:T(8,128)(2,1)}), bf16[16,512,128]{2,1,0:T(8,128)(2,1)}, u32[]{:S(2)}, u32[]{:S(2)}) async-start(bf16[16,512,128]{2,1,0:T(8,128)(2,1)} %bitcast.16), calls=%async_computation.1 | async-start | bytes 4194304 | tf_op jit(solution)/shard_map/all_to_all | solution.py:522
  51.8 13.3 %collective-permute-start.5 = (bf16[352,512]{1,0:T(8,128)(2,1)S(1)}, bf16[352,512]{1,0:T(8,128)(2,1)S(1)}, u32[]{:S(2)}, u32[]{:S(2)}) collective-permute-start(bf16[352,512]{1,0:T(8,128)(2,1)S(1)} %slice.48), channel_id=1, source_target_pairs={{0,2},{1,3},{2,4},{3,5},{4,6},{5,7},{6,0},{7,1},{8,10},{9,11},{10,... | collective-permute-start | bytes 1081352 | tf_op jit(solution)/shard_map/ppermute | solution.py:41
  52.8 12.3 %collective-permute-start.6 = (bf16[352,512]{1,0:T(8,128)(2,1)}, bf16[352,512]{1,0:T(8,128)(2,1)}, u32[]{:S(2)}, u32[]{:S(2)}) collective-permute-start(bf16[352,512]{1,0:T(8,128)(2,1)} %slice.49), channel_id=1, source_target_pairs={{0,6},{1,7},{2,0},{3,1},{4,2},{5,3},{6,4},{7,5},{8,14},{9,15},{10,... | collective-permute-start | bytes 1081352 | tf_op jit(solution)/shard_map/ppermute | solution.py:41
  58.7 15.8 %collective-permute-start = (bf16[704,512]{1,0:T(8,128)(2,1)S(1)}, bf16[704,512]{1,0:T(8,128)(2,1)}, u32[]{:S(2)}, u32[]{:S(2)}) collective-permute-start(bf16[704,512]{1,0:T(8,128)(2,1)S(1)} %copy-done), channel_id=1, source_target_pairs={{0,1},{1,0},{2,3},{3,2},{4,5},{5,4},{6,7},{7,6},{8,9},{9,8},{10,11... | collective-permute-start | bytes 2162696 | tf_op jit(solution)/shard_map/ppermute | solution.py:51
  64.6 9.9 %collective-permute-start.2 = (bf16[704,512]{1,0:T(8,128)(2,1)S(1)}, bf16[704,512]{1,0:T(8,128)(2,1)}, u32[]{:S(2)}, u32[]{:S(2)}) collective-permute-start(bf16[704,512]{1,0:T(8,128)(2,1)S(1)} %collective-permute-done.1.refs_2_.refs_10_), channel_id=1, source_target_pairs={{0,1},{1,0},{2,3},{3,2},{4,5},{5,4},{6,7},{7,6},{8,9},{9,8},{10,11... | collective-permute-start | bytes 2162696 | tf_op jit(solution)/shard_map/ppermute | solution.py:51
  64.7 9.8 %collective-permute-start.4 = (bf16[704,512]{1,0:T(8,128)(2,1)S(1)}, bf16[704,512]{1,0:T(8,128)(2,1)}, u32[]{:S(2)}, u32[]{:S(2)}) collective-permute-start(bf16[704,512]{1,0:T(8,128)(2,1)S(1)} %collective-permute-done.3.refs_4_.refs_12_), channel_id=1, source_target_pairs={{0,1},{1,0},{2,3},{3,2},{4,5},{5,4},{6,7},{7,6},{8,9},{9,8},{10,11... | collective-permute-start | bytes 2162696 | tf_op jit(solution)/shard_map/ppermute | solution.py:51
  66.2 8.3 %collective-permute-start.7 = (bf16[704,512]{1,0:T(8,128)(2,1)S(1)}, bf16[704,512]{1,0:T(8,128)(2,1)}, u32[]{:S(2)}, u32[]{:S(2)}) collective-permute-start(bf16[704,512]{1,0:T(8,128)(2,1)S(1)} %constant_dynamic-update-slice_fusion.refs_6_.refs_14_), channel_id=1, source_target_pairs={{0,1},{1,0},{2,3},{3,2},{4,5},{5,4},{6,7},{7,6},{8,9},{9,8},{10,11... | collective-permute-start | bytes 2162696 | tf_op jit(solution)/shard_map/ppermute | solution.py:51
  118.6 14.3 %collective-permute-start.9 = (bf16[512,512]{1,0:T(8,128)(2,1)S(1)}, bf16[512,512]{1,0:T(8,128)(2,1)S(1)}, u32[]{:S(2)}, u32[]{:S(2)}) collective-permute-start(bf16[512,512]{1,0:T(8,128)(2,1)S(1)} %get-tuple-element.35.refs_0_), channel_id=1, source_target_pairs={{0,2},{1,3},{2,4},{3,5},{4,6},{5,7},{6,0},{7,1},{8,10},{9,11},{10,... | collective-permute-start | bytes 1572872 | tf_op jit(solution)/shard_map/ppermute | solution.py:45
  118.6 14.4 %collective-permute-start.11 = (bf16[512,512]{1,0:T(8,128)(2,1)S(1)}, bf16[512,512]{1,0:T(8,128)(2,1)S(1)}, u32[]{:S(2)}, u32[]{:S(2)}) collective-permute-start(bf16[512,512]{1,0:T(8,128)(2,1)S(1)} %get-tuple-element.35.refs_0_), channel_id=1, source_target_pairs={{0,6},{1,7},{2,0},{3,1},{4,2},{5,3},{6,4},{7,5},{8,14},{9,15},{10,... | collective-permute-start | bytes 1572872 | tf_op jit(solution)/shard_map/ppermute | solution.py:46
  132.9 7.9 %collective-permute-start.13 = (bf16[256,512]{1,0:T(8,128)(2,1)S(1)}, bf16[256,512]{1,0:T(8,128)(2,1)S(1)}, u32[]{:S(2)}, u32[]{:S(2)}) collective-permute-start(bf16[256,512]{1,0:T(8,128)(2,1)S(1)} %slice.50), channel_id=1, source_target_pairs={{0,2},{1,3},{2,4},{3,5},{4,6},{5,7},{6,0},{7,1},{8,10},{9,11},{10,... | collective-permute-start | bytes 786440 | tf_op jit(solution)/shard_map/ppermute | solution.py:41
  133.0 7.8 %collective-permute-start.14 = (bf16[256,512]{1,0:T(8,128)(2,1)S(1)}, bf16[256,512]{1,0:T(8,128)(2,1)S(1)}, u32[]{:S(2)}, u32[]{:S(2)}) collective-permute-start(bf16[256,512]{1,0:T(8,128)(2,1)S(1)} %slice.51), channel_id=1, source_target_pairs={{0,6},{1,7},{2,0},{3,1},{4,2},{5,3},{6,4},{7,5},{8,14},{9,15},{10,... | collective-permute-start | bytes 786440 | tf_op jit(solution)/shard_map/ppermute | solution.py:41
  135.7 15.8 %collective-permute-start.8 = (bf16[512,512]{1,0:T(8,128)(2,1)S(1)}, bf16[512,512]{1,0:T(8,128)(2,1)S(1)}, u32[]{:S(2)}, u32[]{:S(2)}) collective-permute-start(bf16[512,512]{1,0:T(8,128)(2,1)S(1)} %get-tuple-element.35.refs_0_), channel_id=1, source_target_pairs={{0,1},{1,0},{2,3},{3,2},{4,5},{5,4},{6,7},{7,6},{8,9},{9,8},{10,11... | collective-permute-start | bytes 1572872 | tf_op jit(solution)/shard_map/ppermute | solution.py:51
  137.6 14.0 %collective-permute-start.10 = (bf16[512,512]{1,0:T(8,128)(2,1)S(1)}, bf16[512,512]{1,0:T(8,128)(2,1)S(1)}, u32[]{:S(2)}, u32[]{:S(2)}) collective-permute-start(bf16[512,512]{1,0:T(8,128)(2,1)S(1)} %collective-permute-done.9.refs_2_), channel_id=1, source_target_pairs={{0,1},{1,0},{2,3},{3,2},{4,5},{5,4},{6,7},{7,6},{8,9},{9,8},{10,11... | collective-permute-start | bytes 1572872 | tf_op jit(solution)/shard_map/ppermute | solution.py:51
  137.6 14.0 %collective-permute-start.12 = (bf16[512,512]{1,0:T(8,128)(2,1)S(1)}, bf16[512,512]{1,0:T(8,128)(2,1)}, u32[]{:S(2)}, u32[]{:S(2)}) collective-permute-start(bf16[512,512]{1,0:T(8,128)(2,1)S(1)} %collective-permute-done.11.refs_4_), channel_id=1, source_target_pairs={{0,1},{1,0},{2,3},{3,2},{4,5},{5,4},{6,7},{7,6},{8,9},{9,8},{10,11... | collective-permute-start | bytes 1572872 | tf_op jit(solution)/shard_map/ppermute | solution.py:51
  140.9 10.7 %collective-permute-start.15 = (bf16[512,512]{1,0:T(8,128)(2,1)S(1)}, bf16[512,512]{1,0:T(8,128)(2,1)}, u32[]{:S(2)}, u32[]{:S(2)}) collective-permute-start(bf16[512,512]{1,0:T(8,128)(2,1)S(1)} %constant_dynamic-update-slice_fusion.2.refs_6_), channel_id=1, source_target_pairs={{0,1},{1,0},{2,3},{3,2},{4,5},{5,4},{6,7},{7,6},{8,9},{9,8},{10,11... | collective-permute-start | bytes 1572872 | tf_op jit(solution)/shard_map/ppermute | solution.py:51
  (19 other events, 304.9 us)
Sparse Core Ops, SparseCore 0:
  10.9 88.3 all-gather.4
  101.5 50.0 all-gather.6

commit v7 on v6

--- a/solution.py
+++ b/solution.py
@@ -129,62 +129,62 @@
     )(me, owner, index, store)
 
 
-def pack_body(me_ref, qkv_ref, wo_ref, up_ref, oup_ref, down_ref, odown_ref, wide_ref, rest_ref, slots_ref):
-    wide_ref[:256, :] = qkv_ref[...]
-    wide_ref[256:, :640] = up_ref[0]
-    wide_ref[256:, 640:] = jnp.zeros((16, 128), BF)
+def pack_body(me_ref, wo_ref, up_ref, oup_ref, down_ref, odown_ref, rest_ref, slots_ref):
     rest_ref[:256, :] = wo_ref[...]
     rest_ref[256:, :] = oup_ref[0]
     for r in range(16):
-        slots_ref[r, :32, :] = down_ref[0]
-        slots_ref[r, 32:, :] = odown_ref[0]
-
-
-def pack(me, qkv, wo, up, oup, down, odown):
+        for j in range(4):
+            slots_ref[r, j * 48 : j * 48 + 32, :] = down_ref[0, :, j * HEAD : (j + 1) * HEAD]
+            slots_ref[r, j * 48 + 32 : j * 48 + 48, :] = odown_ref[0, :, j * HEAD : (j + 1) * HEAD]
+        for j in range(5):
+            slots_ref[r, 192 + j * 16 : 208 + j * 16, :] = up_ref[0, :, j * HEAD : (j + 1) * HEAD]
+
+
+def pack(me, wo, up, oup, down, odown):
     return pl.pallas_call(
         pack_body,
-        out_shape=(
-            jax.ShapeDtypeStruct((272, 768), BF),
-            jax.ShapeDtypeStruct((272, FEAT), BF),
-            jax.ShapeDtypeStruct((16, 48, FEAT), BF),
-        ),
+        out_shape=(jax.ShapeDtypeStruct((272, FEAT), BF), jax.ShapeDtypeStruct((16, 272, HEAD), BF)),
         grid_spec=pltpu.PrefetchScalarGridSpec(
             num_scalar_prefetch=1,
             grid=(1,),
             in_specs=[
-                whole(256, 768),
                 whole(256, FEAT),
                 whole(1, 16, 640),
                 pl.BlockSpec((1, 16, FEAT), lambda i, me: (0, 0, me[1])),
                 pl.BlockSpec((1, 32, FEAT), lambda i, me: (0, 0, me[1])),
                 whole(1, 16, FEAT),
             ],
-            out_specs=(whole(272, 768), whole(272, FEAT), whole(16, 48, FEAT)),
+            out_specs=(whole(272, FEAT), whole(16, 272, HEAD)),
         ),
         name="pack",
-    )(me, qkv, wo, up, oup, down, odown)
+    )(me, wo, up, oup, down, odown)
 
 
 DOWN, ODOWN, BLOCK_ROWS = TOK, TOK + 128, TOK + 192
 
 
-def select_body(adapter_ref, position_ref, slots_ref, hidden_ref, out_ref):
+def select_body(adapter_ref, position_ref, slots_ref, hidden_ref, out_ref, up_ref):
     out_ref[:TOK, :] = hidden_ref[...]
+    up_ref[...] = jnp.zeros_like(up_ref)
     for p in range(PROMPTS):
         slot = position_ref[adapter_ref[p]]
-        out_ref[DOWN + p * 32 : DOWN + p * 32 + 32, :] = slots_ref[slot, :32, :]
-        out_ref[ODOWN + p * 16 : ODOWN + p * 16 + 16, :] = slots_ref[slot, 32:, :]
+        for j in range(4):
+            cut = slice(j * HEAD, (j + 1) * HEAD)
+            out_ref[DOWN + p * 32 : DOWN + p * 32 + 32, cut] = slots_ref[slot, j * 48 : j * 48 + 32, :]
+            out_ref[ODOWN + p * 16 : ODOWN + p * 16 + 16, cut] = slots_ref[slot, j * 48 + 32 : j * 48 + 48, :]
+            up_ref[p * 32 : p * 32 + 16, cut] = slots_ref[slot, 192 + j * 16 : 208 + j * 16, :]
+        up_ref[p * 32 + 16 : p * 32 + 32, 512:] = slots_ref[slot, 256:272, :]
 
 
 def select_slots(adapter, position, slots, hidden):
     return pl.pallas_call(
         select_body,
-        out_shape=jax.ShapeDtypeStruct((BLOCK_ROWS, FEAT), BF),
+        out_shape=(jax.ShapeDtypeStruct((BLOCK_ROWS, FEAT), BF), pltpu.HBM((128, 640), BF)),
         grid_spec=pltpu.PrefetchScalarGridSpec(
             num_scalar_prefetch=2,
             grid=(1,),
-            in_specs=[whole(16, 48, FEAT), whole(TOK, FEAT)],
-            out_specs=whole(BLOCK_ROWS, FEAT),
+            in_specs=[whole(16, 272, HEAD), whole(TOK, FEAT)],
+            out_specs=(whole(BLOCK_ROWS, FEAT), whole(128, 640)),
         ),
         name="select_slots",
     )(adapter, position, slots, hidden)
@@ -192,7 +192,8 @@
 
 def norm_body(me_ref, length_ref, *refs):
     blocks, maps = refs[:8], refs[8:16]
-    gain_ref, normed_ref, low_ref = refs[16:]
+    outs = refs[16:24]
+    gain_ref, normed_ref, low_ref, turned_ref = refs[24:]
     order = col_order(me_ref[1])
     values = [b[...].astype(F32) for b in blocks]
     total = sum(jnp.sum(v * v, axis=-1, keepdims=True) for v in values)
@@ -207,27 +208,41 @@
     prompt = per_token(prompt_rows(length_ref), range(PROMPTS), token)
     mine = lax.broadcasted_iota(jnp.int32, low.shape, 1) // 32 == prompt
     low_ref[...] = jnp.where(mine, low, 0.0).astype(BF)
+    for k in range(4):
+
+        @pl.when(pl.program_id(0) == k)
+        def _():
+            for b in range(2):
+                down = outs[2 * k + b][...].astype(F32)
+                turned = jnp.concatenate([down, down], axis=0).T.astype(BF)
+                turned_ref[b, 0], turned_ref[b, 1] = turned[:256], turned[256:]
 
 
 def norm_low(me, lengths, blocks, gain):
     rows = 128
     return pl.pallas_call(
         norm_body,
-        out_shape=(pltpu.HBM((4, TOK, 2 * FEAT), BF), pltpu.HBM((TOK, 128), BF)),
+        out_shape=(
+            pltpu.HBM((4, TOK, 2 * FEAT), BF),
+            pltpu.HBM((TOK, 128), BF),
+            pltpu.HBM((8, 2, 256, 128), BF),
+        ),
         grid_spec=pltpu.PrefetchScalarGridSpec(
             num_scalar_prefetch=2,
             grid=(TOK // rows,),
             in_specs=[pl.BlockSpec((rows, FEAT), lambda i, *_: (i, 0))] * 8
             + [pl.BlockSpec((128, FEAT), lambda i, *_: (DOWN // 128, 0))] * 8
+            + [pl.BlockSpec((64, FEAT), lambda i, *_: (ODOWN // 64, 0))] * 8
             + [whole(8, 1, FEAT)],
             out_specs=(
                 pl.BlockSpec((4, rows, 2 * FEAT), lambda i, *_: (0, i, 0)),
                 pl.BlockSpec((rows, 128), lambda i, *_: (i, 0)),
+                pl.BlockSpec((2, 2, 256, 128), lambda i, *_: (i, 0, 0, 0)),
             ),
         ),
         compiler_params=vmem(20),
         name="norm_low",
-    )(me, lengths, *blocks, *blocks, gain)
+    )(me, lengths, *blocks, *blocks, *blocks, gain)
 
 
 BLOCK = 64
@@ -316,13 +331,13 @@
 
 
 def attention_body(
-    length_ref, cache_ref, place_ref, adapter_ref, position_ref,
-    normed_ref, w_ref, low_hbm, rope_hbm, gains_hbm, pages_ref,
+    length_ref, cache_ref, place_ref,
+    normed_ref, w_ref, up_hbm, low_hbm, rope_hbm, gains_hbm, pages_ref,
     out_ref, kv_ref,
     m_ref, l_ref, sum_ref, cached_ref, x, w, up, acc, q_ref, low_ref, rope_ref, gains_ref, sems,
 ):
     def chunk(k):
-        rows = w_ref.at[pl.ds(4 * k, 4), pl.ds(0, 256), pl.ds(0, 768)]
+        rows = w_ref.at[pl.ds(4 * k, 4)]
         return [
             pltpu.make_async_copy(normed_ref.at[k], x.at[k], sems.at[2 * k]),
             pltpu.make_async_copy(rows, w.at[k], sems.at[2 * k + 1]),
@@ -331,14 +346,7 @@
     chunks = [chunk(k) for k in range(4)]
     for copy in chunks[0]:
         copy.start()
-    up[...] = jnp.zeros_like(up)
-    maps = []
-    for p in range(PROMPTS):
-        slot = position_ref[adapter_ref[p]]
-        q_part = w_ref.at[slot, pl.ds(256, 16), pl.ds(0, 512)]
-        v_part = w_ref.at[slot, pl.ds(256, 16), pl.ds(512, HEAD)]
-        maps.append(pltpu.make_async_copy(q_part, up.at[pl.ds(p * 32, 16), pl.ds(0, 512)], sems.at[8 + 2 * p]))
-        maps.append(pltpu.make_async_copy(v_part, up.at[pl.ds(p * 32 + 16, 16), pl.ds(512, HEAD)], sems.at[9 + 2 * p]))
+    maps = [pltpu.make_async_copy(up_hbm, up, sems.at[8])]
     maps.append(pltpu.make_async_copy(low_hbm, low_ref, sems.at[48]))
     maps.append(pltpu.make_async_copy(rope_hbm, rope_ref, sems.at[49]))
     maps.append(pltpu.make_async_copy(gains_hbm, gains_ref, sems.at[50]))
@@ -382,7 +390,7 @@
     attend(length_ref, cache_ref, q_ref, kv_ref, cached_ref, out_ref, m_ref, l_ref, sum_ref)
 
 
-def attention(lengths, cached, place, adapter, position, normed, weight, low, rope, gains, pages):
+def attention(lengths, cached, place, normed, weight, up, low, rope, gains, pages):
     hbm = pl.BlockSpec(memory_space=pl.ANY)
     return pl.pallas_call(
         attention_body,
@@ -391,9 +399,9 @@
             jax.ShapeDtypeStruct((2, TOK, HEAD), BF),
         ),
         grid_spec=pltpu.PrefetchScalarGridSpec(
-            num_scalar_prefetch=5,
+            num_scalar_prefetch=3,
             grid=(1,),
-            in_specs=[hbm] * 6,
+            in_specs=[hbm] * 7,
             out_specs=(whole(TOK, FEAT), whole(2, TOK, HEAD)),
             scratch_shapes=ATTEND_SCRATCH
             + [
@@ -411,24 +419,23 @@
         compiler_params=vmem(32),
         name="attention",
     )(
-        lengths, cached, place, adapter, position,
-        in_hbm(normed), in_hbm(weight), in_hbm(low), in_hbm(rope), in_hbm(gains), in_hbm(pages),
+        lengths, cached, place,
+        in_hbm(normed), in_hbm(weight), in_hbm(up), in_hbm(low), in_hbm(rope), in_hbm(gains), in_hbm(pages),
     )
 
 
-def out_body(
-    me_ref, length_ref, adapter_ref, position_ref, *refs
-):
-    blocks, sources = refs[:8], refs[8:16]
-    weight_ref, hidden_hbm, out_ref, x, w, od, oup, hidden, acc, sems = refs[16:]
+def out_body(me_ref, length_ref, adapter_ref, position_ref, *refs):
+    blocks = refs[:8]
+    turned_ref, weight_ref, hidden_hbm, out_ref, x, w, oup, hidden, acc, sems = refs[8:]
     order = col_order(me_ref[1])
     copies = []
     for b in range(8):
+        part = w.at[b // 2, pl.ds(b % 2 * 2, 2)]
+        rows = weight_ref.at[pl.ds(2 * order[b], 2), pl.ds(0, 256)]
+        copies.append(pltpu.make_async_copy(rows, part.at[:, :, pl.ds(0, FEAT)], sems.at[b]))
         side = pl.ds(b % 2 * FEAT, FEAT)
-        rows = weight_ref.at[pl.ds(2 * order[b], 2), pl.ds(0, 256)]
-        copies.append(pltpu.make_async_copy(rows, w.at[b // 2, pl.ds(b % 2 * 2, 2)], sems.at[b]))
         copies.append(pltpu.make_async_copy(blocks[b], x.at[b // 2, :, side], sems.at[8 + b]))
-        copies.append(pltpu.make_async_copy(sources[b].at[pl.ds(ODOWN, 64)], od.at[b // 2, :, side], sems.at[16 + b]))
+        copies.append(pltpu.make_async_copy(turned_ref.at[b], part.at[:, :, pl.ds(FEAT, 128)], sems.at[16 + b]))
     last = [pltpu.make_async_copy(hidden_hbm, hidden, sems.at[24])]
     for p in range(PROMPTS):
         slot = position_ref[adapter_ref[p]]
@@ -436,27 +443,32 @@
         last.append(pltpu.make_async_copy(rows, oup.at[pl.ds(p * 16, 16)], sems.at[25 + p]))
     for copy in copies + last:
         copy.start()
-    low = jnp.zeros((TOK, 64), F32)
     for i in range(4):
         for copy in copies[6 * i : 6 * i + 6]:
             copy.wait()
-        part = jnp.dot(x[i], w[i].reshape(2 * FEAT, FEAT), preferred_element_type=F32)
+        part = jnp.dot(x[i], w[i].reshape(2 * FEAT, FEAT + 128), preferred_element_type=F32)
         if i == 0:
             acc[...] = part
         else:
             acc[...] += part
-        low += lax.dot_general(x[i], od[i], (((1,), (1,)), ((), ())), preferred_element_type=F32)
-    token = lax.broadcasted_iota(jnp.int32, low.shape, 0)
-    prompt = per_token(prompt_rows(length_ref), range(PROMPTS), token)
-    mine = lax.broadcasted_iota(jnp.int32, low.shape, 1) // 16 == prompt
-    low = jnp.where(mine, low, 0.0)
     for copy in last:
         copy.wait()
-    change = jnp.dot(low, oup[...].astype(F32), precision=lax.Precision.HIGHEST, preferred_element_type=F32)
-    out_ref[...] = (hidden[...].astype(F32) + acc[...] + 0.5 * change).astype(BF)
-
-
-def output(me, lengths, adapter, position, blocks, sources, weight, hidden):
+    low = acc[:, FEAT:]
+    token = lax.broadcasted_iota(jnp.int32, low.shape, 0)
+    lane = lax.broadcasted_iota(jnp.int32, low.shape, 1)
+    prompt = per_token(prompt_rows(length_ref), range(PROMPTS), token)
+    low = jnp.where((lane & 63) // 16 == prompt, low, 0.0)
+    high = low.astype(BF)
+    rest = low - high.astype(F32)
+    middle = rest.astype(BF)
+    least = (rest - middle.astype(F32)).astype(BF)
+    maps = jnp.concatenate([oup[...], oup[...]], axis=0)
+    change = jnp.dot(jnp.where(lane < 64, high, middle), maps, preferred_element_type=F32)
+    change += jnp.dot(jnp.where(lane < 64, least, jnp.zeros_like(least)), maps, preferred_element_type=F32)
+    out_ref[...] = (hidden[...].astype(F32) + acc[:, :FEAT] + 0.5 * change).astype(BF)
+
+
+def output(me, lengths, adapter, position, blocks, turned, weight, hidden):
     hbm = pl.BlockSpec(memory_space=pl.ANY)
     return pl.pallas_call(
         out_body,
@@ -464,15 +476,14 @@
         grid_spec=pltpu.PrefetchScalarGridSpec(
             num_scalar_prefetch=4,
             grid=(1,),
-            in_specs=[hbm] * 18,
+            in_specs=[hbm] * 11,
             out_specs=whole(TOK, FEAT),
             scratch_shapes=[
                 pltpu.VMEM((4, TOK, 2 * FEAT), BF),
-                pltpu.VMEM((4, 4, 256, FEAT), BF),
-                pltpu.VMEM((4, 64, 2 * FEAT), BF),
+                pltpu.VMEM((4, 4, 256, FEAT + 128), BF),
                 pltpu.VMEM((64, FEAT), BF),
                 pltpu.VMEM((TOK, FEAT), BF),
-                pltpu.VMEM((TOK, FEAT), F32),
+                pltpu.VMEM((TOK, FEAT + 128), F32),
                 pltpu.SemaphoreType.DMA((29,)),
             ],
         ),
@@ -480,7 +491,7 @@
         name="output",
     )(
         me, lengths, adapter, position,
-        *map(in_hbm, blocks), *map(in_hbm, sources), in_hbm(weight), in_hbm(hidden),
+        *map(in_hbm, blocks), in_hbm(turned), in_hbm(weight), in_hbm(hidden),
     )
 
 
@@ -504,16 +515,10 @@
     cache_page_store,
 ):
     me = jnp.stack([lax.axis_index("row"), lax.axis_index("col")]).astype(jnp.int32)
-    wide, rest, slots = pack(
-        me,
-        query_key_value_weight,
-        output_weight,
-        adapter_up_maps,
-        output_up_maps,
-        adapter_down_maps,
-        output_down_maps,
+    weight = lax.all_gather(query_key_value_weight, "row", axis=0)
+    rest, slots = pack(
+        me, output_weight, adapter_up_maps, output_up_maps, adapter_down_maps, output_down_maps
     )
-    weight = lax.all_gather(wide, "row", axis=0)
     slots = lax.all_to_all(slots, "row", 0, 0)
 
     picked, place = pick_pages(me, page_owner_row, page_store_index, cache_page_store)
@@ -521,7 +526,8 @@
     rest = lax.all_gather(rest, "row", axis=0)
     pages = lax.all_to_all(picked.reshape(16, 4 * PAGE, HEAD), "row", 0, 0).reshape(32, 2, PAGE, HEAD)
 
-    blocks = gather_col(select_slots(prompt_adapter, adapter_position, slots, hidden_input), BLOCK_ROWS // 2)
+    block, up = select_slots(prompt_adapter, adapter_position, slots, hidden_input)
+    blocks = gather_col(block, BLOCK_ROWS // 2)
 
     token = lax.broadcasted_iota(jnp.int32, (TOK, HEAD), 0)
     position, start = token, jnp.int32(0)
@@ -534,17 +540,16 @@
     front = lax.broadcasted_iota(jnp.int32, (TOK, HEAD), 1) < HEAD // 2
     rope = jnp.where(front, jnp.cos(angles), jnp.sin(angles))
 
-    normed, low = norm_low(me, prompt_length, blocks, input_norm_gain.reshape(8, 1, FEAT))
+    normed, low, turned = norm_low(me, prompt_length, blocks, input_norm_gain.reshape(8, 1, FEAT))
     gains = jnp.stack([query_norm_gain, key_norm_gain]).astype(F32)
     weight, normed, low, pages, rope, gains = lax.optimization_barrier((weight, normed, low, pages, rope, gains))
     attended, new_cache = attention(
         prompt_length,
         cache_length,
         place,
-        prompt_adapter,
-        adapter_position,
         normed,
         weight,
+        up,
         low,
         rope,
         gains,
@@ -552,7 +557,7 @@
     )
     attended = gather_col(attended, 256)
     hidden_output = output(
-        me, prompt_length, prompt_adapter, adapter_position, attended, blocks, rest, hidden_input
+        me, prompt_length, prompt_adapter, adapter_position, attended, turned, rest, hidden_input
     )
     return hidden_output, new_cache
 

time: 170 us -> 174 us (1.024)
  starting transfers between devices: 38.5 us -> 44.5 us
  local copies, waits for them, and re-layouts: 9.67 us -> 5.62 us
  waiting for transfers between devices: 50.5 us -> 54.4 us
    all_gather x1, waiting for transfers between devices: 17.9 us -> 9.15 us  [on_device(): weight = lax.all_gather(query_key_value_weight, 'row', axis=0)]
    all_to_all x1, waiting for transfers between devices: 3.6 us -> 11.6 us  [on_device(): slots = lax.all_to_all(slots, 'row', 0, 0)]
    all_to_all x1, waiting for transfers between devices: 0.01 us -> 6.93 us  [on_device(): lax.all_to_all(picked.reshape(16, 4 * PAGE, HEAD), 'row', 0, 0)]
    ppermute x8, starting transfers between devices: 12.9 us -> 17.1 us  [swap(): return lax.ppermute(block, 'col', SWAP)]
    ppermute x2, waiting for transfers between devices: 17.9 us -> 13.8 us  [ring4(): before = lax.ppermute(block, axis, perm(1))]
    unnamed x49 -> x41, local copies, waits for them, and re-layouts: 6.4 us -> 2.45 us
    all_to_all x1, starting transfers between devices: 5.45 us -> 7.46 us  [on_device(): lax.all_to_all(picked.reshape(16, 4 * PAGE, HEAD), 'row', 0, 0)]
  transfers between devices with their start and end apart: 20 -> 20, of which waited for: 6 -> 7; matrix products, arithmetic and copies ran while one was open for 6% -> 6% of each run, Pallas kernels for 20% -> 21%
where the time goes in v7:
time: 174 us; the launch traced here: 173 us
  waiting for transfers between devices  54.4 us (31%)
  Pallas kernels  44.7 us (26%)
  starting transfers between devices  44.5 us (26%)
  between operations  17 us (10%)
  other arithmetic  7.18 us (4%)
  local copies, waits for them, and re-layouts  5.62 us (3%)
    pallas_call x1, Pallas kernels, attention(): pl.pallas_call(attention_body, out_shape=(jax.ShapeDtypeStruct((TOK, FEAT...  17.6 us
    ppermute x8, starting transfers between devices, swap(): return lax.ppermute(block, 'col', SWAP)  17.1 us
    ppermute x2, waiting for transfers between devices, ring4(): before = lax.ppermute(block, axis, perm(1))  13.8 us
    all_to_all x1, waiting for transfers between devices, on_device(): slots = lax.all_to_all(slots, 'row', 0, 0)  11.6 us
    all_gather x1, waiting for transfers between devices, on_device(): rest = lax.all_gather(rest, 'row', axis=0)  10 us
    all_gather x1, waiting for transfers between devices, on_device(): weight = lax.all_gather(query_key_value_weight, 'row', axis=0)  9.15 us
    pallas_call x1, Pallas kernels, output(): pl.pallas_call(out_body, out_shape=jax.ShapeDtypeStruct((TOK, FEAT), BF),...  8.93 us
    all_to_all x1, starting transfers between devices, on_device(): slots = lax.all_to_all(slots, 'row', 0, 0)  7.63 us
  transfers between devices with their start and end apart: 20, of which 7 were waited for; matrix products, arithmetic and copies ran while one was open for 6% of the time, Pallas kernels for 21%

profile of v7, /device:TPU:1, one launch (start us, length us, event | category | flops | bytes accessed | tf_op | source)
XLA Modules:
  0.0 173.5 jit_solution(7411661757174084345)
XLA Ops:
  8.5 3.0 %pack.1 = (bf16[272,512]{1,0:T(8,128)(2,1)}, bf16[16,272,128]{2,1,0:T(8,128)(2,1)}) custom-call(s32[2]{0:T(128)} %pad_add_fusion.me_ref, bf16[256,512]{1,0:T(8,128)(2,1)} %wo_ref.1, bf16[1,16,640]{2,1,0:T(8,128)(2,1)} %up_ref.1, bf16[1,16,4096]{2,1,0:T(8,128)(2,1)} %oup_ref.1, bf16[1,32,4096]{2,1,0:T(8,128)(2,1)} %down_ref.1, bf16[1,16,512]{2,1,0:T(8,128)(2,1)} %odown_ref.1), custom_call_target="tpu_custom_call" | custom-call | tf_op jit(solution)/shard_map/pack/pallas_call | solution.py:144
  11.5 7.6 %all-to-all-start = ((bf16[16,272,128]{2,1,0:T(8,128)(2,1)}), bf16[16,272,128]{2,1,0:T(8,128)(2,1)}, u32[]{:S(2)}, u32[]{:S(2)}) async-start(bf16[16,272,128]{2,1,0:T(8,128)(2,1)} %get-tuple-element.24), calls=%async_computation | async-start | bytes 2228224 | tf_op jit(solution)/shard_map/all_to_all | solution.py:522
  19.4 4.5 %pick_pages.1 = (bf16[16,2,2,128,128]{4,3,2,1,0:T(8,128)(2,1)S(1)}, s32[16]{0:T(128)S(1)}) custom-call(s32[2]{0:T(128)S(1)} %copy-done.6, s32[256,1]{1,0:T(8,128)S(1)} %copy.20.owner_ref, s32[256]{0:T(256)S(1)} %copy-done.9, bf16[8,2,128,128]{3,2,1,0:T(8,128)(2,1)S(1)} %copy-done.3), custom_call_target="tpu_custom_call" | custom-call | tf_op jit(solution)/shard_map/pick_pages/pallas_call | solution.py:115
  25.2 11.6 %all-to-all-done.slots_ref = bf16[16,272,128]{2,1,0:T(8,128)(2,1)} async-done(((bf16[16,272,128]{2,1,0:T(8,128)(2,1)}), bf16[16,272,128]{2,1,0:T(8,128)(2,1)}, u32[]{:S(2)}, u32[]{:S(2)}) %all-to-all-start) | async-done | bytes 1114144 | tf_op jit(solution)/shard_map/all_to_all | solution.py:522
  36.8 3.1 %select_slots.1 = (bf16[704,512]{1,0:T(8,128)(2,1)}, bf16[128,640]{1,0:T(8,128)(2,1)}) custom-call(s32[4]{0:T(128)} %adapter_ref.3, s32[16]{0:T(128)} %position_ref.3, bf16[16,272,128]{2,1,0:T(8,128)(2,1)} %all-to-all-done.slots_ref, bf16[512,512]{1,0:T(8,128)(2,1)} %refs_10_.1), custom_call_target="tpu_custom_call" | custom-call | tf_op jit(solution)/shard_map/select_slots/pallas_call | solution.py:180
  41.6 2.4 %collective-permute-start.3 = (bf16[704,512]{1,0:T(8,128)(2,1)}, bf16[704,512]{1,0:T(8,128)(2,1)S(1)}, u32[]{:S(2)}, u32[]{:S(2)}) collective-permute-start(bf16[704,512]{1,0:T(8,128)(2,1)} %get-tuple-element.27.refs_0_.refs_8_.refs_16_), channel_id=1, source_target_pairs={{0,6},{1,7},{2,0},{3,1},{4,2},{5,3},{6,4},{7,5},{8,14},{9,15},{10,... | collective-permute-start | bytes 2162696 | tf_op jit(solution)/shard_map/ppermute | solution.py:46
  44.0 7.5 %all-to-all-start.1 = ((bf16[16,512,128]{2,1,0:T(8,128)(2,1)}), bf16[16,512,128]{2,1,0:T(8,128)(2,1)}, u32[]{:S(2)}, u32[]{:S(2)}) async-start(bf16[16,512,128]{2,1,0:T(8,128)(2,1)} %bitcast.16), calls=%async_computation.1 | async-start | bytes 4194304 | tf_op jit(solution)/shard_map/all_to_all | solution.py:527
  52.2 2.6 %collective-permute-done.1.refs_2_.refs_10_.refs_18_ = bf16[704,512]{1,0:T(8,128)(2,1)S(1)} collective-permute-done((bf16[704,512]{1,0:T(8,128)(2,1)}, bf16[704,512]{1,0:T(8,128)(2,1)S(1)}, u32[]{:S(2)}, u32[]{:S(2)}) %collective-permute-start.1) | collective-permute-done | bytes 720928 | tf_op jit(solution)/shard_map/ppermute | solution.py:45
  55.6 2.7 %collective-permute-start.6 = (bf16[352,512]{1,0:T(8,128)(2,1)}, bf16[352,512]{1,0:T(8,128)(2,1)}, u32[]{:S(2)}, u32[]{:S(2)}) collective-permute-start(bf16[352,512]{1,0:T(8,128)(2,1)} %slice.49), channel_id=1, source_target_pairs={{0,6},{1,7},{2,0},{3,1},{4,2},{5,3},{6,4},{7,5},{8,14},{9,15},{10,... | collective-permute-start | bytes 1081352 | tf_op jit(solution)/shard_map/ppermute | solution.py:41
  61.5 9.3 %collective-permute-start = (bf16[704,512]{1,0:T(8,128)(2,1)S(1)}, bf16[704,512]{1,0:T(8,128)(2,1)}, u32[]{:S(2)}, u32[]{:S(2)}) collective-permute-start(bf16[704,512]{1,0:T(8,128)(2,1)S(1)} %copy-done), channel_id=1, source_target_pairs={{0,1},{1,0},{2,3},{3,2},{4,5},{5,4},{6,7},{7,6},{8,9},{9,8},{10,11... | collective-permute-start | bytes 2162696 | tf_op jit(solution)/shard_map/ppermute | solution.py:51
  72.4 1.9 %collective-permute-start.7 = (bf16[704,512]{1,0:T(8,128)(2,1)S(1)}, bf16[704,512]{1,0:T(8,128)(2,1)}, u32[]{:S(2)}, u32[]{:S(2)}) collective-permute-start(bf16[704,512]{1,0:T(8,128)(2,1)S(1)} %constant_dynamic-update-slice_fusion.refs_6_.refs_14_.refs_22_), channel_id=1, source_target_pairs={{0,1},{1,0},{2,3},{3,2},{4,5},{5,4},{6,7},{7,6},{8,9},{9,8},{10,11... | collective-permute-start | bytes 2162696 | tf_op jit(solution)/shard_map/ppermute | solution.py:51
  78.8 2.2 %sine_select_fusion.rope_hbm = f32[512,128]{1,0:T(8,128)} fusion(f32[128]{0:T(128)S(1)} %pad_maximum_fusion, s32[512]{0:T(512)S(1)} %get-tuple-element.54, s32[512]{0:T(512)S(1)} %get-tuple-element.55, s32[512]{0:T(512)S(1)} %get-tuple-element.56, s32[512]{0:T(512)S(1)} %get-tuple-element.57, pred[512]{0:T(512)(128)(4,1)S(1)} %get-tuple-element.50, ...), kind=kLoop, calls=%fused_computation | loop fusion | flops 458752 | bytes 273024 | tf_op jit(solution)/shard_map/jit(_where)/select_n | solution.py:541
  81.0 7.5 %norm_low.1 = (bf16[4,512,1024]{2,1,0:T(8,128)(2,1)}, bf16[512,128]{1,0:T(8,128)(2,1)}, bf16[8,2,256,128]{3,2,1,0:T(8,128)(2,1)}) custom-call(s32[2]{0:T(128)S(1)} %copy-done.6, s32[1,4]{1,0:T(1,128)S(1)} %copy-done.4, bf16[704,512]{1,0:T(8,128)(2,1)S(1)} %copy-done, bf16[704,512]{1,0:T(8,128)(2,1)} %collective-permute-done.refs_1_.refs_9_.refs_17_, ...), custom_call_target="tpu_custom_call" | custom-call | tf_op jit(solution)/shard_map/norm_low/pallas_call | solution.py:223
  88.5 6.9 %all-to-all-done.1 = bf16[16,512,128]{2,1,0:T(8,128)(2,1)} async-done(((bf16[16,512,128]{2,1,0:T(8,128)(2,1)}), bf16[16,512,128]{2,1,0:T(8,128)(2,1)}, u32[]{:S(2)}, u32[]{:S(2)}) %all-to-all-start.1) | async-done | bytes 2097184 | tf_op jit(solution)/shard_map/all_to_all | solution.py:527
  95.4 9.2 %all-gather.5.cloned.1.call-done = bf16[4096,768]{1,0:T(8,128)(2,1)} async-done(((bf16[256,768]{1,0:T(8,128)(2,1)}), bf16[4096,768]{1,0:T(8,128)(2,1)}) %all-gather.5.cloned.1.call-update) | async-done | bytes 6291472 | tf_op jit(solution)/shard_map/all_gather | solution.py:518
  104.6 17.6 %attention.1 = (bf16[512,512]{1,0:T(8,128)(2,1)S(1)}, bf16[2,512,128]{2,1,0:T(8,128)(2,1)}) custom-call(s32[1,4]{1,0:T(1,128)S(1)} %copy-done.4, s32[4]{0:T(128)S(1)} %copy-done.5, s32[16]{0:T(128)S(1)} %get-tuple-element.22.place_ref, bf16[4,512,1024]{2,1,0:T(8,128)(2,1)} %get-tuple-element.31.normed_ref, bf16[16,256,768]{2,1,0:T(8,128)(2,1)} %bitcast.17, ...), custom_call_target="tpu_custom_call" | custom-call | tf_op jit(solution)/shard_map/attention/pallas_call | solution.py:395
  122.3 2.7 %collective-permute-start.11 = (bf16[512,512]{1,0:T(8,128)(2,1)S(1)}, bf16[512,512]{1,0:T(8,128)(2,1)S(1)}, u32[]{:S(2)}, u32[]{:S(2)}) collective-permute-start(bf16[512,512]{1,0:T(8,128)(2,1)S(1)} %get-tuple-element.38.refs_0_), channel_id=1, source_target_pairs={{0,6},{1,7},{2,0},{3,1},{4,2},{5,3},{6,4},{7,5},{8,14},{9,15},{10,... | collective-permute-start | bytes 1572872 | tf_op jit(solution)/shard_map/ppermute | solution.py:46
  125.0 11.3 %collective-permute-done.9.refs_2_ = bf16[512,512]{1,0:T(8,128)(2,1)S(1)} collective-permute-done((bf16[512,512]{1,0:T(8,128)(2,1)S(1)}, bf16[512,512]{1,0:T(8,128)(2,1)S(1)}, u32[]{:S(2)}, u32[]{:S(2)}) %collective-permute-start.9) | collective-permute-done | bytes 524320 | tf_op jit(solution)/shard_map/ppermute | solution.py:45
  136.4 2.7 %collective-permute-start.14 = (bf16[256,512]{1,0:T(8,128)(2,1)S(1)}, bf16[256,512]{1,0:T(8,128)(2,1)S(1)}, u32[]{:S(2)}, u32[]{:S(2)}) collective-permute-start(bf16[256,512]{1,0:T(8,128)(2,1)S(1)} %slice.51), channel_id=1, source_target_pairs={{0,6},{1,7},{2,0},{3,1},{4,2},{5,3},{6,4},{7,5},{8,14},{9,15},{10,... | collective-permute-start | bytes 786440 | tf_op jit(solution)/shard_map/ppermute | solution.py:41
  139.1 2.2 %collective-permute-start.8 = (bf16[512,512]{1,0:T(8,128)(2,1)S(1)}, bf16[512,512]{1,0:T(8,128)(2,1)S(1)}, u32[]{:S(2)}, u32[]{:S(2)}) collective-permute-start(bf16[512,512]{1,0:T(8,128)(2,1)S(1)} %get-tuple-element.38.refs_0_), channel_id=1, source_target_pairs={{0,1},{1,0},{2,3},{3,2},{4,5},{5,4},{6,7},{7,6},{8,9},{9,8},{10,11... | collective-permute-start | bytes 1572872 | tf_op jit(solution)/shard_map/ppermute | solution.py:51
  141.8 2.1 %collective-permute-done.13 = bf16[256,512]{1,0:T(8,128)(2,1)S(1)} collective-permute-done((bf16[256,512]{1,0:T(8,128)(2,1)S(1)}, bf16[256,512]{1,0:T(8,128)(2,1)S(1)}, u32[]{:S(2)}, u32[]{:S(2)}) %collective-permute-start.13) | collective-permute-done | bytes 262176 | tf_op jit(solution)/shard_map/ppermute | solution.py:41
  143.9 2.7 %collective-permute-start.15 = (bf16[512,512]{1,0:T(8,128)(2,1)S(1)}, bf16[512,512]{1,0:T(8,128)(2,1)}, u32[]{:S(2)}, u32[]{:S(2)}) collective-permute-start(bf16[512,512]{1,0:T(8,128)(2,1)S(1)} %constant_dynamic-update-slice_fusion.2.refs_6_), channel_id=1, source_target_pairs={{0,1},{1,0},{2,3},{3,2},{4,5},{5,4},{6,7},{7,6},{8,9},{9,8},{10,11... | collective-permute-start | bytes 1572872 | tf_op jit(solution)/shard_map/ppermute | solution.py:51
  146.6 10.0 %all-gather.7.cloned.1.call-done = bf16[4352,512]{1,0:T(8,128)(2,1)} async-done(((bf16[272,512]{1,0:T(8,128)(2,1)}), bf16[4352,512]{1,0:T(8,128)(2,1)}) %all-gather.7.cloned.1.call-update) | async-done | bytes 4456464 | tf_op jit(solution)/shard_map/all_gather | solution.py:526
  157.7 8.9 %output.1 = bf16[512,512]{1,0:T(8,128)(2,1)} custom-call(s32[2]{0:T(128)S(1)} %copy-done.6, s32[1,4]{1,0:T(1,128)S(1)} %copy-done.4, s32[4]{0:T(128)S(1)} %copy-done.7, s32[16]{0:T(128)S(1)} %copy-done.8, bf16[512,512]{1,0:T(8,128)(2,1)} %copy-done.2, bf16[512,512]{1,0:T(8,128)(2,1)} %copy-done.13, bf16[512,512]{1,0:T(8,128)(2,1)} %copy-done.10, ...), custom_call_target="tpu_custom_call" | custom-call | tf_op jit(solution)/shard_map/output/pallas_call | solution.py:473
  (84 shorter events, 14.3 us)
Async XLA Ops:
  7.2 97.4 %all-gather.5.cloned.1.call-start = ((), (), s32[]{:S(2)}) async-start(), calls=%async_computation.2 | async-start | bytes 6684672 | tf_op jit(solution)/shard_map/all_gather | solution.py:518
  11.5 25.3 %all-to-all-start = ((bf16[16,272,128]{2,1,0:T(8,128)(2,1)}), bf16[16,272,128]{2,1,0:T(8,128)(2,1)}, u32[]{:S(2)}, u32[]{:S(2)}) async-start(bf16[16,272,128]{2,1,0:T(8,128)(2,1)} %get-tuple-element.24), calls=%async_computation | async-start | bytes 2228224 | tf_op jit(solution)/shard_map/all_to_all | solution.py:522
  19.1 137.5 %all-gather.7.cloned.1.call-start = ((), (), s32[]{:S(2)}) async-start(), calls=%async_computation.3 | async-start | bytes 4734976 | tf_op jit(solution)/shard_map/all_gather | solution.py:526
  40.0 14.8 %collective-permute-start.1 = (bf16[704,512]{1,0:T(8,128)(2,1)}, bf16[704,512]{1,0:T(8,128)(2,1)S(1)}, u32[]{:S(2)}, u32[]{:S(2)}) collective-permute-start(bf16[704,512]{1,0:T(8,128)(2,1)} %get-tuple-element.27.refs_0_.refs_8_.refs_16_), channel_id=1, source_target_pairs={{0,2},{1,3},{2,4},{3,5},{4,6},{5,7},{6,0},{7,1},{8,10},{9,11},{10,... | collective-permute-start | bytes 2162696 | tf_op jit(solution)/shard_map/ppermute | solution.py:45
  41.6 13.3 %collective-permute-start.3 = (bf16[704,512]{1,0:T(8,128)(2,1)}, bf16[704,512]{1,0:T(8,128)(2,1)S(1)}, u32[]{:S(2)}, u32[]{:S(2)}) collective-permute-start(bf16[704,512]{1,0:T(8,128)(2,1)} %get-tuple-element.27.refs_0_.refs_8_.refs_16_), channel_id=1, source_target_pairs={{0,6},{1,7},{2,0},{3,1},{4,2},{5,3},{6,4},{7,5},{8,14},{9,15},{10,... | collective-permute-start | bytes 2162696 | tf_op jit(solution)/shard_map/ppermute | solution.py:46
  44.0 51.4 %all-to-all-start.1 = ((bf16[16,512,128]{2,1,0:T(8,128)(2,1)}), bf16[16,512,128]{2,1,0:T(8,128)(2,1)}, u32[]{:S(2)}, u32[]{:S(2)}) async-start(bf16[16,512,128]{2,1,0:T(8,128)(2,1)} %bitcast.16), calls=%async_computation.1 | async-start | bytes 4194304 | tf_op jit(solution)/shard_map/all_to_all | solution.py:527
  51.5 23.5 %copy-start.5 = (s32[4]{0:T(128)S(1)}, s32[4]{0:T(128)}, u32[]{:S(2)}) copy-start(s32[4]{0:T(128)} %cache_ref.1) | copy-start | bytes 52
  54.8 16.5 %collective-permute-start.5 = (bf16[352,512]{1,0:T(8,128)(2,1)S(1)}, bf16[352,512]{1,0:T(8,128)(2,1)S(1)}, u32[]{:S(2)}, u32[]{:S(2)}) collective-permute-start(bf16[352,512]{1,0:T(8,128)(2,1)S(1)} %slice.48), channel_id=1, source_target_pairs={{0,2},{1,3},{2,4},{3,5},{4,6},{5,7},{6,0},{7,1},{8,10},{9,11},{10,... | collective-permute-start | bytes 1081352 | tf_op jit(solution)/shard_map/ppermute | solution.py:41
  55.6 15.7 %collective-permute-start.6 = (bf16[352,512]{1,0:T(8,128)(2,1)}, bf16[352,512]{1,0:T(8,128)(2,1)}, u32[]{:S(2)}, u32[]{:S(2)}) collective-permute-start(bf16[352,512]{1,0:T(8,128)(2,1)} %slice.49), channel_id=1, source_target_pairs={{0,6},{1,7},{2,0},{3,1},{4,2},{5,3},{6,4},{7,5},{8,14},{9,15},{10,... | collective-permute-start | bytes 1081352 | tf_op jit(solution)/shard_map/ppermute | solution.py:41
  61.5 19.4 %collective-permute-start = (bf16[704,512]{1,0:T(8,128)(2,1)S(1)}, bf16[704,512]{1,0:T(8,128)(2,1)}, u32[]{:S(2)}, u32[]{:S(2)}) collective-permute-start(bf16[704,512]{1,0:T(8,128)(2,1)S(1)} %copy-done), channel_id=1, source_target_pairs={{0,1},{1,0},{2,3},{3,2},{4,5},{5,4},{6,7},{7,6},{8,9},{9,8},{10,11... | collective-permute-start | bytes 2162696 | tf_op jit(solution)/shard_map/ppermute | solution.py:51
  70.8 10.2 %collective-permute-start.2 = (bf16[704,512]{1,0:T(8,128)(2,1)S(1)}, bf16[704,512]{1,0:T(8,128)(2,1)}, u32[]{:S(2)}, u32[]{:S(2)}) collective-permute-start(bf16[704,512]{1,0:T(8,128)(2,1)S(1)} %collective-permute-done.1.refs_2_.refs_10_.refs_18_), channel_id=1, source_target_pairs={{0,1},{1,0},{2,3},{3,2},{4,5},{5,4},{6,7},{7,6},{8,9},{9,8},{10,11... | collective-permute-start | bytes 2162696 | tf_op jit(solution)/shard_map/ppermute | solution.py:51
  70.9 10.1 %collective-permute-start.4 = (bf16[704,512]{1,0:T(8,128)(2,1)S(1)}, bf16[704,512]{1,0:T(8,128)(2,1)}, u32[]{:S(2)}, u32[]{:S(2)}) collective-permute-start(bf16[704,512]{1,0:T(8,128)(2,1)S(1)} %collective-permute-done.3.refs_4_.refs_12_.refs_20_), channel_id=1, source_target_pairs={{0,1},{1,0},{2,3},{3,2},{4,5},{5,4},{6,7},{7,6},{8,9},{9,8},{10,11... | collective-permute-start | bytes 2162696 | tf_op jit(solution)/shard_map/ppermute | solution.py:51
  72.4 8.6 %collective-permute-start.7 = (bf16[704,512]{1,0:T(8,128)(2,1)S(1)}, bf16[704,512]{1,0:T(8,128)(2,1)}, u32[]{:S(2)}, u32[]{:S(2)}) collective-permute-start(bf16[704,512]{1,0:T(8,128)(2,1)S(1)} %constant_dynamic-update-slice_fusion.refs_6_.refs_14_.refs_22_), channel_id=1, source_target_pairs={{0,1},{1,0},{2,3},{3,2},{4,5},{5,4},{6,7},{7,6},{8,9},{9,8},{10,11... | collective-permute-start | bytes 2162696 | tf_op jit(solution)/shard_map/ppermute | solution.py:51
  122.2 34.5 %copy-start.2 = (bf16[512,512]{1,0:T(8,128)(2,1)}, bf16[512,512]{1,0:T(8,128)(2,1)S(1)}, u32[]{:S(2)}) copy-start(bf16[512,512]{1,0:T(8,128)(2,1)S(1)} %get-tuple-element.38.refs_0_) | copy-start | bytes 1572868
  122.2 35.5 %copy-start.7 = (s32[4]{0:T(128)S(1)}, s32[4]{0:T(128)}, u32[]{:S(2)}) copy-start(s32[4]{0:T(128)} %adapter_ref.3) | copy-start | bytes 52
  122.2 35.5 %copy-start.8 = (s32[16]{0:T(128)S(1)}, s32[16]{0:T(128)}, u32[]{:S(2)}) copy-start(s32[16]{0:T(128)} %position_ref.3) | copy-start | bytes 196
  122.2 14.0 %collective-permute-start.9 = (bf16[512,512]{1,0:T(8,128)(2,1)S(1)}, bf16[512,512]{1,0:T(8,128)(2,1)S(1)}, u32[]{:S(2)}, u32[]{:S(2)}) collective-permute-start(bf16[512,512]{1,0:T(8,128)(2,1)S(1)} %get-tuple-element.38.refs_0_), channel_id=1, source_target_pairs={{0,2},{1,3},{2,4},{3,5},{4,6},{5,7},{6,0},{7,1},{8,10},{9,11},{10,... | collective-permute-start | bytes 1572872 | tf_op jit(solution)/shard_map/ppermute | solution.py:45
  122.3 14.0 %collective-permute-start.11 = (bf16[512,512]{1,0:T(8,128)(2,1)S(1)}, bf16[512,512]{1,0:T(8,128)(2,1)S(1)}, u32[]{:S(2)}, u32[]{:S(2)}) collective-permute-start(bf16[512,512]{1,0:T(8,128)(2,1)S(1)} %get-tuple-element.38.refs_0_), channel_id=1, source_target_pairs={{0,6},{1,7},{2,0},{3,1},{4,2},{5,3},{6,4},{7,5},{8,14},{9,15},{10,... | collective-permute-start | bytes 1572872 | tf_op jit(solution)/shard_map/ppermute | solution.py:46
  136.3 7.6 %collective-permute-start.13 = (bf16[256,512]{1,0:T(8,128)(2,1)S(1)}, bf16[256,512]{1,0:T(8,128)(2,1)S(1)}, u32[]{:S(2)}, u32[]{:S(2)}) collective-permute-start(bf16[256,512]{1,0:T(8,128)(2,1)S(1)} %slice.50), channel_id=1, source_target_pairs={{0,2},{1,3},{2,4},{3,5},{4,6},{5,7},{6,0},{7,1},{8,10},{9,11},{10,... | collective-permute-start | bytes 786440 | tf_op jit(solution)/shard_map/ppermute | solution.py:41
  136.4 7.5 %collective-permute-start.14 = (bf16[256,512]{1,0:T(8,128)(2,1)S(1)}, bf16[256,512]{1,0:T(8,128)(2,1)S(1)}, u32[]{:S(2)}, u32[]{:S(2)}) collective-permute-start(bf16[256,512]{1,0:T(8,128)(2,1)S(1)} %slice.51), channel_id=1, source_target_pairs={{0,6},{1,7},{2,0},{3,1},{4,2},{5,3},{6,4},{7,5},{8,14},{9,15},{10,... | collective-permute-start | bytes 786440 | tf_op jit(solution)/shard_map/ppermute | solution.py:41
  139.1 17.6 %collective-permute-start.8 = (bf16[512,512]{1,0:T(8,128)(2,1)S(1)}, bf16[512,512]{1,0:T(8,128)(2,1)S(1)}, u32[]{:S(2)}, u32[]{:S(2)}) collective-permute-start(bf16[512,512]{1,0:T(8,128)(2,1)S(1)} %get-tuple-element.38.refs_0_), channel_id=1, source_target_pairs={{0,1},{1,0},{2,3},{3,2},{4,5},{5,4},{6,7},{7,6},{8,9},{9,8},{10,11... | collective-permute-start | bytes 1572872 | tf_op jit(solution)/shard_map/ppermute | solution.py:51
  141.3 15.4 %collective-permute-start.10 = (bf16[512,512]{1,0:T(8,128)(2,1)S(1)}, bf16[512,512]{1,0:T(8,128)(2,1)S(1)}, u32[]{:S(2)}, u32[]{:S(2)}) collective-permute-start(bf16[512,512]{1,0:T(8,128)(2,1)S(1)} %collective-permute-done.9.refs_2_), channel_id=1, source_target_pairs={{0,1},{1,0},{2,3},{3,2},{4,5},{5,4},{6,7},{7,6},{8,9},{9,8},{10,11... | collective-permute-start | bytes 1572872 | tf_op jit(solution)/shard_map/ppermute | solution.py:51
  141.3 15.4 %collective-permute-start.12 = (bf16[512,512]{1,0:T(8,128)(2,1)S(1)}, bf16[512,512]{1,0:T(8,128)(2,1)}, u32[]{:S(2)}, u32[]{:S(2)}) collective-permute-start(bf16[512,512]{1,0:T(8,128)(2,1)S(1)} %collective-permute-done.11.refs_4_), channel_id=1, source_target_pairs={{0,1},{1,0},{2,3},{3,2},{4,5},{5,4},{6,7},{7,6},{8,9},{9,8},{10,11... | collective-permute-start | bytes 1572872 | tf_op jit(solution)/shard_map/ppermute | solution.py:51
  143.9 12.8 %collective-permute-start.15 = (bf16[512,512]{1,0:T(8,128)(2,1)S(1)}, bf16[512,512]{1,0:T(8,128)(2,1)}, u32[]{:S(2)}, u32[]{:S(2)}) collective-permute-start(bf16[512,512]{1,0:T(8,128)(2,1)S(1)} %constant_dynamic-update-slice_fusion.2.refs_6_), channel_id=1, source_target_pairs={{0,1},{1,0},{2,3},{3,2},{4,5},{5,4},{6,7},{7,6},{8,9},{9,8},{10,11... | collective-permute-start | bytes 1572872 | tf_op jit(solution)/shard_map/ppermute | solution.py:51
  (15 other events, 197.6 us)
Sparse Core Ops, SparseCore 0:
  10.2 94.3 all-gather.4
  106.7 49.8 all-gather.6

commit v8 on v6

--- a/solution.py
+++ b/solution.py
@@ -192,7 +192,8 @@
 
 def norm_body(me_ref, length_ref, *refs):
     blocks, maps = refs[:8], refs[8:16]
-    gain_ref, normed_ref, low_ref = refs[16:]
+    outs = refs[16:24]
+    gain_ref, normed_ref, low_ref, turned_ref = refs[24:]
     order = col_order(me_ref[1])
     values = [b[...].astype(F32) for b in blocks]
     total = sum(jnp.sum(v * v, axis=-1, keepdims=True) for v in values)
@@ -207,27 +208,41 @@
     prompt = per_token(prompt_rows(length_ref), range(PROMPTS), token)
     mine = lax.broadcasted_iota(jnp.int32, low.shape, 1) // 32 == prompt
     low_ref[...] = jnp.where(mine, low, 0.0).astype(BF)
+    for k in range(4):
+
+        @pl.when(pl.program_id(0) == k)
+        def _():
+            for b in range(2):
+                down = outs[2 * k + b][...].astype(F32)
+                turned = jnp.concatenate([down, down], axis=0).T.astype(BF)
+                turned_ref[b, 0], turned_ref[b, 1] = turned[:256], turned[256:]
 
 
 def norm_low(me, lengths, blocks, gain):
     rows = 128
     return pl.pallas_call(
         norm_body,
-        out_shape=(pltpu.HBM((4, TOK, 2 * FEAT), BF), pltpu.HBM((TOK, 128), BF)),
+        out_shape=(
+            pltpu.HBM((4, TOK, 2 * FEAT), BF),
+            pltpu.HBM((TOK, 128), BF),
+            pltpu.HBM((8, 2, 256, 128), BF),
+        ),
         grid_spec=pltpu.PrefetchScalarGridSpec(
             num_scalar_prefetch=2,
             grid=(TOK // rows,),
             in_specs=[pl.BlockSpec((rows, FEAT), lambda i, *_: (i, 0))] * 8
             + [pl.BlockSpec((128, FEAT), lambda i, *_: (DOWN // 128, 0))] * 8
+            + [pl.BlockSpec((64, FEAT), lambda i, *_: (ODOWN // 64, 0))] * 8
             + [whole(8, 1, FEAT)],
             out_specs=(
                 pl.BlockSpec((4, rows, 2 * FEAT), lambda i, *_: (0, i, 0)),
                 pl.BlockSpec((rows, 128), lambda i, *_: (i, 0)),
+                pl.BlockSpec((2, 2, 256, 128), lambda i, *_: (i, 0, 0, 0)),
             ),
         ),
         compiler_params=vmem(20),
         name="norm_low",
-    )(me, lengths, *blocks, *blocks, gain)
+    )(me, lengths, *blocks, *blocks, *blocks, gain)
 
 
 BLOCK = 64
@@ -416,71 +431,98 @@
     )
 
 
-def out_body(
-    me_ref, length_ref, adapter_ref, position_ref, *refs
-):
-    blocks, sources = refs[:8], refs[8:16]
-    weight_ref, hidden_hbm, out_ref, x, w, od, oup, hidden, acc, sems = refs[16:]
+def low_body(length_ref, *refs):
+    blocks, turned_ref, low_ref = refs[:8], refs[8], refs[9]
+    low = jnp.zeros((TOK, 128), F32)
+    for b in range(8):
+        low += jnp.dot(blocks[b][...], turned_ref[b].reshape(FEAT, 128), preferred_element_type=F32)
+    token = lax.broadcasted_iota(jnp.int32, low.shape, 0)
+    lane = lax.broadcasted_iota(jnp.int32, low.shape, 1)
+    prompt = per_token(prompt_rows(length_ref), range(PROMPTS), token)
+    low = jnp.where((lane & 63) // 16 == prompt, low, 0.0)
+    high = low.astype(BF)
+    rest = low - high.astype(F32)
+    middle = rest.astype(BF)
+    least = (rest - middle.astype(F32)).astype(BF)
+    low_ref[:, :128] = jnp.where(lane < 64, high, middle)
+    low_ref[:, 128:] = jnp.where(lane < 64, least, jnp.zeros_like(least))
+
+
+def output_low(lengths, blocks, turned):
+    return pl.pallas_call(
+        low_body,
+        out_shape=pltpu.HBM((TOK, 256), BF),
+        grid_spec=pltpu.PrefetchScalarGridSpec(
+            num_scalar_prefetch=1,
+            grid=(1,),
+            in_specs=[whole(TOK, FEAT)] * 8 + [whole(8, 2, 256, 128)],
+            out_specs=whole(TOK, 256),
+        ),
+        compiler_params=vmem(20),
+        name="output_low",
+    )(lengths, *blocks, in_hbm(turned))
+
+
+def out_body(me_ref, adapter_ref, position_ref, *refs):
+    blocks = refs[:8]
+    low_hbm, weight_ref, hidden_hbm, out_ref, x, w, oup, low_ref, hidden, acc, sems = refs[8:]
     order = col_order(me_ref[1])
     copies = []
     for b in range(8):
-        side = pl.ds(b % 2 * FEAT, FEAT)
         rows = weight_ref.at[pl.ds(2 * order[b], 2), pl.ds(0, 256)]
         copies.append(pltpu.make_async_copy(rows, w.at[b // 2, pl.ds(b % 2 * 2, 2)], sems.at[b]))
+        side = pl.ds(b % 2 * FEAT, FEAT)
         copies.append(pltpu.make_async_copy(blocks[b], x.at[b // 2, :, side], sems.at[8 + b]))
-        copies.append(pltpu.make_async_copy(sources[b].at[pl.ds(ODOWN, 64)], od.at[b // 2, :, side], sems.at[16 + b]))
-    last = [pltpu.make_async_copy(hidden_hbm, hidden, sems.at[24])]
+    last = [
+        pltpu.make_async_copy(hidden_hbm, hidden, sems.at[16]),
+        pltpu.make_async_copy(low_hbm, low_ref, sems.at[17]),
+    ]
     for p in range(PROMPTS):
         slot = position_ref[adapter_ref[p]]
         rows = weight_ref.at[slot, pl.ds(256, 16)]
-        last.append(pltpu.make_async_copy(rows, oup.at[pl.ds(p * 16, 16)], sems.at[25 + p]))
+        last.append(pltpu.make_async_copy(rows, oup.at[pl.ds(p * 16, 16)], sems.at[18 + p]))
     for copy in copies + last:
         copy.start()
-    low = jnp.zeros((TOK, 64), F32)
     for i in range(4):
-        for copy in copies[6 * i : 6 * i + 6]:
+        for copy in copies[4 * i : 4 * i + 4]:
             copy.wait()
         part = jnp.dot(x[i], w[i].reshape(2 * FEAT, FEAT), preferred_element_type=F32)
         if i == 0:
             acc[...] = part
         else:
             acc[...] += part
-        low += lax.dot_general(x[i], od[i], (((1,), (1,)), ((), ())), preferred_element_type=F32)
-    token = lax.broadcasted_iota(jnp.int32, low.shape, 0)
-    prompt = per_token(prompt_rows(length_ref), range(PROMPTS), token)
-    mine = lax.broadcasted_iota(jnp.int32, low.shape, 1) // 16 == prompt
-    low = jnp.where(mine, low, 0.0)
     for copy in last:
         copy.wait()
-    change = jnp.dot(low, oup[...].astype(F32), precision=lax.Precision.HIGHEST, preferred_element_type=F32)
+    maps = jnp.concatenate([oup[...]] * 4, axis=0)
+    change = jnp.dot(low_ref[...], maps, preferred_element_type=F32)
     out_ref[...] = (hidden[...].astype(F32) + acc[...] + 0.5 * change).astype(BF)
 
 
-def output(me, lengths, adapter, position, blocks, sources, weight, hidden):
+def output(me, adapter, position, blocks, low, weight, hidden):
     hbm = pl.BlockSpec(memory_space=pl.ANY)
     return pl.pallas_call(
         out_body,
         out_shape=jax.ShapeDtypeStruct((TOK, FEAT), BF),
         grid_spec=pltpu.PrefetchScalarGridSpec(
-            num_scalar_prefetch=4,
+            num_scalar_prefetch=3,
             grid=(1,),
-            in_specs=[hbm] * 18,
+            in_specs=[hbm] * 11,
             out_specs=whole(TOK, FEAT),
             scratch_shapes=[
                 pltpu.VMEM((4, TOK, 2 * FEAT), BF),
                 pltpu.VMEM((4, 4, 256, FEAT), BF),
-                pltpu.VMEM((4, 64, 2 * FEAT), BF),
                 pltpu.VMEM((64, FEAT), BF),
+                pltpu.VMEM((TOK, 256), BF),
                 pltpu.VMEM((TOK, FEAT), BF),
                 pltpu.VMEM((TOK, FEAT), F32),
-                pltpu.SemaphoreType.DMA((29,)),
+                pltpu.SemaphoreType.DMA((22,)),
             ],
         ),
         compiler_params=vmem(24),
         name="output",
     )(
-        me, lengths, adapter, position,
-        *map(in_hbm, blocks), *map(in_hbm, sources), in_hbm(weight), in_hbm(hidden),
+        me, adapter, position,
+        *map(in_hbm, blocks), in_hbm(low), in_hbm(weight), in_hbm(hidden),
     )
 
 
@@ -534,7 +576,7 @@
     front = lax.broadcasted_iota(jnp.int32, (TOK, HEAD), 1) < HEAD // 2
     rope = jnp.where(front, jnp.cos(angles), jnp.sin(angles))
 
-    normed, low = norm_low(me, prompt_length, blocks, input_norm_gain.reshape(8, 1, FEAT))
+    normed, low, turned = norm_low(me, prompt_length, blocks, input_norm_gain.reshape(8, 1, FEAT))
     gains = jnp.stack([query_norm_gain, key_norm_gain]).astype(F32)
     weight, normed, low, pages, rope, gains = lax.optimization_barrier((weight, normed, low, pages, rope, gains))
     attended, new_cache = attention(
@@ -551,9 +593,9 @@
         pages,
     )
     attended = gather_col(attended, 256)
-    hidden_output = output(
-        me, prompt_length, prompt_adapter, adapter_position, attended, blocks, rest, hidden_input
-    )
+    low = output_low(prompt_length, attended, turned)
+    rest, low = lax.optimization_barrier((rest, low))
+    hidden_output = output(me, prompt_adapter, adapter_position, attended, low, rest, hidden_input)
     return hidden_output, new_cache
 
 

time: 170 us -> 165 us (0.971)
  waiting for transfers between devices: 50.5 us -> 46.6 us
    all_gather x1, waiting for transfers between devices: 8.3 us -> 3.39 us  [on_device(): rest = lax.all_gather(rest, 'row', axis=0)]
    pallas_call x1, Pallas kernels: 9.86 us -> 5.94 us  [output(): pl.pallas_call(out_body, out_shape=jax.ShapeDtypeStruct((TOK, FEAT), BF),...]
    pallas_call x0 -> x1, Pallas kernels: none -> 3.73 us  [output_low(): pl.pallas_call(low_body, out_shape=pltpu.HBM((TOK, 256), BF), grid_spec=p...]
    unnamed x49 -> x47, local copies, waits for them, and re-layouts: 6.4 us -> 7.06 us
  transfers between devices with their start and end apart: 20 -> 20, of which waited for: 6 -> 7; matrix products, arithmetic and copies ran while one was open for 6% -> 6% of each run, Pallas kernels for 20% -> 22%
where the time goes in v8:
time: 165 us
  waiting for transfers between devices  46.6 us (28%)
  Pallas kernels  45.3 us (27%)
  starting transfers between devices  38.4 us (23%)
  between operations  17 us (10%)
  local copies, waits for them, and re-layouts  10.2 us (6%)
  other arithmetic  7.08 us (4%)
    ppermute x2, waiting for transfers between devices, ring4(): before = lax.ppermute(block, axis, perm(1))  17.9 us
    pallas_call x1, Pallas kernels, attention(): pl.pallas_call(attention_body, out_shape=(jax.ShapeDtypeStruct((TOK, FEAT...  17.7 us
    all_gather x1, waiting for transfers between devices, on_device(): weight = lax.all_gather(wide, 'row', axis=0)  17.5 us
    ppermute x8, starting transfers between devices, swap(): return lax.ppermute(block, 'col', SWAP)  12.7 us
    all_to_all x1, starting transfers between devices, on_device(): slots = lax.all_to_all(slots, 'row', 0, 0)  7.6 us
    pallas_call x1, Pallas kernels, norm_low(): pl.pallas_call(norm_body, out_shape=(pltpu.HBM((4, TOK, 2 * FEAT), BF), p...  7.47 us
    unnamed x47, local copies, waits for them, and re-layouts  7.06 us
    pallas_call x1, Pallas kernels, output(): pl.pallas_call(out_body, out_shape=jax.ShapeDtypeStruct((TOK, FEAT), BF),...  5.94 us
  transfers between devices with their start and end apart: 20, of which 7 were waited for; matrix products, arithmetic and copies ran while one was open for 6% of the time, Pallas kernels for 22%

profile of v8, /device:TPU:1, one launch (start us, length us, event | category | flops | bytes accessed | tf_op | source)
XLA Modules:
  0.0 164.6 jit_solution(5097540653469308760)
XLA Ops:
  7.9 2.9 %pack.1 = (bf16[272,768]{1,0:T(8,128)(2,1)}, bf16[272,512]{1,0:T(8,128)(2,1)}, bf16[16,48,512]{2,1,0:T(8,128)(2,1)}) custom-call(s32[2]{0:T(128)} %pad_add_fusion.me_ref, bf16[256,768]{1,0:T(8,128)(2,1)} %qkv_ref.1, bf16[256,512]{1,0:T(8,128)(2,1)} %wo_ref.1, bf16[1,16,640]{2,1,0:T(8,128)(2,1)} %up_ref.1, bf16[1,16,4096]{2,1,0:T(8,128)(2,1)} %oup_ref.1, ...), custom_call_target="tpu_custom_call" | custom-call | tf_op jit(solution)/shard_map/pack/pallas_call | solution.py:144
  10.8 7.6 %all-to-all-start = ((bf16[16,48,512]{2,1,0:T(8,128)(2,1)}), bf16[16,48,512]{2,1,0:T(8,128)(2,1)S(1)}, u32[]{:S(2)}, u32[]{:S(2)}) async-start(bf16[16,48,512]{2,1,0:T(8,128)(2,1)} %get-tuple-element.26), calls=%async_computation | async-start | bytes 1572864 | tf_op jit(solution)/shard_map/all_to_all | solution.py:559
  21.7 4.5 %pick_pages.1 = (bf16[16,2,2,128,128]{4,3,2,1,0:T(8,128)(2,1)S(1)}, s32[16]{0:T(128)S(1)}) custom-call(s32[2]{0:T(128)S(1)} %copy-done.13, s32[256,1]{1,0:T(8,128)S(1)} %copy.20.owner_ref, s32[256]{0:T(256)S(1)} %copy-done.17, bf16[8,2,128,128]{3,2,1,0:T(8,128)(2,1)S(1)} %copy-done.10), custom_call_target="tpu_custom_call" | custom-call | tf_op jit(solution)/shard_map/pick_pages/pallas_call | solution.py:115
  27.5 3.6 %all-to-all-done.slots_ref = bf16[16,48,512]{2,1,0:T(8,128)(2,1)S(1)} async-done(((bf16[16,48,512]{2,1,0:T(8,128)(2,1)}), bf16[16,48,512]{2,1,0:T(8,128)(2,1)S(1)}, u32[]{:S(2)}, u32[]{:S(2)}) %all-to-all-start) | async-done | bytes 786464 | tf_op jit(solution)/shard_map/all_to_all | solution.py:559
  32.0 3.1 %select_slots.1.refs_0_.refs_8_.refs_16_ = bf16[704,512]{1,0:T(8,128)(2,1)} custom-call(s32[4]{0:T(128)} %adapter_ref.5, s32[16]{0:T(128)} %position_ref.5, bf16[16,48,512]{2,1,0:T(8,128)(2,1)} %copy-done.18, bf16[512,512]{1,0:T(8,128)(2,1)} %refs_10_.1), custom_call_target="tpu_custom_call" | custom-call | tf_op jit(solution)/shard_map/select_slots/pallas_call | solution.py:180
  35.1 1.8 %collective-permute-start.1 = (bf16[704,512]{1,0:T(8,128)(2,1)}, bf16[704,512]{1,0:T(8,128)(2,1)S(1)}, u32[]{:S(2)}, u32[]{:S(2)}) collective-permute-start(bf16[704,512]{1,0:T(8,128)(2,1)} %select_slots.1.refs_0_.refs_8_.refs_16_), channel_id=1, source_target_pairs={{0,2},{1,3},{2,4},{3,5},{4,6},{5,7},{6,0},{7,1},{8,10},{9,11},{10,... | collective-permute-start | bytes 2162696 | tf_op jit(solution)/shard_map/ppermute | solution.py:45
  36.9 2.5 %collective-permute-start.3 = (bf16[704,512]{1,0:T(8,128)(2,1)}, bf16[704,512]{1,0:T(8,128)(2,1)S(1)}, u32[]{:S(2)}, u32[]{:S(2)}) collective-permute-start(bf16[704,512]{1,0:T(8,128)(2,1)} %select_slots.1.refs_0_.refs_8_.refs_16_), channel_id=1, source_target_pairs={{0,6},{1,7},{2,0},{3,1},{4,2},{5,3},{6,4},{7,5},{8,14},{9,15},{10,... | collective-permute-start | bytes 2162696 | tf_op jit(solution)/shard_map/ppermute | solution.py:46
  39.4 5.5 %all-to-all-start.1 = ((bf16[16,512,128]{2,1,0:T(8,128)(2,1)}), bf16[16,512,128]{2,1,0:T(8,128)(2,1)}, u32[]{:S(2)}, u32[]{:S(2)}) async-start(bf16[16,512,128]{2,1,0:T(8,128)(2,1)} %bitcast.16), calls=%async_computation.1 | async-start | bytes 4194304 | tf_op jit(solution)/shard_map/all_to_all | solution.py:564
  45.6 6.3 %collective-permute-done.1.refs_2_.refs_10_.refs_18_ = bf16[704,512]{1,0:T(8,128)(2,1)S(1)} collective-permute-done((bf16[704,512]{1,0:T(8,128)(2,1)}, bf16[704,512]{1,0:T(8,128)(2,1)S(1)}, u32[]{:S(2)}, u32[]{:S(2)}) %collective-permute-start.1) | collective-permute-done | bytes 720928 | tf_op jit(solution)/shard_map/ppermute | solution.py:45
  52.7 2.7 %collective-permute-start.6 = (bf16[352,512]{1,0:T(8,128)(2,1)}, bf16[352,512]{1,0:T(8,128)(2,1)}, u32[]{:S(2)}, u32[]{:S(2)}) collective-permute-start(bf16[352,512]{1,0:T(8,128)(2,1)} %slice.49), channel_id=1, source_target_pairs={{0,6},{1,7},{2,0},{3,1},{4,2},{5,3},{6,4},{7,5},{8,14},{9,15},{10,... | collective-permute-start | bytes 1081352 | tf_op jit(solution)/shard_map/ppermute | solution.py:41
  58.6 5.9 %collective-permute-start = (bf16[704,512]{1,0:T(8,128)(2,1)S(1)}, bf16[704,512]{1,0:T(8,128)(2,1)}, u32[]{:S(2)}, u32[]{:S(2)}) collective-permute-start(bf16[704,512]{1,0:T(8,128)(2,1)S(1)} %copy-done), channel_id=1, source_target_pairs={{0,1},{1,0},{2,3},{3,2},{4,5},{5,4},{6,7},{7,6},{8,9},{9,8},{10,11... | collective-permute-start | bytes 2162696 | tf_op jit(solution)/shard_map/ppermute | solution.py:51
  72.1 2.2 %sine_select_fusion.rope_hbm = f32[512,128]{1,0:T(8,128)} fusion(f32[128]{0:T(128)S(1)} %pad_maximum_fusion, s32[512]{0:T(512)S(1)} %get-tuple-element.56, s32[512]{0:T(512)S(1)} %get-tuple-element.57, s32[512]{0:T(512)S(1)} %get-tuple-element.58, s32[512]{0:T(512)S(1)} %get-tuple-element.59, pred[512]{0:T(512)(128)(4,1)S(1)} %get-tuple-element.52, ...), kind=kLoop, calls=%fused_computation | loop fusion | flops 458752 | bytes 273024 | tf_op jit(solution)/shard_map/jit(_where)/select_n | solution.py:577
  74.3 7.5 %norm_low.1 = (bf16[4,512,1024]{2,1,0:T(8,128)(2,1)}, bf16[512,128]{1,0:T(8,128)(2,1)}, bf16[8,2,256,128]{3,2,1,0:T(8,128)(2,1)}) custom-call(s32[2]{0:T(128)S(1)} %copy-done.14, s32[1,4]{1,0:T(1,128)S(1)} %copy-done.11, bf16[704,512]{1,0:T(8,128)(2,1)S(1)} %copy-done, bf16[704,512]{1,0:T(8,128)(2,1)} %collective-permute-done.refs_1_.refs_9_.refs_17_, ...), custom_call_target="tpu_custom_call" | custom-call | tf_op jit(solution)/shard_map/norm_low/pallas_call | solution.py:223
  81.8 17.5 %all-gather.5.cloned.1.call-done = bf16[4352,768]{1,0:T(8,128)(2,1)} async-done(((bf16[272,768]{1,0:T(8,128)(2,1)}), bf16[4352,768]{1,0:T(8,128)(2,1)}) %all-gather.5.cloned.1.call-update) | async-done | bytes 6684688 | tf_op jit(solution)/shard_map/all_gather | solution.py:558
  99.3 17.7 %attention.1 = (bf16[512,512]{1,0:T(8,128)(2,1)S(1)}, bf16[2,512,128]{2,1,0:T(8,128)(2,1)}) custom-call(s32[1,4]{1,0:T(1,128)S(1)} %copy-done.11, s32[4]{0:T(128)S(1)} %copy-done.12, s32[16]{0:T(128)S(1)} %get-tuple-element.23.place_ref, s32[4]{0:T(128)S(1)} %copy-done.15, s32[16]{0:T(128)S(1)} %copy-done.16, ...), custom_call_target="tpu_custom_call" | custom-call | tf_op jit(solution)/shard_map/attention/pallas_call | solution.py:402
  117.1 2.7 %collective-permute-start.11 = (bf16[512,512]{1,0:T(8,128)(2,1)S(1)}, bf16[512,512]{1,0:T(8,128)(2,1)S(1)}, u32[]{:S(2)}, u32[]{:S(2)}) collective-permute-start(bf16[512,512]{1,0:T(8,128)(2,1)S(1)} %get-tuple-element.38.refs_0_), channel_id=1, source_target_pairs={{0,6},{1,7},{2,0},{3,1},{4,2},{5,3},{6,4},{7,5},{8,14},{9,15},{10,... | collective-permute-start | bytes 1572872 | tf_op jit(solution)/shard_map/ppermute | solution.py:46
  119.7 11.6 %collective-permute-done.9.refs_2_ = bf16[512,512]{1,0:T(8,128)(2,1)S(1)} collective-permute-done((bf16[512,512]{1,0:T(8,128)(2,1)S(1)}, bf16[512,512]{1,0:T(8,128)(2,1)S(1)}, u32[]{:S(2)}, u32[]{:S(2)}) %collective-permute-start.9) | collective-permute-done | bytes 524320 | tf_op jit(solution)/shard_map/ppermute | solution.py:45
  131.5 2.7 %collective-permute-start.14 = (bf16[256,512]{1,0:T(8,128)(2,1)S(1)}, bf16[256,512]{1,0:T(8,128)(2,1)S(1)}, u32[]{:S(2)}, u32[]{:S(2)}) collective-permute-start(bf16[256,512]{1,0:T(8,128)(2,1)S(1)} %slice.51), channel_id=1, source_target_pairs={{0,6},{1,7},{2,0},{3,1},{4,2},{5,3},{6,4},{7,5},{8,14},{9,15},{10,... | collective-permute-start | bytes 786440 | tf_op jit(solution)/shard_map/ppermute | solution.py:41
  134.2 1.9 %collective-permute-start.8 = (bf16[512,512]{1,0:T(8,128)(2,1)S(1)}, bf16[512,512]{1,0:T(8,128)(2,1)S(1)}, u32[]{:S(2)}, u32[]{:S(2)}) collective-permute-start(bf16[512,512]{1,0:T(8,128)(2,1)S(1)} %get-tuple-element.38.refs_0_), channel_id=1, source_target_pairs={{0,1},{1,0},{2,3},{3,2},{4,5},{5,4},{6,7},{7,6},{8,9},{9,8},{10,11... | collective-permute-start | bytes 1572872 | tf_op jit(solution)/shard_map/ppermute | solution.py:51
  136.6 2.7 %collective-permute-done.13 = bf16[256,512]{1,0:T(8,128)(2,1)S(1)} collective-permute-done((bf16[256,512]{1,0:T(8,128)(2,1)S(1)}, bf16[256,512]{1,0:T(8,128)(2,1)S(1)}, u32[]{:S(2)}, u32[]{:S(2)}) %collective-permute-start.13) | collective-permute-done | bytes 262176 | tf_op jit(solution)/shard_map/ppermute | solution.py:41
  139.3 2.2 %collective-permute-start.15 = (bf16[512,512]{1,0:T(8,128)(2,1)S(1)}, bf16[512,512]{1,0:T(8,128)(2,1)S(1)}, u32[]{:S(2)}, u32[]{:S(2)}) collective-permute-start(bf16[512,512]{1,0:T(8,128)(2,1)S(1)} %constant_dynamic-update-slice_fusion.2.refs_6_), channel_id=1, source_target_pairs={{0,1},{1,0},{2,3},{3,2},{4,5},{5,4},{6,7},{7,6},{8,9},{9,8},{10,11... | collective-permute-start | bytes 1572872 | tf_op jit(solution)/shard_map/ppermute | solution.py:51
  143.0 3.7 %output_low.1.refs_8_ = bf16[512,256]{1,0:T(8,128)(2,1)} custom-call(s32[1,4]{1,0:T(1,128)S(1)} %copy-done.11, bf16[512,512]{1,0:T(8,128)(2,1)S(1)} %get-tuple-element.38.refs_0_, bf16[512,512]{1,0:T(8,128)(2,1)S(1)} %collective-permute-done.8.refs_1_, bf16[512,512]{1,0:T(8,128)(2,1)S(1)} %collective-permute-done.9.refs_2_, ...), custom_call_target="tpu_custom_call" | custom-call | tf_op jit(solution)/shard_map/output_low/pallas_call | solution.py:452
  148.3 3.4 %all-gather.7.cloned.1.call-done = bf16[4352,512]{1,0:T(8,128)(2,1)} async-done(((bf16[272,512]{1,0:T(8,128)(2,1)}), bf16[4352,512]{1,0:T(8,128)(2,1)}) %all-gather.7.cloned.1.call-update) | async-done | bytes 4456464 | tf_op jit(solution)/shard_map/all_gather | solution.py:563
  151.8 5.9 %output.1 = bf16[512,512]{1,0:T(8,128)(2,1)} custom-call(s32[2]{0:T(128)S(1)} %copy-done.14, s32[4]{0:T(128)S(1)} %copy-done.15, s32[16]{0:T(128)S(1)} %copy-done.16, bf16[512,512]{1,0:T(8,128)(2,1)} %copy-done.5, bf16[512,512]{1,0:T(8,128)(2,1)} %copy-done.6, bf16[512,512]{1,0:T(8,128)(2,1)} %copy-done.1, bf16[512,512]{1,0:T(8,128)(2,1)} %copy-done.7, ...), custom_call_target="tpu_custom_call" | custom-call | tf_op jit(solution)/shard_map/output/pallas_call | solution.py:503
  (91 shorter events, 19.8 us)
Async XLA Ops:
  7.2 92.2 %all-gather.5.cloned.1.call-start = ((), (), s32[]{:S(2)}) async-start(), calls=%async_computation.2 | async-start | bytes 7102464 | tf_op jit(solution)/shard_map/all_gather | solution.py:558
  10.8 20.3 %all-to-all-start = ((bf16[16,48,512]{2,1,0:T(8,128)(2,1)}), bf16[16,48,512]{2,1,0:T(8,128)(2,1)S(1)}, u32[]{:S(2)}, u32[]{:S(2)}) async-start(bf16[16,48,512]{2,1,0:T(8,128)(2,1)} %get-tuple-element.26), calls=%async_computation | async-start | bytes 1572864 | tf_op jit(solution)/shard_map/all_to_all | solution.py:559
  18.4 133.3 %all-gather.7.cloned.1.call-start = ((), (), s32[]{:S(2)}) async-start(), calls=%async_computation.3 | async-start | bytes 4734976 | tf_op jit(solution)/shard_map/all_gather | solution.py:563
  32.0 35.9 %copy-start.20 = (bf16[128]{0:T(256)(128)(2,1)S(1)}, bf16[128]{0:T(256)(128)(2,1)}, u32[]{:S(2)}) copy-start(bf16[128]{0:T(256)(128)(2,1)} %param.20) | copy-start | bytes 772
  32.0 35.9 %copy-start.21 = (bf16[128]{0:T(256)(128)(2,1)S(1)}, bf16[128]{0:T(256)(128)(2,1)}, u32[]{:S(2)}) copy-start(bf16[128]{0:T(256)(128)(2,1)} %param.19) | copy-start | bytes 772
  32.0 36.5 %copy-start.12 = (s32[4]{0:T(128)S(1)}, s32[4]{0:T(128)}, u32[]{:S(2)}) copy-start(s32[4]{0:T(128)} %cache_ref.1) | copy-start | bytes 52
  35.1 39.2 %copy-start.14 = (s32[2]{0:T(128)S(1)}, s32[2]{0:T(128)}, u32[]{:S(2)}) copy-start(s32[2]{0:T(128)} %pad_add_fusion.me_ref) | copy-start | bytes 28
  35.1 16.7 %collective-permute-start.1 = (bf16[704,512]{1,0:T(8,128)(2,1)}, bf16[704,512]{1,0:T(8,128)(2,1)S(1)}, u32[]{:S(2)}, u32[]{:S(2)}) collective-permute-start(bf16[704,512]{1,0:T(8,128)(2,1)} %select_slots.1.refs_0_.refs_8_.refs_16_), channel_id=1, source_target_pairs={{0,2},{1,3},{2,4},{3,5},{4,6},{5,7},{6,0},{7,1},{8,10},{9,11},{10,... | collective-permute-start | bytes 2162696 | tf_op jit(solution)/shard_map/ppermute | solution.py:45
  36.9 15.0 %collective-permute-start.3 = (bf16[704,512]{1,0:T(8,128)(2,1)}, bf16[704,512]{1,0:T(8,128)(2,1)S(1)}, u32[]{:S(2)}, u32[]{:S(2)}) collective-permute-start(bf16[704,512]{1,0:T(8,128)(2,1)} %select_slots.1.refs_0_.refs_8_.refs_16_), channel_id=1, source_target_pairs={{0,6},{1,7},{2,0},{3,1},{4,2},{5,3},{6,4},{7,5},{8,14},{9,15},{10,... | collective-permute-start | bytes 2162696 | tf_op jit(solution)/shard_map/ppermute | solution.py:46
  39.4 42.4 %all-to-all-start.1 = ((bf16[16,512,128]{2,1,0:T(8,128)(2,1)}), bf16[16,512,128]{2,1,0:T(8,128)(2,1)}, u32[]{:S(2)}, u32[]{:S(2)}) async-start(bf16[16,512,128]{2,1,0:T(8,128)(2,1)} %bitcast.16), calls=%async_computation.1 | async-start | bytes 4194304 | tf_op jit(solution)/shard_map/all_to_all | solution.py:564
  51.9 13.1 %collective-permute-start.5 = (bf16[352,512]{1,0:T(8,128)(2,1)S(1)}, bf16[352,512]{1,0:T(8,128)(2,1)S(1)}, u32[]{:S(2)}, u32[]{:S(2)}) collective-permute-start(bf16[352,512]{1,0:T(8,128)(2,1)S(1)} %slice.48), channel_id=1, source_target_pairs={{0,2},{1,3},{2,4},{3,5},{4,6},{5,7},{6,0},{7,1},{8,10},{9,11},{10,... | collective-permute-start | bytes 1081352 | tf_op jit(solution)/shard_map/ppermute | solution.py:41
  52.7 12.3 %collective-permute-start.6 = (bf16[352,512]{1,0:T(8,128)(2,1)}, bf16[352,512]{1,0:T(8,128)(2,1)}, u32[]{:S(2)}, u32[]{:S(2)}) collective-permute-start(bf16[352,512]{1,0:T(8,128)(2,1)} %slice.49), channel_id=1, source_target_pairs={{0,6},{1,7},{2,0},{3,1},{4,2},{5,3},{6,4},{7,5},{8,14},{9,15},{10,... | collective-permute-start | bytes 1081352 | tf_op jit(solution)/shard_map/ppermute | solution.py:41
  58.6 15.7 %collective-permute-start = (bf16[704,512]{1,0:T(8,128)(2,1)S(1)}, bf16[704,512]{1,0:T(8,128)(2,1)}, u32[]{:S(2)}, u32[]{:S(2)}) collective-permute-start(bf16[704,512]{1,0:T(8,128)(2,1)S(1)} %copy-done), channel_id=1, source_target_pairs={{0,1},{1,0},{2,3},{3,2},{4,5},{5,4},{6,7},{7,6},{8,9},{9,8},{10,11... | collective-permute-start | bytes 2162696 | tf_op jit(solution)/shard_map/ppermute | solution.py:51
  64.5 9.8 %collective-permute-start.2 = (bf16[704,512]{1,0:T(8,128)(2,1)S(1)}, bf16[704,512]{1,0:T(8,128)(2,1)}, u32[]{:S(2)}, u32[]{:S(2)}) collective-permute-start(bf16[704,512]{1,0:T(8,128)(2,1)S(1)} %collective-permute-done.1.refs_2_.refs_10_.refs_18_), channel_id=1, source_target_pairs={{0,1},{1,0},{2,3},{3,2},{4,5},{5,4},{6,7},{7,6},{8,9},{9,8},{10,11... | collective-permute-start | bytes 2162696 | tf_op jit(solution)/shard_map/ppermute | solution.py:51
  64.6 9.7 %collective-permute-start.4 = (bf16[704,512]{1,0:T(8,128)(2,1)S(1)}, bf16[704,512]{1,0:T(8,128)(2,1)}, u32[]{:S(2)}, u32[]{:S(2)}) collective-permute-start(bf16[704,512]{1,0:T(8,128)(2,1)S(1)} %collective-permute-done.3.refs_4_.refs_12_.refs_20_), channel_id=1, source_target_pairs={{0,1},{1,0},{2,3},{3,2},{4,5},{5,4},{6,7},{7,6},{8,9},{9,8},{10,11... | collective-permute-start | bytes 2162696 | tf_op jit(solution)/shard_map/ppermute | solution.py:51
  66.1 8.2 %collective-permute-start.7 = (bf16[704,512]{1,0:T(8,128)(2,1)S(1)}, bf16[704,512]{1,0:T(8,128)(2,1)}, u32[]{:S(2)}, u32[]{:S(2)}) collective-permute-start(bf16[704,512]{1,0:T(8,128)(2,1)S(1)} %constant_dynamic-update-slice_fusion.refs_6_.refs_14_.refs_22_), channel_id=1, source_target_pairs={{0,1},{1,0},{2,3},{3,2},{4,5},{5,4},{6,7},{7,6},{8,9},{9,8},{10,11... | collective-permute-start | bytes 2162696 | tf_op jit(solution)/shard_map/ppermute | solution.py:51
  117.0 14.3 %collective-permute-start.9 = (bf16[512,512]{1,0:T(8,128)(2,1)S(1)}, bf16[512,512]{1,0:T(8,128)(2,1)S(1)}, u32[]{:S(2)}, u32[]{:S(2)}) collective-permute-start(bf16[512,512]{1,0:T(8,128)(2,1)S(1)} %get-tuple-element.38.refs_0_), channel_id=1, source_target_pairs={{0,2},{1,3},{2,4},{3,5},{4,6},{5,7},{6,0},{7,1},{8,10},{9,11},{10,... | collective-permute-start | bytes 1572872 | tf_op jit(solution)/shard_map/ppermute | solution.py:45
  117.1 14.4 %collective-permute-start.11 = (bf16[512,512]{1,0:T(8,128)(2,1)S(1)}, bf16[512,512]{1,0:T(8,128)(2,1)S(1)}, u32[]{:S(2)}, u32[]{:S(2)}) collective-permute-start(bf16[512,512]{1,0:T(8,128)(2,1)S(1)} %get-tuple-element.38.refs_0_), channel_id=1, source_target_pairs={{0,6},{1,7},{2,0},{3,1},{4,2},{5,3},{6,4},{7,5},{8,14},{9,15},{10,... | collective-permute-start | bytes 1572872 | tf_op jit(solution)/shard_map/ppermute | solution.py:46
  131.3 7.9 %collective-permute-start.13 = (bf16[256,512]{1,0:T(8,128)(2,1)S(1)}, bf16[256,512]{1,0:T(8,128)(2,1)S(1)}, u32[]{:S(2)}, u32[]{:S(2)}) collective-permute-start(bf16[256,512]{1,0:T(8,128)(2,1)S(1)} %slice.50), channel_id=1, source_target_pairs={{0,2},{1,3},{2,4},{3,5},{4,6},{5,7},{6,0},{7,1},{8,10},{9,11},{10,... | collective-permute-start | bytes 786440 | tf_op jit(solution)/shard_map/ppermute | solution.py:41
  131.5 7.8 %collective-permute-start.14 = (bf16[256,512]{1,0:T(8,128)(2,1)S(1)}, bf16[256,512]{1,0:T(8,128)(2,1)S(1)}, u32[]{:S(2)}, u32[]{:S(2)}) collective-permute-start(bf16[256,512]{1,0:T(8,128)(2,1)S(1)} %slice.51), channel_id=1, source_target_pairs={{0,6},{1,7},{2,0},{3,1},{4,2},{5,3},{6,4},{7,5},{8,14},{9,15},{10,... | collective-permute-start | bytes 786440 | tf_op jit(solution)/shard_map/ppermute | solution.py:41
  134.2 7.3 %collective-permute-start.8 = (bf16[512,512]{1,0:T(8,128)(2,1)S(1)}, bf16[512,512]{1,0:T(8,128)(2,1)S(1)}, u32[]{:S(2)}, u32[]{:S(2)}) collective-permute-start(bf16[512,512]{1,0:T(8,128)(2,1)S(1)} %get-tuple-element.38.refs_0_), channel_id=1, source_target_pairs={{0,1},{1,0},{2,3},{3,2},{4,5},{5,4},{6,7},{7,6},{8,9},{9,8},{10,11... | collective-permute-start | bytes 1572872 | tf_op jit(solution)/shard_map/ppermute | solution.py:51
  136.0 5.5 %collective-permute-start.10 = (bf16[512,512]{1,0:T(8,128)(2,1)S(1)}, bf16[512,512]{1,0:T(8,128)(2,1)S(1)}, u32[]{:S(2)}, u32[]{:S(2)}) collective-permute-start(bf16[512,512]{1,0:T(8,128)(2,1)S(1)} %collective-permute-done.9.refs_2_), channel_id=1, source_target_pairs={{0,1},{1,0},{2,3},{3,2},{4,5},{5,4},{6,7},{7,6},{8,9},{9,8},{10,11... | collective-permute-start | bytes 1572872 | tf_op jit(solution)/shard_map/ppermute | solution.py:51
  136.0 5.5 %collective-permute-start.12 = (bf16[512,512]{1,0:T(8,128)(2,1)S(1)}, bf16[512,512]{1,0:T(8,128)(2,1)S(1)}, u32[]{:S(2)}, u32[]{:S(2)}) collective-permute-start(bf16[512,512]{1,0:T(8,128)(2,1)S(1)} %collective-permute-done.11.refs_4_), channel_id=1, source_target_pairs={{0,1},{1,0},{2,3},{3,2},{4,5},{5,4},{6,7},{7,6},{8,9},{9,8},{10,11... | collective-permute-start | bytes 1572872 | tf_op jit(solution)/shard_map/ppermute | solution.py:51
  139.3 3.7 %collective-permute-start.15 = (bf16[512,512]{1,0:T(8,128)(2,1)S(1)}, bf16[512,512]{1,0:T(8,128)(2,1)S(1)}, u32[]{:S(2)}, u32[]{:S(2)}) collective-permute-start(bf16[512,512]{1,0:T(8,128)(2,1)S(1)} %constant_dynamic-update-slice_fusion.2.refs_6_), channel_id=1, source_target_pairs={{0,1},{1,0},{2,3},{3,2},{4,5},{5,4},{6,7},{7,6},{8,9},{9,8},{10,11... | collective-permute-start | bytes 1572872 | tf_op jit(solution)/shard_map/ppermute | solution.py:51
  (18 other events, 258.2 us)
Sparse Core Ops, SparseCore 0:
  10.9 88.3 all-gather.4
  101.5 50.1 all-gather.6

commit v9 on v8

--- a/solution.py
+++ b/solution.py
@@ -135,9 +135,8 @@
     wide_ref[256:, 640:] = jnp.zeros((16, 128), BF)
     rest_ref[:256, :] = wo_ref[...]
     rest_ref[256:, :] = oup_ref[0]
-    for r in range(16):
-        slots_ref[r, :32, :] = down_ref[0]
-        slots_ref[r, 32:, :] = odown_ref[0]
+    slots_ref[:32, :] = down_ref[0]
+    slots_ref[32:, :] = odown_ref[0]
 
 
 def pack(me, qkv, wo, up, oup, down, odown):
@@ -146,7 +145,7 @@
         out_shape=(
             jax.ShapeDtypeStruct((272, 768), BF),
             jax.ShapeDtypeStruct((272, FEAT), BF),
-            jax.ShapeDtypeStruct((16, 48, FEAT), BF),
+            jax.ShapeDtypeStruct((48, FEAT), BF),
         ),
         grid_spec=pltpu.PrefetchScalarGridSpec(
             num_scalar_prefetch=1,
@@ -159,7 +158,7 @@
                 pl.BlockSpec((1, 32, FEAT), lambda i, me: (0, 0, me[1])),
                 whole(1, 16, FEAT),
             ],
-            out_specs=(whole(272, 768), whole(272, FEAT), whole(16, 48, FEAT)),
+            out_specs=(whole(272, 768), whole(272, FEAT), whole(48, FEAT)),
         ),
         name="pack",
     )(me, qkv, wo, up, oup, down, odown)
@@ -168,26 +167,36 @@
 DOWN, ODOWN, BLOCK_ROWS = TOK, TOK + 128, TOK + 192
 
 
-def select_body(adapter_ref, position_ref, slots_ref, hidden_ref, out_ref):
+def select_body(me_ref, adapter_ref, position_ref, y0, y1, y2, y3, hidden_ref, out_ref):
+    def place(index, mine):
+        d = lax.rem(index - mine + 4, 4)
+        return jnp.where(d == 0, 0, jnp.where(d == 3, 1, d + 1))
+
     out_ref[:TOK, :] = hidden_ref[...]
     for p in range(PROMPTS):
         slot = position_ref[adapter_ref[p]]
-        out_ref[DOWN + p * 32 : DOWN + p * 32 + 32, :] = slots_ref[slot, :32, :]
-        out_ref[ODOWN + p * 16 : ODOWN + p * 16 + 16, :] = slots_ref[slot, 32:, :]
-
-
-def select_slots(adapter, position, slots, hidden):
+        x = place(lax.div(slot, 4), lax.div(me_ref[0], 4))
+        y = place(lax.rem(slot, 4), lax.rem(me_ref[0], 4))
+        for k, ref in enumerate((y0, y1, y2, y3)):
+
+            @pl.when(y == k)
+            def _():
+                out_ref[DOWN + p * 32 : DOWN + p * 32 + 32, :] = ref[x, :32, :]
+                out_ref[ODOWN + p * 16 : ODOWN + p * 16 + 16, :] = ref[x, 32:, :]
+
+
+def select_slots(me, adapter, position, pieces, hidden):
     return pl.pallas_call(
         select_body,
         out_shape=jax.ShapeDtypeStruct((BLOCK_ROWS, FEAT), BF),
         grid_spec=pltpu.PrefetchScalarGridSpec(
-            num_scalar_prefetch=2,
+            num_scalar_prefetch=3,
             grid=(1,),
-            in_specs=[whole(16, 48, FEAT), whole(TOK, FEAT)],
+            in_specs=[whole(4, 48, FEAT)] * 4 + [whole(TOK, FEAT)],
             out_specs=whole(BLOCK_ROWS, FEAT),
         ),
         name="select_slots",
-    )(adapter, position, slots, hidden)
+    )(me, adapter, position, *pieces, hidden)
 
 
 def norm_body(me_ref, length_ref, *refs):
@@ -556,14 +565,17 @@
         output_down_maps,
     )
     weight = lax.all_gather(wide, "row", axis=0)
-    slots = lax.all_to_all(slots, "row", 0, 0)
+    along = [slots] + [lax.ppermute(slots, "row", perm_x(k)) for k in (1, -1, 2)]
+    along = jnp.concatenate(along, axis=0)
+    before, after, far = ring4(along, "row", perm_y, 96)
+    far, rest = lax.optimization_barrier((far, rest))
+    pieces = [piece.reshape(4, 48, FEAT) for piece in (along, before, after, far)]
 
     picked, place = pick_pages(me, page_owner_row, page_store_index, cache_page_store)
-    picked, slots, rest = lax.optimization_barrier((picked, slots, rest))
     rest = lax.all_gather(rest, "row", axis=0)
     pages = lax.all_to_all(picked.reshape(16, 4 * PAGE, HEAD), "row", 0, 0).reshape(32, 2, PAGE, HEAD)
 
-    blocks = gather_col(select_slots(prompt_adapter, adapter_position, slots, hidden_input), BLOCK_ROWS // 2)
+    blocks = gather_col(select_slots(me, prompt_adapter, adapter_position, pieces, hidden_input), BLOCK_ROWS // 2)
 
     token = lax.broadcasted_iota(jnp.int32, (TOK, HEAD), 0)
     position, start = token, jnp.int32(0)

time: 165 us -> 168 us (1.018)
  starting transfers between devices: 38.4 us -> 43.6 us
  local copies, waits for them, and re-layouts: 10.2 us -> 7.21 us
    all_gather x1, waiting for transfers between devices: 17.5 us -> 6.55 us  [on_device(): weight = lax.all_gather(wide, 'row', axis=0)]
    all_to_all x1, waiting for transfers between devices: 0.01 us -> 10.2 us  [on_device(): lax.all_to_all(picked.reshape(16, 4 * PAGE, HEAD), 'row', 0, 0)]
    all_to_all x1 -> x0, starting transfers between devices: 7.6 us -> none  [on_device(): slots = lax.all_to_all(slots, 'row', 0, 0)]
    ppermute x0 -> x3, starting transfers between devices: none -> 5.11 us  [on_device(): lax.ppermute(slots, 'row', perm_x(k))]
    ppermute x2 -> x3, waiting for transfers between devices: 2.68 us -> 6.36 us  [ring_far(): lax.ppermute(before[:half], axis, perm(1))]
    ppermute x2 -> x3, waiting for transfers between devices: 17.9 us -> 14.2 us  [ring4(): before = lax.ppermute(block, axis, perm(1))]
    all_to_all x1 -> x0, waiting for transfers between devices: 3.61 us -> none  [on_device(): slots = lax.all_to_all(slots, 'row', 0, 0)]
    unnamed x47 -> x54, local copies, waits for them, and re-layouts: 7.06 us -> 4.01 us
  transfers between devices with their start and end apart: 20 -> 26, of which waited for: 7 -> 9; matrix products, arithmetic and copies ran while one was open for 6% -> 7% of each run, Pallas kernels for 22% -> 22%
where the time goes in v9:
time: 168 us; the launch traced here: 167 us
  Pallas kernels  46.1 us (27%)
  waiting for transfers between devices  45.6 us (27%)
  starting transfers between devices  43.6 us (26%)
  between operations  17 us (10%)
  other arithmetic  7.89 us (5%)
  local copies, waits for them, and re-layouts  7.21 us (4%)
    pallas_call x1, Pallas kernels, attention(): pl.pallas_call(attention_body, out_shape=(jax.ShapeDtypeStruct((TOK, FEAT...  18.4 us
    ppermute x8, starting transfers between devices, swap(): return lax.ppermute(block, 'col', SWAP)  15.3 us
    ppermute x3, waiting for transfers between devices, ring4(): before = lax.ppermute(block, axis, perm(1))  14.2 us
    all_to_all x1, waiting for transfers between devices, on_device(): lax.all_to_all(picked.reshape(16, 4 * PAGE, HEAD), 'row', 0, 0)  10.2 us
    ppermute x3, starting transfers between devices, ring_far(): lax.ppermute(after[half:], axis, perm(-1))  8.05 us
    pallas_call x1, Pallas kernels, norm_low(): pl.pallas_call(norm_body, out_shape=(pltpu.HBM((4, TOK, 2 * FEAT), BF), p...  7.49 us
    all_gather x1, waiting for transfers between devices, on_device(): weight = lax.all_gather(wide, 'row', axis=0)  6.55 us
    ppermute x3, waiting for transfers between devices, ring_far(): lax.ppermute(before[:half], axis, perm(1))  6.36 us
  transfers between devices with their start and end apart: 26, of which 9 were waited for; matrix products, arithmetic and copies ran while one was open for 7% of the time, Pallas kernels for 22%

profile of v9, /device:TPU:1, one launch (start us, length us, event | category | flops | bytes accessed | tf_op | source)
XLA Modules:
  0.0 167.3 jit_solution(14964841560273795502)
XLA Ops:
  7.8 2.8 %pack.1 = (bf16[272,768]{1,0:T(8,128)(2,1)}, bf16[272,512]{1,0:T(8,128)(2,1)}, bf16[48,512]{1,0:T(8,128)(2,1)}) custom-call(s32[2]{0:T(128)} %pad_add_fusion.me_ref, bf16[256,768]{1,0:T(8,128)(2,1)} %qkv_ref.1, bf16[256,512]{1,0:T(8,128)(2,1)} %wo_ref.1, bf16[1,16,640]{2,1,0:T(8,128)(2,1)} %up_ref.1, bf16[1,16,4096]{2,1,0:T(8,128)(2,1)} %oup_ref.1, ...), custom_call_target="tpu_custom_call" | custom-call | tf_op jit(solution)/shard_map/pack/pallas_call | solution.py:143
  10.7 2.1 %collective-permute-start = (bf16[48,512]{1,0:T(8,128)(2,1)}, bf16[48,512]{1,0:T(8,128)(2,1)S(1)}, u32[]{:S(2)}, u32[]{:S(2)}) collective-permute-start(bf16[48,512]{1,0:T(8,128)(2,1)} %get-tuple-element.24), channel_id=1, source_target_pairs={{0,32},{8,40},{16,48},{24,56},{32,64},{40,72},{48,80},{56,88},{64,... | collective-permute-start | bytes 147464 | tf_op jit(solution)/shard_map/ppermute | solution.py:568
  16.7 2.1 %collective-permute-done.2 = bf16[48,512]{1,0:T(8,128)(2,1)S(1)} collective-permute-done((bf16[48,512]{1,0:T(8,128)(2,1)}, bf16[48,512]{1,0:T(8,128)(2,1)S(1)}, u32[]{:S(2)}, u32[]{:S(2)}) %collective-permute-start.2) | collective-permute-done | bytes 49184 | tf_op jit(solution)/shard_map/ppermute | solution.py:568
  21.7 3.0 %collective-permute-done.3 = bf16[192,512]{1,0:T(8,128)(2,1)S(1)} collective-permute-done((bf16[192,512]{1,0:T(8,128)(2,1)S(1)}, bf16[192,512]{1,0:T(8,128)(2,1)S(1)}, u32[]{:S(2)}, u32[]{:S(2)}) %collective-permute-start.3) | collective-permute-done | bytes 196640 | tf_op jit(solution)/shard_map/ppermute | solution.py:45
  24.8 2.7 %collective-permute-start.6 = (bf16[96,512]{1,0:T(8,128)(2,1)S(1)}, bf16[96,512]{1,0:T(8,128)(2,1)S(1)}, u32[]{:S(2)}, u32[]{:S(2)}) collective-permute-start(bf16[96,512]{1,0:T(8,128)(2,1)S(1)} %slice.57), channel_id=1, source_target_pairs={{0,24},{8,0},{16,8},{24,16},{32,56},{40,32},{48,40},{56,48},{64,88... | collective-permute-start | bytes 294920 | tf_op jit(solution)/shard_map/ppermute | solution.py:41
  27.6 4.2 %collective-permute-done.5 = bf16[96,512]{1,0:T(8,128)(2,1)S(1)} collective-permute-done((bf16[96,512]{1,0:T(8,128)(2,1)S(1)}, bf16[96,512]{1,0:T(8,128)(2,1)S(1)}, u32[]{:S(2)}, u32[]{:S(2)}) %collective-permute-start.5) | collective-permute-done | bytes 98336 | tf_op jit(solution)/shard_map/ppermute | solution.py:41
  32.5 3.1 %select_slots.1.refs_0_.refs_8_.refs_16_ = bf16[704,512]{1,0:T(8,128)(2,1)} custom-call(s32[2]{0:T(128)} %pad_add_fusion.me_ref, s32[4]{0:T(128)} %adapter_ref.5, s32[16]{0:T(128)} %position_ref.5, bf16[4,48,512]{2,1,0:T(8,128)(2,1)} %bitcast.26, bf16[4,48,512]{2,1,0:T(8,128)(2,1)} %bitcast.24, bf16[4,48,512]{2,1,0:T(8,128)(2,1)} %bitcast.25, ...), custom_call_target="tpu_custom_call" | custom-call | tf_op jit(solution)/shard_map/select_slots/pallas_call | solution.py:189
  39.3 4.5 %pick_pages.1 = (bf16[16,2,2,128,128]{4,3,2,1,0:T(8,128)(2,1)S(1)}, s32[16]{0:T(128)S(1)}) custom-call(s32[2]{0:T(128)S(1)} %copy-done.12, s32[256,1]{1,0:T(8,128)S(1)} %copy.20.owner_ref, s32[256]{0:T(256)S(1)} %copy-done.16, bf16[8,2,128,128]{3,2,1,0:T(8,128)(2,1)S(1)} %copy-done.10), custom_call_target="tpu_custom_call" | custom-call | tf_op jit(solution)/shard_map/pick_pages/pallas_call | solution.py:115
  45.1 5.6 %all-to-all-start = ((bf16[16,512,128]{2,1,0:T(8,128)(2,1)}), bf16[16,512,128]{2,1,0:T(8,128)(2,1)}, u32[]{:S(2)}, u32[]{:S(2)}) async-start(bf16[16,512,128]{2,1,0:T(8,128)(2,1)} %bitcast.20), calls=%async_computation | async-start | bytes 4194304 | tf_op jit(solution)/shard_map/all_to_all | solution.py:576
  52.3 2.7 %collective-permute-start.13 = (bf16[352,512]{1,0:T(8,128)(2,1)}, bf16[352,512]{1,0:T(8,128)(2,1)}, u32[]{:S(2)}, u32[]{:S(2)}) collective-permute-start(bf16[352,512]{1,0:T(8,128)(2,1)} %slice.59), channel_id=1, source_target_pairs={{0,6},{1,7},{2,0},{3,1},{4,2},{5,3},{6,4},{7,5},{8,14},{9,15},{10,... | collective-permute-start | bytes 1081352 | tf_op jit(solution)/shard_map/ppermute | solution.py:41
  58.1 8.0 %collective-permute-start.7 = (bf16[704,512]{1,0:T(8,128)(2,1)S(1)}, bf16[704,512]{1,0:T(8,128)(2,1)}, u32[]{:S(2)}, u32[]{:S(2)}) collective-permute-start(bf16[704,512]{1,0:T(8,128)(2,1)S(1)} %copy-done), channel_id=1, source_target_pairs={{0,1},{1,0},{2,3},{3,2},{4,5},{5,4},{6,7},{7,6},{8,9},{9,8},{10,11... | collective-permute-start | bytes 2162696 | tf_op jit(solution)/shard_map/ppermute | solution.py:51
  73.9 2.2 %sine_select_fusion.rope_hbm = f32[512,128]{1,0:T(8,128)} fusion(f32[128]{0:T(128)S(1)} %pad_maximum_fusion.1, s32[512]{0:T(512)S(1)} %get-tuple-element.54, s32[512]{0:T(512)S(1)} %get-tuple-element.55, s32[512]{0:T(512)S(1)} %get-tuple-element.56, s32[512]{0:T(512)S(1)} %get-tuple-element.57, pred[512]{0:T(512)(128)(4,1)S(1)} %get-tuple-element.50, ...), kind=kLoop, calls=%fused_computation | loop fusion | flops 458752 | bytes 273024 | tf_op jit(solution)/shard_map/jit(_where)/select_n | solution.py:589
  76.1 7.5 %norm_low.1 = (bf16[4,512,1024]{2,1,0:T(8,128)(2,1)}, bf16[512,128]{1,0:T(8,128)(2,1)}, bf16[8,2,256,128]{3,2,1,0:T(8,128)(2,1)}) custom-call(s32[2]{0:T(128)S(1)} %copy-done.12, s32[1,4]{1,0:T(1,128)S(1)} %copy-done.11, bf16[704,512]{1,0:T(8,128)(2,1)S(1)} %copy-done, bf16[704,512]{1,0:T(8,128)(2,1)} %collective-permute-done.7.refs_1_.refs_9_.refs_17_, ...), custom_call_target="tpu_custom_call" | custom-call | tf_op jit(solution)/shard_map/norm_low/pallas_call | solution.py:232
  83.6 10.2 %all-to-all-done = bf16[16,512,128]{2,1,0:T(8,128)(2,1)} async-done(((bf16[16,512,128]{2,1,0:T(8,128)(2,1)}), bf16[16,512,128]{2,1,0:T(8,128)(2,1)}, u32[]{:S(2)}, u32[]{:S(2)}) %all-to-all-start) | async-done | bytes 2097184 | tf_op jit(solution)/shard_map/all_to_all | solution.py:576
  93.8 6.5 %all-gather.5.cloned.1.call-done = bf16[4352,768]{1,0:T(8,128)(2,1)} async-done(((bf16[272,768]{1,0:T(8,128)(2,1)}), bf16[4352,768]{1,0:T(8,128)(2,1)}) %all-gather.5.cloned.1.call-update) | async-done | bytes 6684688 | tf_op jit(solution)/shard_map/all_gather | solution.py:567
  100.3 18.4 %attention.1 = (bf16[512,512]{1,0:T(8,128)(2,1)S(1)}, bf16[2,512,128]{2,1,0:T(8,128)(2,1)}) custom-call(s32[1,4]{1,0:T(1,128)S(1)} %copy-done.11, s32[4]{0:T(128)S(1)} %copy-done.13, s32[16]{0:T(128)S(1)} %get-tuple-element.22.place_ref, s32[4]{0:T(128)S(1)} %copy-done.14, s32[16]{0:T(128)S(1)} %copy-done.15, ...), custom_call_target="tpu_custom_call" | custom-call | tf_op jit(solution)/shard_map/attention/pallas_call | solution.py:411
  121.6 11.3 %collective-permute-done.16.refs_2_ = bf16[512,512]{1,0:T(8,128)(2,1)S(1)} collective-permute-done((bf16[512,512]{1,0:T(8,128)(2,1)S(1)}, bf16[512,512]{1,0:T(8,128)(2,1)S(1)}, u32[]{:S(2)}, u32[]{:S(2)}) %collective-permute-start.16) | collective-permute-done | bytes 524320 | tf_op jit(solution)/shard_map/ppermute | solution.py:45
  133.0 2.7 %collective-permute-start.21 = (bf16[256,512]{1,0:T(8,128)(2,1)S(1)}, bf16[256,512]{1,0:T(8,128)(2,1)S(1)}, u32[]{:S(2)}, u32[]{:S(2)}) collective-permute-start(bf16[256,512]{1,0:T(8,128)(2,1)S(1)} %slice.61), channel_id=1, source_target_pairs={{0,6},{1,7},{2,0},{3,1},{4,2},{5,3},{6,4},{7,5},{8,14},{9,15},{10,... | collective-permute-start | bytes 786440 | tf_op jit(solution)/shard_map/ppermute | solution.py:41
  135.7 2.1 %collective-permute-start.15 = (bf16[512,512]{1,0:T(8,128)(2,1)S(1)}, bf16[512,512]{1,0:T(8,128)(2,1)S(1)}, u32[]{:S(2)}, u32[]{:S(2)}) collective-permute-start(bf16[512,512]{1,0:T(8,128)(2,1)S(1)} %get-tuple-element.36.refs_0_), channel_id=1, source_target_pairs={{0,1},{1,0},{2,3},{3,2},{4,5},{5,4},{6,7},{7,6},{8,9},{9,8},{10,11... | collective-permute-start | bytes 1572872 | tf_op jit(solution)/shard_map/ppermute | solution.py:51
  138.3 2.2 %collective-permute-done.20 = bf16[256,512]{1,0:T(8,128)(2,1)S(1)} collective-permute-done((bf16[256,512]{1,0:T(8,128)(2,1)S(1)}, bf16[256,512]{1,0:T(8,128)(2,1)S(1)}, u32[]{:S(2)}, u32[]{:S(2)}) %collective-permute-start.20) | collective-permute-done | bytes 262176 | tf_op jit(solution)/shard_map/ppermute | solution.py:41
  140.6 2.4 %collective-permute-start.22 = (bf16[512,512]{1,0:T(8,128)(2,1)S(1)}, bf16[512,512]{1,0:T(8,128)(2,1)S(1)}, u32[]{:S(2)}, u32[]{:S(2)}) collective-permute-start(bf16[512,512]{1,0:T(8,128)(2,1)S(1)} %constant_dynamic-update-slice_fusion.6.refs_6_), channel_id=1, source_target_pairs={{0,1},{1,0},{2,3},{3,2},{4,5},{5,4},{6,7},{7,6},{8,9},{9,8},{10,11... | collective-permute-start | bytes 1572872 | tf_op jit(solution)/shard_map/ppermute | solution.py:51
  144.6 3.8 %output_low.1.refs_8_ = bf16[512,256]{1,0:T(8,128)(2,1)} custom-call(s32[1,4]{1,0:T(1,128)S(1)} %copy-done.11, bf16[512,512]{1,0:T(8,128)(2,1)S(1)} %get-tuple-element.36.refs_0_, bf16[512,512]{1,0:T(8,128)(2,1)S(1)} %collective-permute-done.15.refs_1_, bf16[512,512]{1,0:T(8,128)(2,1)S(1)} %collective-permute-done.16.refs_2_, ...), custom_call_target="tpu_custom_call" | custom-call | tf_op jit(solution)/shard_map/output_low/pallas_call | solution.py:461
  149.9 4.5 %all-gather.7.cloned.1.call-done = bf16[4352,512]{1,0:T(8,128)(2,1)} async-done(((bf16[272,512]{1,0:T(8,128)(2,1)}), bf16[4352,512]{1,0:T(8,128)(2,1)}) %all-gather.7.cloned.1.call-update) | async-done | bytes 4456464 | tf_op jit(solution)/shard_map/all_gather | solution.py:575
  154.5 5.9 %output.1 = bf16[512,512]{1,0:T(8,128)(2,1)} custom-call(s32[2]{0:T(128)S(1)} %copy-done.12, s32[4]{0:T(128)S(1)} %copy-done.14, s32[16]{0:T(128)S(1)} %copy-done.15, bf16[512,512]{1,0:T(8,128)(2,1)} %copy-done.5, bf16[512,512]{1,0:T(8,128)(2,1)} %copy-done.6, bf16[512,512]{1,0:T(8,128)(2,1)} %copy-done.1, bf16[512,512]{1,0:T(8,128)(2,1)} %copy-done.7, ...), custom_call_target="tpu_custom_call" | custom-call | tf_op jit(solution)/shard_map/output/pallas_call | solution.py:512
  (114 shorter events, 29.8 us)
Async XLA Ops:
  7.2 93.1 %all-gather.5.cloned.1.call-start = ((), (), s32[]{:S(2)}) async-start(), calls=%async_computation.1 | async-start | bytes 7102464 | tf_op jit(solution)/shard_map/all_gather | solution.py:567
  10.6 143.8 %all-gather.7.cloned.1.call-start = ((), (), s32[]{:S(2)}) async-start(), calls=%async_computation.2 | async-start | bytes 4734976 | tf_op jit(solution)/shard_map/all_gather | solution.py:575
  10.7 6.0 %collective-permute-start = (bf16[48,512]{1,0:T(8,128)(2,1)}, bf16[48,512]{1,0:T(8,128)(2,1)S(1)}, u32[]{:S(2)}, u32[]{:S(2)}) collective-permute-start(bf16[48,512]{1,0:T(8,128)(2,1)} %get-tuple-element.24), channel_id=1, source_target_pairs={{0,32},{8,40},{16,48},{24,56},{32,64},{40,72},{48,80},{56,88},{64,... | collective-permute-start | bytes 147464 | tf_op jit(solution)/shard_map/ppermute | solution.py:568
  14.1 4.7 %collective-permute-start.2 = (bf16[48,512]{1,0:T(8,128)(2,1)}, bf16[48,512]{1,0:T(8,128)(2,1)S(1)}, u32[]{:S(2)}, u32[]{:S(2)}) collective-permute-start(bf16[48,512]{1,0:T(8,128)(2,1)} %get-tuple-element.24), channel_id=1, source_target_pairs={{0,64},{8,72},{16,80},{24,88},{32,96},{40,104},{48,112},{56,120},{... | collective-permute-start | bytes 147464 | tf_op jit(solution)/shard_map/ppermute | solution.py:568
  18.8 5.9 %collective-permute-start.3 = (bf16[192,512]{1,0:T(8,128)(2,1)S(1)}, bf16[192,512]{1,0:T(8,128)(2,1)S(1)}, u32[]{:S(2)}, u32[]{:S(2)}) collective-permute-start(bf16[192,512]{1,0:T(8,128)(2,1)S(1)} %constant_dynamic-update-slice_fusion), channel_id=1, source_target_pairs={{0,8},{8,16},{16,24},{24,0},{32,40},{40,48},{48,56},{56,32},{64,72... | collective-permute-start | bytes 589832 | tf_op jit(solution)/shard_map/ppermute | solution.py:45
  20.2 4.6 %collective-permute-start.4 = (bf16[192,512]{1,0:T(8,128)(2,1)S(1)}, bf16[192,512]{1,0:T(8,128)(2,1)S(1)}, u32[]{:S(2)}, u32[]{:S(2)}) collective-permute-start(bf16[192,512]{1,0:T(8,128)(2,1)S(1)} %constant_dynamic-update-slice_fusion), channel_id=1, source_target_pairs={{0,24},{8,0},{16,8},{24,16},{32,56},{40,32},{48,40},{56,48},{64,88... | collective-permute-start | bytes 589832 | tf_op jit(solution)/shard_map/ppermute | solution.py:46
  24.7 7.0 %collective-permute-start.5 = (bf16[96,512]{1,0:T(8,128)(2,1)S(1)}, bf16[96,512]{1,0:T(8,128)(2,1)S(1)}, u32[]{:S(2)}, u32[]{:S(2)}) collective-permute-start(bf16[96,512]{1,0:T(8,128)(2,1)S(1)} %slice.56), channel_id=1, source_target_pairs={{0,8},{8,16},{16,24},{24,0},{32,40},{40,48},{48,56},{56,32},{64,72... | collective-permute-start | bytes 294920 | tf_op jit(solution)/shard_map/ppermute | solution.py:41
  24.8 6.9 %collective-permute-start.6 = (bf16[96,512]{1,0:T(8,128)(2,1)S(1)}, bf16[96,512]{1,0:T(8,128)(2,1)S(1)}, u32[]{:S(2)}, u32[]{:S(2)}) collective-permute-start(bf16[96,512]{1,0:T(8,128)(2,1)S(1)} %slice.57), channel_id=1, source_target_pairs={{0,24},{8,0},{16,8},{24,16},{32,56},{40,32},{48,40},{56,48},{64,88... | collective-permute-start | bytes 294920 | tf_op jit(solution)/shard_map/ppermute | solution.py:41
  35.7 15.7 %collective-permute-start.8 = (bf16[704,512]{1,0:T(8,128)(2,1)}, bf16[704,512]{1,0:T(8,128)(2,1)S(1)}, u32[]{:S(2)}, u32[]{:S(2)}) collective-permute-start(bf16[704,512]{1,0:T(8,128)(2,1)} %select_slots.1.refs_0_.refs_8_.refs_16_), channel_id=1, source_target_pairs={{0,2},{1,3},{2,4},{3,5},{4,6},{5,7},{6,0},{7,1},{8,10},{9,11},{10,... | collective-permute-start | bytes 2162696 | tf_op jit(solution)/shard_map/ppermute | solution.py:45
  37.1 14.4 %collective-permute-start.10 = (bf16[704,512]{1,0:T(8,128)(2,1)}, bf16[704,512]{1,0:T(8,128)(2,1)S(1)}, u32[]{:S(2)}, u32[]{:S(2)}) collective-permute-start(bf16[704,512]{1,0:T(8,128)(2,1)} %select_slots.1.refs_0_.refs_8_.refs_16_), channel_id=1, source_target_pairs={{0,6},{1,7},{2,0},{3,1},{4,2},{5,3},{6,4},{7,5},{8,14},{9,15},{10,... | collective-permute-start | bytes 2162696 | tf_op jit(solution)/shard_map/ppermute | solution.py:46
  45.1 48.7 %all-to-all-start = ((bf16[16,512,128]{2,1,0:T(8,128)(2,1)}), bf16[16,512,128]{2,1,0:T(8,128)(2,1)}, u32[]{:S(2)}, u32[]{:S(2)}) async-start(bf16[16,512,128]{2,1,0:T(8,128)(2,1)} %bitcast.20), calls=%async_computation | async-start | bytes 4194304 | tf_op jit(solution)/shard_map/all_to_all | solution.py:576
  51.4 15.3 %collective-permute-start.12 = (bf16[352,512]{1,0:T(8,128)(2,1)S(1)}, bf16[352,512]{1,0:T(8,128)(2,1)S(1)}, u32[]{:S(2)}, u32[]{:S(2)}) collective-permute-start(bf16[352,512]{1,0:T(8,128)(2,1)S(1)} %slice.58), channel_id=1, source_target_pairs={{0,2},{1,3},{2,4},{3,5},{4,6},{5,7},{6,0},{7,1},{8,10},{9,11},{10,... | collective-permute-start | bytes 1081352 | tf_op jit(solution)/shard_map/ppermute | solution.py:41
  52.3 14.4 %collective-permute-start.13 = (bf16[352,512]{1,0:T(8,128)(2,1)}, bf16[352,512]{1,0:T(8,128)(2,1)}, u32[]{:S(2)}, u32[]{:S(2)}) collective-permute-start(bf16[352,512]{1,0:T(8,128)(2,1)} %slice.59), channel_id=1, source_target_pairs={{0,6},{1,7},{2,0},{3,1},{4,2},{5,3},{6,4},{7,5},{8,14},{9,15},{10,... | collective-permute-start | bytes 1081352 | tf_op jit(solution)/shard_map/ppermute | solution.py:41
  58.1 17.9 %collective-permute-start.7 = (bf16[704,512]{1,0:T(8,128)(2,1)S(1)}, bf16[704,512]{1,0:T(8,128)(2,1)}, u32[]{:S(2)}, u32[]{:S(2)}) collective-permute-start(bf16[704,512]{1,0:T(8,128)(2,1)S(1)} %copy-done), channel_id=1, source_target_pairs={{0,1},{1,0},{2,3},{3,2},{4,5},{5,4},{6,7},{7,6},{8,9},{9,8},{10,11... | collective-permute-start | bytes 2162696 | tf_op jit(solution)/shard_map/ppermute | solution.py:51
  66.1 9.9 %collective-permute-start.11 = (bf16[704,512]{1,0:T(8,128)(2,1)S(1)}, bf16[704,512]{1,0:T(8,128)(2,1)}, u32[]{:S(2)}, u32[]{:S(2)}) collective-permute-start(bf16[704,512]{1,0:T(8,128)(2,1)S(1)} %collective-permute-done.10.refs_4_.refs_12_.refs_20_), channel_id=1, source_target_pairs={{0,1},{1,0},{2,3},{3,2},{4,5},{5,4},{6,7},{7,6},{8,9},{9,8},{10,11... | collective-permute-start | bytes 2162696 | tf_op jit(solution)/shard_map/ppermute | solution.py:51
  66.2 9.8 %collective-permute-start.9 = (bf16[704,512]{1,0:T(8,128)(2,1)S(1)}, bf16[704,512]{1,0:T(8,128)(2,1)}, u32[]{:S(2)}, u32[]{:S(2)}) collective-permute-start(bf16[704,512]{1,0:T(8,128)(2,1)S(1)} %collective-permute-done.8.refs_2_.refs_10_.refs_18_), channel_id=1, source_target_pairs={{0,1},{1,0},{2,3},{3,2},{4,5},{5,4},{6,7},{7,6},{8,9},{9,8},{10,11... | collective-permute-start | bytes 2162696 | tf_op jit(solution)/shard_map/ppermute | solution.py:51
  67.7 8.4 %collective-permute-start.14 = (bf16[704,512]{1,0:T(8,128)(2,1)S(1)}, bf16[704,512]{1,0:T(8,128)(2,1)}, u32[]{:S(2)}, u32[]{:S(2)}) collective-permute-start(bf16[704,512]{1,0:T(8,128)(2,1)S(1)} %constant_dynamic-update-slice_fusion.4.refs_6_.refs_14_.refs_22_), channel_id=1, source_target_pairs={{0,1},{1,0},{2,3},{3,2},{4,5},{5,4},{6,7},{7,6},{8,9},{9,8},{10,11... | collective-permute-start | bytes 2162696 | tf_op jit(solution)/shard_map/ppermute | solution.py:51
  118.8 14.1 %collective-permute-start.16 = (bf16[512,512]{1,0:T(8,128)(2,1)S(1)}, bf16[512,512]{1,0:T(8,128)(2,1)S(1)}, u32[]{:S(2)}, u32[]{:S(2)}) collective-permute-start(bf16[512,512]{1,0:T(8,128)(2,1)S(1)} %get-tuple-element.36.refs_0_), channel_id=1, source_target_pairs={{0,2},{1,3},{2,4},{3,5},{4,6},{5,7},{6,0},{7,1},{8,10},{9,11},{10,... | collective-permute-start | bytes 1572872 | tf_op jit(solution)/shard_map/ppermute | solution.py:45
  120.1 12.9 %collective-permute-start.18 = (bf16[512,512]{1,0:T(8,128)(2,1)S(1)}, bf16[512,512]{1,0:T(8,128)(2,1)S(1)}, u32[]{:S(2)}, u32[]{:S(2)}) collective-permute-start(bf16[512,512]{1,0:T(8,128)(2,1)S(1)} %get-tuple-element.36.refs_0_), channel_id=1, source_target_pairs={{0,6},{1,7},{2,0},{3,1},{4,2},{5,3},{6,4},{7,5},{8,14},{9,15},{10,... | collective-permute-start | bytes 1572872 | tf_op jit(solution)/shard_map/ppermute | solution.py:46
  132.9 7.6 %collective-permute-start.20 = (bf16[256,512]{1,0:T(8,128)(2,1)S(1)}, bf16[256,512]{1,0:T(8,128)(2,1)S(1)}, u32[]{:S(2)}, u32[]{:S(2)}) collective-permute-start(bf16[256,512]{1,0:T(8,128)(2,1)S(1)} %slice.60), channel_id=1, source_target_pairs={{0,2},{1,3},{2,4},{3,5},{4,6},{5,7},{6,0},{7,1},{8,10},{9,11},{10,... | collective-permute-start | bytes 786440 | tf_op jit(solution)/shard_map/ppermute | solution.py:41
  133.0 7.5 %collective-permute-start.21 = (bf16[256,512]{1,0:T(8,128)(2,1)S(1)}, bf16[256,512]{1,0:T(8,128)(2,1)S(1)}, u32[]{:S(2)}, u32[]{:S(2)}) collective-permute-start(bf16[256,512]{1,0:T(8,128)(2,1)S(1)} %slice.61), channel_id=1, source_target_pairs={{0,6},{1,7},{2,0},{3,1},{4,2},{5,3},{6,4},{7,5},{8,14},{9,15},{10,... | collective-permute-start | bytes 786440 | tf_op jit(solution)/shard_map/ppermute | solution.py:41
  135.7 7.3 %collective-permute-start.15 = (bf16[512,512]{1,0:T(8,128)(2,1)S(1)}, bf16[512,512]{1,0:T(8,128)(2,1)S(1)}, u32[]{:S(2)}, u32[]{:S(2)}) collective-permute-start(bf16[512,512]{1,0:T(8,128)(2,1)S(1)} %get-tuple-element.36.refs_0_), channel_id=1, source_target_pairs={{0,1},{1,0},{2,3},{3,2},{4,5},{5,4},{6,7},{7,6},{8,9},{9,8},{10,11... | collective-permute-start | bytes 1572872 | tf_op jit(solution)/shard_map/ppermute | solution.py:51
  137.8 5.2 %collective-permute-start.17 = (bf16[512,512]{1,0:T(8,128)(2,1)S(1)}, bf16[512,512]{1,0:T(8,128)(2,1)S(1)}, u32[]{:S(2)}, u32[]{:S(2)}) collective-permute-start(bf16[512,512]{1,0:T(8,128)(2,1)S(1)} %collective-permute-done.16.refs_2_), channel_id=1, source_target_pairs={{0,1},{1,0},{2,3},{3,2},{4,5},{5,4},{6,7},{7,6},{8,9},{9,8},{10,11... | collective-permute-start | bytes 1572872 | tf_op jit(solution)/shard_map/ppermute | solution.py:51
  137.8 5.2 %collective-permute-start.19 = (bf16[512,512]{1,0:T(8,128)(2,1)S(1)}, bf16[512,512]{1,0:T(8,128)(2,1)S(1)}, u32[]{:S(2)}, u32[]{:S(2)}) collective-permute-start(bf16[512,512]{1,0:T(8,128)(2,1)S(1)} %collective-permute-done.18.refs_4_), channel_id=1, source_target_pairs={{0,1},{1,0},{2,3},{3,2},{4,5},{5,4},{6,7},{7,6},{8,9},{9,8},{10,11... | collective-permute-start | bytes 1572872 | tf_op jit(solution)/shard_map/ppermute | solution.py:51
  (26 other events, 523.9 us)
Sparse Core Ops, SparseCore 0:
  10.8 89.4 all-gather.4
  102.5 51.9 all-gather.6

commit v10 on v8

--- a/solution.py
+++ b/solution.py
@@ -470,9 +470,8 @@
     copies = []
     for b in range(8):
         rows = weight_ref.at[pl.ds(2 * order[b], 2), pl.ds(0, 256)]
-        copies.append(pltpu.make_async_copy(rows, w.at[b // 2, pl.ds(b % 2 * 2, 2)], sems.at[b]))
-        side = pl.ds(b % 2 * FEAT, FEAT)
-        copies.append(pltpu.make_async_copy(blocks[b], x.at[b // 2, :, side], sems.at[8 + b]))
+        copies.append(pltpu.make_async_copy(rows, w.at[b], sems.at[b]))
+        copies.append(pltpu.make_async_copy(blocks[b], x.at[b], sems.at[8 + b]))
     last = [
         pltpu.make_async_copy(hidden_hbm, hidden, sems.at[16]),
         pltpu.make_async_copy(low_hbm, low_ref, sems.at[17]),
@@ -483,10 +482,10 @@
         last.append(pltpu.make_async_copy(rows, oup.at[pl.ds(p * 16, 16)], sems.at[18 + p]))
     for copy in copies + last:
         copy.start()
-    for i in range(4):
-        for copy in copies[4 * i : 4 * i + 4]:
+    for i in range(8):
+        for copy in copies[2 * i : 2 * i + 2]:
             copy.wait()
-        part = jnp.dot(x[i], w[i].reshape(2 * FEAT, FEAT), preferred_element_type=F32)
+        part = jnp.dot(x[i], w[i].reshape(FEAT, FEAT), preferred_element_type=F32)
         if i == 0:
             acc[...] = part
         else:
@@ -509,8 +508,8 @@
             in_specs=[hbm] * 11,
             out_specs=whole(TOK, FEAT),
             scratch_shapes=[
-                pltpu.VMEM((4, TOK, 2 * FEAT), BF),
-                pltpu.VMEM((4, 4, 256, FEAT), BF),
+                pltpu.VMEM((8, TOK, FEAT), BF),
+                pltpu.VMEM((8, 2, 256, FEAT), BF),
                 pltpu.VMEM((64, FEAT), BF),
                 pltpu.VMEM((TOK, 256), BF),
                 pltpu.VMEM((TOK, FEAT), BF),

time: 165 us -> 165 us (level)
  transfers between devices with their start and end apart: 20 -> 20, of which waited for: 7 -> 7; matrix products, arithmetic and copies ran while one was open for 6% -> 6% of each run, Pallas kernels for 22% -> 23%
where the time goes in v10:
time: 165 us; the launch traced here: 164 us
  Pallas kernels  46.7 us (28%)
  waiting for transfers between devices  45.1 us (27%)
  starting transfers between devices  38.4 us (23%)
  between operations  17 us (10%)
  local copies, waits for them, and re-layouts  10.2 us (6%)
  other arithmetic  7.08 us (4%)
    pallas_call x1, Pallas kernels, attention(): pl.pallas_call(attention_body, out_shape=(jax.ShapeDtypeStruct((TOK, FEAT...  19.2 us
    ppermute x2, waiting for transfers between devices, ring4(): before = lax.ppermute(block, axis, perm(1))  17.9 us
    all_gather x1, waiting for transfers between devices, on_device(): weight = lax.all_gather(wide, 'row', axis=0)  17.5 us
    ppermute x8, starting transfers between devices, swap(): return lax.ppermute(block, 'col', SWAP)  12.7 us
    all_to_all x1, starting transfers between devices, on_device(): slots = lax.all_to_all(slots, 'row', 0, 0)  7.6 us
    pallas_call x1, Pallas kernels, norm_low(): pl.pallas_call(norm_body, out_shape=(pltpu.HBM((4, TOK, 2 * FEAT), BF), p...  7.47 us
    unnamed x47, local copies, waits for them, and re-layouts  7.06 us
    pallas_call x1, Pallas kernels, output(): pl.pallas_call(out_body, out_shape=jax.ShapeDtypeStruct((TOK, FEAT), BF),...  5.77 us
  transfers between devices with their start and end apart: 20, of which 7 were waited for; matrix products, arithmetic and copies ran while one was open for 6% of the time, Pallas kernels for 23%

profile of v10, /device:TPU:1, one launch (start us, length us, event | category | flops | bytes accessed | tf_op | source)
XLA Modules:
  0.0 164.4 jit_solution(5502069781268675737)
XLA Ops:
  7.9 2.9 %pack.1 = (bf16[272,768]{1,0:T(8,128)(2,1)}, bf16[272,512]{1,0:T(8,128)(2,1)}, bf16[16,48,512]{2,1,0:T(8,128)(2,1)}) custom-call(s32[2]{0:T(128)} %pad_add_fusion.me_ref, bf16[256,768]{1,0:T(8,128)(2,1)} %qkv_ref.1, bf16[256,512]{1,0:T(8,128)(2,1)} %wo_ref.1, bf16[1,16,640]{2,1,0:T(8,128)(2,1)} %up_ref.1, bf16[1,16,4096]{2,1,0:T(8,128)(2,1)} %oup_ref.1, ...), custom_call_target="tpu_custom_call" | custom-call | tf_op jit(solution)/shard_map/pack/pallas_call | solution.py:144
  10.8 7.6 %all-to-all-start = ((bf16[16,48,512]{2,1,0:T(8,128)(2,1)}), bf16[16,48,512]{2,1,0:T(8,128)(2,1)S(1)}, u32[]{:S(2)}, u32[]{:S(2)}) async-start(bf16[16,48,512]{2,1,0:T(8,128)(2,1)} %get-tuple-element.26), calls=%async_computation | async-start | bytes 1572864 | tf_op jit(solution)/shard_map/all_to_all | solution.py:558
  21.7 4.5 %pick_pages.1 = (bf16[16,2,2,128,128]{4,3,2,1,0:T(8,128)(2,1)S(1)}, s32[16]{0:T(128)S(1)}) custom-call(s32[2]{0:T(128)S(1)} %copy-done.13, s32[256,1]{1,0:T(8,128)S(1)} %copy.20.owner_ref, s32[256]{0:T(256)S(1)} %copy-done.17, bf16[8,2,128,128]{3,2,1,0:T(8,128)(2,1)S(1)} %copy-done.10), custom_call_target="tpu_custom_call" | custom-call | tf_op jit(solution)/shard_map/pick_pages/pallas_call | solution.py:115
  27.5 3.6 %all-to-all-done.slots_ref = bf16[16,48,512]{2,1,0:T(8,128)(2,1)S(1)} async-done(((bf16[16,48,512]{2,1,0:T(8,128)(2,1)}), bf16[16,48,512]{2,1,0:T(8,128)(2,1)S(1)}, u32[]{:S(2)}, u32[]{:S(2)}) %all-to-all-start) | async-done | bytes 786464 | tf_op jit(solution)/shard_map/all_to_all | solution.py:558
  32.0 3.1 %select_slots.1.refs_0_.refs_8_.refs_16_ = bf16[704,512]{1,0:T(8,128)(2,1)} custom-call(s32[4]{0:T(128)} %adapter_ref.5, s32[16]{0:T(128)} %position_ref.5, bf16[16,48,512]{2,1,0:T(8,128)(2,1)} %copy-done.18, bf16[512,512]{1,0:T(8,128)(2,1)} %refs_10_.1), custom_call_target="tpu_custom_call" | custom-call | tf_op jit(solution)/shard_map/select_slots/pallas_call | solution.py:180
  35.1 1.8 %collective-permute-start.1 = (bf16[704,512]{1,0:T(8,128)(2,1)}, bf16[704,512]{1,0:T(8,128)(2,1)S(1)}, u32[]{:S(2)}, u32[]{:S(2)}) collective-permute-start(bf16[704,512]{1,0:T(8,128)(2,1)} %select_slots.1.refs_0_.refs_8_.refs_16_), channel_id=1, source_target_pairs={{0,2},{1,3},{2,4},{3,5},{4,6},{5,7},{6,0},{7,1},{8,10},{9,11},{10,... | collective-permute-start | bytes 2162696 | tf_op jit(solution)/shard_map/ppermute | solution.py:45
  36.9 2.5 %collective-permute-start.3 = (bf16[704,512]{1,0:T(8,128)(2,1)}, bf16[704,512]{1,0:T(8,128)(2,1)S(1)}, u32[]{:S(2)}, u32[]{:S(2)}) collective-permute-start(bf16[704,512]{1,0:T(8,128)(2,1)} %select_slots.1.refs_0_.refs_8_.refs_16_), channel_id=1, source_target_pairs={{0,6},{1,7},{2,0},{3,1},{4,2},{5,3},{6,4},{7,5},{8,14},{9,15},{10,... | collective-permute-start | bytes 2162696 | tf_op jit(solution)/shard_map/ppermute | solution.py:46
  39.4 5.5 %all-to-all-start.1 = ((bf16[16,512,128]{2,1,0:T(8,128)(2,1)}), bf16[16,512,128]{2,1,0:T(8,128)(2,1)}, u32[]{:S(2)}, u32[]{:S(2)}) async-start(bf16[16,512,128]{2,1,0:T(8,128)(2,1)} %bitcast.16), calls=%async_computation.1 | async-start | bytes 4194304 | tf_op jit(solution)/shard_map/all_to_all | solution.py:563
  45.6 6.3 %collective-permute-done.1.refs_2_.refs_10_.refs_18_ = bf16[704,512]{1,0:T(8,128)(2,1)S(1)} collective-permute-done((bf16[704,512]{1,0:T(8,128)(2,1)}, bf16[704,512]{1,0:T(8,128)(2,1)S(1)}, u32[]{:S(2)}, u32[]{:S(2)}) %collective-permute-start.1) | collective-permute-done | bytes 720928 | tf_op jit(solution)/shard_map/ppermute | solution.py:45
  52.7 2.7 %collective-permute-start.6 = (bf16[352,512]{1,0:T(8,128)(2,1)}, bf16[352,512]{1,0:T(8,128)(2,1)}, u32[]{:S(2)}, u32[]{:S(2)}) collective-permute-start(bf16[352,512]{1,0:T(8,128)(2,1)} %slice.49), channel_id=1, source_target_pairs={{0,6},{1,7},{2,0},{3,1},{4,2},{5,3},{6,4},{7,5},{8,14},{9,15},{10,... | collective-permute-start | bytes 1081352 | tf_op jit(solution)/shard_map/ppermute | solution.py:41
  58.6 5.9 %collective-permute-start = (bf16[704,512]{1,0:T(8,128)(2,1)S(1)}, bf16[704,512]{1,0:T(8,128)(2,1)}, u32[]{:S(2)}, u32[]{:S(2)}) collective-permute-start(bf16[704,512]{1,0:T(8,128)(2,1)S(1)} %copy-done), channel_id=1, source_target_pairs={{0,1},{1,0},{2,3},{3,2},{4,5},{5,4},{6,7},{7,6},{8,9},{9,8},{10,11... | collective-permute-start | bytes 2162696 | tf_op jit(solution)/shard_map/ppermute | solution.py:51
  66.1 1.8 %collective-permute-start.7 = (bf16[704,512]{1,0:T(8,128)(2,1)S(1)}, bf16[704,512]{1,0:T(8,128)(2,1)}, u32[]{:S(2)}, u32[]{:S(2)}) collective-permute-start(bf16[704,512]{1,0:T(8,128)(2,1)S(1)} %constant_dynamic-update-slice_fusion.refs_6_.refs_14_.refs_22_), channel_id=1, source_target_pairs={{0,1},{1,0},{2,3},{3,2},{4,5},{5,4},{6,7},{7,6},{8,9},{9,8},{10,11... | collective-permute-start | bytes 2162696 | tf_op jit(solution)/shard_map/ppermute | solution.py:51
  72.1 2.2 %sine_select_fusion.rope_hbm = f32[512,128]{1,0:T(8,128)} fusion(f32[128]{0:T(128)S(1)} %pad_maximum_fusion, s32[512]{0:T(512)S(1)} %get-tuple-element.56, s32[512]{0:T(512)S(1)} %get-tuple-element.57, s32[512]{0:T(512)S(1)} %get-tuple-element.58, s32[512]{0:T(512)S(1)} %get-tuple-element.59, pred[512]{0:T(512)(128)(4,1)S(1)} %get-tuple-element.52, ...), kind=kLoop, calls=%fused_computation | loop fusion | flops 458752 | bytes 273024 | tf_op jit(solution)/shard_map/jit(_where)/select_n | solution.py:576
  74.3 7.5 %norm_low.1 = (bf16[4,512,1024]{2,1,0:T(8,128)(2,1)}, bf16[512,128]{1,0:T(8,128)(2,1)}, bf16[8,2,256,128]{3,2,1,0:T(8,128)(2,1)}) custom-call(s32[2]{0:T(128)S(1)} %copy-done.14, s32[1,4]{1,0:T(1,128)S(1)} %copy-done.11, bf16[704,512]{1,0:T(8,128)(2,1)S(1)} %copy-done, bf16[704,512]{1,0:T(8,128)(2,1)} %collective-permute-done.refs_1_.refs_9_.refs_17_, ...), custom_call_target="tpu_custom_call" | custom-call | tf_op jit(solution)/shard_map/norm_low/pallas_call | solution.py:223
  81.8 17.5 %all-gather.5.cloned.1.call-done = bf16[4352,768]{1,0:T(8,128)(2,1)} async-done(((bf16[272,768]{1,0:T(8,128)(2,1)}), bf16[4352,768]{1,0:T(8,128)(2,1)}) %all-gather.5.cloned.1.call-update) | async-done | bytes 6684688 | tf_op jit(solution)/shard_map/all_gather | solution.py:557
  99.3 19.2 %attention.1 = (bf16[512,512]{1,0:T(8,128)(2,1)S(1)}, bf16[2,512,128]{2,1,0:T(8,128)(2,1)}) custom-call(s32[1,4]{1,0:T(1,128)S(1)} %copy-done.11, s32[4]{0:T(128)S(1)} %copy-done.12, s32[16]{0:T(128)S(1)} %get-tuple-element.23.place_ref, s32[4]{0:T(128)S(1)} %copy-done.15, s32[16]{0:T(128)S(1)} %copy-done.16, ...), custom_call_target="tpu_custom_call" | custom-call | tf_op jit(solution)/shard_map/attention/pallas_call | solution.py:402
  118.7 2.7 %collective-permute-start.11 = (bf16[512,512]{1,0:T(8,128)(2,1)S(1)}, bf16[512,512]{1,0:T(8,128)(2,1)S(1)}, u32[]{:S(2)}, u32[]{:S(2)}) collective-permute-start(bf16[512,512]{1,0:T(8,128)(2,1)S(1)} %get-tuple-element.38.refs_0_), channel_id=1, source_target_pairs={{0,6},{1,7},{2,0},{3,1},{4,2},{5,3},{6,4},{7,5},{8,14},{9,15},{10,... | collective-permute-start | bytes 1572872 | tf_op jit(solution)/shard_map/ppermute | solution.py:46
  121.3 11.6 %collective-permute-done.9.refs_2_ = bf16[512,512]{1,0:T(8,128)(2,1)S(1)} collective-permute-done((bf16[512,512]{1,0:T(8,128)(2,1)S(1)}, bf16[512,512]{1,0:T(8,128)(2,1)S(1)}, u32[]{:S(2)}, u32[]{:S(2)}) %collective-permute-start.9) | collective-permute-done | bytes 524320 | tf_op jit(solution)/shard_map/ppermute | solution.py:45
  133.1 2.7 %collective-permute-start.14 = (bf16[256,512]{1,0:T(8,128)(2,1)S(1)}, bf16[256,512]{1,0:T(8,128)(2,1)S(1)}, u32[]{:S(2)}, u32[]{:S(2)}) collective-permute-start(bf16[256,512]{1,0:T(8,128)(2,1)S(1)} %slice.51), channel_id=1, source_target_pairs={{0,6},{1,7},{2,0},{3,1},{4,2},{5,3},{6,4},{7,5},{8,14},{9,15},{10,... | collective-permute-start | bytes 786440 | tf_op jit(solution)/shard_map/ppermute | solution.py:41
  135.8 1.9 %collective-permute-start.8 = (bf16[512,512]{1,0:T(8,128)(2,1)S(1)}, bf16[512,512]{1,0:T(8,128)(2,1)S(1)}, u32[]{:S(2)}, u32[]{:S(2)}) collective-permute-start(bf16[512,512]{1,0:T(8,128)(2,1)S(1)} %get-tuple-element.38.refs_0_), channel_id=1, source_target_pairs={{0,1},{1,0},{2,3},{3,2},{4,5},{5,4},{6,7},{7,6},{8,9},{9,8},{10,11... | collective-permute-start | bytes 1572872 | tf_op jit(solution)/shard_map/ppermute | solution.py:51
  138.1 2.7 %collective-permute-done.13 = bf16[256,512]{1,0:T(8,128)(2,1)S(1)} collective-permute-done((bf16[256,512]{1,0:T(8,128)(2,1)S(1)}, bf16[256,512]{1,0:T(8,128)(2,1)S(1)}, u32[]{:S(2)}, u32[]{:S(2)}) %collective-permute-start.13) | collective-permute-done | bytes 262176 | tf_op jit(solution)/shard_map/ppermute | solution.py:41
  140.9 2.2 %collective-permute-start.15 = (bf16[512,512]{1,0:T(8,128)(2,1)S(1)}, bf16[512,512]{1,0:T(8,128)(2,1)S(1)}, u32[]{:S(2)}, u32[]{:S(2)}) collective-permute-start(bf16[512,512]{1,0:T(8,128)(2,1)S(1)} %constant_dynamic-update-slice_fusion.2.refs_6_), channel_id=1, source_target_pairs={{0,1},{1,0},{2,3},{3,2},{4,5},{5,4},{6,7},{7,6},{8,9},{9,8},{10,11... | collective-permute-start | bytes 1572872 | tf_op jit(solution)/shard_map/ppermute | solution.py:51
  144.6 3.7 %output_low.1.refs_8_ = bf16[512,256]{1,0:T(8,128)(2,1)} custom-call(s32[1,4]{1,0:T(1,128)S(1)} %copy-done.11, bf16[512,512]{1,0:T(8,128)(2,1)S(1)} %get-tuple-element.38.refs_0_, bf16[512,512]{1,0:T(8,128)(2,1)S(1)} %collective-permute-done.8.refs_1_, bf16[512,512]{1,0:T(8,128)(2,1)S(1)} %collective-permute-done.9.refs_2_, ...), custom_call_target="tpu_custom_call" | custom-call | tf_op jit(solution)/shard_map/output_low/pallas_call | solution.py:452
  151.8 5.8 %output.1 = bf16[512,512]{1,0:T(8,128)(2,1)} custom-call(s32[2]{0:T(128)S(1)} %copy-done.14, s32[4]{0:T(128)S(1)} %copy-done.15, s32[16]{0:T(128)S(1)} %copy-done.16, bf16[512,512]{1,0:T(8,128)(2,1)} %copy-done.5, bf16[512,512]{1,0:T(8,128)(2,1)} %copy-done.6, bf16[512,512]{1,0:T(8,128)(2,1)} %copy-done.1, bf16[512,512]{1,0:T(8,128)(2,1)} %copy-done.7, ...), custom_call_target="tpu_custom_call" | custom-call | tf_op jit(solution)/shard_map/output/pallas_call | solution.py:502
  (91 shorter events, 19.8 us)
Async XLA Ops:
  7.2 92.2 %all-gather.5.cloned.1.call-start = ((), (), s32[]{:S(2)}) async-start(), calls=%async_computation.2 | async-start | bytes 7102464 | tf_op jit(solution)/shard_map/all_gather | solution.py:557
  10.8 20.3 %all-to-all-start = ((bf16[16,48,512]{2,1,0:T(8,128)(2,1)}), bf16[16,48,512]{2,1,0:T(8,128)(2,1)S(1)}, u32[]{:S(2)}, u32[]{:S(2)}) async-start(bf16[16,48,512]{2,1,0:T(8,128)(2,1)} %get-tuple-element.26), calls=%async_computation | async-start | bytes 1572864 | tf_op jit(solution)/shard_map/all_to_all | solution.py:558
  18.4 133.3 %all-gather.7.cloned.1.call-start = ((), (), s32[]{:S(2)}) async-start(), calls=%async_computation.3 | async-start | bytes 4734976 | tf_op jit(solution)/shard_map/all_gather | solution.py:562
  32.0 35.9 %copy-start.20 = (bf16[128]{0:T(256)(128)(2,1)S(1)}, bf16[128]{0:T(256)(128)(2,1)}, u32[]{:S(2)}) copy-start(bf16[128]{0:T(256)(128)(2,1)} %param.20) | copy-start | bytes 772
  32.0 35.9 %copy-start.21 = (bf16[128]{0:T(256)(128)(2,1)S(1)}, bf16[128]{0:T(256)(128)(2,1)}, u32[]{:S(2)}) copy-start(bf16[128]{0:T(256)(128)(2,1)} %param.19) | copy-start | bytes 772
  32.0 36.5 %copy-start.12 = (s32[4]{0:T(128)S(1)}, s32[4]{0:T(128)}, u32[]{:S(2)}) copy-start(s32[4]{0:T(128)} %cache_ref.1) | copy-start | bytes 52
  35.1 39.2 %copy-start.14 = (s32[2]{0:T(128)S(1)}, s32[2]{0:T(128)}, u32[]{:S(2)}) copy-start(s32[2]{0:T(128)} %pad_add_fusion.me_ref) | copy-start | bytes 28
  35.1 16.7 %collective-permute-start.1 = (bf16[704,512]{1,0:T(8,128)(2,1)}, bf16[704,512]{1,0:T(8,128)(2,1)S(1)}, u32[]{:S(2)}, u32[]{:S(2)}) collective-permute-start(bf16[704,512]{1,0:T(8,128)(2,1)} %select_slots.1.refs_0_.refs_8_.refs_16_), channel_id=1, source_target_pairs={{0,2},{1,3},{2,4},{3,5},{4,6},{5,7},{6,0},{7,1},{8,10},{9,11},{10,... | collective-permute-start | bytes 2162696 | tf_op jit(solution)/shard_map/ppermute | solution.py:45
  36.9 15.0 %collective-permute-start.3 = (bf16[704,512]{1,0:T(8,128)(2,1)}, bf16[704,512]{1,0:T(8,128)(2,1)S(1)}, u32[]{:S(2)}, u32[]{:S(2)}) collective-permute-start(bf16[704,512]{1,0:T(8,128)(2,1)} %select_slots.1.refs_0_.refs_8_.refs_16_), channel_id=1, source_target_pairs={{0,6},{1,7},{2,0},{3,1},{4,2},{5,3},{6,4},{7,5},{8,14},{9,15},{10,... | collective-permute-start | bytes 2162696 | tf_op jit(solution)/shard_map/ppermute | solution.py:46
  39.4 42.4 %all-to-all-start.1 = ((bf16[16,512,128]{2,1,0:T(8,128)(2,1)}), bf16[16,512,128]{2,1,0:T(8,128)(2,1)}, u32[]{:S(2)}, u32[]{:S(2)}) async-start(bf16[16,512,128]{2,1,0:T(8,128)(2,1)} %bitcast.16), calls=%async_computation.1 | async-start | bytes 4194304 | tf_op jit(solution)/shard_map/all_to_all | solution.py:563
  51.9 13.1 %collective-permute-start.5 = (bf16[352,512]{1,0:T(8,128)(2,1)S(1)}, bf16[352,512]{1,0:T(8,128)(2,1)S(1)}, u32[]{:S(2)}, u32[]{:S(2)}) collective-permute-start(bf16[352,512]{1,0:T(8,128)(2,1)S(1)} %slice.48), channel_id=1, source_target_pairs={{0,2},{1,3},{2,4},{3,5},{4,6},{5,7},{6,0},{7,1},{8,10},{9,11},{10,... | collective-permute-start | bytes 1081352 | tf_op jit(solution)/shard_map/ppermute | solution.py:41
  52.7 12.3 %collective-permute-start.6 = (bf16[352,512]{1,0:T(8,128)(2,1)}, bf16[352,512]{1,0:T(8,128)(2,1)}, u32[]{:S(2)}, u32[]{:S(2)}) collective-permute-start(bf16[352,512]{1,0:T(8,128)(2,1)} %slice.49), channel_id=1, source_target_pairs={{0,6},{1,7},{2,0},{3,1},{4,2},{5,3},{6,4},{7,5},{8,14},{9,15},{10,... | collective-permute-start | bytes 1081352 | tf_op jit(solution)/shard_map/ppermute | solution.py:41
  58.6 15.7 %collective-permute-start = (bf16[704,512]{1,0:T(8,128)(2,1)S(1)}, bf16[704,512]{1,0:T(8,128)(2,1)}, u32[]{:S(2)}, u32[]{:S(2)}) collective-permute-start(bf16[704,512]{1,0:T(8,128)(2,1)S(1)} %copy-done), channel_id=1, source_target_pairs={{0,1},{1,0},{2,3},{3,2},{4,5},{5,4},{6,7},{7,6},{8,9},{9,8},{10,11... | collective-permute-start | bytes 2162696 | tf_op jit(solution)/shard_map/ppermute | solution.py:51
  64.5 9.8 %collective-permute-start.2 = (bf16[704,512]{1,0:T(8,128)(2,1)S(1)}, bf16[704,512]{1,0:T(8,128)(2,1)}, u32[]{:S(2)}, u32[]{:S(2)}) collective-permute-start(bf16[704,512]{1,0:T(8,128)(2,1)S(1)} %collective-permute-done.1.refs_2_.refs_10_.refs_18_), channel_id=1, source_target_pairs={{0,1},{1,0},{2,3},{3,2},{4,5},{5,4},{6,7},{7,6},{8,9},{9,8},{10,11... | collective-permute-start | bytes 2162696 | tf_op jit(solution)/shard_map/ppermute | solution.py:51
  64.6 9.7 %collective-permute-start.4 = (bf16[704,512]{1,0:T(8,128)(2,1)S(1)}, bf16[704,512]{1,0:T(8,128)(2,1)}, u32[]{:S(2)}, u32[]{:S(2)}) collective-permute-start(bf16[704,512]{1,0:T(8,128)(2,1)S(1)} %collective-permute-done.3.refs_4_.refs_12_.refs_20_), channel_id=1, source_target_pairs={{0,1},{1,0},{2,3},{3,2},{4,5},{5,4},{6,7},{7,6},{8,9},{9,8},{10,11... | collective-permute-start | bytes 2162696 | tf_op jit(solution)/shard_map/ppermute | solution.py:51
  66.1 8.2 %collective-permute-start.7 = (bf16[704,512]{1,0:T(8,128)(2,1)S(1)}, bf16[704,512]{1,0:T(8,128)(2,1)}, u32[]{:S(2)}, u32[]{:S(2)}) collective-permute-start(bf16[704,512]{1,0:T(8,128)(2,1)S(1)} %constant_dynamic-update-slice_fusion.refs_6_.refs_14_.refs_22_), channel_id=1, source_target_pairs={{0,1},{1,0},{2,3},{3,2},{4,5},{5,4},{6,7},{7,6},{8,9},{9,8},{10,11... | collective-permute-start | bytes 2162696 | tf_op jit(solution)/shard_map/ppermute | solution.py:51
  118.6 14.3 %collective-permute-start.9 = (bf16[512,512]{1,0:T(8,128)(2,1)S(1)}, bf16[512,512]{1,0:T(8,128)(2,1)S(1)}, u32[]{:S(2)}, u32[]{:S(2)}) collective-permute-start(bf16[512,512]{1,0:T(8,128)(2,1)S(1)} %get-tuple-element.38.refs_0_), channel_id=1, source_target_pairs={{0,2},{1,3},{2,4},{3,5},{4,6},{5,7},{6,0},{7,1},{8,10},{9,11},{10,... | collective-permute-start | bytes 1572872 | tf_op jit(solution)/shard_map/ppermute | solution.py:45
  118.7 14.4 %collective-permute-start.11 = (bf16[512,512]{1,0:T(8,128)(2,1)S(1)}, bf16[512,512]{1,0:T(8,128)(2,1)S(1)}, u32[]{:S(2)}, u32[]{:S(2)}) collective-permute-start(bf16[512,512]{1,0:T(8,128)(2,1)S(1)} %get-tuple-element.38.refs_0_), channel_id=1, source_target_pairs={{0,6},{1,7},{2,0},{3,1},{4,2},{5,3},{6,4},{7,5},{8,14},{9,15},{10,... | collective-permute-start | bytes 1572872 | tf_op jit(solution)/shard_map/ppermute | solution.py:46
  132.9 7.9 %collective-permute-start.13 = (bf16[256,512]{1,0:T(8,128)(2,1)S(1)}, bf16[256,512]{1,0:T(8,128)(2,1)S(1)}, u32[]{:S(2)}, u32[]{:S(2)}) collective-permute-start(bf16[256,512]{1,0:T(8,128)(2,1)S(1)} %slice.50), channel_id=1, source_target_pairs={{0,2},{1,3},{2,4},{3,5},{4,6},{5,7},{6,0},{7,1},{8,10},{9,11},{10,... | collective-permute-start | bytes 786440 | tf_op jit(solution)/shard_map/ppermute | solution.py:41
  133.1 7.8 %collective-permute-start.14 = (bf16[256,512]{1,0:T(8,128)(2,1)S(1)}, bf16[256,512]{1,0:T(8,128)(2,1)S(1)}, u32[]{:S(2)}, u32[]{:S(2)}) collective-permute-start(bf16[256,512]{1,0:T(8,128)(2,1)S(1)} %slice.51), channel_id=1, source_target_pairs={{0,6},{1,7},{2,0},{3,1},{4,2},{5,3},{6,4},{7,5},{8,14},{9,15},{10,... | collective-permute-start | bytes 786440 | tf_op jit(solution)/shard_map/ppermute | solution.py:41
  135.8 7.3 %collective-permute-start.8 = (bf16[512,512]{1,0:T(8,128)(2,1)S(1)}, bf16[512,512]{1,0:T(8,128)(2,1)S(1)}, u32[]{:S(2)}, u32[]{:S(2)}) collective-permute-start(bf16[512,512]{1,0:T(8,128)(2,1)S(1)} %get-tuple-element.38.refs_0_), channel_id=1, source_target_pairs={{0,1},{1,0},{2,3},{3,2},{4,5},{5,4},{6,7},{7,6},{8,9},{9,8},{10,11... | collective-permute-start | bytes 1572872 | tf_op jit(solution)/shard_map/ppermute | solution.py:51
  137.6 5.5 %collective-permute-start.10 = (bf16[512,512]{1,0:T(8,128)(2,1)S(1)}, bf16[512,512]{1,0:T(8,128)(2,1)S(1)}, u32[]{:S(2)}, u32[]{:S(2)}) collective-permute-start(bf16[512,512]{1,0:T(8,128)(2,1)S(1)} %collective-permute-done.9.refs_2_), channel_id=1, source_target_pairs={{0,1},{1,0},{2,3},{3,2},{4,5},{5,4},{6,7},{7,6},{8,9},{9,8},{10,11... | collective-permute-start | bytes 1572872 | tf_op jit(solution)/shard_map/ppermute | solution.py:51
  137.6 5.5 %collective-permute-start.12 = (bf16[512,512]{1,0:T(8,128)(2,1)S(1)}, bf16[512,512]{1,0:T(8,128)(2,1)S(1)}, u32[]{:S(2)}, u32[]{:S(2)}) collective-permute-start(bf16[512,512]{1,0:T(8,128)(2,1)S(1)} %collective-permute-done.11.refs_4_), channel_id=1, source_target_pairs={{0,1},{1,0},{2,3},{3,2},{4,5},{5,4},{6,7},{7,6},{8,9},{9,8},{10,11... | collective-permute-start | bytes 1572872 | tf_op jit(solution)/shard_map/ppermute | solution.py:51
  140.9 3.7 %collective-permute-start.15 = (bf16[512,512]{1,0:T(8,128)(2,1)S(1)}, bf16[512,512]{1,0:T(8,128)(2,1)S(1)}, u32[]{:S(2)}, u32[]{:S(2)}) collective-permute-start(bf16[512,512]{1,0:T(8,128)(2,1)S(1)} %constant_dynamic-update-slice_fusion.2.refs_6_), channel_id=1, source_target_pairs={{0,1},{1,0},{2,3},{3,2},{4,5},{5,4},{6,7},{7,6},{8,9},{9,8},{10,11... | collective-permute-start | bytes 1572872 | tf_op jit(solution)/shard_map/ppermute | solution.py:51
  (18 other events, 248.6 us)
Sparse Core Ops, SparseCore 0:
  10.9 88.3 all-gather.4
  101.5 50.1 all-gather.6
